TPU v7x, 512 devices: a whole 4x8x8 slice. The times are simulated.
512 devices in a mesh: rows: 8 (over y), mp: 64 (over z, x, core).
Axes of the slice: x: 4, y: 8, z: 8, core: 2. Of those that a mesh axis runs over, the one named last changes fastest.
Arguments:
- lam_out: bfloat16 [1024, 64, 1024], P('mp', 'rows'), may hold values from -6 to 6
- q_down: bfloat16 [1024, 4096], P(None, 'rows'), may hold values from -127 to 127, as said below
- down_scale: float32 [1024], replicated, may hold values from 0.0001 to 0.001
- q_up: bfloat16 [4096, 1024], P('rows'), may hold values from -127 to 127, as said below
- up_scale: float32 [4096], P('rows'), may hold values from 5e-05 to 0.0005
- chan_slopes: bfloat16 [2, 1024, 8, 4096], P(None, 'mp', 'rows'), may hold values from -0.14941406 to 1.09375
- chan_icpt: bfloat16 [2, 1024, 8, 4096], P(None, 'mp', 'rows')
- tok_in_blocks: bfloat16 [16, 128, 128], replicated, may hold values from -0.25 to 0.25
- tok_out_blocks: bfloat16 [16, 128, 128], replicated, may hold values from -0.25 to 0.25
- block_cells: int32 [16], replicated, may hold values from 0 to 31, as said below
- tok_slopes: bfloat16 [2, 512, 8, 1024], P(None, None, 'rows', 'mp'), may hold values from -0.14941406 to 1.09375
- tok_icpt: bfloat16 [2, 512, 8, 1024], P(None, None, 'rows', 'mp')
Outputs:
- lam_in: bfloat16 [1024, 64, 1024], P(None, 'rows', 'mp')
- bias: float32 [64], P('rows')
Inputs may be any that keep to these rules, and one draw needn't show every extreme that they name: `q_down`: integer values, 8-bit signed codes; a program may carry them across devices in any exact packed form, several codes to an element. `q_up`: integer values, 8-bit signed codes; a program may carry them across devices in any exact packed form, several codes to an element. `block_cells`: 16 distinct cells; cell h * 8 + u is hidden block h and token block u.
All inputs are finite; a program needn't handle non-finite values.
Results may differ from a plain program's by a relative error of at most 0.012.
Values may be sent and summed in bfloat16 or wider, within the bound.
No kernel may reach another device: no remote copies, remote signals or barrier semaphores. Data moves between devices by JAX's collectives and lax.ppermute only.
A program may use at most 64 MiB of HBM per device.

v0:
```python
import jax
import jax.numpy as jnp
from jax import lax
from jax.sharding import PartitionSpec as P

D = 1024
CH = 4096
TH = 512
TOK = 1024
BLK = 128
SPEC = 8
IMG_DEV = 1
NHB = 4
NTB = 8


def dense_blocks(blocks, cells, count_rows, count_cols):
    row_hot = (
        cells[:, None] // count_cols == jnp.arange(count_rows, dtype=jnp.int32)[None, :]
    ).astype(jnp.float32)
    col_hot = (
        cells[:, None] % count_cols == jnp.arange(count_cols, dtype=jnp.int32)[None, :]
    ).astype(jnp.float32)
    dense = jnp.einsum("bh,bt,bij->hitj", row_hot, col_hot, blocks.astype(jnp.float32))
    return dense.reshape(count_rows * BLK, count_cols * BLK).astype(jnp.bfloat16)


def relax(pre, slopes, icpt):
    pos = jnp.maximum(pre, 0.0)
    neg = jnp.minimum(pre, 0.0)
    lower = slopes[0].astype(jnp.float32)[:, :, None, :]
    upper = slopes[1].astype(jnp.float32)[:, :, None, :]
    icpt_low = icpt[0].astype(jnp.float32)[:, :, None, :]
    icpt_high = icpt[1].astype(jnp.float32)[:, :, None, :]
    mid = pos * lower + neg * upper
    row_bias = jnp.sum(pos * icpt_low + neg * icpt_high, axis=(0, 3)).reshape(-1)
    return (mid, row_bias)


def on_device(
    lam_out,
    q_down,
    down_scale,
    q_up,
    up_scale,
    chan_slopes,
    chan_icpt,
    tok_in_blocks,
    tok_out_blocks,
    block_cells,
    tok_slopes,
    tok_icpt,
):
    tok_dev = lam_out.shape[0]
    rows_dev = lam_out.shape[1]
    rows_all = rows_dev * lax.axis_size("rows")
    offset = lax.axis_index("rows") * rows_dev
    scaled = (lam_out.astype(jnp.float32) * down_scale).astype(jnp.bfloat16)
    flat = scaled.reshape(-1, D)
    pre = jnp.dot(
        flat, lax.all_gather(q_down, "rows", axis=1, tiled=True), preferred_element_type=jnp.float32
    )
    pre = pre.reshape(tok_dev, IMG_DEV, SPEC, CH)
    mid, own_bias = relax(pre, chan_slopes, chan_icpt)
    mid_flat = mid.reshape(-1, CH)
    codes = lax.all_gather(q_up, "rows", axis=0, tiled=True)
    scales = lax.all_gather(up_scale.astype(jnp.bfloat16), "rows", axis=0, tiled=True).astype(
        jnp.float32
    )
    weighted = (mid_flat * scales).astype(jnp.bfloat16)
    summed = jnp.dot(weighted, codes, preferred_element_type=jnp.float32)
    summed = summed.reshape(tok_dev, rows_dev, D)
    chan_bias = lax.dynamic_update_slice_in_dim(
        jnp.zeros((rows_all,), jnp.float32), own_bias, offset, 0
    )
    lam_res = (lam_out.astype(jnp.float32) + summed).astype(jnp.bfloat16)
    turned = lax.all_to_all(lam_res, "mp", split_axis=2, concat_axis=0, tiled=True)
    chan_dev = turned.shape[2]
    columns = turned.reshape(TOK, rows_dev * chan_dev)
    tok_in = dense_blocks(tok_in_blocks, block_cells, NHB, NTB)
    swapped = block_cells % NTB * NHB + block_cells // NTB
    tok_out = dense_blocks(tok_out_blocks, swapped, NTB, NHB)
    tpre = lax.dot_general(
        tok_out, columns, (((0,), (0,)), ((), ())), preferred_element_type=jnp.float32
    )
    tpre = tpre.reshape(TH, IMG_DEV, SPEC, chan_dev)
    tmid, tok_bias = relax(tpre, tok_slopes, tok_icpt)
    tmid = tmid.astype(jnp.bfloat16).reshape(TH, rows_dev * chan_dev)
    back = lax.dot_general(
        tok_in, tmid, (((0,), (0,)), ((), ())), preferred_element_type=jnp.float32
    )
    lam_in = (turned.astype(jnp.float32) + back.reshape(TOK, rows_dev, chan_dev)).astype(
        jnp.bfloat16
    )
    placed = lax.dynamic_update_slice_in_dim(
        jnp.zeros((rows_all,), jnp.float32), tok_bias, offset, 0
    )
    totals = lax.psum(chan_bias + placed, ("rows", "mp"))
    bias = lax.dynamic_slice_in_dim(totals, offset, rows_dev, 0)
    return (lam_in, bias)


def solution(mesh):
    return jax.shard_map(
        on_device,
        mesh=mesh,
        in_specs=(
            P("mp", "rows", None),
            P(None, "rows"),
            P(),
            P("rows", None),
            P("rows"),
            P(None, "mp", "rows", None),
            P(None, "mp", "rows", None),
            P(),
            P(),
            P(),
            P(None, None, "rows", "mp"),
            P(None, None, "rows", "mp"),
        ),
        out_specs=(P(None, "rows", "mp"), P("rows")),
        check_vma=False,
    )
```

profile of v0, /device:TPU:1, one launch (start us, length us, event | category | flops | bytes accessed | tf_op | source)
XLA Modules:
  0.0 366.1 jit_solution(10095562536390558608)
XLA Ops:
  7.2 0.0 copy-start.9
  7.2 0.0 copy-start.10
  7.2 0.0 copy-start.2
  7.2 0.0 copy-start.4
  7.2 0.0 copy-start.5
  7.2 0.0 all-gather.4.cloned.1.call-start
  7.3 0.7 all-gather.4.cloned.1.call-update
  8.0 0.0 copy-start.1
  8.0 0.0 copy-start.8
  8.0 0.0 all-gather.6.cloned.1.call-start
  8.0 0.7 all-gather.6.cloned.1.call-update
  8.7 0.0 copy-done.9
  8.8 19.1 %all-gather = bf16[8,1,512]{2,1,0:T(2,128)(2,1)S(1)} all-gather(bf16[1,1,512]{2,1,0:T(2,128)(2,1)S(1)} %reshape.231), channel_id=1, replica_groups=mesh['rows'=8,'mp'=64] {'rows'}, dimensions={0}, use_global_device_ids=true | all-gather | bytes 9216 | tf_op jit(solution)/shard_map/all_gather | solution.py:67
  28.0 1.4 fusion.8
  29.4 0.0 copy-done.5
  29.5 82.6 %all-gather.4.cloned.1.call-done = bf16[1024,4096]{1,0:T(8,128)(2,1)} async-done(((bf16[1024,512]{1,0:T(8,128)(2,1)}), bf16[1024,4096]{1,0:T(8,128)(2,1)}) %all-gather.4.cloned.1.call-update) | async-done | bytes 8388624 | tf_op jit(solution)/shard_map/all_gather | solution.py:61
  112.1 0.0 copy-done.8
  112.1 5.1 %fusion.3 = (f32[128]{0:T(128)S(1)}, f32[128,4096]{1,0:T(8,128)S(1)}) fusion(f32[16,4096]{1,0:T(8,128)S(1)} %get-tuple-element.9, f32[16,4096]{1,0:T(8,128)S(1)} %get-tuple-element.8, bf16[1024,4096]{1,0:T(8,128)(2,1)} %all-gather.4.cloned.1.call-done, bf16[16,8,1024]{2,1,0:T(8,128)(2,1)S(1)} %copy-done.1, f32[1024]{0:T(1024)S(1)} %copy-done.8), kind=kOutput, calls=%fused_computation.4 | convolution fusion | flops 1077280640 | bytes 11276800 | tf_op jit(solution)/shard_map/dot_general | solution.py:60
  117.2 92.5 %all-gather.6.cloned.1.call-done = bf16[4096,1024]{1,0:T(8,128)(2,1)} async-done(((bf16[512,1024]{1,0:T(8,128)(2,1)}), bf16[4096,1024]{1,0:T(8,128)(2,1)}) %all-gather.6.cloned.1.call-update) | async-done | bytes 8388624 | tf_op jit(solution)/shard_map/all_gather | solution.py:66
  209.7 4.8 %fusion.12 = bf16[16,8,1024]{2,1,0:T(8,128)(2,1)S(1)} fusion(bf16[4096,1024]{1,0:T(8,128)(2,1)} %all-gather.6.cloned.1.call-done, f32[128,4096]{1,0:T(8,128)S(1)} %get-tuple-element.17, f32[4096]{0:T(1024)S(1)} %bitcast.143, f32[16,4096]{1,0:T(8,128)S(1)} %get-tuple-element.11, f32[16,4096]{1,0:T(8,128)S(1)} %get-tuple-element.10, ...), kind=kOutput, calls=%fused_computation.17 | convolution fusion | flops 1077805056 | bytes 11550720 | tf_op jit(solution)/shard_map/dot_general | solution.py:71
  214.6 1.7 copy.36
  216.3 2.9 reshape.241
  219.2 11.2 %all-to-all-start = ((bf16[64,2,1024]{2,1,0:T(2,128)(2,1)}), bf16[64,2,1024]{2,1,0:T(2,128)(2,1)S(1)}, u32[]{:S(2)}, u32[]{:S(2)}) async-start(bf16[64,2,1024]{2,1,0:T(2,128)(2,1)} %reshape.241), calls=%async_computation | async-start | bytes 524288 | tf_op jit(solution)/shard_map/all_to_all | solution.py:77
  230.4 2.0 copy.42
  232.3 0.0 copy-start.6
  232.4 0.0 copy-start.7
  232.4 0.5 fusion.7
  232.9 1.3 reshape.239
  234.1 0.0 copy-done.7
  234.1 0.7 bitcast_convert_fusion.6
  234.8 0.1 reduce_sum.24
  234.9 0.2 dynamic_update_slice.8
  235.2 8.4 %all-to-all-done = bf16[64,2,1024]{2,1,0:T(2,128)(2,1)S(1)} async-done(((bf16[64,2,1024]{2,1,0:T(2,128)(2,1)}), bf16[64,2,1024]{2,1,0:T(2,128)(2,1)S(1)}, u32[]{:S(2)}, u32[]{:S(2)}) %all-to-all-start) | async-done | bytes 262176 | tf_op jit(solution)/shard_map/all_to_all | solution.py:77
  243.5 1.4 reshape.242
  245.0 3.4 copy.43
  248.4 3.0 reshape.221
  251.4 1.4 fusion.34
  252.8 0.1 reduce_sum.36
  252.9 0.1 reduce_sum.37
  253.0 0.2 add_dynamic-update-slice_fusion
  253.2 94.2 %psum.7 = f32[64]{0:T(128)S(1)} all-reduce(f32[64]{0:T(128)S(1)} %add_dynamic-update-slice_fusion), channel_id=1, replica_groups=mesh['rows'=8,'mp'=64] {'rows','mp'}, use_global_device_ids=true, to_apply=%region_4.5 | all-reduce | flops 64 | bytes 512 | tf_op jit(solution)/shard_map/psum | solution.py:98
  347.4 0.6 dynamic_slice.3
  348.0 2.6 copy.38
  350.6 0.1 bitcast_convert_fusion
  350.7 2.7 copy.39
  353.4 4.8 %reshape.224 = f32[1024,8,16]{0,2,1:T(8,128)S(1)} reshape(f32[64,16,8,16]{1,0,3,2:T(8,128)} %copy.39) | data formatting | bytes 1048576 | tf_op jit(solution)/shard_map/convert_element_type | solution.py:92
  358.2 0.0 copy-done
  358.2 1.0 fusion.15
  (20 shorter events, 0.2 us)
Async XLA Ops:
  7.2 1.6 copy-start.9
  7.2 20.7 %copy-start.10 = (s32[16]{0:T(128)S(1)}, s32[16]{0:T(128)}, u32[]{:S(2)}) copy-start(s32[16]{0:T(128)} %param.21) | copy-start | bytes 196
  7.2 20.8 %copy-start.2 = (bf16[16,128,128]{2,1,0:T(8,128)(2,1)S(1)}, bf16[16,128,128]{2,1,0:T(8,128)(2,1)}, u32[]{:S(2)}) copy-start(bf16[16,128,128]{2,1,0:T(8,128)(2,1)} %param.20) | copy-start | bytes 1572868
  7.2 22.2 %copy-start.4 = (bf16[2,16,1,4096]{3,1,2,0:T(8,128)(2,1)S(1)}, bf16[2,16,1,4096]{3,1,2,0:T(8,128)(2,1)}, u32[]{:S(2)}) copy-start(bf16[2,16,1,4096]{3,1,2,0:T(8,128)(2,1)} %param.18) | copy-start | bytes 786436
  7.2 22.2 %copy-start.5 = (bf16[2,16,1,4096]{3,1,2,0:T(8,128)(2,1)S(1)}, bf16[2,16,1,4096]{3,1,2,0:T(8,128)(2,1)}, u32[]{:S(2)}) copy-start(bf16[2,16,1,4096]{3,1,2,0:T(8,128)(2,1)} %param.17) | copy-start | bytes 786436
  7.2 104.9 %all-gather.4.cloned.1.call-start = ((), (), s32[]{:S(2)}) async-start(), calls=%async_computation.1 | async-start | bytes 9437184 | tf_op jit(solution)/shard_map/all_gather | solution.py:61
  8.0 104.2 %copy-start.1 = (bf16[16,8,1024]{2,1,0:T(8,128)(2,1)S(1)}, bf16[16,8,1024]{2,1,0:T(8,128)(2,1)}, u32[]{:S(2)}) copy-start(bf16[16,8,1024]{2,1,0:T(8,128)(2,1)} %param.12) | copy-start | bytes 786436
  8.0 104.1 %copy-start.8 = (f32[1024]{0:T(1024)S(1)}, f32[1024]{0:T(1024)}, u32[]{:S(2)}) copy-start(f32[1024]{0:T(1024)} %param.14) | copy-start | bytes 12292
  8.0 201.8 %all-gather.6.cloned.1.call-start = ((), (), s32[]{:S(2)}) async-start(), calls=%async_computation.2 | async-start | bytes 9437184 | tf_op jit(solution)/shard_map/all_gather | solution.py:66
  219.2 13.2 %copy-start.3 = (bf16[16,128,128]{2,1,0:T(8,128)(2,1)S(1)}, bf16[16,128,128]{2,1,0:T(8,128)(2,1)}, u32[]{:S(2)}) copy-start(bf16[16,128,128]{2,1,0:T(8,128)(2,1)} %param.19) | copy-start | bytes 1572868
  219.2 24.3 %all-to-all-start = ((bf16[64,2,1024]{2,1,0:T(2,128)(2,1)}), bf16[64,2,1024]{2,1,0:T(2,128)(2,1)S(1)}, u32[]{:S(2)}, u32[]{:S(2)}) async-start(bf16[64,2,1024]{2,1,0:T(2,128)(2,1)} %reshape.241), calls=%async_computation | async-start | bytes 524288 | tf_op jit(solution)/shard_map/all_to_all | solution.py:77
  232.3 1.8 copy-start.6
  232.4 1.8 copy-start.7
  353.4 4.8 %copy-start = (bf16[512,1024,1]{1,0,2:T(8,128)(2,1)S(1)}, bf16[512,1024,1]{1,0,2:T(8,128)(2,1)}, u32[]{:S(2)}) copy-start(bf16[512,1024,1]{1,0,2:T(8,128)(2,1)} %reshape.239) | copy-start | bytes 3145732
Sparse Core Ops, SparseCore 0:
  10.1 101.9 all-gather.3
  114.2 95.5 all-gather.5
where the time goes:
time: 367 us; the launch traced here: 366 us
  waiting for transfers between devices  185 us (50%)
  blocking collectives  113 us (31%)
  local copies, waits for them, and re-layouts  26.8 us (7%)
  matrix products  14.3 us (4%)
  between operations  14.3 us (4%)
  starting transfers between devices  11.2 us (3%)
    psum x1, blocking collectives, on_device(): totals = lax.psum(chan_bias + placed, ('rows', 'mp'))  94.2 us
    all_gather x1, waiting for transfers between devices, on_device(): codes = lax.all_gather(q_up, 'rows', axis=0, tiled=True)  92.5 us
    all_gather x1, waiting for transfers between devices, on_device(): lax.all_gather(q_down, 'rows', axis=1, tiled=True)  82.6 us
    all_gather x1, blocking collectives, on_device(): lax.all_gather(up_scale.astype(jnp.bfloat16), 'rows', axis=0, tiled=True)  19.1 us
    all_to_all x1, starting transfers between devices, on_device(): lax.all_to_all(lam_res, 'mp', split_axis=2, concat_axis=0, tiled=True)  11.2 us
    all_to_all x1, waiting for transfers between devices, on_device(): lax.all_to_all(lam_res, 'mp', split_axis=2, concat_axis=0, tiled=True)  8.38 us
    convert_element_type x2, local copies, waits for them, and re-layouts, on_device(): turned.astype(jnp.float32) + back.reshape(TOK, rows_dev, chan_dev)  7.48 us
  transfers between devices with their start and end apart: 3, of which 3 were waited for; matrix products, arithmetic and copies ran while one was open for 3% of the time, Pallas kernels for 0%

commit v1 on v0

v1 whole, which is shorter than its diff:
```python
import functools

import jax
import jax.numpy as jnp
from jax import lax
from jax.experimental import pallas as pl
from jax.experimental.pallas import tpu as pltpu
from jax.sharding import Mesh
from jax.sharding import PartitionSpec as P

D = 1024
CH = 4096
TH = 512
TOK = 1024
BLK = 128
NB = 16
SPEC = 8
NHB = 4
NTB = 8
F32 = jnp.float32
BF16 = jnp.bfloat16
I32 = jnp.int32
MP = ("z", "x", "core")
SWAP = [(0, 1), (1, 0)]
VMEM = 32 * 1024 * 1024

PART = 256
PACKED = 136
SCALE_ONE = float(2**38)


def pack_codes(parts):
    a, b, c, d = (p.astype(F32).astype(I32) for p in parts)
    return (a & 255) | ((b & 255) << 8) | ((c & 255) << 16) | (d << 24)


def unpack_codes(words, m):
    shifted = words << (24 - 8 * m) if m < 3 else words
    return (shifted >> 24).astype(F32).astype(BF16)


def pack_kernel(core_ref, down_ref, up_ref, scale_ref, out_ref):
    down = pack_codes([down_ref[m * 256 : (m + 1) * 256, :] for m in range(4)])
    for k in range(4):
        out_ref[0:64, k * PART : (k + 1) * PART] = down[k * 64 : (k + 1) * 64, :]
    out_ref[64:128, :] = pack_codes([up_ref[m * 64 : (m + 1) * 64, :] for m in range(4)])
    scale = (scale_ref[...] * SCALE_ONE).astype(I32)
    out_ref[128:136, :] = jnp.zeros((8, D), I32)
    out_ref[128:136, 0:PART] = jnp.broadcast_to(scale, (8, PART))


def pack(core, q_down, q_up, up_scale):
    return pl.pallas_call(
        pack_kernel,
        out_shape=jax.ShapeDtypeStruct((PACKED, D), I32),
        grid_spec=pltpu.PrefetchScalarGridSpec(
            num_scalar_prefetch=1,
            grid=(1,),
            in_specs=[
                pl.BlockSpec((D, PART), lambda i, c: (0, c[0])),
                pl.BlockSpec((PART, D), lambda i, c: (c[0], 0)),
                pl.BlockSpec((1, PART), lambda i, c: (0, c[0])),
            ],
            out_specs=pl.BlockSpec((PACKED, D), lambda i, c: (0, 0)),
        ),
        compiler_params=pltpu.CompilerParams(vmem_limit_bytes=VMEM),
        name="pack",
    )(core, q_down, q_up, up_scale.reshape(1, -1))


def dense_kernel(cells_ref, in_ref, out_ref, dense_in_ref, dense_out_ref):
    dense_in_ref[...] = jnp.zeros_like(dense_in_ref)
    dense_out_ref[...] = jnp.zeros_like(dense_out_ref)
    for b in range(NB):
        h = pl.multiple_of(cells_ref[b] // NTB * BLK, BLK)
        u = pl.multiple_of(cells_ref[b] % NTB * BLK, BLK)
        dense_in_ref[pl.ds(h, BLK), pl.ds(u, BLK)] = in_ref[b]
        dense_out_ref[pl.ds(u, BLK), pl.ds(h, BLK)] = out_ref[b]


def dense_blocks(cells, in_blocks, out_blocks):
    return pl.pallas_call(
        dense_kernel,
        out_shape=(
            jax.ShapeDtypeStruct((TH, TOK), BF16),
            jax.ShapeDtypeStruct((TOK, TH), BF16),
        ),
        in_specs=[
            pl.BlockSpec(memory_space=pltpu.SMEM),
            pl.BlockSpec(memory_space=pltpu.VMEM),
            pl.BlockSpec(memory_space=pltpu.VMEM),
        ],
        out_specs=(
            pl.BlockSpec(memory_space=pltpu.VMEM),
            pl.BlockSpec(memory_space=pltpu.VMEM),
        ),
        compiler_params=pltpu.CompilerParams(vmem_limit_bytes=VMEM),
        name="dense",
    )(cells, in_blocks, out_blocks)


def relaxed(pre, lower, upper, icpt_low, icpt_high):
    pos = jnp.maximum(pre, 0.0)
    neg = jnp.minimum(pre, 0.0)
    mid = pos * lower.astype(F32) + neg * upper.astype(F32)
    return mid, pos * icpt_low.astype(F32) + neg * icpt_high.astype(F32)


def channel_kernel(
    core_ref, words_ref, lam_ref, scaled_ref, relax_ref, keep_ref, send_ref, bias_ref, acc, down, up
):
    step = pl.program_id(0)
    for m in range(4):
        codes = unpack_codes(words_ref[0:64, :], m)
        for k in range(4):
            down[m * 256 + k * 64 : m * 256 + (k + 1) * 64, :] = codes[:, k * PART : (k + 1) * PART]
        up[m * 64 : (m + 1) * 64, :] = unpack_codes(words_ref[64:128, :], m)
    pre = jnp.dot(scaled_ref[...], down[...], preferred_element_type=F32)
    pre = pre.reshape(SPEC, 32, PART)
    mid, terms = relaxed(pre, relax_ref[0, 0], relax_ref[0, 1], relax_ref[0, 2], relax_ref[0, 3])
    terms = jnp.sum(terms.reshape(SPEC, 4, 8, PART), axis=1)
    terms = terms[:, :, 0:128] + terms[:, :, 128:256]
    scale = words_ref[128:129, 0:PART].astype(F32) * (1.0 / SCALE_ONE)
    weighted = (mid.reshape(SPEC * 32, PART) * scale).astype(BF16)
    part = jnp.dot(weighted, up[...], preferred_element_type=F32)

    @pl.when(step == 0)
    def _():
        acc[...] = part + 0.5 * lam_ref[...].astype(F32)
        bias_ref[...] = terms

    @pl.when(step > 0)
    def _():
        acc[...] += part
        bias_ref[...] += terms

    @pl.when(step == pl.num_programs(0) - 1)
    def _():
        own = core_ref[0] == 0
        turned = acc[...].T.reshape(32, 2, 16, 256)
        keep_ref[...] = jnp.where(own, turned[:, 0], turned[:, 1])
        send_ref[...] = jnp.where(own, turned[:, 1], turned[:, 0]).astype(BF16)


def channel_mlp(core, words, lam, scaled, relax):
    slices = words.shape[0] // PACKED
    whole = lambda *shape: pl.BlockSpec(shape, lambda i, c: (0,) * len(shape))
    return pl.pallas_call(
        channel_kernel,
        out_shape=(
            jax.ShapeDtypeStruct((32, 16, 256), F32),
            jax.ShapeDtypeStruct((32, 16, 256), BF16),
            jax.ShapeDtypeStruct((SPEC, 8, 128), F32),
        ),
        grid_spec=pltpu.PrefetchScalarGridSpec(
            num_scalar_prefetch=1,
            grid=(slices,),
            in_specs=[
                pl.BlockSpec((PACKED, D), lambda i, c: (i, 0)),
                whole(256, D),
                whole(256, D),
                pl.BlockSpec((1, 4, 32, PART), lambda i, c: (i, 0, 0, 0)),
            ],
            out_specs=(whole(32, 16, 256), whole(32, 16, 256), whole(SPEC, 8, 128)),
            scratch_shapes=[
                pltpu.VMEM((256, D), F32),
                pltpu.VMEM((D, PART), BF16),
                pltpu.VMEM((PART, D), BF16),
            ],
        ),
        compiler_params=pltpu.CompilerParams(vmem_limit_bytes=VMEM),
        name="channel",
    )(core, words, lam, scaled, relax)


def token_kernel(got_ref, dense_ref, slopes_ref, icpt_ref, columns_ref, mid_ref, bias_ref):
    lane = lax.broadcasted_iota(I32, (16, 128), 1) // 32
    for u in range(NTB):
        for a in range(2):
            v = [got_ref[4 * u + p, :, a * 128 : (a + 1) * 128].astype(F32) for p in range(4)]
            for bit in (1, 2):
                low = (lane & bit) == 0
                new = list(v)
                for p in range(4):
                    if p & bit == 0:
                        q = p + bit
                        new[p] = jnp.where(low, v[p], pltpu.roll(v[q], 32 * bit, 1))
                        new[q] = jnp.where(low, pltpu.roll(v[p], 128 - 32 * bit, 1), v[q])
                v = new
            for q in range(4):
                r = 4 * a + q
                columns_ref[r * 16 : (r + 1) * 16, u * 128 : (u + 1) * 128] = v[q].astype(BF16)
    pre = jnp.dot(columns_ref[...], dense_ref[...], preferred_element_type=F32)
    pre = pre.reshape(SPEC, 16, TH)
    mid, terms = relaxed(pre, slopes_ref[0], slopes_ref[1], icpt_ref[0], icpt_ref[1])
    mid_ref[...] = mid.reshape(SPEC * 16, TH).astype(BF16)
    terms = terms[:, 0:8, :] + terms[:, 8:16, :]
    bias_ref[...] = sum(terms[:, :, k * 128 : (k + 1) * 128] for k in range(NHB))


def token_mlp(got, dense_out, slopes, icpt):
    return pl.pallas_call(
        token_kernel,
        out_shape=(
            jax.ShapeDtypeStruct((SPEC * 16, TOK), BF16),
            jax.ShapeDtypeStruct((SPEC * 16, TH), BF16),
            jax.ShapeDtypeStruct((SPEC, 8, 128), F32),
        ),
        compiler_params=pltpu.CompilerParams(vmem_limit_bytes=VMEM),
        name="token",
    )(got, dense_out, slopes, icpt)


def back_kernel(columns_ref, mid_ref, dense_ref, out_ref):
    back = jnp.dot(mid_ref[...], dense_ref[...], preferred_element_type=F32)
    out_ref[...] = (columns_ref[...].astype(F32) + back).astype(BF16)


def token_back(columns, mid, dense_in):
    return pl.pallas_call(
        back_kernel,
        out_shape=jax.ShapeDtypeStruct((SPEC * 16, TOK), BF16),
        compiler_params=pltpu.CompilerParams(vmem_limit_bytes=VMEM),
        name="back",
    )(columns, mid, dense_in)


def on_device(
    lam_out,
    q_down,
    down_scale,
    q_up,
    up_scale,
    chan_slopes,
    chan_icpt,
    tok_in_blocks,
    tok_out_blocks,
    block_cells,
    tok_slopes,
    tok_icpt,
):
    core = lax.axis_index("core")
    first = core == 0
    core_arg = core.astype(I32).reshape(1)
    tok_dev = lam_out.shape[0]
    slices = lax.axis_size("rows")

    packed = pack(core_arg, q_down, q_up, up_scale)
    words = lax.all_gather(packed, "rows", axis=0, tiled=True)

    def paired(own, other, axis):
        return jnp.where(
            first,
            jnp.concatenate([own, other], axis),
            jnp.concatenate([other, own], axis),
        )

    by_row = jnp.swapaxes(lam_out, 0, 1)
    lam = paired(by_row, lax.ppermute(by_row, "core", SWAP), 1).reshape(-1, D)
    scaled = (lam.astype(F32) * down_scale).astype(BF16)
    relax = jnp.concatenate([chan_slopes, chan_icpt], 0).reshape(4, tok_dev, slices, 2, PART)
    relax = jnp.transpose(relax, (3, 2, 0, 1, 4))
    own = jnp.where(first, relax[0], relax[1])
    other = lax.ppermute(jnp.where(first, relax[1], relax[0]), "core", SWAP)
    relax = paired(own, other, 2)

    dense_in, dense_out = dense_blocks(block_cells, tok_in_blocks, tok_out_blocks)
    slopes = jnp.transpose(tok_slopes, (0, 2, 3, 1)).reshape(2, 16, TH)
    icpt = jnp.transpose(tok_icpt, (0, 2, 3, 1)).reshape(2, 16, TH)

    keep, send, chan_bias = channel_mlp(core_arg, words, lam, scaled, relax)
    summed = (keep + lax.ppermute(send, "core", SWAP).astype(F32)).astype(BF16)
    got = lax.all_to_all(summed, ("z", "x"), 0, 0, tiled=True)
    columns, mid, tok_bias = token_mlp(got, dense_out, slopes, icpt)
    own_bias = jnp.sum(chan_bias + tok_bias, axis=(1, 2))
    all_bias = lax.all_to_all(
        jnp.broadcast_to(own_bias[None, :], (64, SPEC)), MP, 0, 0, tiled=True
    )
    lam_in = token_back(columns, mid, dense_in)
    lam_in = jnp.transpose(lam_in.reshape(SPEC, 16, TOK), (2, 0, 1))
    return (lam_in, jnp.sum(all_bias, axis=0))


def solution(mesh):
    axes = Mesh(mesh.devices.reshape(8, 8, 4, 2), ("rows", "z", "x", "core"))
    return jax.shard_map(
        on_device,
        mesh=axes,
        in_specs=(
            P(MP, "rows", None),
            P(None, "rows"),
            P(),
            P("rows", None),
            P("rows"),
            P(None, MP, "rows", None),
            P(None, MP, "rows", None),
            P(),
            P(),
            P(),
            P(None, None, "rows", MP),
            P(None, None, "rows", MP),
        ),
        out_specs=(P(None, "rows", MP), P("rows")),
        check_vma=False,
    )
```

time: 367 us -> 138 us (0.38)
  blocking collectives: 113 us -> 0 us
  waiting for transfers between devices: 185 us -> 72.2 us
  local copies, waits for them, and re-layouts: 26.8 us -> 6.88 us
  starting transfers between devices: 11.2 us -> 29.6 us
  matrix products: 14.3 us -> 0 us
  Pallas kernels: 0 us -> 11.2 us
    all_gather x2 -> x1, waiting for transfers between devices: 175 us -> 50.9 us  [on_device(): words = lax.all_gather(packed, 'rows', axis=0, tiled=True)]
    psum x1 -> x0, blocking collectives: 94.2 us -> none  [on_device(): totals = lax.psum(chan_bias + placed, ('rows', 'mp'))]
    all_gather x1 -> x0, blocking collectives: 19.1 us -> none  [on_device(): lax.all_gather(up_scale.astype(jnp.bfloat16), 'rows', axis=0, tiled=True)]
    dot_general x6 -> x0, matrix products: 14.3 us -> none  [the longest x1 5.1 us: on_device(): jnp.dot(flat, lax.all_gather(q_down, 'rows', axis=1, tiled=True), preferr...]
    ppermute x0 -> x3, starting transfers between devices: none -> 13.3 us  [the longest x1 8.79 us: on_device(): lam = paired(by_row, lax.ppermute(by_row, 'core', SWAP), 1).reshape(-1, D)]
    convert_element_type x5 -> x0, local copies, waits for them, and re-layouts: 12.4 us -> none  [the longest x2 7.48 us: on_device(): turned.astype(jnp.float32) + back.reshape(TOK, rows_dev, chan_dev)]
    pallas_call x0 -> x5, Pallas kernels: none -> 11.2 us  [the longest x1 7.53 us: channel_mlp(): pl.pallas_call(channel_kernel, out_shape=(jax.ShapeDtypeStruct((32, 16, 2...]
    all_to_all x1 -> x2, waiting for transfers between devices: 8.38 us -> 19.1 us  [the longest x1 10.6 us: on_device(): got = lax.all_to_all(summed, ('z', 'x'), 0, 0, tiled=True)]
  transfers between devices with their start and end apart: 3 -> 6, of which waited for: 3 -> 5; matrix products, arithmetic and copies ran while one was open for 3% -> 2% of each run, Pallas kernels for 0% -> 1%
where the time goes in v1:
time: 138 us; the launch traced here: 137 us
  waiting for transfers between devices  72.2 us (52%)
  starting transfers between devices  29.6 us (21%)
  between operations  14.2 us (10%)
  Pallas kernels  11.2 us (8%)
  local copies, waits for them, and re-layouts  6.88 us (5%)
  other arithmetic  3.09 us (2%)
    all_gather x1, waiting for transfers between devices, on_device(): words = lax.all_gather(packed, 'rows', axis=0, tiled=True)  50.9 us
    all_to_all x1, waiting for transfers between devices, on_device(): got = lax.all_to_all(summed, ('z', 'x'), 0, 0, tiled=True)  10.6 us
    all_to_all x1, starting transfers between devices, on_device(): got = lax.all_to_all(summed, ('z', 'x'), 0, 0, tiled=True)  9.9 us
    ppermute x1, starting transfers between devices, on_device(): lam = paired(by_row, lax.ppermute(by_row, 'core', SWAP), 1).reshape(-1, D)  8.79 us
    all_to_all x1, waiting for transfers between devices, on_device(): lax.all_to_all(jnp.broadcast_to(own_bias[None, :], (64, SPEC)), MP, 0, 0,...  8.46 us
    pallas_call x1, Pallas kernels, channel_mlp(): pl.pallas_call(channel_kernel, out_shape=(jax.ShapeDtypeStruct((32, 16, 2...  7.53 us
    all_to_all x1, starting transfers between devices, on_device(): lax.all_to_all(jnp.broadcast_to(own_bias[None, :], (64, SPEC)), MP, 0, 0,...  6.35 us
    unnamed x22, local copies, waits for them, and re-layouts  5.42 us
  transfers between devices with their start and end apart: 6, of which 5 were waited for; matrix products, arithmetic and copies ran while one was open for 2% of the time, Pallas kernels for 1%

profile of v1, /device:TPU:1, one launch (start us, length us, event | category | flops | bytes accessed | tf_op | source)
XLA Modules:
  0.0 137.3 jit_solution(17215851933538707655)
XLA Ops:
  7.2 0.0 all-gather.2.cloned.1.call-start
  7.2 0.0 copy-start.1
  7.2 1.2 copy-done.1
  8.4 0.0 copy-start.2
  8.4 1.2 copy-done.2
  9.7 0.0 copy-start.7
  9.7 0.7 copy-done.7
  10.3 0.0 copy-start.9
  10.3 1.2 pack.1
  11.5 0.0 copy-start.10
  11.5 0.0 all-gather.2.cloned.1.call-update
  11.5 8.8 %collective-permute-start = (bf16[8,16,1024]{2,0,1:T(8,128)(2,1)}, bf16[8,16,1024]{2,0,1:T(8,128)(2,1)S(1)}, u32[]{:S(2)}, u32[]{:S(2)}) collective-permute-start(bf16[8,16,1024]{2,0,1:T(8,128)(2,1)} %bitcast.34), channel_id=1, source_target_pairs={{0,1},{1,0},{2,3},{3,2},{4,5},{5,4},{6,7},{7,6},{8,9},{9,8},{10,11... | collective-permute-start | bytes 786440 | tf_op jit(solution)/shard_map/ppermute | solution.py:259
  20.3 1.1 pad_maximum_fusion
  21.4 0.4 reshape.40
  21.8 0.2 copy.32
  22.0 1.9 %collective-permute-start.1 = (bf16[8,4,16,256]{3,2,1,0:T(8,128)(2,1)S(1)}, bf16[8,4,16,256]{3,2,1,0:T(8,128)(2,1)S(1)}, u32[]{:S(2)}, u32[]{:S(2)}) collective-permute-start(bf16[8,4,16,256]{3,2,1,0:T(8,128)(2,1)S(1)} %get-tuple-element.19), channel_id=1, source_target_pairs={{0,1},{1,0},{2,3},{3,2},{4,5},{5,4},{6,7},{7,6},{8,9},{9,8},{10,11... | collective-permute-start | bytes 786440 | tf_op jit(solution)/shard_map/ppermute | solution.py:264
  23.9 0.0 collective-permute-done
  24.0 0.0 copy-done.9
  24.0 0.1 maximum_select_fusion
  24.1 0.3 copy.25
  24.4 1.1 collective-permute-done.1
  25.4 0.2 maximum_select_fusion.1.relax_ref
  25.7 0.0 copy-done.10
  25.7 0.0 copy-start.3
  25.7 0.0 copy-start.4
  25.7 0.0 copy-start.8
  25.7 0.1 multiply_convert_fusion.scaled_ref
  25.9 50.9 %all-gather.2.cloned.1.call-done.words_ref = s32[1088,1024]{1,0:T(8,128)} async-done(((s32[136,1024]{1,0:T(8,128)}), s32[1088,1024]{1,0:T(8,128)}) %all-gather.2.cloned.1.call-update) | async-done | bytes 4456464 | tf_op jit(solution)/shard_map/all_gather | solution.py:249
  76.8 2.3 %copy-done = s32[1088,1024]{1,0:T(8,128)S(1)} copy-done((s32[1088,1024]{1,0:T(8,128)S(1)}, s32[1088,1024]{1,0:T(8,128)}, u32[]{:S(2)}) %copy-start) | copy-done | bytes 4456472
  79.0 7.5 %channel.1 = (f32[32,16,256]{2,1,0:T(8,128)S(1)}, bf16[32,16,256]{2,1,0:T(8,128)(2,1)S(1)}, f32[8,8,128]{2,1,0:T(8,128)S(1)}) custom-call(s32[1]{0:T(128)} %bitcast.core_ref, s32[1088,1024]{1,0:T(8,128)S(1)} %copy-done, bf16[256,1024]{1,0:T(8,128)(2,1)S(1)} %bitcast.29, bf16[256,1024]{1,0:T(8,128)(2,1)S(1)} %multiply_convert_fusion.scaled_ref, ...), custom_call_target="tpu_custom_call" | custom-call | tf_op jit(solution)/shard_map/channel/pallas_call | solution.py:148
  86.6 2.6 %collective-permute-start.2 = (bf16[32,16,256]{2,1,0:T(8,128)(2,1)S(1)}, bf16[32,16,256]{2,1,0:T(8,128)(2,1)S(1)}, u32[]{:S(2)}, u32[]{:S(2)}) collective-permute-start(bf16[32,16,256]{2,1,0:T(8,128)(2,1)S(1)} %get-tuple-element.11), channel_id=1, source_target_pairs={{0,1},{1,0},{2,3},{3,2},{4,5},{5,4},{6,7},{7,6},{8,9},{9,8},{10,11... | collective-permute-start | bytes 786440 | tf_op jit(solution)/shard_map/ppermute | solution.py:272
  89.2 1.1 collective-permute-done.2
  90.3 0.8 add_convert_fusion
  91.1 9.9 %all-to-all-start = ((bf16[32,16,256]{2,1,0:T(8,128)(2,1)}), bf16[32,16,256]{2,1,0:T(8,128)(2,1)S(1)}, u32[]{:S(2)}, u32[]{:S(2)}) async-start(bf16[32,16,256]{2,1,0:T(8,128)(2,1)} %add_convert_fusion), calls=%async_computation | async-start | bytes 524288 | tf_op jit(solution)/shard_map/all_to_all | solution.py:273
  101.0 0.0 copy-done.3
  101.0 0.0 copy-done.4
  101.0 0.0 copy-done.8
  101.0 0.9 dense.1
  102.0 10.6 %all-to-all-done.got_ref = bf16[32,16,256]{2,1,0:T(8,128)(2,1)S(1)} async-done(((bf16[32,16,256]{2,1,0:T(8,128)(2,1)}), bf16[32,16,256]{2,1,0:T(8,128)(2,1)S(1)}, u32[]{:S(2)}, u32[]{:S(2)}) %all-to-all-start) | async-done | bytes 262176 | tf_op jit(solution)/shard_map/all_to_all | solution.py:273
  112.6 0.0 copy-done.5
  112.6 0.0 copy-done.6
  112.6 0.6 token_.1
  113.2 0.1 add_reduce_fusion
  113.3 0.6 broadcast_in_dim.2
  114.0 6.3 %all-to-all-start.1 = ((f32[64,1,8]{2,1,0:T(1,128)}), f32[64,1,8]{2,1,0:T(1,128)S(1)}, u32[]{:S(2)}, u32[]{:S(2)}) async-start(f32[64,1,8]{2,1,0:T(1,128)} %broadcast_in_dim.2), calls=%async_computation.1 | async-start | bytes 65536 | tf_op jit(solution)/shard_map/all_to_all | solution.py:276
  120.3 1.0 back.1
  121.4 8.5 %all-to-all-done.1 = f32[64,1,8]{2,1,0:T(1,128)S(1)} async-done(((f32[64,1,8]{2,1,0:T(1,128)}), f32[64,1,8]{2,1,0:T(1,128)S(1)}, u32[]{:S(2)}, u32[]{:S(2)}) %all-to-all-start.1) | async-done | bytes 2080 | tf_op jit(solution)/shard_map/all_to_all | solution.py:276
  129.8 0.6 reduce_sum.19
  (4 shorter events, 0.0 us)
Async XLA Ops:
  7.2 69.6 %all-gather.2.cloned.1.call-start = ((), (), s32[]{:S(2)}) async-start(), calls=%async_computation.2 | async-start | bytes 5013504 | tf_op jit(solution)/shard_map/all_gather | solution.py:249
  7.2 1.2 copy-start.1
  8.4 1.2 copy-start.2
  9.7 0.7 copy-start.7
  10.3 13.6 %copy-start.9 = (bf16[16,8,1024]{2,1,0:T(8,128)(2,1)S(1)}, bf16[16,8,1024]{2,1,0:T(8,128)(2,1)}, u32[]{:S(2)}) copy-start(bf16[16,8,1024]{2,1,0:T(8,128)(2,1)} %param.12) | copy-start | bytes 786436
  11.5 14.2 %copy-start.10 = (f32[1024]{0:T(1024)S(1)}, f32[1024]{0:T(1024)}, u32[]{:S(2)}) copy-start(f32[1024]{0:T(1024)} %param.14) | copy-start | bytes 12292
  11.5 12.4 %collective-permute-start = (bf16[8,16,1024]{2,0,1:T(8,128)(2,1)}, bf16[8,16,1024]{2,0,1:T(8,128)(2,1)S(1)}, u32[]{:S(2)}, u32[]{:S(2)}) collective-permute-start(bf16[8,16,1024]{2,0,1:T(8,128)(2,1)} %bitcast.34), channel_id=1, source_target_pairs={{0,1},{1,0},{2,3},{3,2},{4,5},{5,4},{6,7},{7,6},{8,9},{9,8},{10,11... | collective-permute-start | bytes 786440 | tf_op jit(solution)/shard_map/ppermute | solution.py:259
  22.0 3.4 %collective-permute-start.1 = (bf16[8,4,16,256]{3,2,1,0:T(8,128)(2,1)S(1)}, bf16[8,4,16,256]{3,2,1,0:T(8,128)(2,1)S(1)}, u32[]{:S(2)}, u32[]{:S(2)}) collective-permute-start(bf16[8,4,16,256]{3,2,1,0:T(8,128)(2,1)S(1)} %get-tuple-element.19), channel_id=1, source_target_pairs={{0,1},{1,0},{2,3},{3,2},{4,5},{5,4},{6,7},{7,6},{8,9},{9,8},{10,11... | collective-permute-start | bytes 786440 | tf_op jit(solution)/shard_map/ppermute | solution.py:264
  25.7 75.3 %copy-start.3 = (bf16[16,128,128]{2,1,0:T(8,128)(2,1)S(1)}, bf16[16,128,128]{2,1,0:T(8,128)(2,1)}, u32[]{:S(2)}) copy-start(bf16[16,128,128]{2,1,0:T(8,128)(2,1)} %in_ref.1) | copy-start | bytes 1572868
  25.7 75.3 %copy-start.4 = (bf16[16,128,128]{2,1,0:T(8,128)(2,1)S(1)}, bf16[16,128,128]{2,1,0:T(8,128)(2,1)}, u32[]{:S(2)}) copy-start(bf16[16,128,128]{2,1,0:T(8,128)(2,1)} %out_ref.1) | copy-start | bytes 1572868
  25.7 75.3 %copy-start.8 = (s32[16]{0:T(128)S(1)}, s32[16]{0:T(128)}, u32[]{:S(2)}) copy-start(s32[16]{0:T(128)} %cells_ref.1) | copy-start | bytes 196
  76.8 2.3 %copy-start = (s32[1088,1024]{1,0:T(8,128)S(1)}, s32[1088,1024]{1,0:T(8,128)}, u32[]{:S(2)}) copy-start(s32[1088,1024]{1,0:T(8,128)} %all-gather.2.cloned.1.call-done.words_ref) | copy-start | bytes 13369348
  79.0 33.6 %copy-start.5 = (bf16[2,512,1,16]{1,3,2,0:T(8,128)(2,1)S(1)}, bf16[2,512,1,16]{1,3,2,0:T(8,128)(2,1)}, u32[]{:S(2)}) copy-start(bf16[2,512,1,16]{1,3,2,0:T(8,128)(2,1)} %param.22) | copy-start | bytes 98308
  79.0 33.6 %copy-start.6 = (bf16[2,512,1,16]{1,3,2,0:T(8,128)(2,1)S(1)}, bf16[2,512,1,16]{1,3,2,0:T(8,128)(2,1)}, u32[]{:S(2)}) copy-start(bf16[2,512,1,16]{1,3,2,0:T(8,128)(2,1)} %param.23) | copy-start | bytes 98308
  86.6 3.7 %collective-permute-start.2 = (bf16[32,16,256]{2,1,0:T(8,128)(2,1)S(1)}, bf16[32,16,256]{2,1,0:T(8,128)(2,1)S(1)}, u32[]{:S(2)}, u32[]{:S(2)}) collective-permute-start(bf16[32,16,256]{2,1,0:T(8,128)(2,1)S(1)} %get-tuple-element.11), channel_id=1, source_target_pairs={{0,1},{1,0},{2,3},{3,2},{4,5},{5,4},{6,7},{7,6},{8,9},{9,8},{10,11... | collective-permute-start | bytes 786440 | tf_op jit(solution)/shard_map/ppermute | solution.py:272
  91.1 21.5 %all-to-all-start = ((bf16[32,16,256]{2,1,0:T(8,128)(2,1)}), bf16[32,16,256]{2,1,0:T(8,128)(2,1)S(1)}, u32[]{:S(2)}, u32[]{:S(2)}) async-start(bf16[32,16,256]{2,1,0:T(8,128)(2,1)} %add_convert_fusion), calls=%async_computation | async-start | bytes 524288 | tf_op jit(solution)/shard_map/all_to_all | solution.py:273
  114.0 15.8 %all-to-all-start.1 = ((f32[64,1,8]{2,1,0:T(1,128)}), f32[64,1,8]{2,1,0:T(1,128)S(1)}, u32[]{:S(2)}, u32[]{:S(2)}) async-start(f32[64,1,8]{2,1,0:T(1,128)} %broadcast_in_dim.2), calls=%async_computation.1 | async-start | bytes 65536 | tf_op jit(solution)/shard_map/all_to_all | solution.py:276
Sparse Core Ops, SparseCore 0:
  11.7 65.0 all-gather.1

commit v2 on v1

--- a/solution.py
+++ b/solution.py
@@ -39,13 +39,24 @@
     return (shifted >> 24).astype(F32).astype(BF16)
 
 
-def pack_kernel(core_ref, down_ref, up_ref, scale_ref, out_ref):
+def pack_kernel(core_ref, down_hbm, up_hbm, scale_hbm, out_ref, down_ref, up_ref, scale_ref, sems):
+    start = pl.multiple_of(core_ref[0] * PART, PART)
+    copies = [
+        pltpu.make_async_copy(down_hbm.at[:, pl.ds(start, PART)], down_ref, sems.at[0]),
+        pltpu.make_async_copy(up_hbm.at[pl.ds(start, PART), :], up_ref, sems.at[1]),
+        pltpu.make_async_copy(scale_hbm.at[:, pl.ds(start, PART)], scale_ref, sems.at[2]),
+    ]
+    for copy in copies:
+        copy.start()
+    out_ref[128:136, :] = jnp.zeros((8, D), I32)
+    copies[0].wait()
     down = pack_codes([down_ref[m * 256 : (m + 1) * 256, :] for m in range(4)])
     for k in range(4):
         out_ref[0:64, k * PART : (k + 1) * PART] = down[k * 64 : (k + 1) * 64, :]
+    copies[1].wait()
     out_ref[64:128, :] = pack_codes([up_ref[m * 64 : (m + 1) * 64, :] for m in range(4)])
+    copies[2].wait()
     scale = (scale_ref[...] * SCALE_ONE).astype(I32)
-    out_ref[128:136, :] = jnp.zeros((8, D), I32)
     out_ref[128:136, 0:PART] = jnp.broadcast_to(scale, (8, PART))
 
 
@@ -53,17 +64,16 @@
     return pl.pallas_call(
         pack_kernel,
         out_shape=jax.ShapeDtypeStruct((PACKED, D), I32),
-        grid_spec=pltpu.PrefetchScalarGridSpec(
-            num_scalar_prefetch=1,
-            grid=(1,),
-            in_specs=[
-                pl.BlockSpec((D, PART), lambda i, c: (0, c[0])),
-                pl.BlockSpec((PART, D), lambda i, c: (c[0], 0)),
-                pl.BlockSpec((1, PART), lambda i, c: (0, c[0])),
-            ],
-            out_specs=pl.BlockSpec((PACKED, D), lambda i, c: (0, 0)),
-        ),
-        compiler_params=pltpu.CompilerParams(vmem_limit_bytes=VMEM),
+        in_specs=[pl.BlockSpec(memory_space=pltpu.SMEM)]
+        + [pl.BlockSpec(memory_space=pltpu.HBM)] * 3,
+        out_specs=pl.BlockSpec(memory_space=pltpu.VMEM),
+        scratch_shapes=[
+            pltpu.VMEM((D, PART), BF16),
+            pltpu.VMEM((PART, D), BF16),
+            pltpu.VMEM((1, PART), F32),
+            pltpu.SemaphoreType.DMA((3,)),
+        ],
+        compiler_params=pltpu.CompilerParams(vmem_limit_bytes=60 * 1024 * 1024),
         name="pack",
     )(core, q_down, q_up, up_scale.reshape(1, -1))
 
@@ -106,71 +116,91 @@
     return mid, pos * icpt_low.astype(F32) + neg * icpt_high.astype(F32)
 
 
-def channel_kernel(
-    core_ref, words_ref, lam_ref, scaled_ref, relax_ref, keep_ref, send_ref, bias_ref, acc, down, up
-):
-    step = pl.program_id(0)
-    for m in range(4):
-        codes = unpack_codes(words_ref[0:64, :], m)
-        for k in range(4):
-            down[m * 256 + k * 64 : m * 256 + (k + 1) * 64, :] = codes[:, k * PART : (k + 1) * PART]
-        up[m * 64 : (m + 1) * 64, :] = unpack_codes(words_ref[64:128, :], m)
-    pre = jnp.dot(scaled_ref[...], down[...], preferred_element_type=F32)
-    pre = pre.reshape(SPEC, 32, PART)
-    mid, terms = relaxed(pre, relax_ref[0, 0], relax_ref[0, 1], relax_ref[0, 2], relax_ref[0, 3])
-    terms = jnp.sum(terms.reshape(SPEC, 4, 8, PART), axis=1)
-    terms = terms[:, :, 0:128] + terms[:, :, 128:256]
-    scale = words_ref[128:129, 0:PART].astype(F32) * (1.0 / SCALE_ONE)
-    weighted = (mid.reshape(SPEC * 32, PART) * scale).astype(BF16)
-    part = jnp.dot(weighted, up[...], preferred_element_type=F32)
-
-    @pl.when(step == 0)
-    def _():
-        acc[...] = part + 0.5 * lam_ref[...].astype(F32)
-        bias_ref[...] = terms
-
-    @pl.when(step > 0)
-    def _():
-        acc[...] += part
-        bias_ref[...] += terms
-
-    @pl.when(step == pl.num_programs(0) - 1)
-    def _():
+def channel_kernel(count, split, first, last, *refs):
+    where_ref, core_ref, lam_ref, scaled_ref, relax_ref = refs[:5]
+    refs = refs[5:]
+    if split:
+        words, refs = [(refs[0], refs[1])], refs[2:]
+    else:
+        words, refs = [(w.at[0:64], w.at[64:PACKED]) for w in refs[:count]], refs[count:]
+    if not first:
+        acc_in, bias_in, *refs = refs
+    *outs, down, up = refs
+    total = bias = None
+    for k, (down_words, up_words) in enumerate(words):
+        for m in range(4):
+            codes = unpack_codes(down_words[...], m)
+            for q in range(4):
+                rows = m * 256 + q * 64
+                down[k, rows : rows + 64, :] = codes[:, q * PART : (q + 1) * PART]
+            up[k, m * 64 : (m + 1) * 64, :] = unpack_codes(up_words[0:64, :], m)
+        pre = jnp.dot(scaled_ref[...], down[k], preferred_element_type=F32)
+        pre = pre.reshape(SPEC, 32, PART)
+        bounds = relax_ref.at[where_ref[k]]
+        mid, terms = relaxed(pre, bounds[0], bounds[1], bounds[2], bounds[3])
+        terms = jnp.sum(terms.reshape(SPEC, 4, 8, PART), axis=1)
+        terms = terms[:, :, 0:128] + terms[:, :, 128:256]
+        scale = up_words[64:65, 0:PART].astype(F32) * (1.0 / SCALE_ONE)
+        weighted = (mid.reshape(SPEC * 32, PART) * scale).astype(BF16)
+        part = jnp.dot(weighted, up[k], preferred_element_type=F32)
+        total = part if total is None else total + part
+        bias = terms if bias is None else bias + terms
+    if first:
+        total = total + 0.5 * lam_ref[...].astype(F32)
+    else:
+        total = total + acc_in[...]
+        bias = bias + bias_in[...]
+    if last:
+        keep_ref, send_ref, bias_ref = outs
         own = core_ref[0] == 0
-        turned = acc[...].T.reshape(32, 2, 16, 256)
+        turned = total.T.reshape(32, 2, 16, 256)
         keep_ref[...] = jnp.where(own, turned[:, 0], turned[:, 1])
         send_ref[...] = jnp.where(own, turned[:, 1], turned[:, 0]).astype(BF16)
-
-
-def channel_mlp(core, words, lam, scaled, relax):
-    slices = words.shape[0] // PACKED
-    whole = lambda *shape: pl.BlockSpec(shape, lambda i, c: (0,) * len(shape))
-    return pl.pallas_call(
-        channel_kernel,
-        out_shape=(
+        bias_ref[...] = bias
+    else:
+        acc_ref, bias_ref = outs
+        acc_ref[...] = total
+        bias_ref[...] = bias
+
+
+def channel_part(where, core, lam, scaled, relax, words, carried, last=False):
+    split = isinstance(words, tuple)
+    count = 1 if split else len(words)
+    first = carried is None
+    bias_shape = jax.ShapeDtypeStruct((SPEC, 8, 128), F32)
+    if last:
+        out_shape = (
             jax.ShapeDtypeStruct((32, 16, 256), F32),
             jax.ShapeDtypeStruct((32, 16, 256), BF16),
-            jax.ShapeDtypeStruct((SPEC, 8, 128), F32),
-        ),
-        grid_spec=pltpu.PrefetchScalarGridSpec(
-            num_scalar_prefetch=1,
-            grid=(slices,),
-            in_specs=[
-                pl.BlockSpec((PACKED, D), lambda i, c: (i, 0)),
-                whole(256, D),
-                whole(256, D),
-                pl.BlockSpec((1, 4, 32, PART), lambda i, c: (i, 0, 0, 0)),
-            ],
-            out_specs=(whole(32, 16, 256), whole(32, 16, 256), whole(SPEC, 8, 128)),
-            scratch_shapes=[
-                pltpu.VMEM((256, D), F32),
-                pltpu.VMEM((D, PART), BF16),
-                pltpu.VMEM((PART, D), BF16),
-            ],
-        ),
+            bias_shape,
+        )
+    else:
+        out_shape = (jax.ShapeDtypeStruct((256, D), F32), bias_shape)
+    operands = [where.astype(I32), core, lam, scaled, relax, *words]
+    aliases = {}
+    if not first:
+        if not last:
+            aliases = {len(operands): 0, len(operands) + 1: 1}
+        operands += list(carried)
+    smem, vmem = pl.BlockSpec(memory_space=pltpu.SMEM), pl.BlockSpec(memory_space=pltpu.VMEM)
+    return pl.pallas_call(
+        functools.partial(channel_kernel, count, split, first, last),
+        out_shape=out_shape,
+        in_specs=[smem, smem] + [vmem] * (len(operands) - 2),
+        out_specs=(vmem,) * len(out_shape),
+        scratch_shapes=[
+            pltpu.VMEM((count, D, PART), BF16),
+            pltpu.VMEM((count, PART, D), BF16),
+        ],
+        input_output_aliases=aliases,
         compiler_params=pltpu.CompilerParams(vmem_limit_bytes=VMEM),
+        cost_estimate=pl.CostEstimate(
+            flops=count * 4 * 256 * PART * D,
+            bytes_accessed=count * PACKED * D * 4 + 3 * 256 * D * 4,
+            transcendentals=0,
+        ),
         name="channel",
-    )(core, words, lam, scaled, relax)
+    )(*operands)
 
 
 def token_kernel(got_ref, dense_ref, slopes_ref, icpt_ref, columns_ref, mid_ref, bias_ref):
@@ -246,7 +276,11 @@
     slices = lax.axis_size("rows")
 
     packed = pack(core_arg, q_down, q_up, up_scale)
-    words = lax.all_gather(packed, "rows", axis=0, tiled=True)
+
+    ahead = [(i, (i + 1) % slices) for i in range(slices)]
+    behind = [(i, (i - 1) % slices) for i in range(slices)]
+    me = lax.axis_index("rows")
+    near = (lax.ppermute(packed, "rows", ahead), lax.ppermute(packed, "rows", behind))
 
     def paired(own, other, axis):
         return jnp.where(
@@ -268,7 +302,25 @@
     slopes = jnp.transpose(tok_slopes, (0, 2, 3, 1)).reshape(2, 16, TH)
     icpt = jnp.transpose(tok_icpt, (0, 2, 3, 1)).reshape(2, 16, TH)
 
-    keep, send, chan_bias = channel_mlp(core_arg, words, lam, scaled, relax)
+    common = (core_arg, lam, scaled, relax)
+
+    def two(k, words, carried):
+        return channel_part(jnp.stack([me - k, me + k]) % slices, *common, list(words), carried)
+
+    def forward(words, carried):
+        (a, b), carried = lax.optimization_barrier((words, carried))
+        return (lax.ppermute(a, "rows", ahead), lax.ppermute(b, "rows", behind)), carried
+
+    second = (lax.ppermute(near[0], "rows", ahead), lax.ppermute(near[1], "rows", behind))
+    carried = channel_part(me.reshape(1), *common, [packed], None)
+    third, carried = forward(second, carried)
+    carried = two(1, near, carried)
+    (a, b), carried = lax.optimization_barrier((third, carried))
+    far = (lax.ppermute(a[0:64], "rows", ahead), lax.ppermute(b[64:PACKED], "rows", behind))
+    carried = two(2, second, carried)
+    carried = two(3, third, carried)
+    at = ((me + slices // 2) % slices).reshape(1)
+    keep, send, chan_bias = channel_part(at, *common, far, carried, last=True)
     summed = (keep + lax.ppermute(send, "core", SWAP).astype(F32)).astype(BF16)
     got = lax.all_to_all(summed, ("z", "x"), 0, 0, tiled=True)
     columns, mid, tok_bias = token_mlp(got, dense_out, slopes, icpt)

time: 138 us -> 126 us (0.913)
  waiting for transfers between devices: 72.2 us -> 37.8 us
  starting transfers between devices: 29.6 us -> 63.6 us
  between operations: 14.2 us -> 1.01 us
  Pallas kernels: 11.2 us -> 13.7 us
    all_gather x1 -> x0, waiting for transfers between devices: 50.9 us -> none  [on_device(): words = lax.all_gather(packed, 'rows', axis=0, tiled=True)]
    ppermute x0 -> x8, starting transfers between devices: none -> 27.4 us  [the longest x1 4.57 us: on_device(): lax.ppermute(near[1], 'rows', behind)]
    ppermute x0 -> x8, waiting for transfers between devices: none -> 17.6 us  [the longest x1 6.74 us: on_device(): lax.ppermute(near[0], 'rows', ahead)]
    ppermute x1, starting transfers between devices: 2.58 us -> 6.79 us  [on_device(): summed = (keep + lax.ppermute(send, 'core', SWAP).astype(F32)).astype(BF16)]
    all_to_all x1, starting transfers between devices: 9.9 us -> 13.2 us  [on_device(): got = lax.all_to_all(summed, ('z', 'x'), 0, 0, tiled=True)]
    slice x0 -> x2, local copies, waits for them, and re-layouts: none -> 2.41 us  [the longest x1 1.67 us: on_device(): a[0:64]]
    unnamed x22 -> x24, local copies, waits for them, and re-layouts: 5.42 us -> 3.25 us
    pallas_call x1 -> x5, Pallas kernels: 7.53 us -> 8.88 us  [channel_part(): pl.pallas_call(functools.partial(channel_kernel, count, split, first, las...]
  transfers between devices with their start and end apart: 6 -> 13, of which waited for: 5 -> 8; matrix products, arithmetic and copies ran while one was open for 2% -> 3% of each run, Pallas kernels for 1% -> 7%
where the time goes in v2:
time: 126 us
  starting transfers between devices  63.6 us (50%)
  waiting for transfers between devices  37.8 us (30%)
  Pallas kernels  13.7 us (11%)
  local copies, waits for them, and re-layouts  7.11 us (6%)
  other arithmetic  2.32 us (2%)
    all_to_all x1, starting transfers between devices, on_device(): got = lax.all_to_all(summed, ('z', 'x'), 0, 0, tiled=True)  13.2 us
    all_to_all x1, waiting for transfers between devices, on_device(): got = lax.all_to_all(summed, ('z', 'x'), 0, 0, tiled=True)  10.6 us
    pallas_call x5, Pallas kernels, channel_part(): pl.pallas_call(functools.partial(channel_kernel, count, split, first, las...  8.88 us
    all_to_all x1, waiting for transfers between devices, on_device(): lax.all_to_all(jnp.broadcast_to(own_bias[None, :], (64, SPEC)), MP, 0, 0,...  8.44 us
    ppermute x1, starting transfers between devices, on_device(): lam = paired(by_row, lax.ppermute(by_row, 'core', SWAP), 1).reshape(-1, D)  7.99 us
    ppermute x1, starting transfers between devices, on_device(): summed = (keep + lax.ppermute(send, 'core', SWAP).astype(F32)).astype(BF16)  6.79 us
    ppermute x1, waiting for transfers between devices, on_device(): lax.ppermute(near[0], 'rows', ahead)  6.74 us
    ppermute x1, waiting for transfers between devices, forward(): lax.ppermute(a, 'rows', ahead)  6.47 us
  transfers between devices with their start and end apart: 13, of which 8 were waited for; matrix products, arithmetic and copies ran while one was open for 3% of the time, Pallas kernels for 7%

profile of v2, /device:TPU:1, one launch (start us, length us, event | category | flops | bytes accessed | tf_op | source)
XLA Modules:
  0.0 125.6 jit_solution(2172785691093054009)
XLA Ops:
  0.7 2.3 %pack.1.refs_5_ = s32[136,1024]{1,0:T(8,128)} custom-call(s32[1]{0:T(128)} %bitcast.1.core_ref.refs_1_, bf16[1024,512]{1,0:T(8,128)(2,1)} %down_hbm.1, bf16[512,1024]{1,0:T(8,128)(2,1)} %up_hbm.1, f32[1,512]{1,0:T(1,128)} %bitcast.48), custom_call_target="tpu_custom_call" | custom-call | tf_op jit(solution)/shard_map/pack/pallas_call | solution.py:64
  3.0 4.0 %collective-permute-start.2 = (s32[136,1024]{1,0:T(8,128)}, s32[136,1024]{1,0:T(8,128)}, u32[]{:S(2)}, u32[]{:S(2)}) collective-permute-start(s32[136,1024]{1,0:T(8,128)} %pack.1.refs_5_), channel_id=1, source_target_pairs={{0,64},{64,128},{128,192},{192,256},{256,320},{320,384},{384,448},... | collective-permute-start | bytes 1671176 | tf_op jit(solution)/shard_map/ppermute | solution.py:283
  7.0 3.8 %collective-permute-start.4 = (s32[136,1024]{1,0:T(8,128)}, s32[136,1024]{1,0:T(8,128)}, u32[]{:S(2)}, u32[]{:S(2)}) collective-permute-start(s32[136,1024]{1,0:T(8,128)} %pack.1.refs_5_), channel_id=1, source_target_pairs={{0,448},{64,0},{128,64},{192,128},{256,192},{320,256},{384,320},{4... | collective-permute-start | bytes 1671176 | tf_op jit(solution)/shard_map/ppermute | solution.py:283
  10.9 8.0 %collective-permute-start = (bf16[8,16,1024]{2,0,1:T(8,128)(2,1)S(1)}, bf16[8,16,1024]{2,0,1:T(8,128)(2,1)S(1)}, u32[]{:S(2)}, u32[]{:S(2)}) collective-permute-start(bf16[8,16,1024]{2,0,1:T(8,128)(2,1)S(1)} %bitcast.45), channel_id=1, source_target_pairs={{0,1},{1,0},{2,3},{3,2},{4,5},{5,4},{6,7},{7,6},{8,9},{9,8},{10,11... | collective-permute-start | bytes 786440 | tf_op jit(solution)/shard_map/ppermute | solution.py:293
  18.9 0.4 reshape.46
  19.3 0.2 copy.38
  19.5 1.9 %collective-permute-start.1 = (bf16[8,4,16,256]{3,2,1,0:T(8,128)(2,1)S(1)}, bf16[8,4,16,256]{3,2,1,0:T(8,128)(2,1)S(1)}, u32[]{:S(2)}, u32[]{:S(2)}) collective-permute-start(bf16[8,4,16,256]{3,2,1,0:T(8,128)(2,1)S(1)} %get-tuple-element.51), channel_id=1, source_target_pairs={{0,1},{1,0},{2,3},{3,2},{4,5},{5,4},{6,7},{7,6},{8,9},{9,8},{10,11... | collective-permute-start | bytes 786440 | tf_op jit(solution)/shard_map/ppermute | solution.py:298
  21.5 1.9 %collective-permute-start.3 = (s32[136,1024]{1,0:T(8,128)}, s32[136,1024]{1,0:T(8,128)}, u32[]{:S(2)}, u32[]{:S(2)}) collective-permute-start(s32[136,1024]{1,0:T(8,128)} %collective-permute-done.2.refs_5_), channel_id=1, source_target_pairs={{0,64},{64,128},{128,192},{192,256},{256,320},{320,384},{384,448},... | collective-permute-start | bytes 1671176 | tf_op jit(solution)/shard_map/ppermute | solution.py:314
  23.4 4.6 %collective-permute-start.5 = (s32[136,1024]{1,0:T(8,128)}, s32[136,1024]{1,0:T(8,128)S(1)}, u32[]{:S(2)}, u32[]{:S(2)}) collective-permute-start(s32[136,1024]{1,0:T(8,128)} %collective-permute-done.4.refs_6_), channel_id=1, source_target_pairs={{0,448},{64,0},{128,64},{192,128},{256,192},{320,256},{384,320},{4... | collective-permute-start | bytes 1671176 | tf_op jit(solution)/shard_map/ppermute | solution.py:314
  28.0 0.1 maximum_select_fusion
  28.1 0.3 copy.31
  28.4 0.2 maximum_select_fusion.1.refs_4_
  28.7 0.5 copy-done.11
  29.1 0.1 multiply_convert_fusion.refs_3_
  29.3 0.9 copy-done
  30.2 0.8 channel.5
  30.9 6.7 %collective-permute-done.3.refs_5_ = s32[136,1024]{1,0:T(8,128)} collective-permute-done((s32[136,1024]{1,0:T(8,128)}, s32[136,1024]{1,0:T(8,128)}, u32[]{:S(2)}, u32[]{:S(2)}) %collective-permute-start.3) | collective-permute-done | bytes 557088 | tf_op jit(solution)/shard_map/ppermute | solution.py:314
  37.7 0.9 collective-permute-done.5.refs_6_
  38.6 0.8 copy-done.1
  39.4 3.2 %collective-permute-start.6 = (s32[136,1024]{1,0:T(8,128)}, s32[136,1024]{1,0:T(8,128)}, u32[]{:S(2)}, u32[]{:S(2)}) collective-permute-start(s32[136,1024]{1,0:T(8,128)} %collective-permute-done.3.refs_5_), channel_id=1, source_target_pairs={{0,64},{64,128},{128,192},{192,256},{256,320},{320,384},{384,448},... | collective-permute-start | bytes 1671176 | tf_op jit(solution)/shard_map/ppermute | solution.py:312
  42.6 4.0 %collective-permute-start.7 = (s32[136,1024]{1,0:T(8,128)}, s32[136,1024]{1,0:T(8,128)S(1)}, u32[]{:S(2)}, u32[]{:S(2)}) collective-permute-start(s32[136,1024]{1,0:T(8,128)} %copy-done.1), channel_id=1, source_target_pairs={{0,448},{64,0},{128,64},{192,128},{256,192},{320,256},{384,320},{4... | collective-permute-start | bytes 1671176 | tf_op jit(solution)/shard_map/ppermute | solution.py:312
  46.5 0.1 and_select_fusion.2.refs_0_
  46.6 2.2 %channel.6 = (f32[256,1024]{1,0:T(8,128)S(1)}, f32[8,8,128]{2,1,0:T(8,128)S(1)}) custom-call(s32[2]{0:T(128)S(1)} %and_select_fusion.2.refs_0_, s32[1]{0:T(128)} %bitcast.1.core_ref.refs_1_, bf16[256,1024]{1,0:T(8,128)(2,1)S(1)} %bitcast.38, bf16[256,1024]{1,0:T(8,128)(2,1)S(1)} %multiply_convert_fusion.refs_3_, ...), custom_call_target="tpu_custom_call", output_to_operand_aliasing={{0}: (7, {}), {1}: (8, {})} | custom-call | flops 536870912 | bytes 4259840 | tf_op jit(solution)/shard_map/channel/pallas_call | solution.py:186
  48.8 6.5 %collective-permute-done.6.refs_5_ = s32[136,1024]{1,0:T(8,128)} collective-permute-done((s32[136,1024]{1,0:T(8,128)}, s32[136,1024]{1,0:T(8,128)}, u32[]{:S(2)}, u32[]{:S(2)}) %collective-permute-start.6) | collective-permute-done | bytes 557088 | tf_op jit(solution)/shard_map/ppermute | solution.py:312
  55.3 2.1 %collective-permute-done.7.refs_6_ = s32[136,1024]{1,0:T(8,128)S(1)} collective-permute-done((s32[136,1024]{1,0:T(8,128)}, s32[136,1024]{1,0:T(8,128)S(1)}, u32[]{:S(2)}, u32[]{:S(2)}) %collective-permute-start.7) | collective-permute-done | bytes 557088 | tf_op jit(solution)/shard_map/ppermute | solution.py:312
  57.4 0.7 slice.17
  58.1 4.0 %collective-permute-start.9 = (s32[72,1024]{1,0:T(8,128)}, s32[72,1024]{1,0:T(8,128)S(1)}, u32[]{:S(2)}, u32[]{:S(2)}) collective-permute-start(s32[72,1024]{1,0:T(8,128)} %slice.17), channel_id=1, source_target_pairs={{0,448},{64,0},{128,64},{192,128},{256,192},{320,256},{384,320},{4... | collective-permute-start | bytes 884744 | tf_op jit(solution)/shard_map/ppermute | solution.py:319
  62.2 1.7 %slice.16 = s32[64,1024]{1,0:T(8,128)} slice(s32[136,1024]{1,0:T(8,128)} %collective-permute-done.6.refs_5_), slice={[0:64], [0:1024]} | slice | bytes 524288 | tf_op jit(solution)/shard_map/slice | solution.py:319
  63.8 1.9 %collective-permute-start.8 = (s32[64,1024]{1,0:T(8,128)}, s32[64,1024]{1,0:T(8,128)}, u32[]{:S(2)}, u32[]{:S(2)}) collective-permute-start(s32[64,1024]{1,0:T(8,128)} %slice.16), channel_id=1, source_target_pairs={{0,64},{64,128},{128,192},{192,256},{256,320},{320,384},{384,448},... | collective-permute-start | bytes 786440 | tf_op jit(solution)/shard_map/ppermute | solution.py:319
  65.8 0.1 and_select_fusion.refs_0_
  65.9 1.1 copy-done.2
  67.0 2.0 %channel.7 = (f32[256,1024]{1,0:T(8,128)S(1)}, f32[8,8,128]{2,1,0:T(8,128)S(1)}) custom-call(s32[2]{0:T(128)S(1)} %and_select_fusion.refs_0_, s32[1]{0:T(128)} %bitcast.1.core_ref.refs_1_, bf16[256,1024]{1,0:T(8,128)(2,1)S(1)} %bitcast.39, bf16[256,1024]{1,0:T(8,128)(2,1)S(1)} %multiply_convert_fusion.refs_3_, ...), custom_call_target="tpu_custom_call", output_to_operand_aliasing={{0}: (7, {}), {1}: (8, {})} | custom-call | flops 536870912 | bytes 4259840 | tf_op jit(solution)/shard_map/channel/pallas_call | solution.py:186
  69.0 2.1 %channel.8 = (f32[256,1024]{1,0:T(8,128)S(1)}, f32[8,8,128]{2,1,0:T(8,128)S(1)}) custom-call(s32[2]{0:T(128)S(1)} %and_select_fusion.1.refs_0_, s32[1]{0:T(128)} %bitcast.1.core_ref.refs_1_, bf16[256,1024]{1,0:T(8,128)(2,1)S(1)} %bitcast.40, bf16[256,1024]{1,0:T(8,128)(2,1)S(1)} %multiply_convert_fusion.refs_3_, ...), custom_call_target="tpu_custom_call", output_to_operand_aliasing={{0}: (7, {}), {1}: (8, {})} | custom-call | flops 536870912 | bytes 4259840 | tf_op jit(solution)/shard_map/channel/pallas_call | solution.py:186
  71.1 1.4 %collective-permute-done.8.refs_5_ = s32[64,1024]{1,0:T(8,128)} collective-permute-done((s32[64,1024]{1,0:T(8,128)}, s32[64,1024]{1,0:T(8,128)}, u32[]{:S(2)}, u32[]{:S(2)}) %collective-permute-start.8) | collective-permute-done | bytes 262176 | tf_op jit(solution)/shard_map/ppermute | solution.py:319
  72.5 1.8 %channel.9 = (f32[32,16,256]{2,1,0:T(8,128)S(1)}, bf16[32,16,256]{2,1,0:T(8,128)(2,1)S(1)}, f32[8,8,128]{2,1,0:T(8,128)S(1)}) custom-call(s32[1]{0:T(128)} %bitcast.refs_0_, s32[1]{0:T(128)} %bitcast.1.core_ref.refs_1_, bf16[256,1024]{1,0:T(8,128)(2,1)S(1)} %bitcast.41, bf16[256,1024]{1,0:T(8,128)(2,1)S(1)} %multiply_convert_fusion.refs_3_, ...), custom_call_target="tpu_custom_call" | custom-call | flops 268435456 | bytes 3702784 | tf_op jit(solution)/shard_map/channel/pallas_call | solution.py:186
  74.3 6.8 %collective-permute-start.10 = (bf16[32,16,256]{2,1,0:T(8,128)(2,1)S(1)}, bf16[32,16,256]{2,1,0:T(8,128)(2,1)S(1)}, u32[]{:S(2)}, u32[]{:S(2)}) collective-permute-start(bf16[32,16,256]{2,1,0:T(8,128)(2,1)S(1)} %get-tuple-element.43), channel_id=1, source_target_pairs={{0,1},{1,0},{2,3},{3,2},{4,5},{5,4},{6,7},{7,6},{8,9},{9,8},{10,11... | collective-permute-start | bytes 786440 | tf_op jit(solution)/shard_map/ppermute | solution.py:324
  81.1 1.1 collective-permute-done.10
  82.2 0.8 add_convert_fusion
  83.0 13.2 %all-to-all-start = ((bf16[32,16,256]{2,1,0:T(8,128)(2,1)}), bf16[32,16,256]{2,1,0:T(8,128)(2,1)S(1)}, u32[]{:S(2)}, u32[]{:S(2)}) async-start(bf16[32,16,256]{2,1,0:T(8,128)(2,1)} %add_convert_fusion), calls=%async_computation | async-start | bytes 524288 | tf_op jit(solution)/shard_map/all_to_all | solution.py:325
  96.3 0.9 dense.1
  97.2 10.6 %all-to-all-done.got_ref = bf16[32,16,256]{2,1,0:T(8,128)(2,1)S(1)} async-done(((bf16[32,16,256]{2,1,0:T(8,128)(2,1)}), bf16[32,16,256]{2,1,0:T(8,128)(2,1)S(1)}, u32[]{:S(2)}, u32[]{:S(2)}) %all-to-all-start) | async-done | bytes 262176 | tf_op jit(solution)/shard_map/all_to_all | solution.py:325
  107.8 0.6 token_.1
  108.4 0.1 add_reduce_fusion
  108.6 0.6 broadcast_in_dim.2
  109.2 6.3 %all-to-all-start.1 = ((f32[64,1,8]{2,1,0:T(1,128)}), f32[64,1,8]{2,1,0:T(1,128)S(1)}, u32[]{:S(2)}, u32[]{:S(2)}) async-start(f32[64,1,8]{2,1,0:T(1,128)} %broadcast_in_dim.2), calls=%async_computation.1 | async-start | bytes 65536 | tf_op jit(solution)/shard_map/all_to_all | solution.py:328
  115.5 1.0 back.1
  116.5 8.4 %all-to-all-done.1 = f32[64,1,8]{2,1,0:T(1,128)S(1)} async-done(((f32[64,1,8]{2,1,0:T(1,128)}), f32[64,1,8]{2,1,0:T(1,128)S(1)}, u32[]{:S(2)}, u32[]{:S(2)}) %all-to-all-start.1) | async-done | bytes 2080 | tf_op jit(solution)/shard_map/all_to_all | solution.py:328
  125.0 0.6 reduce_sum.19
  (28 shorter events, 0.2 us)
Async XLA Ops:
  0.6 10.2 %copy-start.10 = (bf16[16,8,1024]{2,1,0:T(8,128)(2,1)S(1)}, bf16[16,8,1024]{2,1,0:T(8,128)(2,1)}, u32[]{:S(2)}) copy-start(bf16[16,8,1024]{2,1,0:T(8,128)(2,1)} %param.12) | copy-start | bytes 786436
  0.6 18.2 %copy-start.8 = (bf16[2,16,1,4096]{3,1,2,0:T(8,128)(2,1)S(1)}, bf16[2,16,1,4096]{3,1,2,0:T(8,128)(2,1)}, u32[]{:S(2)}) copy-start(bf16[2,16,1,4096]{3,1,2,0:T(8,128)(2,1)} %param.18) | copy-start | bytes 786436
  0.7 18.2 %copy-start.9 = (bf16[2,16,1,4096]{3,1,2,0:T(8,128)(2,1)S(1)}, bf16[2,16,1,4096]{3,1,2,0:T(8,128)(2,1)}, u32[]{:S(2)}) copy-start(bf16[2,16,1,4096]{3,1,2,0:T(8,128)(2,1)} %param.17) | copy-start | bytes 786436
  3.0 18.5 %collective-permute-start.2 = (s32[136,1024]{1,0:T(8,128)}, s32[136,1024]{1,0:T(8,128)}, u32[]{:S(2)}, u32[]{:S(2)}) collective-permute-start(s32[136,1024]{1,0:T(8,128)} %pack.1.refs_5_), channel_id=1, source_target_pairs={{0,64},{64,128},{128,192},{192,256},{256,320},{320,384},{384,448},... | collective-permute-start | bytes 1671176 | tf_op jit(solution)/shard_map/ppermute | solution.py:283
  7.0 16.4 %collective-permute-start.4 = (s32[136,1024]{1,0:T(8,128)}, s32[136,1024]{1,0:T(8,128)}, u32[]{:S(2)}, u32[]{:S(2)}) collective-permute-start(s32[136,1024]{1,0:T(8,128)} %pack.1.refs_5_), channel_id=1, source_target_pairs={{0,448},{64,0},{128,64},{192,128},{256,192},{320,256},{384,320},{4... | collective-permute-start | bytes 1671176 | tf_op jit(solution)/shard_map/ppermute | solution.py:283
  10.9 17.1 %collective-permute-start = (bf16[8,16,1024]{2,0,1:T(8,128)(2,1)S(1)}, bf16[8,16,1024]{2,0,1:T(8,128)(2,1)S(1)}, u32[]{:S(2)}, u32[]{:S(2)}) collective-permute-start(bf16[8,16,1024]{2,0,1:T(8,128)(2,1)S(1)} %bitcast.45), channel_id=1, source_target_pairs={{0,1},{1,0},{2,3},{3,2},{4,5},{5,4},{6,7},{7,6},{8,9},{9,8},{10,11... | collective-permute-start | bytes 786440 | tf_op jit(solution)/shard_map/ppermute | solution.py:293
  19.5 8.9 %collective-permute-start.1 = (bf16[8,4,16,256]{3,2,1,0:T(8,128)(2,1)S(1)}, bf16[8,4,16,256]{3,2,1,0:T(8,128)(2,1)S(1)}, u32[]{:S(2)}, u32[]{:S(2)}) collective-permute-start(bf16[8,4,16,256]{3,2,1,0:T(8,128)(2,1)S(1)} %get-tuple-element.51), channel_id=1, source_target_pairs={{0,1},{1,0},{2,3},{3,2},{4,5},{5,4},{6,7},{7,6},{8,9},{9,8},{10,11... | collective-permute-start | bytes 786440 | tf_op jit(solution)/shard_map/ppermute | solution.py:298
  21.5 16.2 %collective-permute-start.3 = (s32[136,1024]{1,0:T(8,128)}, s32[136,1024]{1,0:T(8,128)}, u32[]{:S(2)}, u32[]{:S(2)}) collective-permute-start(s32[136,1024]{1,0:T(8,128)} %collective-permute-done.2.refs_5_), channel_id=1, source_target_pairs={{0,64},{64,128},{128,192},{192,256},{256,320},{320,384},{384,448},... | collective-permute-start | bytes 1671176 | tf_op jit(solution)/shard_map/ppermute | solution.py:314
  23.4 15.2 %collective-permute-start.5 = (s32[136,1024]{1,0:T(8,128)}, s32[136,1024]{1,0:T(8,128)S(1)}, u32[]{:S(2)}, u32[]{:S(2)}) collective-permute-start(s32[136,1024]{1,0:T(8,128)} %collective-permute-done.4.refs_6_), channel_id=1, source_target_pairs={{0,448},{64,0},{128,64},{192,128},{256,192},{320,256},{384,320},{4... | collective-permute-start | bytes 1671176 | tf_op jit(solution)/shard_map/ppermute | solution.py:314
  28.4 0.7 copy-start.11
  29.1 1.1 copy-start
  38.6 0.8 copy-start.1
  39.4 15.9 %collective-permute-start.6 = (s32[136,1024]{1,0:T(8,128)}, s32[136,1024]{1,0:T(8,128)}, u32[]{:S(2)}, u32[]{:S(2)}) collective-permute-start(s32[136,1024]{1,0:T(8,128)} %collective-permute-done.3.refs_5_), channel_id=1, source_target_pairs={{0,64},{64,128},{128,192},{192,256},{256,320},{320,384},{384,448},... | collective-permute-start | bytes 1671176 | tf_op jit(solution)/shard_map/ppermute | solution.py:312
  42.6 14.8 %collective-permute-start.7 = (s32[136,1024]{1,0:T(8,128)}, s32[136,1024]{1,0:T(8,128)S(1)}, u32[]{:S(2)}, u32[]{:S(2)}) collective-permute-start(s32[136,1024]{1,0:T(8,128)} %copy-done.1), channel_id=1, source_target_pairs={{0,448},{64,0},{128,64},{192,128},{256,192},{320,256},{384,320},{4... | collective-permute-start | bytes 1671176 | tf_op jit(solution)/shard_map/ppermute | solution.py:312
  58.1 14.4 %collective-permute-start.9 = (s32[72,1024]{1,0:T(8,128)}, s32[72,1024]{1,0:T(8,128)S(1)}, u32[]{:S(2)}, u32[]{:S(2)}) collective-permute-start(s32[72,1024]{1,0:T(8,128)} %slice.17), channel_id=1, source_target_pairs={{0,448},{64,0},{128,64},{192,128},{256,192},{320,256},{384,320},{4... | collective-permute-start | bytes 884744 | tf_op jit(solution)/shard_map/ppermute | solution.py:319
  63.8 8.6 %collective-permute-start.8 = (s32[64,1024]{1,0:T(8,128)}, s32[64,1024]{1,0:T(8,128)}, u32[]{:S(2)}, u32[]{:S(2)}) collective-permute-start(s32[64,1024]{1,0:T(8,128)} %slice.16), channel_id=1, source_target_pairs={{0,64},{64,128},{128,192},{192,256},{256,320},{320,384},{384,448},... | collective-permute-start | bytes 786440 | tf_op jit(solution)/shard_map/ppermute | solution.py:319
  65.9 1.1 copy-start.2
  74.3 7.9 %collective-permute-start.10 = (bf16[32,16,256]{2,1,0:T(8,128)(2,1)S(1)}, bf16[32,16,256]{2,1,0:T(8,128)(2,1)S(1)}, u32[]{:S(2)}, u32[]{:S(2)}) collective-permute-start(bf16[32,16,256]{2,1,0:T(8,128)(2,1)S(1)} %get-tuple-element.43), channel_id=1, source_target_pairs={{0,1},{1,0},{2,3},{3,2},{4,5},{5,4},{6,7},{7,6},{8,9},{9,8},{10,11... | collective-permute-start | bytes 786440 | tf_op jit(solution)/shard_map/ppermute | solution.py:324
  82.2 14.0 %copy-start.4 = (bf16[16,128,128]{2,1,0:T(8,128)(2,1)S(1)}, bf16[16,128,128]{2,1,0:T(8,128)(2,1)}, u32[]{:S(2)}) copy-start(bf16[16,128,128]{2,1,0:T(8,128)(2,1)} %out_ref.1) | copy-start | bytes 1572868
  82.2 14.0 %copy-start.7 = (s32[16]{0:T(128)S(1)}, s32[16]{0:T(128)}, u32[]{:S(2)}) copy-start(s32[16]{0:T(128)} %cells_ref.1) | copy-start | bytes 196
  83.0 13.2 %copy-start.3 = (bf16[16,128,128]{2,1,0:T(8,128)(2,1)S(1)}, bf16[16,128,128]{2,1,0:T(8,128)(2,1)}, u32[]{:S(2)}) copy-start(bf16[16,128,128]{2,1,0:T(8,128)(2,1)} %in_ref.1) | copy-start | bytes 1572868
  83.0 24.8 %all-to-all-start = ((bf16[32,16,256]{2,1,0:T(8,128)(2,1)}), bf16[32,16,256]{2,1,0:T(8,128)(2,1)S(1)}, u32[]{:S(2)}, u32[]{:S(2)}) async-start(bf16[32,16,256]{2,1,0:T(8,128)(2,1)} %add_convert_fusion), calls=%async_computation | async-start | bytes 524288 | tf_op jit(solution)/shard_map/all_to_all | solution.py:325
  96.3 11.6 %copy-start.5 = (bf16[2,512,1,16]{1,3,2,0:T(8,128)(2,1)S(1)}, bf16[2,512,1,16]{1,3,2,0:T(8,128)(2,1)}, u32[]{:S(2)}) copy-start(bf16[2,512,1,16]{1,3,2,0:T(8,128)(2,1)} %param.22) | copy-start | bytes 98308
  96.3 11.5 %copy-start.6 = (bf16[2,512,1,16]{1,3,2,0:T(8,128)(2,1)S(1)}, bf16[2,512,1,16]{1,3,2,0:T(8,128)(2,1)}, u32[]{:S(2)}) copy-start(bf16[2,512,1,16]{1,3,2,0:T(8,128)(2,1)} %param.23) | copy-start | bytes 98308
  109.2 15.8 %all-to-all-start.1 = ((f32[64,1,8]{2,1,0:T(1,128)}), f32[64,1,8]{2,1,0:T(1,128)S(1)}, u32[]{:S(2)}, u32[]{:S(2)}) async-start(f32[64,1,8]{2,1,0:T(1,128)} %broadcast_in_dim.2), calls=%async_computation.1 | async-start | bytes 65536 | tf_op jit(solution)/shard_map/all_to_all | solution.py:328

commit v3 on v2

v3 whole, which is shorter than its diff:
```python
import functools

import jax
import jax.numpy as jnp
from jax import lax
from jax.experimental import pallas as pl
from jax.experimental.pallas import tpu as pltpu
from jax.sharding import Mesh
from jax.sharding import PartitionSpec as P

D = 1024
CH = 4096
TH = 512
TOK = 1024
BLK = 128
NB = 16
SPEC = 8
NHB = 4
NTB = 8
F32 = jnp.float32
BF16 = jnp.bfloat16
I32 = jnp.int32
MP = ("z", "xh", "xl", "core")
TEAM = ("xl", "core")
SWAP = [(0, 1), (1, 0)]
VMEM = 32 * 1024 * 1024

PART = 128
SHARED = 64
ROWS_DEV = SPEC * SHARED
PACKED = 72
LAM_TILES = SPEC * (D // 128)
SCALE_ONE = float(2**38)


def pack_codes(parts):
    a, b, c, d = (p.astype(F32).astype(I32) for p in parts)
    return (a & 255) | ((b & 255) << 8) | ((c & 255) << 16) | (d << 24)


def unpack_codes(words, m):
    shifted = words << (24 - 8 * m) if m < 3 else words
    return (shifted >> 24).astype(F32).astype(BF16)


def pack_kernel(quarter_ref, down_hbm, up_hbm, scale_hbm, out_ref, down_ref, up_ref, scale_ref, sems):
    start = pl.multiple_of(quarter_ref[0] * PART, PART)
    copies = [
        pltpu.make_async_copy(down_hbm.at[:, pl.ds(start, PART)], down_ref, sems.at[0]),
        pltpu.make_async_copy(up_hbm.at[pl.ds(start, PART), :], up_ref, sems.at[1]),
        pltpu.make_async_copy(scale_hbm.at[:, pl.ds(start, PART)], scale_ref, sems.at[2]),
    ]
    for copy in copies:
        copy.start()
    out_ref[64:72, :] = jnp.zeros((8, D), I32)
    copies[0].wait()
    down = pack_codes([down_ref[m * 256 : (m + 1) * 256, :] for m in range(4)])
    for k in range(8):
        out_ref[0:32, k * PART : (k + 1) * PART] = down[k * 32 : (k + 1) * 32, :]
    copies[1].wait()
    out_ref[32:64, :] = pack_codes([up_ref[m * 32 : (m + 1) * 32, :] for m in range(4)])
    copies[2].wait()
    scale = (scale_ref[...] * SCALE_ONE).astype(I32)
    out_ref[64:72, 0:PART] = jnp.broadcast_to(scale, (8, PART))


def pack(quarter, q_down, q_up, up_scale):
    return pl.pallas_call(
        pack_kernel,
        out_shape=jax.ShapeDtypeStruct((PACKED, D), I32),
        in_specs=[pl.BlockSpec(memory_space=pltpu.SMEM)]
        + [pl.BlockSpec(memory_space=pltpu.HBM)] * 3,
        out_specs=pl.BlockSpec(memory_space=pltpu.VMEM),
        scratch_shapes=[
            pltpu.VMEM((D, PART), BF16),
            pltpu.VMEM((PART, D), BF16),
            pltpu.VMEM((1, PART), F32),
            pltpu.SemaphoreType.DMA((3,)),
        ],
        compiler_params=pltpu.CompilerParams(vmem_limit_bytes=60 * 1024 * 1024),
        name="pack",
    )(quarter, q_down, q_up, up_scale.reshape(1, -1))


def dense_kernel(cells_ref, in_ref, out_ref, dense_in_ref, dense_out_ref):
    dense_in_ref[...] = jnp.zeros_like(dense_in_ref)
    dense_out_ref[...] = jnp.zeros_like(dense_out_ref)
    for b in range(NB):
        h = pl.multiple_of(cells_ref[b] // NTB * BLK, BLK)
        u = pl.multiple_of(cells_ref[b] % NTB * BLK, BLK)
        dense_in_ref[pl.ds(h, BLK), pl.ds(u, BLK)] = in_ref[b]
        dense_out_ref[pl.ds(u, BLK), pl.ds(h, BLK)] = out_ref[b]


def dense_blocks(cells, in_blocks, out_blocks):
    return pl.pallas_call(
        dense_kernel,
        out_shape=(
            jax.ShapeDtypeStruct((TH, TOK), BF16),
            jax.ShapeDtypeStruct((TOK, TH), BF16),
        ),
        in_specs=[
            pl.BlockSpec(memory_space=pltpu.SMEM),
            pl.BlockSpec(memory_space=pltpu.VMEM),
            pl.BlockSpec(memory_space=pltpu.VMEM),
        ],
        out_specs=(
            pl.BlockSpec(memory_space=pltpu.VMEM),
            pl.BlockSpec(memory_space=pltpu.VMEM),
        ),
        compiler_params=pltpu.CompilerParams(vmem_limit_bytes=VMEM),
        name="dense",
    )(cells, in_blocks, out_blocks)


def relaxed(pre, lower, upper, icpt_low, icpt_high):
    pos = jnp.maximum(pre, 0.0)
    neg = jnp.minimum(pre, 0.0)
    mid = pos * lower.astype(F32) + neg * upper.astype(F32)
    return mid, pos * icpt_low.astype(F32) + neg * icpt_high.astype(F32)


def share_kernel(quarter_ref, lam_ref, slopes_ref, icpt_ref, *out_refs):
    for r in range(SPEC):
        for k in range(D // 128):
            tile = lam_ref[r, :, k * 128 : (k + 1) * 128]
            for out_ref in out_refs:
                out_ref[r * (D // 128) + k] = tile
    for k, out_ref in enumerate(out_refs):
        for y in range(CH // TH):
            start = pl.multiple_of(y * TH + (quarter_ref[0] ^ k) * PART, PART)
            for kind in range(2):
                out_ref[LAM_TILES + y * 4 + kind] = slopes_ref[kind, :, pl.ds(start, PART)]
                out_ref[LAM_TILES + y * 4 + 2 + kind] = icpt_ref[kind, :, pl.ds(start, PART)]


def share(quarter, by_row, slopes, icpt):
    tiles = LAM_TILES + 4 * (CH // TH)
    return pl.pallas_call(
        share_kernel,
        out_shape=(jax.ShapeDtypeStruct((tiles, 16, 128), BF16),) * 4,
        in_specs=[pl.BlockSpec(memory_space=pltpu.SMEM)]
        + [pl.BlockSpec(memory_space=pltpu.VMEM)] * 3,
        compiler_params=pltpu.CompilerParams(vmem_limit_bytes=60 * 1024 * 1024),
        name="share",
    )(quarter, by_row, slopes, icpt)


def channel_kernel(count, first, last, *refs):
    where_ref, place_ref = refs[:2]
    refs = refs[2:]
    words, refs = refs[:count], refs[count:]
    if first:
        down_scale_ref, *team, acc_ref, bias_ref, scaled_ref, bounds_ref, down, up = refs
        for j, got_ref in enumerate(team):
            start = (place_ref[0] ^ j) * 16
            for r in range(SPEC):
                rows = pl.ds(pl.multiple_of(r * SHARED + start, 16), 16)
                for k in range(D // 128):
                    cut = slice(k * 128, (k + 1) * 128)
                    lam = got_ref[r * (D // 128) + k].astype(F32)
                    scaled_ref[rows, cut] = (lam * down_scale_ref[:, cut]).astype(BF16)
                    acc_ref[rows, cut] = 0.25 * lam
            rows = pl.ds(pl.multiple_of(start, 16), 16)
            for y in range(CH // TH):
                for kind in range(4):
                    bounds_ref[y, kind, rows, :] = got_ref[LAM_TILES + y * 4 + kind]
        acc_in, bias_in = acc_ref, None
    else:
        scaled_ref, bounds_ref, acc_in, bias_in, *outs, down, up = refs
    scales, bounds = [], []
    for k, words_ref in enumerate(words):
        for m in range(4):
            codes = unpack_codes(words_ref[0:32, :], m)
            for q in range(8):
                rows = m * 256 + q * 32
                cut = slice(q * PART, (q + 1) * PART)
                down[rows : rows + 32, k * PART : (k + 1) * PART] = codes[:, cut]
            rows = k * PART + m * 32
            up[rows : rows + 32, :] = unpack_codes(words_ref[32:64, :], m)
        scales.append(words_ref[64:65, 0:PART].astype(F32) * (1.0 / SCALE_ONE))
        bounds.append(bounds_ref.at[where_ref[k]])
    scale = jnp.concatenate(scales, axis=1)
    bounds = [jnp.concatenate([b[kind] for b in bounds], axis=1) for kind in range(4)]
    pre = jnp.dot(scaled_ref[...], down[...], preferred_element_type=F32)
    pre = pre.reshape(SPEC, SHARED, count * PART)
    mid, terms = relaxed(pre, *bounds)
    terms = jnp.sum(terms.reshape(SPEC, SHARED // 8, 8, count * PART), axis=1)
    bias = sum(terms[:, :, k * PART : (k + 1) * PART] for k in range(count))
    weighted = (mid.reshape(ROWS_DEV, count * PART) * scale).astype(BF16)
    part = jnp.dot(weighted, up[...], preferred_element_type=F32)
    total = acc_in[...] + part
    if not first:
        bias = bias + bias_in[...]
    if last:
        keep_ref, send_ref, bias_ref = outs
        own = place_ref[0] % 2 == 0
        turned = total.T.reshape(32, 2, 16, ROWS_DEV)
        keep_ref[...] = jnp.where(own, turned[:, 0], turned[:, 1])
        send_ref[...] = jnp.where(own, turned[:, 1], turned[:, 0]).astype(BF16)
    else:
        if not first:
            acc_ref, bias_ref = outs
        acc_ref[...] = total
    bias_ref[...] = bias


def channel_part(where, place, words, rest, first=False, last=False):
    count = len(words)
    acc_shape = jax.ShapeDtypeStruct((ROWS_DEV, D), F32)
    bias_shape = jax.ShapeDtypeStruct((SPEC, 8, 128), F32)
    operands = [where.astype(I32), place, *words, *rest]
    aliases = {}
    if first:
        scaled_shape = jax.ShapeDtypeStruct((ROWS_DEV, D), BF16)
        bounds_shape = jax.ShapeDtypeStruct((CH // TH, 4, SHARED, PART), BF16)
        out_shape = (acc_shape, bias_shape, scaled_shape, bounds_shape)
    elif last:
        out_shape = (
            jax.ShapeDtypeStruct((32, 16, ROWS_DEV), F32),
            jax.ShapeDtypeStruct((32, 16, ROWS_DEV), BF16),
            bias_shape,
        )
    else:
        out_shape = (acc_shape, bias_shape)
        aliases = {len(operands) - 2: 0, len(operands) - 1: 1}
    smem, vmem = pl.BlockSpec(memory_space=pltpu.SMEM), pl.BlockSpec(memory_space=pltpu.VMEM)
    return pl.pallas_call(
        functools.partial(channel_kernel, count, first, last),
        out_shape=out_shape,
        in_specs=[smem, smem] + [vmem] * (len(operands) - 2),
        out_specs=(vmem,) * len(out_shape),
        scratch_shapes=[
            pltpu.VMEM((D, count * PART), BF16),
            pltpu.VMEM((count * PART, D), BF16),
        ],
        input_output_aliases=aliases,
        compiler_params=pltpu.CompilerParams(vmem_limit_bytes=VMEM),
        cost_estimate=pl.CostEstimate(
            flops=count * 4 * ROWS_DEV * PART * D,
            bytes_accessed=count * PACKED * D * 4 + 3 * ROWS_DEV * D * 4,
            transcendentals=0,
        ),
        name="channel",
    )(*operands)


def token_kernel(got_ref, dense_ref, slopes_ref, icpt_ref, columns_ref, mid_ref, bias_ref):
    low = lax.broadcasted_iota(I32, (16, 128), 1) < SHARED
    for u in range(NTB):
        for a in range(SPEC // 2):
            cut = slice(a * 128, (a + 1) * 128)
            v = [
                got_ref[s, :, cut].astype(F32) + got_ref[s + 1, :, cut].astype(F32)
                for s in (4 * u, 4 * u + 2)
            ]
            even = jnp.where(low, v[0], pltpu.roll(v[1], SHARED, 1))
            odd = jnp.where(low, pltpu.roll(v[0], SHARED, 1), v[1])
            for r, value in ((2 * a, even), (2 * a + 1, odd)):
                columns_ref[r * 16 : (r + 1) * 16, u * 128 : (u + 1) * 128] = value.astype(BF16)
    pre = jnp.dot(columns_ref[...], dense_ref[...], preferred_element_type=F32)
    pre = pre.reshape(SPEC, 16, TH)
    mid, terms = relaxed(pre, slopes_ref[0], slopes_ref[1], icpt_ref[0], icpt_ref[1])
    mid_ref[...] = mid.reshape(SPEC * 16, TH).astype(BF16)
    terms = terms[:, 0:8, :] + terms[:, 8:16, :]
    bias_ref[...] = sum(terms[:, :, k * 128 : (k + 1) * 128] for k in range(NHB))


def token_mlp(got, dense_out, slopes, icpt):
    return pl.pallas_call(
        token_kernel,
        out_shape=(
            jax.ShapeDtypeStruct((SPEC * 16, TOK), BF16),
            jax.ShapeDtypeStruct((SPEC * 16, TH), BF16),
            jax.ShapeDtypeStruct((SPEC, 8, 128), F32),
        ),
        compiler_params=pltpu.CompilerParams(vmem_limit_bytes=VMEM),
        name="token",
    )(got, dense_out, slopes, icpt)


def back_kernel(columns_ref, mid_ref, dense_ref, out_ref):
    back = jnp.dot(mid_ref[...], dense_ref[...], preferred_element_type=F32)
    out_ref[...] = (columns_ref[...].astype(F32) + back).astype(BF16)


def token_back(columns, mid, dense_in):
    return pl.pallas_call(
        back_kernel,
        out_shape=jax.ShapeDtypeStruct((SPEC * 16, TOK), BF16),
        compiler_params=pltpu.CompilerParams(vmem_limit_bytes=VMEM),
        name="back",
    )(columns, mid, dense_in)


def on_device(
    lam_out,
    q_down,
    down_scale,
    q_up,
    up_scale,
    chan_slopes,
    chan_icpt,
    tok_in_blocks,
    tok_out_blocks,
    block_cells,
    tok_slopes,
    tok_icpt,
):
    quarter = lax.axis_index(TEAM).astype(I32).reshape(1)
    tok_dev = lam_out.shape[0]
    slices = lax.axis_size("rows")
    ahead = [(i, (i + 1) % slices) for i in range(slices)]
    behind = [(i, (i - 1) % slices) for i in range(slices)]

    own = pack(quarter, q_down, q_up, up_scale)
    near = (lax.ppermute(own, "rows", ahead), lax.ppermute(own, "rows", behind))
    own_part, *parts = share(
        quarter,
        jnp.swapaxes(lam_out, 0, 1),
        chan_slopes.reshape(2, tok_dev, CH),
        chan_icpt.reshape(2, tok_dev, CH),
    )
    onward, parts = lax.optimization_barrier((near[1], parts))
    team = [own_part] + [
        lax.ppermute(part, TEAM, [(i, i ^ k) for i in range(4)]) for k, part in enumerate(parts, 1)
    ]
    second = (lax.ppermute(near[0], "rows", ahead), lax.ppermute(onward, "rows", behind))
    onward, team[2] = lax.optimization_barrier((second[0], team[2]))
    back, team[3] = lax.optimization_barrier((second[1], team[3]))
    third = (lax.ppermute(onward, "rows", ahead), lax.ppermute(back, "rows", behind))
    far = lax.ppermute(third[0], "rows", ahead)

    dense_in, dense_out = dense_blocks(block_cells, tok_in_blocks, tok_out_blocks)
    slopes = jnp.transpose(tok_slopes, (0, 2, 3, 1)).reshape(2, 16, TH)
    icpt = jnp.transpose(tok_icpt, (0, 2, 3, 1)).reshape(2, 16, TH)

    me = lax.axis_index("rows")
    acc, chan_bias, *given = channel_part(
        me.reshape(1), quarter, [own], [down_scale.reshape(1, D), *team], first=True
    )
    for k, words in enumerate((near, second, third), 1):
        at = jnp.stack([me - k, me + k]) % slices
        acc, chan_bias = channel_part(at, quarter, words, [*given, acc, chan_bias])
    at = ((me + slices // 2) % slices).reshape(1)
    keep, send, chan_bias = channel_part(
        at, quarter, [far], [*given, acc, chan_bias], last=True
    )
    summed = (keep + lax.ppermute(send, "core", SWAP).astype(F32)).astype(BF16)
    got = lax.all_to_all(summed, ("z", "xh", "xl"), 0, 0, tiled=True)
    columns, mid, tok_bias = token_mlp(got, dense_out, slopes, icpt)
    own_bias = jnp.sum(chan_bias + tok_bias, axis=(1, 2))
    all_bias = lax.all_to_all(
        jnp.broadcast_to(own_bias[None, :], (64, SPEC)), MP, 0, 0, tiled=True
    )
    lam_in = token_back(columns, mid, dense_in)
    lam_in = jnp.transpose(lam_in.reshape(SPEC, 16, TOK), (2, 0, 1))
    return (lam_in, jnp.sum(all_bias, axis=0))


def solution(mesh):
    axes = Mesh(mesh.devices.reshape(8, 8, 2, 2, 2), ("rows",) + MP)
    return jax.shard_map(
        on_device,
        mesh=axes,
        in_specs=(
            P(MP, "rows", None),
            P(None, "rows"),
            P(),
            P("rows", None),
            P("rows"),
            P(None, MP, "rows", None),
            P(None, MP, "rows", None),
            P(),
            P(),
            P(),
            P(None, None, "rows", MP),
            P(None, None, "rows", MP),
        ),
        out_specs=(P(None, "rows", MP), P("rows")),
        check_vma=False,
    )
```

time: 126 us -> 109 us (0.87)
  waiting for transfers between devices: 37.8 us -> 26.9 us
  starting transfers between devices: 63.6 us -> 58.5 us
  local copies, waits for them, and re-layouts: 7.11 us -> 4.5 us
  Pallas kernels: 13.7 us -> 15.7 us
    ppermute x9, waiting for transfers between devices: 10.8 us -> 2.45 us  [the longest x1 2.23 us: on_device(): lax.ppermute(onward, 'rows', behind)]
    ppermute x1, waiting for transfers between devices: 6.74 us -> 0.01 us  [on_device(): lax.ppermute(near[0], 'rows', ahead)]
    all_to_all x1, waiting for transfers between devices: 10.6 us -> 14.6 us  [on_device(): got = lax.all_to_all(summed, ('z', 'xh', 'xl'), 0, 0, tiled=True)]
    ppermute x1, starting transfers between devices: 6.79 us -> 3.01 us  [on_device(): summed = (keep + lax.ppermute(send, 'core', SWAP).astype(F32)).astype(BF16)]
    pallas_call x5 -> x6, Pallas kernels: 8.88 us -> 11.4 us  [the longest x5 8.88 us: channel_part(): pl.pallas_call(functools.partial(channel_kernel, count, first, last), out...]
    slice x2 -> x0, local copies, waits for them, and re-layouts: 2.41 us -> none  [the longest x1 1.67 us: on_device(): a[0:64]]
    ppermute x9, starting transfers between devices: 35.4 us -> 33.8 us  [the longest x3 12.3 us: on_device(): lax.ppermute(part, TEAM, [(i, i ^ k) for i in range(4)])]
    unnamed x24 -> x19, local copies, waits for them, and re-layouts: 3.25 us -> 3.87 us
  transfers between devices with their start and end apart: 13 -> 13, of which waited for: 8 -> 5; matrix products, arithmetic and copies ran while one was open for 3% -> 1% of each run, Pallas kernels for 7% -> 11%
where the time goes in v3:
time: 109 us; the launch traced here: 108 us
  starting transfers between devices  58.5 us (54%)
  waiting for transfers between devices  26.9 us (25%)
  Pallas kernels  15.7 us (14%)
  local copies, waits for them, and re-layouts  4.5 us (4%)
  other arithmetic  1.97 us (2%)
    all_to_all x1, waiting for transfers between devices, on_device(): got = lax.all_to_all(summed, ('z', 'xh', 'xl'), 0, 0, tiled=True)  14.6 us
    all_to_all x1, starting transfers between devices, on_device(): got = lax.all_to_all(summed, ('z', 'xh', 'xl'), 0, 0, tiled=True)  12.6 us
    ppermute x3, starting transfers between devices, on_device(): lax.ppermute(part, TEAM, [(i, i ^ k) for i in range(4)])  12.3 us
    pallas_call x5, Pallas kernels, channel_part(): pl.pallas_call(functools.partial(channel_kernel, count, first, last), out...  8.88 us
    all_to_all x1, waiting for transfers between devices, on_device(): lax.all_to_all(jnp.broadcast_to(own_bias[None, :], (64, SPEC)), MP, 0, 0,...  8.36 us
    ppermute x2, starting transfers between devices, on_device(): near = (lax.ppermute(own, 'rows', ahead), lax.ppermute(own, 'rows', behind))  7.85 us
    all_to_all x1, starting transfers between devices, on_device(): lax.all_to_all(jnp.broadcast_to(own_bias[None, :], (64, SPEC)), MP, 0, 0,...  6.93 us
    ppermute x1, starting transfers between devices, on_device(): lax.ppermute(back, 'rows', behind)  5.01 us
  transfers between devices with their start and end apart: 13, of which 5 were waited for; matrix products, arithmetic and copies ran while one was open for 1% of the time, Pallas kernels for 11%

profile of v3, /device:TPU:1, one launch (start us, length us, event | category | flops | bytes accessed | tf_op | source)
XLA Modules:
  0.0 108.5 jit_solution(8866990075080546011)
XLA Ops:
  0.7 1.9 %pack.1.refs_2_ = s32[72,1024]{1,0:T(8,128)} custom-call(s32[1]{0:T(128)} %bitcast.1.quarter_ref.refs_1_, bf16[1024,512]{1,0:T(8,128)(2,1)} %down_hbm.1, bf16[512,1024]{1,0:T(8,128)(2,1)} %up_hbm.1, f32[1,512]{1,0:T(1,128)} %bitcast.36), custom_call_target="tpu_custom_call" | custom-call | tf_op jit(solution)/shard_map/pack/pallas_call | solution.py:68
  2.6 5.9 %collective-permute-start.2 = (s32[72,1024]{1,0:T(8,128)}, s32[72,1024]{1,0:T(8,128)S(1)}, u32[]{:S(2)}, u32[]{:S(2)}) collective-permute-start(s32[72,1024]{1,0:T(8,128)} %pack.1.refs_2_), channel_id=1, source_target_pairs={{0,448},{64,0},{128,64},{192,128},{256,192},{320,256},{384,320},{4... | collective-permute-start | bytes 884744 | tf_op jit(solution)/shard_map/ppermute | solution.py:317
  8.5 1.9 %collective-permute-start = (s32[72,1024]{1,0:T(8,128)}, s32[72,1024]{1,0:T(8,128)S(1)}, u32[]{:S(2)}, u32[]{:S(2)}) collective-permute-start(s32[72,1024]{1,0:T(8,128)} %pack.1.refs_2_), channel_id=1, source_target_pairs={{0,64},{64,128},{128,192},{192,256},{256,320},{320,384},{384,448},... | collective-permute-start | bytes 884744 | tf_op jit(solution)/shard_map/ppermute | solution.py:317
  10.5 0.9 copy.32
  11.3 2.5 %share.1 = (bf16[96,16,128]{2,1,0:T(8,128)(2,1)}, bf16[96,16,128]{2,1,0:T(8,128)(2,1)}, bf16[96,16,128]{2,1,0:T(8,128)(2,1)}, bf16[96,16,128]{2,1,0:T(8,128)(2,1)}) custom-call(s32[1]{0:T(128)} %bitcast.1.quarter_ref.refs_1_, bf16[8,16,1024]{2,1,0:T(8,128)(2,1)} %bitcast.32, bf16[2,16,4096]{2,1,0:T(8,128)(2,1)} %bitcast.33, bf16[2,16,4096]{2,1,0:T(8,128)(2,1)} %bitcast.34), custom_call_target="tpu_custom_call" | custom-call | tf_op jit(solution)/shard_map/share/pallas_call | solution.py:139
  13.8 0.0 collective-permute-done.2.refs_3_
  13.8 3.8 %collective-permute-start.3 = (bf16[96,16,128]{2,1,0:T(8,128)(2,1)}, bf16[96,16,128]{2,1,0:T(8,128)(2,1)S(1)}, u32[]{:S(2)}, u32[]{:S(2)}) collective-permute-start(bf16[96,16,128]{2,1,0:T(8,128)(2,1)} %get-tuple-element.35), channel_id=1, source_target_pairs={{0,2},{1,3},{2,0},{3,1},{4,6},{5,7},{6,4},{7,5},{8,10},{9,11},{10,... | collective-permute-start | bytes 1179656 | tf_op jit(solution)/shard_map/ppermute | solution.py:326
  17.6 0.0 collective-permute-done.refs_2_
  17.6 2.1 %collective-permute-start.1 = (s32[72,1024]{1,0:T(8,128)S(1)}, s32[72,1024]{1,0:T(8,128)S(1)}, u32[]{:S(2)}, u32[]{:S(2)}) collective-permute-start(s32[72,1024]{1,0:T(8,128)S(1)} %collective-permute-done.refs_2_), channel_id=1, source_target_pairs={{0,64},{64,128},{128,192},{192,256},{256,320},{320,384},{384,448},... | collective-permute-start | bytes 884744 | tf_op jit(solution)/shard_map/ppermute | solution.py:328
  19.8 6.4 %collective-permute-start.8 = (bf16[96,16,128]{2,1,0:T(8,128)(2,1)}, bf16[96,16,128]{2,1,0:T(8,128)(2,1)S(1)}, u32[]{:S(2)}, u32[]{:S(2)}) collective-permute-start(bf16[96,16,128]{2,1,0:T(8,128)(2,1)} %get-tuple-element.41), channel_id=1, source_target_pairs={{0,3},{1,2},{2,1},{3,0},{4,7},{5,6},{6,5},{7,4},{8,11},{9,10},{10,... | collective-permute-start | bytes 1179656 | tf_op jit(solution)/shard_map/ppermute | solution.py:326
  26.2 4.9 %collective-permute-start.7 = (s32[72,1024]{1,0:T(8,128)S(1)}, s32[72,1024]{1,0:T(8,128)S(1)}, u32[]{:S(2)}, u32[]{:S(2)}) collective-permute-start(s32[72,1024]{1,0:T(8,128)S(1)} %collective-permute-done.2.refs_3_), channel_id=1, source_target_pairs={{0,448},{64,0},{128,64},{192,128},{256,192},{320,256},{384,320},{4... | collective-permute-start | bytes 884744 | tf_op jit(solution)/shard_map/ppermute | solution.py:328
  31.1 0.0 collective-permute-done.1.refs_2_
  31.1 1.9 %collective-permute-start.4 = (s32[72,1024]{1,0:T(8,128)S(1)}, s32[72,1024]{1,0:T(8,128)S(1)}, u32[]{:S(2)}, u32[]{:S(2)}) collective-permute-start(s32[72,1024]{1,0:T(8,128)S(1)} %collective-permute-done.1.refs_2_), channel_id=1, source_target_pairs={{0,64},{64,128},{128,192},{192,256},{256,320},{320,384},{384,448},... | collective-permute-start | bytes 884744 | tf_op jit(solution)/shard_map/ppermute | solution.py:331
  33.0 2.1 %collective-permute-start.6 = (bf16[96,16,128]{2,1,0:T(8,128)(2,1)}, bf16[96,16,128]{2,1,0:T(8,128)(2,1)S(1)}, u32[]{:S(2)}, u32[]{:S(2)}) collective-permute-start(bf16[96,16,128]{2,1,0:T(8,128)(2,1)} %get-tuple-element.38), channel_id=1, source_target_pairs={{0,1},{1,0},{2,3},{3,2},{4,5},{5,4},{6,7},{7,6},{8,9},{9,8},{10,11... | collective-permute-start | bytes 1179656 | tf_op jit(solution)/shard_map/ppermute | solution.py:326
  35.1 0.1 and_select_fusion.refs_0_
  35.2 2.2 %collective-permute-done.7.refs_3_ = s32[72,1024]{1,0:T(8,128)S(1)} collective-permute-done((s32[72,1024]{1,0:T(8,128)S(1)}, s32[72,1024]{1,0:T(8,128)S(1)}, u32[]{:S(2)}, u32[]{:S(2)}) %collective-permute-start.7) | collective-permute-done | bytes 294944 | tf_op jit(solution)/shard_map/ppermute | solution.py:328
  37.4 5.0 %collective-permute-start.9 = (s32[72,1024]{1,0:T(8,128)S(1)}, s32[72,1024]{1,0:T(8,128)S(1)}, u32[]{:S(2)}, u32[]{:S(2)}) collective-permute-start(s32[72,1024]{1,0:T(8,128)S(1)} %collective-permute-done.7.refs_3_), channel_id=1, source_target_pairs={{0,448},{64,0},{128,64},{192,128},{256,192},{320,256},{384,320},{4... | collective-permute-start | bytes 884744 | tf_op jit(solution)/shard_map/ppermute | solution.py:331
  42.4 0.2 collective-permute-done.4.refs_2_
  42.6 1.9 %collective-permute-start.5 = (s32[72,1024]{1,0:T(8,128)S(1)}, s32[72,1024]{1,0:T(8,128)S(1)}, u32[]{:S(2)}, u32[]{:S(2)}) collective-permute-start(s32[72,1024]{1,0:T(8,128)S(1)} %collective-permute-done.4.refs_2_), channel_id=1, source_target_pairs={{0,64},{64,128},{128,192},{192,256},{256,320},{320,384},{384,448},... | collective-permute-start | bytes 884744 | tf_op jit(solution)/shard_map/ppermute | solution.py:332
  44.6 0.1 and_select_fusion.1.refs_0_
  44.6 0.1 and_select_fusion.2.refs_0_
  44.7 0.0 collective-permute-done.6.refs_5_
  44.7 1.0 copy-done
  45.7 1.0 copy-done.3
  46.7 1.6 %channel.5 = (f32[512,1024]{1,0:T(8,128)S(1)}, f32[8,8,128]{2,1,0:T(8,128)S(1)}, bf16[512,1024]{1,0:T(8,128)(2,1)S(1)}, bf16[8,4,64,128]{3,2,1,0:T(8,128)(2,1)S(1)}) custom-call(s32[1]{0:T(128)} %bitcast.6.refs_0_, s32[1]{0:T(128)} %bitcast.1.quarter_ref.refs_1_, s32[72,1024]{1,0:T(8,128)S(1)} %copy-done, f32[1,1024]{1,0:T(1,128)S(1)} %bitcast.31, ...), custom_call_target="tpu_custom_call" | custom-call | flops 268435456 | bytes 6586368 | tf_op jit(solution)/shard_map/channel/pallas_call | solution.py:228
  48.3 2.0 %channel.6 = (f32[512,1024]{1,0:T(8,128)S(1)}, f32[8,8,128]{2,1,0:T(8,128)S(1)}) custom-call(s32[2]{0:T(128)S(1)} %and_select_fusion.refs_0_, s32[1]{0:T(128)} %bitcast.1.quarter_ref.refs_1_, s32[72,1024]{1,0:T(8,128)S(1)} %collective-permute-done.refs_2_, ...), custom_call_target="tpu_custom_call", output_to_operand_aliasing={{0}: (6, {}), {1}: (7, {})} | custom-call | flops 536870912 | bytes 6881280 | tf_op jit(solution)/shard_map/channel/pallas_call | solution.py:228
  50.3 2.0 %channel.7 = (f32[512,1024]{1,0:T(8,128)S(1)}, f32[8,8,128]{2,1,0:T(8,128)S(1)}) custom-call(s32[2]{0:T(128)S(1)} %and_select_fusion.1.refs_0_, s32[1]{0:T(128)} %bitcast.1.quarter_ref.refs_1_, s32[72,1024]{1,0:T(8,128)S(1)} %collective-permute-done.1.refs_2_, ...), custom_call_target="tpu_custom_call", output_to_operand_aliasing={{0}: (6, {}), {1}: (7, {})} | custom-call | flops 536870912 | bytes 6881280 | tf_op jit(solution)/shard_map/channel/pallas_call | solution.py:228
  52.3 0.0 collective-permute-done.9.refs_3_
  52.3 2.0 %channel.8 = (f32[512,1024]{1,0:T(8,128)S(1)}, f32[8,8,128]{2,1,0:T(8,128)S(1)}) custom-call(s32[2]{0:T(128)S(1)} %and_select_fusion.2.refs_0_, s32[1]{0:T(128)} %bitcast.1.quarter_ref.refs_1_, s32[72,1024]{1,0:T(8,128)S(1)} %collective-permute-done.4.refs_2_, ...), custom_call_target="tpu_custom_call", output_to_operand_aliasing={{0}: (6, {}), {1}: (7, {})} | custom-call | flops 536870912 | bytes 6881280 | tf_op jit(solution)/shard_map/channel/pallas_call | solution.py:228
  54.3 0.0 collective-permute-done.5.refs_2_
  54.3 1.3 %channel.9 = (f32[32,16,512]{2,1,0:T(8,128)S(1)}, bf16[32,16,512]{2,1,0:T(8,128)(2,1)S(1)}, f32[8,8,128]{2,1,0:T(8,128)S(1)}) custom-call(s32[1]{0:T(128)} %bitcast.refs_0_, s32[1]{0:T(128)} %bitcast.1.quarter_ref.refs_1_, s32[72,1024]{1,0:T(8,128)S(1)} %collective-permute-done.5.refs_2_, bf16[512,1024]{1,0:T(8,128)(2,1)S(1)} %get-tuple-element.43.refs_4_.refs_3_, ...), custom_call_target="tpu_custom_call" | custom-call | flops 268435456 | bytes 6586368 | tf_op jit(solution)/shard_map/channel/pallas_call | solution.py:228
  55.6 0.0 copy-start.1
  55.7 0.0 copy-start.7
  55.7 3.0 %collective-permute-start.10 = (bf16[32,16,512]{2,1,0:T(8,128)(2,1)S(1)}, bf16[32,16,512]{2,1,0:T(8,128)(2,1)S(1)}, u32[]{:S(2)}, u32[]{:S(2)}) collective-permute-start(bf16[32,16,512]{2,1,0:T(8,128)(2,1)S(1)} %get-tuple-element.55), channel_id=1, source_target_pairs={{0,1},{1,0},{2,3},{3,2},{4,5},{5,4},{6,7},{7,6},{8,9},{9,8},{10,11... | collective-permute-start | bytes 1572872 | tf_op jit(solution)/shard_map/ppermute | solution.py:349
  58.7 1.5 %collective-permute-done.10 = bf16[32,16,512]{2,1,0:T(8,128)(2,1)S(1)} collective-permute-done((bf16[32,16,512]{2,1,0:T(8,128)(2,1)S(1)}, bf16[32,16,512]{2,1,0:T(8,128)(2,1)S(1)}, u32[]{:S(2)}, u32[]{:S(2)}) %collective-permute-start.10) | collective-permute-done | bytes 524320 | tf_op jit(solution)/shard_map/ppermute | solution.py:349
  60.2 1.0 add_convert_fusion
  61.2 12.6 %all-to-all-start = ((bf16[32,16,512]{2,1,0:T(8,128)(2,1)}), bf16[32,16,512]{2,1,0:T(8,128)(2,1)S(1)}, u32[]{:S(2)}, u32[]{:S(2)}) async-start(bf16[32,16,512]{2,1,0:T(8,128)(2,1)} %add_convert_fusion), calls=%async_computation | async-start | bytes 1048576 | tf_op jit(solution)/shard_map/all_to_all | solution.py:350
  73.8 0.0 copy-start.2
  73.8 1.0 copy-done.2
  74.8 0.9 dense.1
  75.8 14.6 %all-to-all-done.got_ref = bf16[32,16,512]{2,1,0:T(8,128)(2,1)S(1)} async-done(((bf16[32,16,512]{2,1,0:T(8,128)(2,1)}), bf16[32,16,512]{2,1,0:T(8,128)(2,1)S(1)}, u32[]{:S(2)}, u32[]{:S(2)}) %all-to-all-start) | async-done | bytes 524320 | tf_op jit(solution)/shard_map/all_to_all | solution.py:350
  90.4 0.4 token_.1
  90.8 0.1 add_reduce_fusion
  90.9 0.6 broadcast_in_dim.2
  91.6 6.9 %all-to-all-start.1 = ((f32[64,1,8]{2,1,0:T(1,128)}), f32[64,1,8]{2,1,0:T(1,128)S(1)}, u32[]{:S(2)}, u32[]{:S(2)}) async-start(f32[64,1,8]{2,1,0:T(1,128)} %broadcast_in_dim.2), calls=%async_computation.1 | async-start | bytes 65536 | tf_op jit(solution)/shard_map/all_to_all | solution.py:353
  98.5 1.0 back.1
  99.5 8.4 %all-to-all-done.1 = f32[64,1,8]{2,1,0:T(1,128)S(1)} async-done(((f32[64,1,8]{2,1,0:T(1,128)}), f32[64,1,8]{2,1,0:T(1,128)S(1)}, u32[]{:S(2)}, u32[]{:S(2)}) %all-to-all-start.1) | async-done | bytes 2080 | tf_op jit(solution)/shard_map/all_to_all | solution.py:353
  107.9 0.6 reduce_sum.19
  (14 shorter events, 0.0 us)
Async XLA Ops:
  0.6 9.8 %copy-start.8 = (bf16[16,8,1024]{2,1,0:T(8,128)(2,1)S(1)}, bf16[16,8,1024]{2,1,0:T(8,128)(2,1)}, u32[]{:S(2)}) copy-start(bf16[16,8,1024]{2,1,0:T(8,128)(2,1)} %param.12) | copy-start | bytes 786436
  0.6 44.1 %copy-start.6 = (f32[1024]{0:T(1024)S(1)}, f32[1024]{0:T(1024)}, u32[]{:S(2)}) copy-start(f32[1024]{0:T(1024)} %param.14) | copy-start | bytes 12292
  2.6 11.2 %collective-permute-start.2 = (s32[72,1024]{1,0:T(8,128)}, s32[72,1024]{1,0:T(8,128)S(1)}, u32[]{:S(2)}, u32[]{:S(2)}) collective-permute-start(s32[72,1024]{1,0:T(8,128)} %pack.1.refs_2_), channel_id=1, source_target_pairs={{0,448},{64,0},{128,64},{192,128},{256,192},{320,256},{384,320},{4... | collective-permute-start | bytes 884744 | tf_op jit(solution)/shard_map/ppermute | solution.py:317
  8.5 9.1 %collective-permute-start = (s32[72,1024]{1,0:T(8,128)}, s32[72,1024]{1,0:T(8,128)S(1)}, u32[]{:S(2)}, u32[]{:S(2)}) collective-permute-start(s32[72,1024]{1,0:T(8,128)} %pack.1.refs_2_), channel_id=1, source_target_pairs={{0,64},{64,128},{128,192},{192,256},{256,320},{320,384},{384,448},... | collective-permute-start | bytes 884744 | tf_op jit(solution)/shard_map/ppermute | solution.py:317
  13.8 17.2 %collective-permute-start.3 = (bf16[96,16,128]{2,1,0:T(8,128)(2,1)}, bf16[96,16,128]{2,1,0:T(8,128)(2,1)S(1)}, u32[]{:S(2)}, u32[]{:S(2)}) collective-permute-start(bf16[96,16,128]{2,1,0:T(8,128)(2,1)} %get-tuple-element.35), channel_id=1, source_target_pairs={{0,2},{1,3},{2,0},{3,1},{4,6},{5,7},{6,4},{7,5},{8,10},{9,11},{10,... | collective-permute-start | bytes 1179656 | tf_op jit(solution)/shard_map/ppermute | solution.py:326
  17.6 13.4 %collective-permute-start.1 = (s32[72,1024]{1,0:T(8,128)S(1)}, s32[72,1024]{1,0:T(8,128)S(1)}, u32[]{:S(2)}, u32[]{:S(2)}) collective-permute-start(s32[72,1024]{1,0:T(8,128)S(1)} %collective-permute-done.refs_2_), channel_id=1, source_target_pairs={{0,64},{64,128},{128,192},{192,256},{256,320},{320,384},{384,448},... | collective-permute-start | bytes 884744 | tf_op jit(solution)/shard_map/ppermute | solution.py:328
  19.8 17.7 %collective-permute-start.8 = (bf16[96,16,128]{2,1,0:T(8,128)(2,1)}, bf16[96,16,128]{2,1,0:T(8,128)(2,1)S(1)}, u32[]{:S(2)}, u32[]{:S(2)}) collective-permute-start(bf16[96,16,128]{2,1,0:T(8,128)(2,1)} %get-tuple-element.41), channel_id=1, source_target_pairs={{0,3},{1,2},{2,1},{3,0},{4,7},{5,6},{6,5},{7,4},{8,11},{9,10},{10,... | collective-permute-start | bytes 1179656 | tf_op jit(solution)/shard_map/ppermute | solution.py:326
  26.2 11.2 %collective-permute-start.7 = (s32[72,1024]{1,0:T(8,128)S(1)}, s32[72,1024]{1,0:T(8,128)S(1)}, u32[]{:S(2)}, u32[]{:S(2)}) collective-permute-start(s32[72,1024]{1,0:T(8,128)S(1)} %collective-permute-done.2.refs_3_), channel_id=1, source_target_pairs={{0,448},{64,0},{128,64},{192,128},{256,192},{320,256},{384,320},{4... | collective-permute-start | bytes 884744 | tf_op jit(solution)/shard_map/ppermute | solution.py:328
  31.1 11.6 %collective-permute-start.4 = (s32[72,1024]{1,0:T(8,128)S(1)}, s32[72,1024]{1,0:T(8,128)S(1)}, u32[]{:S(2)}, u32[]{:S(2)}) collective-permute-start(s32[72,1024]{1,0:T(8,128)S(1)} %collective-permute-done.1.refs_2_), channel_id=1, source_target_pairs={{0,64},{64,128},{128,192},{192,256},{256,320},{320,384},{384,448},... | collective-permute-start | bytes 884744 | tf_op jit(solution)/shard_map/ppermute | solution.py:331
  33.0 11.7 %collective-permute-start.6 = (bf16[96,16,128]{2,1,0:T(8,128)(2,1)}, bf16[96,16,128]{2,1,0:T(8,128)(2,1)S(1)}, u32[]{:S(2)}, u32[]{:S(2)}) collective-permute-start(bf16[96,16,128]{2,1,0:T(8,128)(2,1)} %get-tuple-element.38), channel_id=1, source_target_pairs={{0,1},{1,0},{2,3},{3,2},{4,5},{5,4},{6,7},{7,6},{8,9},{9,8},{10,11... | collective-permute-start | bytes 1179656 | tf_op jit(solution)/shard_map/ppermute | solution.py:326
  37.4 14.9 %collective-permute-start.9 = (s32[72,1024]{1,0:T(8,128)S(1)}, s32[72,1024]{1,0:T(8,128)S(1)}, u32[]{:S(2)}, u32[]{:S(2)}) collective-permute-start(s32[72,1024]{1,0:T(8,128)S(1)} %collective-permute-done.7.refs_3_), channel_id=1, source_target_pairs={{0,448},{64,0},{128,64},{192,128},{256,192},{320,256},{384,320},{4... | collective-permute-start | bytes 884744 | tf_op jit(solution)/shard_map/ppermute | solution.py:331
  42.6 11.6 %collective-permute-start.5 = (s32[72,1024]{1,0:T(8,128)S(1)}, s32[72,1024]{1,0:T(8,128)S(1)}, u32[]{:S(2)}, u32[]{:S(2)}) collective-permute-start(s32[72,1024]{1,0:T(8,128)S(1)} %collective-permute-done.4.refs_2_), channel_id=1, source_target_pairs={{0,64},{64,128},{128,192},{192,256},{256,320},{320,384},{384,448},... | collective-permute-start | bytes 884744 | tf_op jit(solution)/shard_map/ppermute | solution.py:332
  44.7 1.0 copy-start
  45.7 1.0 copy-start.3
  55.6 18.1 %copy-start.1 = (bf16[16,128,128]{2,1,0:T(8,128)(2,1)S(1)}, bf16[16,128,128]{2,1,0:T(8,128)(2,1)}, u32[]{:S(2)}) copy-start(bf16[16,128,128]{2,1,0:T(8,128)(2,1)} %in_ref.1) | copy-start | bytes 1572868
  55.7 18.1 %copy-start.7 = (s32[16]{0:T(128)S(1)}, s32[16]{0:T(128)}, u32[]{:S(2)}) copy-start(s32[16]{0:T(128)} %cells_ref.1) | copy-start | bytes 196
  55.7 4.5 %collective-permute-start.10 = (bf16[32,16,512]{2,1,0:T(8,128)(2,1)S(1)}, bf16[32,16,512]{2,1,0:T(8,128)(2,1)S(1)}, u32[]{:S(2)}, u32[]{:S(2)}) collective-permute-start(bf16[32,16,512]{2,1,0:T(8,128)(2,1)S(1)} %get-tuple-element.55), channel_id=1, source_target_pairs={{0,1},{1,0},{2,3},{3,2},{4,5},{5,4},{6,7},{7,6},{8,9},{9,8},{10,11... | collective-permute-start | bytes 1572872 | tf_op jit(solution)/shard_map/ppermute | solution.py:349
  60.2 30.2 %copy-start.4 = (bf16[2,512,1,16]{1,3,2,0:T(8,128)(2,1)S(1)}, bf16[2,512,1,16]{1,3,2,0:T(8,128)(2,1)}, u32[]{:S(2)}) copy-start(bf16[2,512,1,16]{1,3,2,0:T(8,128)(2,1)} %param.22) | copy-start | bytes 98308
  60.2 30.2 %copy-start.5 = (bf16[2,512,1,16]{1,3,2,0:T(8,128)(2,1)S(1)}, bf16[2,512,1,16]{1,3,2,0:T(8,128)(2,1)}, u32[]{:S(2)}) copy-start(bf16[2,512,1,16]{1,3,2,0:T(8,128)(2,1)} %param.23) | copy-start | bytes 98308
  61.2 29.2 %all-to-all-start = ((bf16[32,16,512]{2,1,0:T(8,128)(2,1)}), bf16[32,16,512]{2,1,0:T(8,128)(2,1)S(1)}, u32[]{:S(2)}, u32[]{:S(2)}) async-start(bf16[32,16,512]{2,1,0:T(8,128)(2,1)} %add_convert_fusion), calls=%async_computation | async-start | bytes 1048576 | tf_op jit(solution)/shard_map/all_to_all | solution.py:350
  73.8 1.0 copy-start.2
  91.6 16.3 %all-to-all-start.1 = ((f32[64,1,8]{2,1,0:T(1,128)}), f32[64,1,8]{2,1,0:T(1,128)S(1)}, u32[]{:S(2)}, u32[]{:S(2)}) async-start(f32[64,1,8]{2,1,0:T(1,128)} %broadcast_in_dim.2), calls=%async_computation.1 | async-start | bytes 65536 | tf_op jit(solution)/shard_map/all_to_all | solution.py:353

commit v4 on v3

--- a/solution.py
+++ b/solution.py
@@ -25,10 +25,11 @@
 SWAP = [(0, 1), (1, 0)]
 VMEM = 32 * 1024 * 1024
 
-PART = 128
+PART = 256
+STEPS = 4
 SHARED = 64
 ROWS_DEV = SPEC * SHARED
-PACKED = 72
+PACKED = 136
 LAM_TILES = SPEC * (D // 128)
 SCALE_ONE = float(2**38)
 
@@ -43,8 +44,8 @@
     return (shifted >> 24).astype(F32).astype(BF16)
 
 
-def pack_kernel(quarter_ref, down_hbm, up_hbm, scale_hbm, out_ref, down_ref, up_ref, scale_ref, sems):
-    start = pl.multiple_of(quarter_ref[0] * PART, PART)
+def pack_kernel(half_ref, down_hbm, up_hbm, scale_hbm, out_ref, down_ref, up_ref, scale_ref, sems):
+    start = pl.multiple_of(half_ref[0] * PART, PART)
     copies = [
         pltpu.make_async_copy(down_hbm.at[:, pl.ds(start, PART)], down_ref, sems.at[0]),
         pltpu.make_async_copy(up_hbm.at[pl.ds(start, PART), :], up_ref, sems.at[1]),
@@ -52,19 +53,19 @@
     ]
     for copy in copies:
         copy.start()
-    out_ref[64:72, :] = jnp.zeros((8, D), I32)
+    out_ref[128:136, :] = jnp.zeros((8, D), I32)
     copies[0].wait()
     down = pack_codes([down_ref[m * 256 : (m + 1) * 256, :] for m in range(4)])
-    for k in range(8):
-        out_ref[0:32, k * PART : (k + 1) * PART] = down[k * 32 : (k + 1) * 32, :]
+    for k in range(4):
+        out_ref[0:64, k * PART : (k + 1) * PART] = down[k * 64 : (k + 1) * 64, :]
     copies[1].wait()
-    out_ref[32:64, :] = pack_codes([up_ref[m * 32 : (m + 1) * 32, :] for m in range(4)])
+    out_ref[64:128, :] = pack_codes([up_ref[m * 64 : (m + 1) * 64, :] for m in range(4)])
     copies[2].wait()
     scale = (scale_ref[...] * SCALE_ONE).astype(I32)
-    out_ref[64:72, 0:PART] = jnp.broadcast_to(scale, (8, PART))
-
-
-def pack(quarter, q_down, q_up, up_scale):
+    out_ref[128:136, 0:PART] = jnp.broadcast_to(scale, (8, PART))
+
+
+def pack(half, q_down, q_up, up_scale):
     return pl.pallas_call(
         pack_kernel,
         out_shape=jax.ShapeDtypeStruct((PACKED, D), I32),
@@ -79,7 +80,7 @@
         ],
         compiler_params=pltpu.CompilerParams(vmem_limit_bytes=60 * 1024 * 1024),
         name="pack",
-    )(quarter, q_down, q_up, up_scale.reshape(1, -1))
+    )(half, q_down, q_up, up_scale.reshape(1, -1))
 
 
 def dense_kernel(cells_ref, in_ref, out_ref, dense_in_ref, dense_out_ref):
@@ -120,22 +121,31 @@
     return mid, pos * icpt_low.astype(F32) + neg * icpt_high.astype(F32)
 
 
-def share_kernel(quarter_ref, lam_ref, slopes_ref, icpt_ref, *out_refs):
+def share_kernel(place_ref, lam_ref, slopes_ref, icpt_ref, *out_refs):
     for r in range(SPEC):
         for k in range(D // 128):
             tile = lam_ref[r, :, k * 128 : (k + 1) * 128]
             for out_ref in out_refs:
                 out_ref[r * (D // 128) + k] = tile
+    row = place_ref[1]
     for k, out_ref in enumerate(out_refs):
-        for y in range(CH // TH):
-            start = pl.multiple_of(y * TH + (quarter_ref[0] ^ k) * PART, PART)
-            for kind in range(2):
-                out_ref[LAM_TILES + y * 4 + kind] = slopes_ref[kind, :, pl.ds(start, PART)]
-                out_ref[LAM_TILES + y * 4 + 2 + kind] = icpt_ref[kind, :, pl.ds(start, PART)]
-
-
-def share(quarter, by_row, slopes, icpt):
-    tiles = LAM_TILES + 4 * (CH // TH)
+        to = place_ref[0] ^ k
+        sign = 2 * (to & 1) - 1
+        for j in range(STEPS):
+            if j < STEPS - 1:
+                owner = row + sign * (j + 1)
+            else:
+                owner = row - STEPS * (1 - (to & 1))
+            start = pl.multiple_of((owner & 7) * TH + (to >> 1) * PART, PART)
+            for kind in range(4):
+                ref = slopes_ref if kind < 2 else icpt_ref
+                values = ref[kind % 2, :, pl.ds(start, PART)]
+                for h in range(2):
+                    out_ref[LAM_TILES + (j * 4 + kind) * 2 + h] = values[:, h * 128 : (h + 1) * 128]
+
+
+def share(place, by_row, slopes, icpt):
+    tiles = LAM_TILES + 4 * STEPS * 2
     return pl.pallas_call(
         share_kernel,
         out_shape=(jax.ShapeDtypeStruct((tiles, 16, 128), BF16),) * 4,
@@ -143,51 +153,49 @@
         + [pl.BlockSpec(memory_space=pltpu.VMEM)] * 3,
         compiler_params=pltpu.CompilerParams(vmem_limit_bytes=60 * 1024 * 1024),
         name="share",
-    )(quarter, by_row, slopes, icpt)
-
-
-def channel_kernel(count, first, last, *refs):
-    where_ref, place_ref = refs[:2]
-    refs = refs[2:]
-    words, refs = refs[:count], refs[count:]
+    )(place, by_row, slopes, icpt)
+
+
+def channel_kernel(step, *refs):
+    first, last = step == 0, step == STEPS - 1
+    place_ref, words_ref, *refs = refs
     if first:
         down_scale_ref, *team, acc_ref, bias_ref, scaled_ref, bounds_ref, down, up = refs
-        for j, got_ref in enumerate(team):
-            start = (place_ref[0] ^ j) * 16
+        for k, got_ref in enumerate(team):
+            start = (place_ref[0] ^ k) * 16
             for r in range(SPEC):
                 rows = pl.ds(pl.multiple_of(r * SHARED + start, 16), 16)
-                for k in range(D // 128):
-                    cut = slice(k * 128, (k + 1) * 128)
-                    lam = got_ref[r * (D // 128) + k].astype(F32)
+                for c in range(D // 128):
+                    cut = slice(c * 128, (c + 1) * 128)
+                    lam = got_ref[r * (D // 128) + c].astype(F32)
                     scaled_ref[rows, cut] = (lam * down_scale_ref[:, cut]).astype(BF16)
                     acc_ref[rows, cut] = 0.25 * lam
             rows = pl.ds(pl.multiple_of(start, 16), 16)
-            for y in range(CH // TH):
-                for kind in range(4):
-                    bounds_ref[y, kind, rows, :] = got_ref[LAM_TILES + y * 4 + kind]
+            for i in range(STEPS * 4):
+                for h in range(2):
+                    tile = got_ref[LAM_TILES + i * 2 + h]
+                    bounds_ref[i // 4, i % 4, rows, h * 128 : (h + 1) * 128] = tile
         acc_in, bias_in = acc_ref, None
     else:
+        if last:
+            own_ref, *refs = refs
         scaled_ref, bounds_ref, acc_in, bias_in, *outs, down, up = refs
-    scales, bounds = [], []
-    for k, words_ref in enumerate(words):
-        for m in range(4):
-            codes = unpack_codes(words_ref[0:32, :], m)
-            for q in range(8):
-                rows = m * 256 + q * 32
-                cut = slice(q * PART, (q + 1) * PART)
-                down[rows : rows + 32, k * PART : (k + 1) * PART] = codes[:, cut]
-            rows = k * PART + m * 32
-            up[rows : rows + 32, :] = unpack_codes(words_ref[32:64, :], m)
-        scales.append(words_ref[64:65, 0:PART].astype(F32) * (1.0 / SCALE_ONE))
-        bounds.append(bounds_ref.at[where_ref[k]])
-    scale = jnp.concatenate(scales, axis=1)
-    bounds = [jnp.concatenate([b[kind] for b in bounds], axis=1) for kind in range(4)]
+    words = words_ref[...]
+    if last:
+        words = jnp.where(place_ref[0] % 2 == 0, words, own_ref[...])
+    for m in range(4):
+        codes = unpack_codes(words[0:64], m)
+        for q in range(4):
+            rows = m * 256 + q * 64
+            down[rows : rows + 64, :] = codes[:, q * PART : (q + 1) * PART]
+        up[m * 64 : (m + 1) * 64, :] = unpack_codes(words[64:128], m)
+    scale = words[128:129, 0:PART].astype(F32) * (1.0 / SCALE_ONE)
     pre = jnp.dot(scaled_ref[...], down[...], preferred_element_type=F32)
-    pre = pre.reshape(SPEC, SHARED, count * PART)
-    mid, terms = relaxed(pre, *bounds)
-    terms = jnp.sum(terms.reshape(SPEC, SHARED // 8, 8, count * PART), axis=1)
-    bias = sum(terms[:, :, k * PART : (k + 1) * PART] for k in range(count))
-    weighted = (mid.reshape(ROWS_DEV, count * PART) * scale).astype(BF16)
+    pre = pre.reshape(SPEC, SHARED, PART)
+    mid, terms = relaxed(pre, *(bounds_ref[step, kind] for kind in range(4)))
+    terms = jnp.sum(terms.reshape(SPEC, SHARED // 8, 8, PART), axis=1)
+    bias = terms[:, :, 0:128] + terms[:, :, 128:256]
+    weighted = (mid.reshape(ROWS_DEV, PART) * scale).astype(BF16)
     part = jnp.dot(weighted, up[...], preferred_element_type=F32)
     total = acc_in[...] + part
     if not first:
@@ -205,17 +213,16 @@
     bias_ref[...] = bias
 
 
-def channel_part(where, place, words, rest, first=False, last=False):
-    count = len(words)
+def channel_part(step, place, *rest):
     acc_shape = jax.ShapeDtypeStruct((ROWS_DEV, D), F32)
     bias_shape = jax.ShapeDtypeStruct((SPEC, 8, 128), F32)
-    operands = [where.astype(I32), place, *words, *rest]
+    operands = [place, *rest]
     aliases = {}
-    if first:
+    if step == 0:
         scaled_shape = jax.ShapeDtypeStruct((ROWS_DEV, D), BF16)
-        bounds_shape = jax.ShapeDtypeStruct((CH // TH, 4, SHARED, PART), BF16)
+        bounds_shape = jax.ShapeDtypeStruct((STEPS, 4, SHARED, PART), BF16)
         out_shape = (acc_shape, bias_shape, scaled_shape, bounds_shape)
-    elif last:
+    elif step == STEPS - 1:
         out_shape = (
             jax.ShapeDtypeStruct((32, 16, ROWS_DEV), F32),
             jax.ShapeDtypeStruct((32, 16, ROWS_DEV), BF16),
@@ -226,19 +233,16 @@
         aliases = {len(operands) - 2: 0, len(operands) - 1: 1}
     smem, vmem = pl.BlockSpec(memory_space=pltpu.SMEM), pl.BlockSpec(memory_space=pltpu.VMEM)
     return pl.pallas_call(
-        functools.partial(channel_kernel, count, first, last),
+        functools.partial(channel_kernel, step),
         out_shape=out_shape,
-        in_specs=[smem, smem] + [vmem] * (len(operands) - 2),
+        in_specs=[smem] + [vmem] * (len(operands) - 1),
         out_specs=(vmem,) * len(out_shape),
-        scratch_shapes=[
-            pltpu.VMEM((D, count * PART), BF16),
-            pltpu.VMEM((count * PART, D), BF16),
-        ],
+        scratch_shapes=[pltpu.VMEM((D, PART), BF16), pltpu.VMEM((PART, D), BF16)],
         input_output_aliases=aliases,
         compiler_params=pltpu.CompilerParams(vmem_limit_bytes=VMEM),
         cost_estimate=pl.CostEstimate(
-            flops=count * 4 * ROWS_DEV * PART * D,
-            bytes_accessed=count * PACKED * D * 4 + 3 * ROWS_DEV * D * 4,
+            flops=4 * ROWS_DEV * PART * D,
+            bytes_accessed=PACKED * D * 4 + 3 * ROWS_DEV * D * 4,
             transcendentals=0,
         ),
         name="channel",
@@ -307,45 +311,43 @@
     tok_slopes,
     tok_icpt,
 ):
-    quarter = lax.axis_index(TEAM).astype(I32).reshape(1)
+    quarter, row = lax.axis_index(TEAM).astype(I32), lax.axis_index("rows").astype(I32)
+    place = jnp.stack([quarter, row])
+    half = (quarter >> 1).reshape(1)
     tok_dev = lam_out.shape[0]
     slices = lax.axis_size("rows")
-    ahead = [(i, (i + 1) % slices) for i in range(slices)]
-    behind = [(i, (i - 1) % slices) for i in range(slices)]
-
-    own = pack(quarter, q_down, q_up, up_scale)
-    near = (lax.ppermute(own, "rows", ahead), lax.ppermute(own, "rows", behind))
+    ahead = [(i * 2, (i + 1) % slices * 2) for i in range(slices)]
+    behind = [(i * 2 + 1, (i - 1) % slices * 2 + 1) for i in range(slices)]
+
+    def forward(words, pairs):
+        return lax.ppermute(words, ("rows", "core"), pairs)
+
+    own = pack(half, q_down, q_up, up_scale)
+    first = forward(own, ahead + behind)
     own_part, *parts = share(
-        quarter,
+        place,
         jnp.swapaxes(lam_out, 0, 1),
         chan_slopes.reshape(2, tok_dev, CH),
         chan_icpt.reshape(2, tok_dev, CH),
     )
-    onward, parts = lax.optimization_barrier((near[1], parts))
+    words, parts = lax.optimization_barrier((first, parts))
+    second = forward(words, ahead + behind)
     team = [own_part] + [
         lax.ppermute(part, TEAM, [(i, i ^ k) for i in range(4)]) for k, part in enumerate(parts, 1)
     ]
-    second = (lax.ppermute(near[0], "rows", ahead), lax.ppermute(onward, "rows", behind))
-    onward, team[2] = lax.optimization_barrier((second[0], team[2]))
-    back, team[3] = lax.optimization_barrier((second[1], team[3]))
-    third = (lax.ppermute(onward, "rows", ahead), lax.ppermute(back, "rows", behind))
-    far = lax.ppermute(third[0], "rows", ahead)
+    words, team[2] = lax.optimization_barrier((second, team[2]))
+    third = forward(words, ahead + behind)
+    words, team[1], team[3] = lax.optimization_barrier((third, team[1], team[3]))
+    far = forward(words, ahead)
 
     dense_in, dense_out = dense_blocks(block_cells, tok_in_blocks, tok_out_blocks)
     slopes = jnp.transpose(tok_slopes, (0, 2, 3, 1)).reshape(2, 16, TH)
     icpt = jnp.transpose(tok_icpt, (0, 2, 3, 1)).reshape(2, 16, TH)
 
-    me = lax.axis_index("rows")
-    acc, chan_bias, *given = channel_part(
-        me.reshape(1), quarter, [own], [down_scale.reshape(1, D), *team], first=True
-    )
-    for k, words in enumerate((near, second, third), 1):
-        at = jnp.stack([me - k, me + k]) % slices
-        acc, chan_bias = channel_part(at, quarter, words, [*given, acc, chan_bias])
-    at = ((me + slices // 2) % slices).reshape(1)
-    keep, send, chan_bias = channel_part(
-        at, quarter, [far], [*given, acc, chan_bias], last=True
-    )
+    acc, chan_bias, *given = channel_part(0, place, first, down_scale.reshape(1, D), *team)
+    acc, chan_bias = channel_part(1, place, second, *given, acc, chan_bias)
+    acc, chan_bias = channel_part(2, place, third, *given, acc, chan_bias)
+    keep, send, chan_bias = channel_part(3, place, far, own, *given, acc, chan_bias)
     summed = (keep + lax.ppermute(send, "core", SWAP).astype(F32)).astype(BF16)
     got = lax.all_to_all(summed, ("z", "xh", "xl"), 0, 0, tiled=True)
     columns, mid, tok_bias = token_mlp(got, dense_out, slopes, icpt)

time: 109 us -> 118 us (1.083)
  waiting for transfers between devices: 26.9 us -> 44.4 us
  starting transfers between devices: 58.5 us -> 50.4 us
    ppermute x3, waiting for transfers between devices: 0.01 us -> 17.1 us  [on_device(): lax.ppermute(part, TEAM, [(i, i ^ k) for i in range(4)])]
    ppermute x7 -> x4, starting transfers between devices: 23.7 us -> 13.7 us  [forward(): return lax.ppermute(words, ('rows', 'core'), pairs)]
    ppermute x1, starting transfers between devices: 3.01 us -> 6.28 us  [on_device(): summed = (keep + lax.ppermute(send, 'core', SWAP).astype(F32)).astype(BF16)]
    all_to_all x1, starting transfers between devices: 12.6 us -> 11.4 us  [on_device(): got = lax.all_to_all(summed, ('z', 'xh', 'xl'), 0, 0, tiled=True)]
    pallas_call x5 -> x4, Pallas kernels: 8.88 us -> 7.97 us  [channel_part(): pl.pallas_call(functools.partial(channel_kernel, step), out_shape=out_sha...]
    ppermute x7 -> x4, waiting for transfers between devices: 2.44 us -> 2.84 us  [forward(): return lax.ppermute(words, ('rows', 'core'), pairs)]
    unnamed x19 -> x23, local copies, waits for them, and re-layouts: 3.87 us -> 3.53 us
  transfers between devices with their start and end apart: 13 -> 10, of which waited for: 5 -> 6; matrix products, arithmetic and copies ran while one was open for 1% -> 1% of each run, Pallas kernels for 11% -> 9%
where the time goes in v4:
time: 118 us; the launch traced here: 117 us
  starting transfers between devices  50.4 us (43%)
  waiting for transfers between devices  44.4 us (38%)
  Pallas kernels  15 us (13%)
  local copies, waits for them, and re-layouts  4.18 us (4%)
  other arithmetic  2.33 us (2%)
    ppermute x3, waiting for transfers between devices, on_device(): lax.ppermute(part, TEAM, [(i, i ^ k) for i in range(4)])  17.1 us
    all_to_all x1, waiting for transfers between devices, on_device(): got = lax.all_to_all(summed, ('z', 'xh', 'xl'), 0, 0, tiled=True)  14.6 us
    ppermute x4, starting transfers between devices, forward(): return lax.ppermute(words, ('rows', 'core'), pairs)  13.7 us
    ppermute x3, starting transfers between devices, on_device(): lax.ppermute(part, TEAM, [(i, i ^ k) for i in range(4)])  12.1 us
    all_to_all x1, starting transfers between devices, on_device(): got = lax.all_to_all(summed, ('z', 'xh', 'xl'), 0, 0, tiled=True)  11.4 us
    all_to_all x1, waiting for transfers between devices, on_device(): lax.all_to_all(jnp.broadcast_to(own_bias[None, :], (64, SPEC)), MP, 0, 0,...  8.36 us
    pallas_call x4, Pallas kernels, channel_part(): pl.pallas_call(functools.partial(channel_kernel, step), out_shape=out_sha...  7.97 us
    all_to_all x1, starting transfers between devices, on_device(): lax.all_to_all(jnp.broadcast_to(own_bias[None, :], (64, SPEC)), MP, 0, 0,...  6.93 us
  transfers between devices with their start and end apart: 10, of which 6 were waited for; matrix products, arithmetic and copies ran while one was open for 1% of the time, Pallas kernels for 9%

profile of v4, /device:TPU:1, one launch (start us, length us, event | category | flops | bytes accessed | tf_op | source)
XLA Modules:
  0.0 117.3 jit_solution(14335176435256867096)
XLA Ops:
  0.6 0.0 copy-start.10
  0.6 0.0 copy-start.8
  0.7 2.3 %pack.1.refs_2_ = s32[136,1024]{1,0:T(8,128)} custom-call(s32[1]{0:T(128)} %bitcast.2.half_ref, bf16[1024,512]{1,0:T(8,128)(2,1)} %down_hbm.1, bf16[512,1024]{1,0:T(8,128)(2,1)} %up_hbm.1, f32[1,512]{1,0:T(1,128)} %bitcast.30), custom_call_target="tpu_custom_call" | custom-call | tf_op jit(solution)/shard_map/pack/pallas_call | solution.py:69
  2.9 5.9 %collective-permute-start = (s32[136,1024]{1,0:T(8,128)}, s32[136,1024]{1,0:T(8,128)S(1)}, u32[]{:S(2)}, u32[]{:S(2)}) collective-permute-start(s32[136,1024]{1,0:T(8,128)} %pack.1.refs_2_), channel_id=1, source_target_pairs={{0,64},{64,128},{128,192},{192,256},{256,320},{320,384},{384,448},... | collective-permute-start | bytes 1671176 | tf_op jit(solution)/shard_map/ppermute | solution.py:323
  8.9 0.0 copy-done.10
  8.9 0.9 copy.30
  9.7 0.6 pad_add_fusion.place_ref.refs_0_
  10.3 2.5 %share.1 = (bf16[96,16,128]{2,1,0:T(8,128)(2,1)}, bf16[96,16,128]{2,1,0:T(8,128)(2,1)}, bf16[96,16,128]{2,1,0:T(8,128)(2,1)}, bf16[96,16,128]{2,1,0:T(8,128)(2,1)}) custom-call(s32[2]{0:T(128)} %pad_add_fusion.place_ref.refs_0_, bf16[8,16,1024]{2,1,0:T(8,128)(2,1)} %bitcast.26, bf16[2,16,4096]{2,1,0:T(8,128)(2,1)} %bitcast.27, bf16[2,16,4096]{2,1,0:T(8,128)(2,1)} %bitcast.28), custom_call_target="tpu_custom_call" | custom-call | tf_op jit(solution)/shard_map/share/pallas_call | solution.py:149
  12.8 2.8 %collective-permute-done.refs_1_ = s32[136,1024]{1,0:T(8,128)S(1)} collective-permute-done((s32[136,1024]{1,0:T(8,128)}, s32[136,1024]{1,0:T(8,128)S(1)}, u32[]{:S(2)}, u32[]{:S(2)}) %collective-permute-start) | collective-permute-done | bytes 557088 | tf_op jit(solution)/shard_map/ppermute | solution.py:323
  15.6 4.9 %collective-permute-start.1 = (s32[136,1024]{1,0:T(8,128)S(1)}, s32[136,1024]{1,0:T(8,128)S(1)}, u32[]{:S(2)}, u32[]{:S(2)}) collective-permute-start(s32[136,1024]{1,0:T(8,128)S(1)} %collective-permute-done.refs_1_), channel_id=1, source_target_pairs={{0,64},{64,128},{128,192},{192,256},{256,320},{320,384},{384,448},... | collective-permute-start | bytes 1671176 | tf_op jit(solution)/shard_map/ppermute | solution.py:323
  20.6 3.1 %collective-permute-start.2 = (bf16[96,16,128]{2,1,0:T(8,128)(2,1)}, bf16[96,16,128]{2,1,0:T(8,128)(2,1)S(1)}, u32[]{:S(2)}, u32[]{:S(2)}) collective-permute-start(bf16[96,16,128]{2,1,0:T(8,128)(2,1)} %get-tuple-element.35), channel_id=1, source_target_pairs={{0,2},{1,3},{2,0},{3,1},{4,6},{5,7},{6,4},{7,5},{8,10},{9,11},{10,... | collective-permute-start | bytes 1179656 | tf_op jit(solution)/shard_map/ppermute | solution.py:336
  23.7 6.2 %collective-permute-done.2.refs_5_ = bf16[96,16,128]{2,1,0:T(8,128)(2,1)S(1)} collective-permute-done((bf16[96,16,128]{2,1,0:T(8,128)(2,1)}, bf16[96,16,128]{2,1,0:T(8,128)(2,1)S(1)}, u32[]{:S(2)}, u32[]{:S(2)}) %collective-permute-start.2) | collective-permute-done | bytes 393248 | tf_op jit(solution)/shard_map/ppermute | solution.py:336
  29.8 0.0 collective-permute-done.1.refs_1_
  29.8 2.2 %collective-permute-start.3 = (s32[136,1024]{1,0:T(8,128)S(1)}, s32[136,1024]{1,0:T(8,128)S(1)}, u32[]{:S(2)}, u32[]{:S(2)}) collective-permute-start(s32[136,1024]{1,0:T(8,128)S(1)} %collective-permute-done.1.refs_1_), channel_id=1, source_target_pairs={{0,64},{64,128},{128,192},{192,256},{256,320},{320,384},{384,448},... | collective-permute-start | bytes 1671176 | tf_op jit(solution)/shard_map/ppermute | solution.py:323
  32.0 7.1 %collective-permute-start.4 = (bf16[96,16,128]{2,1,0:T(8,128)(2,1)}, bf16[96,16,128]{2,1,0:T(8,128)(2,1)S(1)}, u32[]{:S(2)}, u32[]{:S(2)}) collective-permute-start(bf16[96,16,128]{2,1,0:T(8,128)(2,1)} %get-tuple-element.37), channel_id=1, source_target_pairs={{0,1},{1,0},{2,3},{3,2},{4,5},{5,4},{6,7},{7,6},{8,9},{9,8},{10,11... | collective-permute-start | bytes 1179656 | tf_op jit(solution)/shard_map/ppermute | solution.py:336
  39.1 1.9 %collective-permute-start.5 = (bf16[96,16,128]{2,1,0:T(8,128)(2,1)}, bf16[96,16,128]{2,1,0:T(8,128)(2,1)S(1)}, u32[]{:S(2)}, u32[]{:S(2)}) collective-permute-start(bf16[96,16,128]{2,1,0:T(8,128)(2,1)} %get-tuple-element.38), channel_id=1, source_target_pairs={{0,3},{1,2},{2,1},{3,0},{4,7},{5,6},{6,5},{7,4},{8,11},{9,10},{10,... | collective-permute-start | bytes 1179656 | tf_op jit(solution)/shard_map/ppermute | solution.py:336
  41.1 0.0 collective-permute-done.4.refs_4_
  41.1 10.9 %collective-permute-done.5.refs_6_ = bf16[96,16,128]{2,1,0:T(8,128)(2,1)S(1)} collective-permute-done((bf16[96,16,128]{2,1,0:T(8,128)(2,1)}, bf16[96,16,128]{2,1,0:T(8,128)(2,1)S(1)}, u32[]{:S(2)}, u32[]{:S(2)}) %collective-permute-start.5) | collective-permute-done | bytes 393248 | tf_op jit(solution)/shard_map/ppermute | solution.py:336
  52.0 0.0 collective-permute-done.3.refs_1_
  52.0 0.7 collective-permute-start.6
  52.7 0.0 copy-done.8
  52.7 0.0 copy-start.3
  52.7 1.0 copy-done.3
  53.7 0.6 copy-done.6
  54.3 2.2 %channel.4 = (f32[512,1024]{1,0:T(8,128)S(1)}, f32[8,8,128]{2,1,0:T(8,128)S(1)}, bf16[512,1024]{1,0:T(8,128)(2,1)S(1)}, bf16[4,4,64,256]{3,2,1,0:T(8,128)(2,1)S(1)}) custom-call(s32[2]{0:T(128)S(1)} %copy-done.6, s32[136,1024]{1,0:T(8,128)S(1)} %collective-permute-done.refs_1_, f32[1,1024]{1,0:T(1,128)S(1)} %bitcast.25, bf16[96,16,128]{2,1,0:T(8,128)(2,1)S(1)} %copy-done.3, ...), custom_call_target="tpu_custom_call" | custom-call | flops 536870912 | bytes 6848512 | tf_op jit(solution)/shard_map/channel/pallas_call | solution.py:235
  56.5 1.9 %channel.5 = (f32[512,1024]{1,0:T(8,128)S(1)}, f32[8,8,128]{2,1,0:T(8,128)S(1)}) custom-call(s32[2]{0:T(128)S(1)} %copy-done.6, s32[136,1024]{1,0:T(8,128)S(1)} %collective-permute-done.1.refs_1_, bf16[512,1024]{1,0:T(8,128)(2,1)S(1)} %get-tuple-element.44.refs_2_.refs_3_, ...), custom_call_target="tpu_custom_call", output_to_operand_aliasing={{0}: (4, {}), {1}: (5, {})} | custom-call | flops 536870912 | bytes 6848512 | tf_op jit(solution)/shard_map/channel/pallas_call | solution.py:235
  58.4 0.0 copy-start
  58.5 1.9 %channel.6 = (f32[512,1024]{1,0:T(8,128)S(1)}, f32[8,8,128]{2,1,0:T(8,128)S(1)}) custom-call(s32[2]{0:T(128)S(1)} %copy-done.6, s32[136,1024]{1,0:T(8,128)S(1)} %collective-permute-done.3.refs_1_, bf16[512,1024]{1,0:T(8,128)(2,1)S(1)} %get-tuple-element.44.refs_2_.refs_3_, ...), custom_call_target="tpu_custom_call", output_to_operand_aliasing={{0}: (4, {}), {1}: (5, {})} | custom-call | flops 536870912 | bytes 6848512 | tf_op jit(solution)/shard_map/channel/pallas_call | solution.py:235
  60.4 0.0 collective-permute-done.6.refs_1_
  60.4 1.9 %channel.7 = (f32[32,16,512]{2,1,0:T(8,128)S(1)}, bf16[32,16,512]{2,1,0:T(8,128)(2,1)S(1)}, f32[8,8,128]{2,1,0:T(8,128)S(1)}) custom-call(s32[2]{0:T(128)S(1)} %copy-done.7, s32[136,1024]{1,0:T(8,128)S(1)} %collective-permute-done.6.refs_1_, s32[136,1024]{1,0:T(8,128)S(1)} %copy-done, bf16[512,1024]{1,0:T(8,128)(2,1)S(1)} %get-tuple-element.44.refs_2_.refs_3_, ...), custom_call_target="tpu_custom_call" | custom-call | flops 536870912 | bytes 6848512 | tf_op jit(solution)/shard_map/channel/pallas_call | solution.py:235
  62.3 0.0 copy-start.1
  62.3 0.0 copy-start.9
  62.4 6.3 %collective-permute-start.7 = (bf16[32,16,512]{2,1,0:T(8,128)(2,1)S(1)}, bf16[32,16,512]{2,1,0:T(8,128)(2,1)S(1)}, u32[]{:S(2)}, u32[]{:S(2)}) collective-permute-start(bf16[32,16,512]{2,1,0:T(8,128)(2,1)S(1)} %get-tuple-element.53), channel_id=1, source_target_pairs={{0,1},{1,0},{2,3},{3,2},{4,5},{5,4},{6,7},{7,6},{8,9},{9,8},{10,11... | collective-permute-start | bytes 1572872 | tf_op jit(solution)/shard_map/ppermute | solution.py:351
  68.6 1.5 %collective-permute-done.7 = bf16[32,16,512]{2,1,0:T(8,128)(2,1)S(1)} collective-permute-done((bf16[32,16,512]{2,1,0:T(8,128)(2,1)S(1)}, bf16[32,16,512]{2,1,0:T(8,128)(2,1)S(1)}, u32[]{:S(2)}, u32[]{:S(2)}) %collective-permute-start.7) | collective-permute-done | bytes 524320 | tf_op jit(solution)/shard_map/ppermute | solution.py:351
  70.2 1.0 add_convert_fusion
  71.2 11.4 %all-to-all-start = ((bf16[32,16,512]{2,1,0:T(8,128)(2,1)}), bf16[32,16,512]{2,1,0:T(8,128)(2,1)S(1)}, u32[]{:S(2)}, u32[]{:S(2)}) async-start(bf16[32,16,512]{2,1,0:T(8,128)(2,1)} %add_convert_fusion), calls=%async_computation | async-start | bytes 1048576 | tf_op jit(solution)/shard_map/all_to_all | solution.py:352
  82.6 0.0 copy-start.2
  82.6 1.0 copy-done.2
  83.6 0.9 dense.1
  84.5 14.6 %all-to-all-done.got_ref = bf16[32,16,512]{2,1,0:T(8,128)(2,1)S(1)} async-done(((bf16[32,16,512]{2,1,0:T(8,128)(2,1)}), bf16[32,16,512]{2,1,0:T(8,128)(2,1)S(1)}, u32[]{:S(2)}, u32[]{:S(2)}) %all-to-all-start) | async-done | bytes 524320 | tf_op jit(solution)/shard_map/all_to_all | solution.py:352
  99.1 0.0 copy-done.4
  99.1 0.4 token_.1
  99.6 0.1 add_reduce_fusion
  99.7 0.6 broadcast_in_dim.2
  100.4 6.9 %all-to-all-start.1 = ((f32[64,1,8]{2,1,0:T(1,128)}), f32[64,1,8]{2,1,0:T(1,128)S(1)}, u32[]{:S(2)}, u32[]{:S(2)}) async-start(f32[64,1,8]{2,1,0:T(1,128)} %broadcast_in_dim.2), calls=%async_computation.1 | async-start | bytes 65536 | tf_op jit(solution)/shard_map/all_to_all | solution.py:355
  107.3 1.0 back.1
  108.3 8.4 %all-to-all-done.1 = f32[64,1,8]{2,1,0:T(1,128)S(1)} async-done(((f32[64,1,8]{2,1,0:T(1,128)}), f32[64,1,8]{2,1,0:T(1,128)S(1)}, u32[]{:S(2)}, u32[]{:S(2)}) %all-to-all-start.1) | async-done | bytes 2080 | tf_op jit(solution)/shard_map/all_to_all | solution.py:355
  116.7 0.6 reduce_sum.19
  (9 shorter events, 0.0 us)
Async XLA Ops:
  0.6 8.2 %copy-start.10 = (bf16[16,8,1024]{2,1,0:T(8,128)(2,1)S(1)}, bf16[16,8,1024]{2,1,0:T(8,128)(2,1)}, u32[]{:S(2)}) copy-start(bf16[16,8,1024]{2,1,0:T(8,128)(2,1)} %param.12) | copy-start | bytes 786436
  0.6 52.0 %copy-start.8 = (f32[1024]{0:T(1024)S(1)}, f32[1024]{0:T(1024)}, u32[]{:S(2)}) copy-start(f32[1024]{0:T(1024)} %param.14) | copy-start | bytes 12292
  2.9 12.7 %collective-permute-start = (s32[136,1024]{1,0:T(8,128)}, s32[136,1024]{1,0:T(8,128)S(1)}, u32[]{:S(2)}, u32[]{:S(2)}) collective-permute-start(s32[136,1024]{1,0:T(8,128)} %pack.1.refs_2_), channel_id=1, source_target_pairs={{0,64},{64,128},{128,192},{192,256},{256,320},{320,384},{384,448},... | collective-permute-start | bytes 1671176 | tf_op jit(solution)/shard_map/ppermute | solution.py:323
  15.6 14.2 %collective-permute-start.1 = (s32[136,1024]{1,0:T(8,128)S(1)}, s32[136,1024]{1,0:T(8,128)S(1)}, u32[]{:S(2)}, u32[]{:S(2)}) collective-permute-start(s32[136,1024]{1,0:T(8,128)S(1)} %collective-permute-done.refs_1_), channel_id=1, source_target_pairs={{0,64},{64,128},{128,192},{192,256},{256,320},{320,384},{384,448},... | collective-permute-start | bytes 1671176 | tf_op jit(solution)/shard_map/ppermute | solution.py:323
  20.6 9.3 %collective-permute-start.2 = (bf16[96,16,128]{2,1,0:T(8,128)(2,1)}, bf16[96,16,128]{2,1,0:T(8,128)(2,1)S(1)}, u32[]{:S(2)}, u32[]{:S(2)}) collective-permute-start(bf16[96,16,128]{2,1,0:T(8,128)(2,1)} %get-tuple-element.35), channel_id=1, source_target_pairs={{0,2},{1,3},{2,0},{3,1},{4,6},{5,7},{6,4},{7,5},{8,10},{9,11},{10,... | collective-permute-start | bytes 1179656 | tf_op jit(solution)/shard_map/ppermute | solution.py:336
  29.8 22.1 %collective-permute-start.3 = (s32[136,1024]{1,0:T(8,128)S(1)}, s32[136,1024]{1,0:T(8,128)S(1)}, u32[]{:S(2)}, u32[]{:S(2)}) collective-permute-start(s32[136,1024]{1,0:T(8,128)S(1)} %collective-permute-done.1.refs_1_), channel_id=1, source_target_pairs={{0,64},{64,128},{128,192},{192,256},{256,320},{320,384},{384,448},... | collective-permute-start | bytes 1671176 | tf_op jit(solution)/shard_map/ppermute | solution.py:323
  32.0 9.0 %collective-permute-start.4 = (bf16[96,16,128]{2,1,0:T(8,128)(2,1)}, bf16[96,16,128]{2,1,0:T(8,128)(2,1)S(1)}, u32[]{:S(2)}, u32[]{:S(2)}) collective-permute-start(bf16[96,16,128]{2,1,0:T(8,128)(2,1)} %get-tuple-element.37), channel_id=1, source_target_pairs={{0,1},{1,0},{2,3},{3,2},{4,5},{5,4},{6,7},{7,6},{8,9},{9,8},{10,11... | collective-permute-start | bytes 1179656 | tf_op jit(solution)/shard_map/ppermute | solution.py:336
  39.1 12.8 %collective-permute-start.5 = (bf16[96,16,128]{2,1,0:T(8,128)(2,1)}, bf16[96,16,128]{2,1,0:T(8,128)(2,1)S(1)}, u32[]{:S(2)}, u32[]{:S(2)}) collective-permute-start(bf16[96,16,128]{2,1,0:T(8,128)(2,1)} %get-tuple-element.38), channel_id=1, source_target_pairs={{0,3},{1,2},{2,1},{3,0},{4,7},{5,6},{6,5},{7,4},{8,11},{9,10},{10,... | collective-permute-start | bytes 1179656 | tf_op jit(solution)/shard_map/ppermute | solution.py:336
  52.0 8.4 %collective-permute-start.6 = (s32[136,1024]{1,0:T(8,128)S(1)}, s32[136,1024]{1,0:T(8,128)S(1)}, u32[]{:S(2)}, u32[]{:S(2)}) collective-permute-start(s32[136,1024]{1,0:T(8,128)S(1)} %collective-permute-done.3.refs_1_), channel_id=1, source_target_pairs={{0,64},{64,128},{128,192},{192,256},{256,320},{320,384},{384,448},... | collective-permute-start | bytes 1671176 | tf_op jit(solution)/shard_map/ppermute | solution.py:323
  52.7 1.0 copy-start.3
  53.7 0.6 copy-start.6
  58.4 1.9 %copy-start = (s32[136,1024]{1,0:T(8,128)S(1)}, s32[136,1024]{1,0:T(8,128)}, u32[]{:S(2)}) copy-start(s32[136,1024]{1,0:T(8,128)} %pack.1.refs_2_) | copy-start | bytes 1671172
  58.4 1.9 %copy-start.7 = (s32[2]{0:T(128)S(1)}, s32[2]{0:T(128)}, u32[]{:S(2)}) copy-start(s32[2]{0:T(128)} %pad_add_fusion.place_ref.refs_0_) | copy-start | bytes 28
  62.3 20.2 %copy-start.1 = (bf16[16,128,128]{2,1,0:T(8,128)(2,1)S(1)}, bf16[16,128,128]{2,1,0:T(8,128)(2,1)}, u32[]{:S(2)}) copy-start(bf16[16,128,128]{2,1,0:T(8,128)(2,1)} %in_ref.1) | copy-start | bytes 1572868
  62.3 20.2 %copy-start.9 = (s32[16]{0:T(128)S(1)}, s32[16]{0:T(128)}, u32[]{:S(2)}) copy-start(s32[16]{0:T(128)} %cells_ref.1) | copy-start | bytes 196
  62.4 7.8 %collective-permute-start.7 = (bf16[32,16,512]{2,1,0:T(8,128)(2,1)S(1)}, bf16[32,16,512]{2,1,0:T(8,128)(2,1)S(1)}, u32[]{:S(2)}, u32[]{:S(2)}) collective-permute-start(bf16[32,16,512]{2,1,0:T(8,128)(2,1)S(1)} %get-tuple-element.53), channel_id=1, source_target_pairs={{0,1},{1,0},{2,3},{3,2},{4,5},{5,4},{6,7},{7,6},{8,9},{9,8},{10,11... | collective-permute-start | bytes 1572872 | tf_op jit(solution)/shard_map/ppermute | solution.py:351
  70.2 29.0 %copy-start.4 = (bf16[2,512,1,16]{1,3,2,0:T(8,128)(2,1)S(1)}, bf16[2,512,1,16]{1,3,2,0:T(8,128)(2,1)}, u32[]{:S(2)}) copy-start(bf16[2,512,1,16]{1,3,2,0:T(8,128)(2,1)} %param.22) | copy-start | bytes 98308
  70.2 29.0 %copy-start.5 = (bf16[2,512,1,16]{1,3,2,0:T(8,128)(2,1)S(1)}, bf16[2,512,1,16]{1,3,2,0:T(8,128)(2,1)}, u32[]{:S(2)}) copy-start(bf16[2,512,1,16]{1,3,2,0:T(8,128)(2,1)} %param.23) | copy-start | bytes 98308
  71.2 28.0 %all-to-all-start = ((bf16[32,16,512]{2,1,0:T(8,128)(2,1)}), bf16[32,16,512]{2,1,0:T(8,128)(2,1)S(1)}, u32[]{:S(2)}, u32[]{:S(2)}) async-start(bf16[32,16,512]{2,1,0:T(8,128)(2,1)} %add_convert_fusion), calls=%async_computation | async-start | bytes 1048576 | tf_op jit(solution)/shard_map/all_to_all | solution.py:352
  82.6 1.0 copy-start.2
  100.4 16.3 %all-to-all-start.1 = ((f32[64,1,8]{2,1,0:T(1,128)}), f32[64,1,8]{2,1,0:T(1,128)S(1)}, u32[]{:S(2)}, u32[]{:S(2)}) async-start(f32[64,1,8]{2,1,0:T(1,128)} %broadcast_in_dim.2), calls=%async_computation.1 | async-start | bytes 65536 | tf_op jit(solution)/shard_map/all_to_all | solution.py:355

commit v5 on v4

--- a/solution.py
+++ b/solution.py
@@ -121,60 +121,55 @@
     return mid, pos * icpt_low.astype(F32) + neg * icpt_high.astype(F32)
 
 
-def share_kernel(place_ref, lam_ref, slopes_ref, icpt_ref, *out_refs):
+def share_kernel(row_ref, lam_ref, slopes_ref, icpt_ref, out_ref):
     for r in range(SPEC):
         for k in range(D // 128):
             tile = lam_ref[r, :, k * 128 : (k + 1) * 128]
-            for out_ref in out_refs:
-                out_ref[r * (D // 128) + k] = tile
-    row = place_ref[1]
-    for k, out_ref in enumerate(out_refs):
-        to = place_ref[0] ^ k
-        sign = 2 * (to & 1) - 1
+            for to in range(4):
+                out_ref[to, r * (D // 128) + k] = tile
+    row = row_ref[0]
+    for to in range(4):
+        half, core = to // 2, to % 2
         for j in range(STEPS):
-            if j < STEPS - 1:
-                owner = row + sign * (j + 1)
-            else:
-                owner = row - STEPS * (1 - (to & 1))
-            start = pl.multiple_of((owner & 7) * TH + (to >> 1) * PART, PART)
+            owner = row + (j + 1) % STEPS if core else row - (j + 1)
+            start = pl.multiple_of((owner & 7) * TH + half * PART, PART)
             for kind in range(4):
                 ref = slopes_ref if kind < 2 else icpt_ref
                 values = ref[kind % 2, :, pl.ds(start, PART)]
                 for h in range(2):
-                    out_ref[LAM_TILES + (j * 4 + kind) * 2 + h] = values[:, h * 128 : (h + 1) * 128]
-
-
-def share(place, by_row, slopes, icpt):
+                    tile = LAM_TILES + (j * 4 + kind) * 2 + h
+                    out_ref[to, tile] = values[:, h * 128 : (h + 1) * 128]
+
+
+def share(row, by_row, slopes, icpt):
     tiles = LAM_TILES + 4 * STEPS * 2
     return pl.pallas_call(
         share_kernel,
-        out_shape=(jax.ShapeDtypeStruct((tiles, 16, 128), BF16),) * 4,
+        out_shape=jax.ShapeDtypeStruct((4, tiles, 16, 128), BF16),
         in_specs=[pl.BlockSpec(memory_space=pltpu.SMEM)]
         + [pl.BlockSpec(memory_space=pltpu.VMEM)] * 3,
         compiler_params=pltpu.CompilerParams(vmem_limit_bytes=60 * 1024 * 1024),
         name="share",
-    )(place, by_row, slopes, icpt)
+    )(row, by_row, slopes, icpt)
 
 
 def channel_kernel(step, *refs):
     first, last = step == 0, step == STEPS - 1
-    place_ref, words_ref, *refs = refs
+    core_ref, words_ref, *refs = refs
     if first:
-        down_scale_ref, *team, acc_ref, bias_ref, scaled_ref, bounds_ref, down, up = refs
-        for k, got_ref in enumerate(team):
-            start = (place_ref[0] ^ k) * 16
+        down_scale_ref, got_ref, acc_ref, bias_ref, scaled_ref, bounds_ref, down, up = refs
+        for q in range(4):
             for r in range(SPEC):
-                rows = pl.ds(pl.multiple_of(r * SHARED + start, 16), 16)
+                rows = slice(r * SHARED + q * 16, r * SHARED + (q + 1) * 16)
                 for c in range(D // 128):
                     cut = slice(c * 128, (c + 1) * 128)
-                    lam = got_ref[r * (D // 128) + c].astype(F32)
+                    lam = got_ref[q, r * (D // 128) + c].astype(F32)
                     scaled_ref[rows, cut] = (lam * down_scale_ref[:, cut]).astype(BF16)
                     acc_ref[rows, cut] = 0.25 * lam
-            rows = pl.ds(pl.multiple_of(start, 16), 16)
             for i in range(STEPS * 4):
                 for h in range(2):
-                    tile = got_ref[LAM_TILES + i * 2 + h]
-                    bounds_ref[i // 4, i % 4, rows, h * 128 : (h + 1) * 128] = tile
+                    tile = got_ref[q, LAM_TILES + i * 2 + h]
+                    bounds_ref[i // 4, i % 4, q * 16 : (q + 1) * 16, h * 128 : (h + 1) * 128] = tile
         acc_in, bias_in = acc_ref, None
     else:
         if last:
@@ -182,7 +177,7 @@
         scaled_ref, bounds_ref, acc_in, bias_in, *outs, down, up = refs
     words = words_ref[...]
     if last:
-        words = jnp.where(place_ref[0] % 2 == 0, words, own_ref[...])
+        words = jnp.where(core_ref[0] == 0, words, own_ref[...])
     for m in range(4):
         codes = unpack_codes(words[0:64], m)
         for q in range(4):
@@ -202,7 +197,7 @@
         bias = bias + bias_in[...]
     if last:
         keep_ref, send_ref, bias_ref = outs
-        own = place_ref[0] % 2 == 0
+        own = core_ref[0] == 0
         turned = total.T.reshape(32, 2, 16, ROWS_DEV)
         keep_ref[...] = jnp.where(own, turned[:, 0], turned[:, 1])
         send_ref[...] = jnp.where(own, turned[:, 1], turned[:, 0]).astype(BF16)
@@ -213,10 +208,10 @@
     bias_ref[...] = bias
 
 
-def channel_part(step, place, *rest):
+def channel_part(step, core, *rest):
     acc_shape = jax.ShapeDtypeStruct((ROWS_DEV, D), F32)
     bias_shape = jax.ShapeDtypeStruct((SPEC, 8, 128), F32)
-    operands = [place, *rest]
+    operands = [core, *rest]
     aliases = {}
     if step == 0:
         scaled_shape = jax.ShapeDtypeStruct((ROWS_DEV, D), BF16)
@@ -311,9 +306,9 @@
     tok_slopes,
     tok_icpt,
 ):
-    quarter, row = lax.axis_index(TEAM).astype(I32), lax.axis_index("rows").astype(I32)
-    place = jnp.stack([quarter, row])
-    half = (quarter >> 1).reshape(1)
+    row = lax.axis_index("rows").astype(I32).reshape(1)
+    core = lax.axis_index("core").astype(I32).reshape(1)
+    half = lax.axis_index("xl").astype(I32).reshape(1)
     tok_dev = lam_out.shape[0]
     slices = lax.axis_size("rows")
     ahead = [(i * 2, (i + 1) % slices * 2) for i in range(slices)]
@@ -324,30 +319,26 @@
 
     own = pack(half, q_down, q_up, up_scale)
     first = forward(own, ahead + behind)
-    own_part, *parts = share(
-        place,
+    blocks = share(
+        row,
         jnp.swapaxes(lam_out, 0, 1),
         chan_slopes.reshape(2, tok_dev, CH),
         chan_icpt.reshape(2, tok_dev, CH),
     )
-    words, parts = lax.optimization_barrier((first, parts))
-    second = forward(words, ahead + behind)
-    team = [own_part] + [
-        lax.ppermute(part, TEAM, [(i, i ^ k) for i in range(4)]) for k, part in enumerate(parts, 1)
-    ]
-    words, team[2] = lax.optimization_barrier((second, team[2]))
-    third = forward(words, ahead + behind)
-    words, team[1], team[3] = lax.optimization_barrier((third, team[1], team[3]))
-    far = forward(words, ahead)
+    _, blocks = lax.optimization_barrier((first, blocks))
+    team = lax.all_to_all(blocks, TEAM, 0, 0, tiled=True)
+    second = forward(first, ahead + behind)
+    third = forward(second, ahead + behind)
+    far = forward(third, ahead)
 
     dense_in, dense_out = dense_blocks(block_cells, tok_in_blocks, tok_out_blocks)
     slopes = jnp.transpose(tok_slopes, (0, 2, 3, 1)).reshape(2, 16, TH)
     icpt = jnp.transpose(tok_icpt, (0, 2, 3, 1)).reshape(2, 16, TH)
 
-    acc, chan_bias, *given = channel_part(0, place, first, down_scale.reshape(1, D), *team)
-    acc, chan_bias = channel_part(1, place, second, *given, acc, chan_bias)
-    acc, chan_bias = channel_part(2, place, third, *given, acc, chan_bias)
-    keep, send, chan_bias = channel_part(3, place, far, own, *given, acc, chan_bias)
+    acc, chan_bias, *given = channel_part(0, core, first, down_scale.reshape(1, D), team)
+    acc, chan_bias = channel_part(1, core, second, *given, acc, chan_bias)
+    acc, chan_bias = channel_part(2, core, third, *given, acc, chan_bias)
+    keep, send, chan_bias = channel_part(3, core, far, own, *given, acc, chan_bias)
     summed = (keep + lax.ppermute(send, "core", SWAP).astype(F32)).astype(BF16)
     got = lax.all_to_all(summed, ("z", "xh", "xl"), 0, 0, tiled=True)
     columns, mid, tok_bias = token_mlp(got, dense_out, slopes, icpt)

time: 118 us -> 110 us (0.932)
  starting transfers between devices: 50.4 us -> 45.3 us
  Pallas kernels: 15 us -> 12.5 us
    ppermute x3 -> x0, waiting for transfers between devices: 17.1 us -> none  [on_device(): lax.ppermute(part, TEAM, [(i, i ^ k) for i in range(4)])]
    ppermute x3 -> x0, starting transfers between devices: 12.1 us -> none  [on_device(): lax.ppermute(part, TEAM, [(i, i ^ k) for i in range(4)])]
    ppermute x4, waiting for transfers between devices: 2.84 us -> 13.2 us  [forward(): return lax.ppermute(words, ('rows', 'core'), pairs)]
    all_to_all x0 -> x1, starting transfers between devices: none -> 7.68 us  [on_device(): team = lax.all_to_all(blocks, TEAM, 0, 0, tiled=True)]
    all_to_all x0 -> x1, waiting for transfers between devices: none -> 7.21 us  [on_device(): team = lax.all_to_all(blocks, TEAM, 0, 0, tiled=True)]
    all_to_all x1, starting transfers between devices: 11.4 us -> 7.76 us  [on_device(): got = lax.all_to_all(summed, ('z', 'xh', 'xl'), 0, 0, tiled=True)]
    ppermute x4, starting transfers between devices: 13.7 us -> 16.4 us  [forward(): return lax.ppermute(words, ('rows', 'core'), pairs)]
    pallas_call x4, Pallas kernels: 7.97 us -> 5.44 us  [channel_part(): pl.pallas_call(functools.partial(channel_kernel, step), out_shape=out_sha...]
  transfers between devices with their start and end apart: 10 -> 8, of which waited for: 6 -> 6; matrix products, arithmetic and copies ran while one was open for 1% -> 1% of each run, Pallas kernels for 9% -> 8%
where the time goes in v5:
time: 110 us; the launch traced here: 109 us
  starting transfers between devices  45.3 us (41%)
  waiting for transfers between devices  44.9 us (41%)
  Pallas kernels  12.5 us (11%)
  local copies, waits for them, and re-layouts  3.61 us (3%)
  other arithmetic  1.72 us (2%)
    ppermute x4, starting transfers between devices, forward(): return lax.ppermute(words, ('rows', 'core'), pairs)  16.4 us
    all_to_all x1, waiting for transfers between devices, on_device(): got = lax.all_to_all(summed, ('z', 'xh', 'xl'), 0, 0, tiled=True)  14.6 us
    ppermute x4, waiting for transfers between devices, forward(): return lax.ppermute(words, ('rows', 'core'), pairs)  13.2 us
    all_to_all x1, waiting for transfers between devices, on_device(): lax.all_to_all(jnp.broadcast_to(own_bias[None, :], (64, SPEC)), MP, 0, 0,...  8.36 us
    all_to_all x1, starting transfers between devices, on_device(): got = lax.all_to_all(summed, ('z', 'xh', 'xl'), 0, 0, tiled=True)  7.76 us
    all_to_all x1, starting transfers between devices, on_device(): team = lax.all_to_all(blocks, TEAM, 0, 0, tiled=True)  7.68 us
    all_to_all x1, waiting for transfers between devices, on_device(): team = lax.all_to_all(blocks, TEAM, 0, 0, tiled=True)  7.21 us
    all_to_all x1, starting transfers between devices, on_device(): lax.all_to_all(jnp.broadcast_to(own_bias[None, :], (64, SPEC)), MP, 0, 0,...  6.94 us
  transfers between devices with their start and end apart: 8, of which 6 were waited for; matrix products, arithmetic and copies ran while one was open for 1% of the time, Pallas kernels for 8%

profile of v5, /device:TPU:1, one launch (start us, length us, event | category | flops | bytes accessed | tf_op | source)
XLA Modules:
  0.0 109.0 jit_solution(7553931299577730136)
XLA Ops:
  0.6 0.0 copy-start.9
  0.6 2.3 %pack.1.refs_2_ = s32[136,1024]{1,0:T(8,128)} custom-call(s32[1]{0:T(128)} %bitcast.1.half_ref, bf16[1024,512]{1,0:T(8,128)(2,1)} %down_hbm.1, bf16[512,1024]{1,0:T(8,128)(2,1)} %up_hbm.1, f32[1,512]{1,0:T(1,128)} %bitcast.30), custom_call_target="tpu_custom_call" | custom-call | tf_op jit(solution)/shard_map/pack/pallas_call | solution.py:69
  2.9 5.9 %collective-permute-start = (s32[136,1024]{1,0:T(8,128)}, s32[136,1024]{1,0:T(8,128)S(1)}, u32[]{:S(2)}, u32[]{:S(2)}) collective-permute-start(s32[136,1024]{1,0:T(8,128)} %pack.1.refs_2_), channel_id=1, source_target_pairs={{0,64},{64,128},{128,192},{192,256},{256,320},{320,384},{384,448},... | collective-permute-start | bytes 1671176 | tf_op jit(solution)/shard_map/ppermute | solution.py:318
  8.9 6.8 %collective-permute-done.refs_1_ = s32[136,1024]{1,0:T(8,128)S(1)} collective-permute-done((s32[136,1024]{1,0:T(8,128)}, s32[136,1024]{1,0:T(8,128)S(1)}, u32[]{:S(2)}, u32[]{:S(2)}) %collective-permute-start) | collective-permute-done | bytes 557088 | tf_op jit(solution)/shard_map/ppermute | solution.py:318
  15.6 0.0 copy-start.1
  15.6 4.9 %collective-permute-start.1 = (s32[136,1024]{1,0:T(8,128)S(1)}, s32[136,1024]{1,0:T(8,128)S(1)}, u32[]{:S(2)}, u32[]{:S(2)}) collective-permute-start(s32[136,1024]{1,0:T(8,128)S(1)} %collective-permute-done.refs_1_), channel_id=1, source_target_pairs={{0,64},{64,128},{128,192},{192,256},{256,320},{320,384},{384,448},... | collective-permute-start | bytes 1671176 | tf_op jit(solution)/shard_map/ppermute | solution.py:318
  20.6 0.0 copy-done.9
  20.6 0.9 copy.30
  21.4 2.5 %share.1 = bf16[4,96,16,128]{3,2,1,0:T(8,128)(2,1)} custom-call(s32[1]{0:T(128)} %bitcast.4.row_ref, bf16[8,16,1024]{2,1,0:T(8,128)(2,1)} %bitcast.26, bf16[2,16,4096]{2,1,0:T(8,128)(2,1)} %bitcast.27, bf16[2,16,4096]{2,1,0:T(8,128)(2,1)} %bitcast.28), custom_call_target="tpu_custom_call" | custom-call | tf_op jit(solution)/shard_map/share/pallas_call | solution.py:146
  23.9 0.0 copy-start.7
  23.9 0.0 copy-done.1
  23.9 7.7 %all-to-all-start = ((bf16[4,96,16,128]{3,2,1,0:T(8,128)(2,1)}), bf16[4,96,16,128]{3,2,1,0:T(8,128)(2,1)S(1)}, u32[]{:S(2)}, u32[]{:S(2)}) async-start(bf16[4,96,16,128]{3,2,1,0:T(8,128)(2,1)} %share.1), calls=%async_computation | async-start | bytes 3145728 | tf_op jit(solution)/shard_map/all_to_all | solution.py:329
  31.6 0.0 collective-permute-done.1.refs_1_
  31.6 4.8 %collective-permute-start.2 = (s32[136,1024]{1,0:T(8,128)S(1)}, s32[136,1024]{1,0:T(8,128)S(1)}, u32[]{:S(2)}, u32[]{:S(2)}) collective-permute-start(s32[136,1024]{1,0:T(8,128)S(1)} %collective-permute-done.1.refs_1_), channel_id=1, source_target_pairs={{0,64},{64,128},{128,192},{192,256},{256,320},{320,384},{384,448},... | collective-permute-start | bytes 1671176 | tf_op jit(solution)/shard_map/ppermute | solution.py:318
  36.4 6.5 %collective-permute-done.2.refs_1_ = s32[136,1024]{1,0:T(8,128)S(1)} collective-permute-done((s32[136,1024]{1,0:T(8,128)S(1)}, s32[136,1024]{1,0:T(8,128)S(1)}, u32[]{:S(2)}, u32[]{:S(2)}) %collective-permute-start.2) | collective-permute-done | bytes 557088 | tf_op jit(solution)/shard_map/ppermute | solution.py:318
  42.9 0.7 collective-permute-start.3
  43.6 7.2 %all-to-all-done.refs_3_ = bf16[4,96,16,128]{3,2,1,0:T(8,128)(2,1)S(1)} async-done(((bf16[4,96,16,128]{3,2,1,0:T(8,128)(2,1)}), bf16[4,96,16,128]{3,2,1,0:T(8,128)(2,1)S(1)}, u32[]{:S(2)}, u32[]{:S(2)}) %all-to-all-start) | async-done | bytes 1572896 | tf_op jit(solution)/shard_map/all_to_all | solution.py:329
  50.8 0.0 copy-done.7
  50.8 1.1 copy-done.2
  51.9 1.3 %channel.4 = (f32[512,1024]{1,0:T(8,128)S(1)}, f32[8,8,128]{2,1,0:T(8,128)S(1)}, bf16[512,1024]{1,0:T(8,128)(2,1)S(1)}, bf16[4,4,64,256]{3,2,1,0:T(8,128)(2,1)S(1)}) custom-call(s32[1]{0:T(128)} %bitcast.refs_0_, s32[136,1024]{1,0:T(8,128)S(1)} %copy-done.2, f32[1,1024]{1,0:T(1,128)S(1)} %bitcast.25, bf16[4,96,16,128]{3,2,1,0:T(8,128)(2,1)S(1)} %all-to-all-done.refs_3_), custom_call_target="tpu_custom_call" | custom-call | flops 536870912 | bytes 6848512 | tf_op jit(solution)/shard_map/channel/pallas_call | solution.py:230
  53.2 1.4 %channel.5 = (f32[512,1024]{1,0:T(8,128)S(1)}, f32[8,8,128]{2,1,0:T(8,128)S(1)}) custom-call(s32[1]{0:T(128)} %bitcast.refs_0_, s32[136,1024]{1,0:T(8,128)S(1)} %collective-permute-done.1.refs_1_, bf16[512,1024]{1,0:T(8,128)(2,1)S(1)} %get-tuple-element.20.refs_2_.refs_3_, ...), custom_call_target="tpu_custom_call", output_to_operand_aliasing={{0}: (4, {}), {1}: (5, {})} | custom-call | flops 536870912 | bytes 6848512 | tf_op jit(solution)/shard_map/channel/pallas_call | solution.py:230
  54.6 0.0 copy-start
  54.6 1.4 %channel.6 = (f32[512,1024]{1,0:T(8,128)S(1)}, f32[8,8,128]{2,1,0:T(8,128)S(1)}) custom-call(s32[1]{0:T(128)} %bitcast.refs_0_, s32[136,1024]{1,0:T(8,128)S(1)} %collective-permute-done.2.refs_1_, bf16[512,1024]{1,0:T(8,128)(2,1)S(1)} %get-tuple-element.20.refs_2_.refs_3_, ...), custom_call_target="tpu_custom_call", output_to_operand_aliasing={{0}: (4, {}), {1}: (5, {})} | custom-call | flops 536870912 | bytes 6848512 | tf_op jit(solution)/shard_map/channel/pallas_call | solution.py:230
  56.0 0.0 collective-permute-done.3.refs_1_
  56.0 0.0 copy-done
  56.0 1.4 %channel.7 = (f32[32,16,512]{2,1,0:T(8,128)S(1)}, bf16[32,16,512]{2,1,0:T(8,128)(2,1)S(1)}, f32[8,8,128]{2,1,0:T(8,128)S(1)}) custom-call(s32[1]{0:T(128)} %bitcast.refs_0_, s32[136,1024]{1,0:T(8,128)S(1)} %collective-permute-done.3.refs_1_, s32[136,1024]{1,0:T(8,128)S(1)} %copy-done, bf16[512,1024]{1,0:T(8,128)(2,1)S(1)} %get-tuple-element.20.refs_2_.refs_3_, ...), custom_call_target="tpu_custom_call" | custom-call | flops 536870912 | bytes 6848512 | tf_op jit(solution)/shard_map/channel/pallas_call | solution.py:230
  57.4 0.0 copy-start.3
  57.4 0.0 copy-start.8
  57.4 6.6 %collective-permute-start.4 = (bf16[32,16,512]{2,1,0:T(8,128)(2,1)S(1)}, bf16[32,16,512]{2,1,0:T(8,128)(2,1)S(1)}, u32[]{:S(2)}, u32[]{:S(2)}) collective-permute-start(bf16[32,16,512]{2,1,0:T(8,128)(2,1)S(1)} %get-tuple-element.29), channel_id=1, source_target_pairs={{0,1},{1,0},{2,3},{3,2},{4,5},{5,4},{6,7},{7,6},{8,9},{9,8},{10,11... | collective-permute-start | bytes 1572872 | tf_op jit(solution)/shard_map/ppermute | solution.py:342
  64.0 1.5 %collective-permute-done.4 = bf16[32,16,512]{2,1,0:T(8,128)(2,1)S(1)} collective-permute-done((bf16[32,16,512]{2,1,0:T(8,128)(2,1)S(1)}, bf16[32,16,512]{2,1,0:T(8,128)(2,1)S(1)}, u32[]{:S(2)}, u32[]{:S(2)}) %collective-permute-start.4) | collective-permute-done | bytes 524320 | tf_op jit(solution)/shard_map/ppermute | solution.py:342
  65.5 0.0 copy-start.5
  65.5 1.0 add_convert_fusion
  66.5 7.8 %all-to-all-start.1 = ((bf16[32,16,512]{2,1,0:T(8,128)(2,1)}), bf16[32,16,512]{2,1,0:T(8,128)(2,1)S(1)}, u32[]{:S(2)}, u32[]{:S(2)}) async-start(bf16[32,16,512]{2,1,0:T(8,128)(2,1)} %add_convert_fusion), calls=%async_computation.1 | async-start | bytes 1048576 | tf_op jit(solution)/shard_map/all_to_all | solution.py:343
  74.3 0.0 copy-done.3
  74.3 0.0 copy-done.8
  74.3 0.0 copy-start.4
  74.3 1.0 copy-done.4
  75.3 0.9 dense.1
  76.2 14.6 %all-to-all-done.1.got_ref = bf16[32,16,512]{2,1,0:T(8,128)(2,1)S(1)} async-done(((bf16[32,16,512]{2,1,0:T(8,128)(2,1)}), bf16[32,16,512]{2,1,0:T(8,128)(2,1)S(1)}, u32[]{:S(2)}, u32[]{:S(2)}) %all-to-all-start.1) | async-done | bytes 524320 | tf_op jit(solution)/shard_map/all_to_all | solution.py:343
  90.8 0.0 copy-done.5
  90.8 0.0 copy-done.6
  90.8 0.4 token_.1
  91.3 0.1 add_reduce_fusion
  91.4 0.6 broadcast_in_dim.2
  92.0 6.9 %all-to-all-start.2 = ((f32[64,1,8]{2,1,0:T(1,128)}), f32[64,1,8]{2,1,0:T(1,128)S(1)}, u32[]{:S(2)}, u32[]{:S(2)}) async-start(f32[64,1,8]{2,1,0:T(1,128)} %broadcast_in_dim.2), calls=%async_computation.2 | async-start | bytes 65536 | tf_op jit(solution)/shard_map/all_to_all | solution.py:346
  99.0 1.0 back.1
  100.0 8.4 %all-to-all-done.2 = f32[64,1,8]{2,1,0:T(1,128)S(1)} async-done(((f32[64,1,8]{2,1,0:T(1,128)}), f32[64,1,8]{2,1,0:T(1,128)S(1)}, u32[]{:S(2)}, u32[]{:S(2)}) %all-to-all-start.2) | async-done | bytes 2080 | tf_op jit(solution)/shard_map/all_to_all | solution.py:346
  108.4 0.6 reduce_sum.19
  (2 shorter events, 0.0 us)
Async XLA Ops:
  0.6 19.9 %copy-start.9 = (bf16[16,8,1024]{2,1,0:T(8,128)(2,1)S(1)}, bf16[16,8,1024]{2,1,0:T(8,128)(2,1)}, u32[]{:S(2)}) copy-start(bf16[16,8,1024]{2,1,0:T(8,128)(2,1)} %param.12) | copy-start | bytes 786436
  2.9 12.7 %collective-permute-start = (s32[136,1024]{1,0:T(8,128)}, s32[136,1024]{1,0:T(8,128)S(1)}, u32[]{:S(2)}, u32[]{:S(2)}) collective-permute-start(s32[136,1024]{1,0:T(8,128)} %pack.1.refs_2_), channel_id=1, source_target_pairs={{0,64},{64,128},{128,192},{192,256},{256,320},{320,384},{384,448},... | collective-permute-start | bytes 1671176 | tf_op jit(solution)/shard_map/ppermute | solution.py:318
  15.6 8.3 %copy-start.1 = (s32[136,1024]{1,0:T(8,128)}, s32[136,1024]{1,0:T(8,128)S(1)}, u32[]{:S(2)}) copy-start(s32[136,1024]{1,0:T(8,128)S(1)} %collective-permute-done.refs_1_) | copy-start | bytes 1671172
  15.6 16.0 %collective-permute-start.1 = (s32[136,1024]{1,0:T(8,128)S(1)}, s32[136,1024]{1,0:T(8,128)S(1)}, u32[]{:S(2)}, u32[]{:S(2)}) collective-permute-start(s32[136,1024]{1,0:T(8,128)S(1)} %collective-permute-done.refs_1_), channel_id=1, source_target_pairs={{0,64},{64,128},{128,192},{192,256},{256,320},{320,384},{384,448},... | collective-permute-start | bytes 1671176 | tf_op jit(solution)/shard_map/ppermute | solution.py:318
  23.9 26.9 %copy-start.7 = (f32[1024]{0:T(1024)S(1)}, f32[1024]{0:T(1024)}, u32[]{:S(2)}) copy-start(f32[1024]{0:T(1024)} %param.14) | copy-start | bytes 12292
  23.9 26.9 %all-to-all-start = ((bf16[4,96,16,128]{3,2,1,0:T(8,128)(2,1)}), bf16[4,96,16,128]{3,2,1,0:T(8,128)(2,1)S(1)}, u32[]{:S(2)}, u32[]{:S(2)}) async-start(bf16[4,96,16,128]{3,2,1,0:T(8,128)(2,1)} %share.1), calls=%async_computation | async-start | bytes 3145728 | tf_op jit(solution)/shard_map/all_to_all | solution.py:329
  31.6 11.3 %collective-permute-start.2 = (s32[136,1024]{1,0:T(8,128)S(1)}, s32[136,1024]{1,0:T(8,128)S(1)}, u32[]{:S(2)}, u32[]{:S(2)}) collective-permute-start(s32[136,1024]{1,0:T(8,128)S(1)} %collective-permute-done.1.refs_1_), channel_id=1, source_target_pairs={{0,64},{64,128},{128,192},{192,256},{256,320},{320,384},{384,448},... | collective-permute-start | bytes 1671176 | tf_op jit(solution)/shard_map/ppermute | solution.py:318
  42.9 13.1 %collective-permute-start.3 = (s32[136,1024]{1,0:T(8,128)S(1)}, s32[136,1024]{1,0:T(8,128)S(1)}, u32[]{:S(2)}, u32[]{:S(2)}) collective-permute-start(s32[136,1024]{1,0:T(8,128)S(1)} %collective-permute-done.2.refs_1_), channel_id=1, source_target_pairs={{0,64},{64,128},{128,192},{192,256},{256,320},{320,384},{384,448},... | collective-permute-start | bytes 1671176 | tf_op jit(solution)/shard_map/ppermute | solution.py:318
  50.8 1.1 copy-start.2
  54.6 1.4 %copy-start = (s32[136,1024]{1,0:T(8,128)S(1)}, s32[136,1024]{1,0:T(8,128)}, u32[]{:S(2)}) copy-start(s32[136,1024]{1,0:T(8,128)} %pack.1.refs_2_) | copy-start | bytes 1671172
  57.4 16.9 %copy-start.3 = (bf16[16,128,128]{2,1,0:T(8,128)(2,1)S(1)}, bf16[16,128,128]{2,1,0:T(8,128)(2,1)}, u32[]{:S(2)}) copy-start(bf16[16,128,128]{2,1,0:T(8,128)(2,1)} %in_ref.1) | copy-start | bytes 1572868
  57.4 16.9 %copy-start.8 = (s32[16]{0:T(128)S(1)}, s32[16]{0:T(128)}, u32[]{:S(2)}) copy-start(s32[16]{0:T(128)} %cells_ref.1) | copy-start | bytes 196
  57.4 8.1 %collective-permute-start.4 = (bf16[32,16,512]{2,1,0:T(8,128)(2,1)S(1)}, bf16[32,16,512]{2,1,0:T(8,128)(2,1)S(1)}, u32[]{:S(2)}, u32[]{:S(2)}) collective-permute-start(bf16[32,16,512]{2,1,0:T(8,128)(2,1)S(1)} %get-tuple-element.29), channel_id=1, source_target_pairs={{0,1},{1,0},{2,3},{3,2},{4,5},{5,4},{6,7},{7,6},{8,9},{9,8},{10,11... | collective-permute-start | bytes 1572872 | tf_op jit(solution)/shard_map/ppermute | solution.py:342
  65.5 25.3 %copy-start.5 = (bf16[2,512,1,16]{1,3,2,0:T(8,128)(2,1)S(1)}, bf16[2,512,1,16]{1,3,2,0:T(8,128)(2,1)}, u32[]{:S(2)}) copy-start(bf16[2,512,1,16]{1,3,2,0:T(8,128)(2,1)} %param.22) | copy-start | bytes 98308
  65.5 25.3 %copy-start.6 = (bf16[2,512,1,16]{1,3,2,0:T(8,128)(2,1)S(1)}, bf16[2,512,1,16]{1,3,2,0:T(8,128)(2,1)}, u32[]{:S(2)}) copy-start(bf16[2,512,1,16]{1,3,2,0:T(8,128)(2,1)} %param.23) | copy-start | bytes 98308
  66.5 24.3 %all-to-all-start.1 = ((bf16[32,16,512]{2,1,0:T(8,128)(2,1)}), bf16[32,16,512]{2,1,0:T(8,128)(2,1)S(1)}, u32[]{:S(2)}, u32[]{:S(2)}) async-start(bf16[32,16,512]{2,1,0:T(8,128)(2,1)} %add_convert_fusion), calls=%async_computation.1 | async-start | bytes 1048576 | tf_op jit(solution)/shard_map/all_to_all | solution.py:343
  74.3 1.0 copy-start.4
  92.0 16.3 %all-to-all-start.2 = ((f32[64,1,8]{2,1,0:T(1,128)}), f32[64,1,8]{2,1,0:T(1,128)S(1)}, u32[]{:S(2)}, u32[]{:S(2)}) async-start(f32[64,1,8]{2,1,0:T(1,128)} %broadcast_in_dim.2), calls=%async_computation.2 | async-start | bytes 65536 | tf_op jit(solution)/shard_map/all_to_all | solution.py:346

commit v6 on v5

--- a/solution.py
+++ b/solution.py
@@ -29,7 +29,6 @@
 STEPS = 4
 SHARED = 64
 ROWS_DEV = SPEC * SHARED
-PACKED = 136
 LAM_TILES = SPEC * (D // 128)
 SCALE_ONE = float(2**38)
 
@@ -44,43 +43,59 @@
     return (shifted >> 24).astype(F32).astype(BF16)
 
 
-def pack_kernel(half_ref, down_hbm, up_hbm, scale_hbm, out_ref, down_ref, up_ref, scale_ref, sems):
+def pack_down_kernel(half_ref, down_hbm, out_ref, down_ref, sem):
+    start = pl.multiple_of(half_ref[0] * PART, PART)
+    copy = pltpu.make_async_copy(down_hbm.at[:, pl.ds(start, PART)], down_ref, sem)
+    copy.start()
+    copy.wait()
+    down = pack_codes([down_ref[m * 256 : (m + 1) * 256, :] for m in range(4)])
+    for k in range(4):
+        out_ref[:, k * PART : (k + 1) * PART] = down[k * 64 : (k + 1) * 64, :]
+
+
+def pack_up_kernel(half_ref, up_hbm, scale_hbm, out_ref, up_ref, scale_ref, sems):
     start = pl.multiple_of(half_ref[0] * PART, PART)
     copies = [
-        pltpu.make_async_copy(down_hbm.at[:, pl.ds(start, PART)], down_ref, sems.at[0]),
-        pltpu.make_async_copy(up_hbm.at[pl.ds(start, PART), :], up_ref, sems.at[1]),
-        pltpu.make_async_copy(scale_hbm.at[:, pl.ds(start, PART)], scale_ref, sems.at[2]),
+        pltpu.make_async_copy(up_hbm.at[pl.ds(start, PART), :], up_ref, sems.at[0]),
+        pltpu.make_async_copy(scale_hbm.at[:, pl.ds(start, PART)], scale_ref, sems.at[1]),
     ]
     for copy in copies:
         copy.start()
-    out_ref[128:136, :] = jnp.zeros((8, D), I32)
+    out_ref[64:72, :] = jnp.zeros((8, D), I32)
+    copies[1].wait()
+    scale = (scale_ref[...] * SCALE_ONE).astype(I32)
+    out_ref[64:72, 0:PART] = jnp.broadcast_to(scale, (8, PART))
     copies[0].wait()
-    down = pack_codes([down_ref[m * 256 : (m + 1) * 256, :] for m in range(4)])
-    for k in range(4):
-        out_ref[0:64, k * PART : (k + 1) * PART] = down[k * 64 : (k + 1) * 64, :]
-    copies[1].wait()
-    out_ref[64:128, :] = pack_codes([up_ref[m * 64 : (m + 1) * 64, :] for m in range(4)])
-    copies[2].wait()
-    scale = (scale_ref[...] * SCALE_ONE).astype(I32)
-    out_ref[128:136, 0:PART] = jnp.broadcast_to(scale, (8, PART))
+    out_ref[0:64, :] = pack_codes([up_ref[m * 64 : (m + 1) * 64, :] for m in range(4)])
 
 
 def pack(half, q_down, q_up, up_scale):
-    return pl.pallas_call(
-        pack_kernel,
-        out_shape=jax.ShapeDtypeStruct((PACKED, D), I32),
-        in_specs=[pl.BlockSpec(memory_space=pltpu.SMEM)]
-        + [pl.BlockSpec(memory_space=pltpu.HBM)] * 3,
-        out_specs=pl.BlockSpec(memory_space=pltpu.VMEM),
+    smem, hbm = pl.BlockSpec(memory_space=pltpu.SMEM), pl.BlockSpec(memory_space=pltpu.HBM)
+    vmem = pl.BlockSpec(memory_space=pltpu.VMEM)
+    params = pltpu.CompilerParams(vmem_limit_bytes=60 * 1024 * 1024)
+    down = pl.pallas_call(
+        pack_down_kernel,
+        out_shape=jax.ShapeDtypeStruct((64, D), I32),
+        in_specs=[smem, hbm],
+        out_specs=vmem,
+        scratch_shapes=[pltpu.VMEM((D, PART), BF16), pltpu.SemaphoreType.DMA(())],
+        compiler_params=params,
+        name="pack_down",
+    )(half, q_down)
+    up = pl.pallas_call(
+        pack_up_kernel,
+        out_shape=jax.ShapeDtypeStruct((72, D), I32),
+        in_specs=[smem, hbm, hbm],
+        out_specs=vmem,
         scratch_shapes=[
-            pltpu.VMEM((D, PART), BF16),
             pltpu.VMEM((PART, D), BF16),
             pltpu.VMEM((1, PART), F32),
-            pltpu.SemaphoreType.DMA((3,)),
+            pltpu.SemaphoreType.DMA((2,)),
         ],
-        compiler_params=pltpu.CompilerParams(vmem_limit_bytes=60 * 1024 * 1024),
-        name="pack",
-    )(half, q_down, q_up, up_scale.reshape(1, -1))
+        compiler_params=params,
+        name="pack_up",
+    )(half, q_up, up_scale.reshape(1, -1))
+    return down, up
 
 
 def dense_kernel(cells_ref, in_ref, out_ref, dense_in_ref, dense_out_ref):
@@ -155,7 +170,7 @@
 
 def channel_kernel(step, *refs):
     first, last = step == 0, step == STEPS - 1
-    core_ref, words_ref, *refs = refs
+    core_ref, down_words_ref, up_words_ref, *refs = refs
     if first:
         down_scale_ref, got_ref, acc_ref, bias_ref, scaled_ref, bounds_ref, down, up = refs
         for q in range(4):
@@ -173,18 +188,19 @@
         acc_in, bias_in = acc_ref, None
     else:
         if last:
-            own_ref, *refs = refs
+            own_down_ref, own_up_ref, *refs = refs
         scaled_ref, bounds_ref, acc_in, bias_in, *outs, down, up = refs
-    words = words_ref[...]
+    down_words, up_words = down_words_ref[...], up_words_ref[...]
     if last:
-        words = jnp.where(core_ref[0] == 0, words, own_ref[...])
+        down_words = jnp.where(core_ref[0] == 0, down_words, own_down_ref[...])
+        up_words = jnp.where(core_ref[0] == 0, up_words, own_up_ref[...])
     for m in range(4):
-        codes = unpack_codes(words[0:64], m)
+        codes = unpack_codes(down_words, m)
         for q in range(4):
             rows = m * 256 + q * 64
             down[rows : rows + 64, :] = codes[:, q * PART : (q + 1) * PART]
-        up[m * 64 : (m + 1) * 64, :] = unpack_codes(words[64:128], m)
-    scale = words[128:129, 0:PART].astype(F32) * (1.0 / SCALE_ONE)
+        up[m * 64 : (m + 1) * 64, :] = unpack_codes(up_words[0:64], m)
+    scale = up_words[64:65, 0:PART].astype(F32) * (1.0 / SCALE_ONE)
     pre = jnp.dot(scaled_ref[...], down[...], preferred_element_type=F32)
     pre = pre.reshape(SPEC, SHARED, PART)
     mid, terms = relaxed(pre, *(bounds_ref[step, kind] for kind in range(4)))
@@ -237,7 +253,7 @@
         compiler_params=pltpu.CompilerParams(vmem_limit_bytes=VMEM),
         cost_estimate=pl.CostEstimate(
             flops=4 * ROWS_DEV * PART * D,
-            bytes_accessed=PACKED * D * 4 + 3 * ROWS_DEV * D * 4,
+            bytes_accessed=136 * D * 4 + 3 * ROWS_DEV * D * 4,
             transcendentals=0,
         ),
         name="channel",
@@ -315,16 +331,12 @@
     behind = [(i * 2 + 1, (i - 1) % slices * 2 + 1) for i in range(slices)]
 
     def forward(words, pairs):
-        return lax.ppermute(words, ("rows", "core"), pairs)
+        return tuple(lax.ppermute(w, ("rows", "core"), pairs) for w in words)
 
     own = pack(half, q_down, q_up, up_scale)
     first = forward(own, ahead + behind)
-    blocks = share(
-        row,
-        jnp.swapaxes(lam_out, 0, 1),
-        chan_slopes.reshape(2, tok_dev, CH),
-        chan_icpt.reshape(2, tok_dev, CH),
-    )
+    _, lam, *bounds = lax.optimization_barrier((own, lam_out, chan_slopes, chan_icpt))
+    blocks = share(row, jnp.swapaxes(lam, 0, 1), *(b.reshape(2, tok_dev, CH) for b in bounds))
     _, blocks = lax.optimization_barrier((first, blocks))
     team = lax.all_to_all(blocks, TEAM, 0, 0, tiled=True)
     second = forward(first, ahead + behind)
@@ -335,10 +347,10 @@
     slopes = jnp.transpose(tok_slopes, (0, 2, 3, 1)).reshape(2, 16, TH)
     icpt = jnp.transpose(tok_icpt, (0, 2, 3, 1)).reshape(2, 16, TH)
 
-    acc, chan_bias, *given = channel_part(0, core, first, down_scale.reshape(1, D), team)
-    acc, chan_bias = channel_part(1, core, second, *given, acc, chan_bias)
-    acc, chan_bias = channel_part(2, core, third, *given, acc, chan_bias)
-    keep, send, chan_bias = channel_part(3, core, far, own, *given, acc, chan_bias)
+    acc, chan_bias, *given = channel_part(0, core, *first, down_scale.reshape(1, D), team)
+    acc, chan_bias = channel_part(1, core, *second, *given, acc, chan_bias)
+    acc, chan_bias = channel_part(2, core, *third, *given, acc, chan_bias)
+    keep, send, chan_bias = channel_part(3, core, *far, *own, *given, acc, chan_bias)
     summed = (keep + lax.ppermute(send, "core", SWAP).astype(F32)).astype(BF16)
     got = lax.all_to_all(summed, ("z", "xh", "xl"), 0, 0, tiled=True)
     columns, mid, tok_bias = token_mlp(got, dense_out, slopes, icpt)

time: 110 us -> 110 us (level)
  waiting for transfers between devices: 44.9 us -> 32 us
  starting transfers between devices: 45.3 us -> 56.8 us
  Pallas kernels: 12.5 us -> 15.2 us
    all_to_all x1, waiting for transfers between devices: 7.21 us -> 0.01 us  [on_device(): team = lax.all_to_all(blocks, TEAM, 0, 0, tiled=True)]
    ppermute x4 -> x8, starting transfers between devices: 16.4 us -> 23.1 us  [forward(): return tuple((lax.ppermute(w, ('rows', 'core'), pairs) for w in words))]
    ppermute x4 -> x8, waiting for transfers between devices: 13.2 us -> 7.55 us  [forward(): return tuple((lax.ppermute(w, ('rows', 'core'), pairs) for w in words))]
    ppermute x1, starting transfers between devices: 6.59 us -> 8.65 us  [on_device(): summed = (keep + lax.ppermute(send, 'core', SWAP).astype(F32)).astype(BF16)]
    unnamed x21 -> x18, local copies, waits for them, and re-layouts: 2.98 us -> 1.08 us
    all_to_all x1, starting transfers between devices: 7.76 us -> 9.59 us  [on_device(): got = lax.all_to_all(summed, ('z', 'xh', 'xl'), 0, 0, tiled=True)]
    pallas_call x1 -> x2, Pallas kernels: 2.28 us -> 3.93 us  [the longest x1 2 us: pack(): pl.pallas_call(pack_up_kernel, out_shape=jax.ShapeDtypeStruct((72, D), I3...]
  transfers between devices with their start and end apart: 8 -> 12, of which waited for: 6 -> 7; matrix products, arithmetic and copies ran while one was open for 1% -> 1% of each run, Pallas kernels for 8% -> 10%
where the time goes in v6:
time: 110 us; the launch traced here: 109 us
  starting transfers between devices  56.8 us (52%)
  waiting for transfers between devices  32 us (29%)
  Pallas kernels  15.2 us (14%)
  local copies, waits for them, and re-layouts  2.57 us (2%)
  other arithmetic  1.73 us (2%)
    ppermute x8, starting transfers between devices, forward(): return tuple((lax.ppermute(w, ('rows', 'core'), pairs) for w in words))  23.1 us
    all_to_all x1, waiting for transfers between devices, on_device(): got = lax.all_to_all(summed, ('z', 'xh', 'xl'), 0, 0, tiled=True)  14.6 us
    all_to_all x1, starting transfers between devices, on_device(): got = lax.all_to_all(summed, ('z', 'xh', 'xl'), 0, 0, tiled=True)  9.59 us
    ppermute x1, starting transfers between devices, on_device(): summed = (keep + lax.ppermute(send, 'core', SWAP).astype(F32)).astype(BF16)  8.65 us
    all_to_all x1, starting transfers between devices, on_device(): team = lax.all_to_all(blocks, TEAM, 0, 0, tiled=True)  8.47 us
    all_to_all x1, waiting for transfers between devices, on_device(): lax.all_to_all(jnp.broadcast_to(own_bias[None, :], (64, SPEC)), MP, 0, 0,...  8.36 us
    ppermute x8, waiting for transfers between devices, forward(): return tuple((lax.ppermute(w, ('rows', 'core'), pairs) for w in words))  7.55 us
    all_to_all x1, starting transfers between devices, on_device(): lax.all_to_all(jnp.broadcast_to(own_bias[None, :], (64, SPEC)), MP, 0, 0,...  6.94 us
  transfers between devices with their start and end apart: 12, of which 7 were waited for; matrix products, arithmetic and copies ran while one was open for 1% of the time, Pallas kernels for 10%

profile of v6, /device:TPU:1, one launch (start us, length us, event | category | flops | bytes accessed | tf_op | source)
XLA Modules:
  0.0 109.2 jit_solution(8620346987388092869)
XLA Ops:
  0.6 2.0 %pack_up.1.refs_4_ = s32[72,1024]{1,0:T(8,128)} custom-call(s32[1]{0:T(128)} %bitcast.1.half_ref, bf16[512,1024]{1,0:T(8,128)(2,1)} %up_hbm.1, f32[1,512]{1,0:T(1,128)} %bitcast.30), custom_call_target="tpu_custom_call" | custom-call | tf_op jit(solution)/shard_map/pack_up/pallas_call | solution.py:85
  2.7 5.9 %collective-permute-start.4 = (s32[72,1024]{1,0:T(8,128)}, s32[72,1024]{1,0:T(8,128)S(1)}, u32[]{:S(2)}, u32[]{:S(2)}) collective-permute-start(s32[72,1024]{1,0:T(8,128)} %pack_up.1.refs_4_), channel_id=1, source_target_pairs={{0,64},{64,128},{128,192},{192,256},{256,320},{320,384},{384,448},... | collective-permute-start | bytes 884744 | tf_op jit(solution)/shard_map/ppermute | solution.py:334
  8.6 1.9 %pack_down.1.refs_3_ = s32[64,1024]{1,0:T(8,128)} custom-call(s32[1]{0:T(128)} %bitcast.1.half_ref, bf16[1024,512]{1,0:T(8,128)(2,1)} %down_hbm.1), custom_call_target="tpu_custom_call" | custom-call | tf_op jit(solution)/shard_map/pack_down/pallas_call | solution.py:76
  10.5 3.0 %collective-permute-start = (s32[64,1024]{1,0:T(8,128)}, s32[64,1024]{1,0:T(8,128)S(1)}, u32[]{:S(2)}, u32[]{:S(2)}) collective-permute-start(s32[64,1024]{1,0:T(8,128)} %pack_down.1.refs_3_), channel_id=1, source_target_pairs={{0,64},{64,128},{128,192},{192,256},{256,320},{320,384},{384,448},... | collective-permute-start | bytes 786440 | tf_op jit(solution)/shard_map/ppermute | solution.py:334
  13.5 0.0 copy-done.8
  13.5 0.8 copy.30
  14.4 2.5 %share.1 = bf16[4,96,16,128]{3,2,1,0:T(8,128)(2,1)} custom-call(s32[1]{0:T(128)} %bitcast.4.row_ref, bf16[8,16,1024]{2,1,0:T(8,128)(2,1)} %bitcast.26, bf16[2,16,4096]{2,1,0:T(8,128)(2,1)} %bitcast.27, bf16[2,16,4096]{2,1,0:T(8,128)(2,1)} %bitcast.28), custom_call_target="tpu_custom_call" | custom-call | tf_op jit(solution)/shard_map/share/pallas_call | solution.py:161
  16.8 1.3 %collective-permute-done.refs_1_ = s32[64,1024]{1,0:T(8,128)S(1)} collective-permute-done((s32[64,1024]{1,0:T(8,128)}, s32[64,1024]{1,0:T(8,128)S(1)}, u32[]{:S(2)}, u32[]{:S(2)}) %collective-permute-start) | collective-permute-done | bytes 262176 | tf_op jit(solution)/shard_map/ppermute | solution.py:334
  18.1 0.0 collective-permute-done.4.refs_2_
  18.2 8.5 %all-to-all-start = ((bf16[4,96,16,128]{3,2,1,0:T(8,128)(2,1)}), bf16[4,96,16,128]{3,2,1,0:T(8,128)(2,1)S(1)}, u32[]{:S(2)}, u32[]{:S(2)}) async-start(bf16[4,96,16,128]{3,2,1,0:T(8,128)(2,1)} %share.1), calls=%async_computation | async-start | bytes 3145728 | tf_op jit(solution)/shard_map/all_to_all | solution.py:341
  26.6 3.6 %collective-permute-start.5 = (s32[72,1024]{1,0:T(8,128)S(1)}, s32[72,1024]{1,0:T(8,128)S(1)}, u32[]{:S(2)}, u32[]{:S(2)}) collective-permute-start(s32[72,1024]{1,0:T(8,128)S(1)} %collective-permute-done.4.refs_2_), channel_id=1, source_target_pairs={{0,64},{64,128},{128,192},{192,256},{256,320},{320,384},{384,448},... | collective-permute-start | bytes 884744 | tf_op jit(solution)/shard_map/ppermute | solution.py:334
  30.3 1.9 %collective-permute-start.1 = (s32[64,1024]{1,0:T(8,128)S(1)}, s32[64,1024]{1,0:T(8,128)S(1)}, u32[]{:S(2)}, u32[]{:S(2)}) collective-permute-start(s32[64,1024]{1,0:T(8,128)S(1)} %collective-permute-done.refs_1_), channel_id=1, source_target_pairs={{0,64},{64,128},{128,192},{192,256},{256,320},{320,384},{384,448},... | collective-permute-start | bytes 786440 | tf_op jit(solution)/shard_map/ppermute | solution.py:334
  32.2 2.2 %collective-permute-done.5.refs_2_ = s32[72,1024]{1,0:T(8,128)S(1)} collective-permute-done((s32[72,1024]{1,0:T(8,128)S(1)}, s32[72,1024]{1,0:T(8,128)S(1)}, u32[]{:S(2)}, u32[]{:S(2)}) %collective-permute-start.5) | collective-permute-done | bytes 294944 | tf_op jit(solution)/shard_map/ppermute | solution.py:334
  34.4 4.5 %collective-permute-start.6 = (s32[72,1024]{1,0:T(8,128)S(1)}, s32[72,1024]{1,0:T(8,128)S(1)}, u32[]{:S(2)}, u32[]{:S(2)}) collective-permute-start(s32[72,1024]{1,0:T(8,128)S(1)} %collective-permute-done.5.refs_2_), channel_id=1, source_target_pairs={{0,64},{64,128},{128,192},{192,256},{256,320},{320,384},{384,448},... | collective-permute-start | bytes 884744 | tf_op jit(solution)/shard_map/ppermute | solution.py:334
  38.9 0.0 collective-permute-done.1.refs_1_
  38.9 2.8 %collective-permute-start.2 = (s32[64,1024]{1,0:T(8,128)S(1)}, s32[64,1024]{1,0:T(8,128)}, u32[]{:S(2)}, u32[]{:S(2)}) collective-permute-start(s32[64,1024]{1,0:T(8,128)S(1)} %collective-permute-done.1.refs_1_), channel_id=1, source_target_pairs={{0,64},{64,128},{128,192},{192,256},{256,320},{320,384},{384,448},... | collective-permute-start | bytes 786440 | tf_op jit(solution)/shard_map/ppermute | solution.py:334
  41.7 0.8 collective-permute-done.6.refs_2_
  42.6 0.7 collective-permute-start.7
  43.2 3.2 %collective-permute-done.2.refs_1_ = s32[64,1024]{1,0:T(8,128)} collective-permute-done((s32[64,1024]{1,0:T(8,128)S(1)}, s32[64,1024]{1,0:T(8,128)}, u32[]{:S(2)}, u32[]{:S(2)}) %collective-permute-start.2) | collective-permute-done | bytes 262176 | tf_op jit(solution)/shard_map/ppermute | solution.py:334
  46.5 0.7 collective-permute-start.3
  47.1 0.0 all-to-all-done.refs_4_
  47.1 0.0 copy-done.6
  47.2 1.4 %channel.4 = (f32[512,1024]{1,0:T(8,128)S(1)}, f32[8,8,128]{2,1,0:T(8,128)S(1)}, bf16[512,1024]{1,0:T(8,128)(2,1)S(1)}, bf16[4,4,64,256]{3,2,1,0:T(8,128)(2,1)S(1)}) custom-call(s32[1]{0:T(128)} %bitcast.refs_0_, s32[64,1024]{1,0:T(8,128)S(1)} %collective-permute-done.refs_1_, s32[72,1024]{1,0:T(8,128)S(1)} %collective-permute-done.4.refs_2_, ...), custom_call_target="tpu_custom_call" | custom-call | flops 536870912 | bytes 6848512 | tf_op jit(solution)/shard_map/channel/pallas_call | solution.py:246
  48.5 1.4 %channel.5 = (f32[512,1024]{1,0:T(8,128)S(1)}, f32[8,8,128]{2,1,0:T(8,128)S(1)}) custom-call(s32[1]{0:T(128)} %bitcast.refs_0_, s32[64,1024]{1,0:T(8,128)S(1)} %collective-permute-done.1.refs_1_, s32[72,1024]{1,0:T(8,128)S(1)} %collective-permute-done.5.refs_2_, ...), custom_call_target="tpu_custom_call", output_to_operand_aliasing={{0}: (5, {}), {1}: (6, {})} | custom-call | flops 536870912 | bytes 6848512 | tf_op jit(solution)/shard_map/channel/pallas_call | solution.py:246
  49.9 0.0 copy-start.1
  49.9 2.4 %channel.6 = (f32[512,1024]{1,0:T(8,128)S(1)}, f32[8,8,128]{2,1,0:T(8,128)S(1)}) custom-call(s32[1]{0:T(128)} %bitcast.refs_0_, s32[64,1024]{1,0:T(8,128)} %collective-permute-done.2.refs_1_, s32[72,1024]{1,0:T(8,128)S(1)} %collective-permute-done.6.refs_2_, ...), custom_call_target="tpu_custom_call", output_to_operand_aliasing={{0}: (5, {}), {1}: (6, {})} | custom-call | flops 536870912 | bytes 6848512 | tf_op jit(solution)/shard_map/channel/pallas_call | solution.py:246
  52.3 0.0 collective-permute-done.3.refs_1_
  52.3 0.0 collective-permute-done.7.refs_2_
  52.3 0.0 copy-done
  52.3 0.0 copy-done.1
  52.3 1.4 %channel.7 = (f32[32,16,512]{2,1,0:T(8,128)S(1)}, bf16[32,16,512]{2,1,0:T(8,128)(2,1)S(1)}, f32[8,8,128]{2,1,0:T(8,128)S(1)}) custom-call(s32[1]{0:T(128)} %bitcast.refs_0_, s32[64,1024]{1,0:T(8,128)S(1)} %collective-permute-done.3.refs_1_, s32[72,1024]{1,0:T(8,128)S(1)} %collective-permute-done.7.refs_2_, s32[64,1024]{1,0:T(8,128)S(1)} %copy-done.1, ...), custom_call_target="tpu_custom_call" | custom-call | flops 536870912 | bytes 6848512 | tf_op jit(solution)/shard_map/channel/pallas_call | solution.py:246
  53.7 0.0 copy-start.2
  53.7 0.0 copy-start.7
  53.7 8.7 %collective-permute-start.8 = (bf16[32,16,512]{2,1,0:T(8,128)(2,1)S(1)}, bf16[32,16,512]{2,1,0:T(8,128)(2,1)S(1)}, u32[]{:S(2)}, u32[]{:S(2)}) collective-permute-start(bf16[32,16,512]{2,1,0:T(8,128)(2,1)S(1)} %get-tuple-element.35), channel_id=1, source_target_pairs={{0,1},{1,0},{2,3},{3,2},{4,5},{5,4},{6,7},{7,6},{8,9},{9,8},{10,11... | collective-permute-start | bytes 1572872 | tf_op jit(solution)/shard_map/ppermute | solution.py:354
  62.4 1.5 %collective-permute-done.8 = bf16[32,16,512]{2,1,0:T(8,128)(2,1)S(1)} collective-permute-done((bf16[32,16,512]{2,1,0:T(8,128)(2,1)S(1)}, bf16[32,16,512]{2,1,0:T(8,128)(2,1)S(1)}, u32[]{:S(2)}, u32[]{:S(2)}) %collective-permute-start.8) | collective-permute-done | bytes 524320 | tf_op jit(solution)/shard_map/ppermute | solution.py:354
  63.9 1.0 add_convert_fusion
  64.9 9.6 %all-to-all-start.1 = ((bf16[32,16,512]{2,1,0:T(8,128)(2,1)}), bf16[32,16,512]{2,1,0:T(8,128)(2,1)S(1)}, u32[]{:S(2)}, u32[]{:S(2)}) async-start(bf16[32,16,512]{2,1,0:T(8,128)(2,1)} %add_convert_fusion), calls=%async_computation.1 | async-start | bytes 1048576 | tf_op jit(solution)/shard_map/all_to_all | solution.py:355
  74.5 0.0 copy-start.3
  74.5 1.0 copy-done.3
  75.6 0.9 dense.1
  76.5 14.6 %all-to-all-done.1.got_ref = bf16[32,16,512]{2,1,0:T(8,128)(2,1)S(1)} async-done(((bf16[32,16,512]{2,1,0:T(8,128)(2,1)}), bf16[32,16,512]{2,1,0:T(8,128)(2,1)S(1)}, u32[]{:S(2)}, u32[]{:S(2)}) %all-to-all-start.1) | async-done | bytes 524320 | tf_op jit(solution)/shard_map/all_to_all | solution.py:355
  91.1 0.4 token_.1
  91.5 0.1 add_reduce_fusion
  91.7 0.6 broadcast_in_dim.2
  92.3 6.9 %all-to-all-start.2 = ((f32[64,1,8]{2,1,0:T(1,128)}), f32[64,1,8]{2,1,0:T(1,128)S(1)}, u32[]{:S(2)}, u32[]{:S(2)}) async-start(f32[64,1,8]{2,1,0:T(1,128)} %broadcast_in_dim.2), calls=%async_computation.2 | async-start | bytes 65536 | tf_op jit(solution)/shard_map/all_to_all | solution.py:358
  99.3 1.0 back.1
  100.3 8.4 %all-to-all-done.2 = f32[64,1,8]{2,1,0:T(1,128)S(1)} async-done(((f32[64,1,8]{2,1,0:T(1,128)}), f32[64,1,8]{2,1,0:T(1,128)S(1)}, u32[]{:S(2)}, u32[]{:S(2)}) %all-to-all-start.2) | async-done | bytes 2080 | tf_op jit(solution)/shard_map/all_to_all | solution.py:358
  108.6 0.6 reduce_sum.19
  (9 shorter events, 0.0 us)
Async XLA Ops:
  0.6 12.9 %copy-start.8 = (bf16[16,8,1024]{2,1,0:T(8,128)(2,1)S(1)}, bf16[16,8,1024]{2,1,0:T(8,128)(2,1)}, u32[]{:S(2)}) copy-start(bf16[16,8,1024]{2,1,0:T(8,128)(2,1)} %param.12) | copy-start | bytes 786436
  2.7 15.5 %collective-permute-start.4 = (s32[72,1024]{1,0:T(8,128)}, s32[72,1024]{1,0:T(8,128)S(1)}, u32[]{:S(2)}, u32[]{:S(2)}) collective-permute-start(s32[72,1024]{1,0:T(8,128)} %pack_up.1.refs_4_), channel_id=1, source_target_pairs={{0,64},{64,128},{128,192},{192,256},{256,320},{320,384},{384,448},... | collective-permute-start | bytes 884744 | tf_op jit(solution)/shard_map/ppermute | solution.py:334
  10.5 7.6 %collective-permute-start = (s32[64,1024]{1,0:T(8,128)}, s32[64,1024]{1,0:T(8,128)S(1)}, u32[]{:S(2)}, u32[]{:S(2)}) collective-permute-start(s32[64,1024]{1,0:T(8,128)} %pack_down.1.refs_3_), channel_id=1, source_target_pairs={{0,64},{64,128},{128,192},{192,256},{256,320},{320,384},{384,448},... | collective-permute-start | bytes 786440 | tf_op jit(solution)/shard_map/ppermute | solution.py:334
  16.8 30.3 %copy-start.6 = (f32[1024]{0:T(1024)S(1)}, f32[1024]{0:T(1024)}, u32[]{:S(2)}) copy-start(f32[1024]{0:T(1024)} %param.14) | copy-start | bytes 12292
  18.2 29.0 %all-to-all-start = ((bf16[4,96,16,128]{3,2,1,0:T(8,128)(2,1)}), bf16[4,96,16,128]{3,2,1,0:T(8,128)(2,1)S(1)}, u32[]{:S(2)}, u32[]{:S(2)}) async-start(bf16[4,96,16,128]{3,2,1,0:T(8,128)(2,1)} %share.1), calls=%async_computation | async-start | bytes 3145728 | tf_op jit(solution)/shard_map/all_to_all | solution.py:341
  26.6 7.8 %collective-permute-start.5 = (s32[72,1024]{1,0:T(8,128)S(1)}, s32[72,1024]{1,0:T(8,128)S(1)}, u32[]{:S(2)}, u32[]{:S(2)}) collective-permute-start(s32[72,1024]{1,0:T(8,128)S(1)} %collective-permute-done.4.refs_2_), channel_id=1, source_target_pairs={{0,64},{64,128},{128,192},{192,256},{256,320},{320,384},{384,448},... | collective-permute-start | bytes 884744 | tf_op jit(solution)/shard_map/ppermute | solution.py:334
  30.3 8.7 %collective-permute-start.1 = (s32[64,1024]{1,0:T(8,128)S(1)}, s32[64,1024]{1,0:T(8,128)S(1)}, u32[]{:S(2)}, u32[]{:S(2)}) collective-permute-start(s32[64,1024]{1,0:T(8,128)S(1)} %collective-permute-done.refs_1_), channel_id=1, source_target_pairs={{0,64},{64,128},{128,192},{192,256},{256,320},{320,384},{384,448},... | collective-permute-start | bytes 786440 | tf_op jit(solution)/shard_map/ppermute | solution.py:334
  34.4 8.2 %collective-permute-start.6 = (s32[72,1024]{1,0:T(8,128)S(1)}, s32[72,1024]{1,0:T(8,128)S(1)}, u32[]{:S(2)}, u32[]{:S(2)}) collective-permute-start(s32[72,1024]{1,0:T(8,128)S(1)} %collective-permute-done.5.refs_2_), channel_id=1, source_target_pairs={{0,64},{64,128},{128,192},{192,256},{256,320},{320,384},{384,448},... | collective-permute-start | bytes 884744 | tf_op jit(solution)/shard_map/ppermute | solution.py:334
  38.9 7.5 %collective-permute-start.2 = (s32[64,1024]{1,0:T(8,128)S(1)}, s32[64,1024]{1,0:T(8,128)}, u32[]{:S(2)}, u32[]{:S(2)}) collective-permute-start(s32[64,1024]{1,0:T(8,128)S(1)} %collective-permute-done.1.refs_1_), channel_id=1, source_target_pairs={{0,64},{64,128},{128,192},{192,256},{256,320},{320,384},{384,448},... | collective-permute-start | bytes 786440 | tf_op jit(solution)/shard_map/ppermute | solution.py:334
  42.6 9.7 %collective-permute-start.7 = (s32[72,1024]{1,0:T(8,128)S(1)}, s32[72,1024]{1,0:T(8,128)S(1)}, u32[]{:S(2)}, u32[]{:S(2)}) collective-permute-start(s32[72,1024]{1,0:T(8,128)S(1)} %collective-permute-done.6.refs_2_), channel_id=1, source_target_pairs={{0,64},{64,128},{128,192},{192,256},{256,320},{320,384},{384,448},... | collective-permute-start | bytes 884744 | tf_op jit(solution)/shard_map/ppermute | solution.py:334
  46.5 5.8 %collective-permute-start.3 = (s32[64,1024]{1,0:T(8,128)}, s32[64,1024]{1,0:T(8,128)S(1)}, u32[]{:S(2)}, u32[]{:S(2)}) collective-permute-start(s32[64,1024]{1,0:T(8,128)} %collective-permute-done.2.refs_1_), channel_id=1, source_target_pairs={{0,64},{64,128},{128,192},{192,256},{256,320},{320,384},{384,448},... | collective-permute-start | bytes 786440 | tf_op jit(solution)/shard_map/ppermute | solution.py:334
  49.9 2.4 %copy-start = (s32[72,1024]{1,0:T(8,128)S(1)}, s32[72,1024]{1,0:T(8,128)}, u32[]{:S(2)}) copy-start(s32[72,1024]{1,0:T(8,128)} %pack_up.1.refs_4_) | copy-start | bytes 884740
  49.9 2.4 %copy-start.1 = (s32[64,1024]{1,0:T(8,128)S(1)}, s32[64,1024]{1,0:T(8,128)}, u32[]{:S(2)}) copy-start(s32[64,1024]{1,0:T(8,128)} %pack_down.1.refs_3_) | copy-start | bytes 786436
  53.7 20.8 %copy-start.2 = (bf16[16,128,128]{2,1,0:T(8,128)(2,1)S(1)}, bf16[16,128,128]{2,1,0:T(8,128)(2,1)}, u32[]{:S(2)}) copy-start(bf16[16,128,128]{2,1,0:T(8,128)(2,1)} %in_ref.1) | copy-start | bytes 1572868
  53.7 20.8 %copy-start.7 = (s32[16]{0:T(128)S(1)}, s32[16]{0:T(128)}, u32[]{:S(2)}) copy-start(s32[16]{0:T(128)} %cells_ref.1) | copy-start | bytes 196
  53.7 10.2 %collective-permute-start.8 = (bf16[32,16,512]{2,1,0:T(8,128)(2,1)S(1)}, bf16[32,16,512]{2,1,0:T(8,128)(2,1)S(1)}, u32[]{:S(2)}, u32[]{:S(2)}) collective-permute-start(bf16[32,16,512]{2,1,0:T(8,128)(2,1)S(1)} %get-tuple-element.35), channel_id=1, source_target_pairs={{0,1},{1,0},{2,3},{3,2},{4,5},{5,4},{6,7},{7,6},{8,9},{9,8},{10,11... | collective-permute-start | bytes 1572872 | tf_op jit(solution)/shard_map/ppermute | solution.py:354
  63.9 27.2 %copy-start.4 = (bf16[2,512,1,16]{1,3,2,0:T(8,128)(2,1)S(1)}, bf16[2,512,1,16]{1,3,2,0:T(8,128)(2,1)}, u32[]{:S(2)}) copy-start(bf16[2,512,1,16]{1,3,2,0:T(8,128)(2,1)} %param.22) | copy-start | bytes 98308
  63.9 27.2 %copy-start.5 = (bf16[2,512,1,16]{1,3,2,0:T(8,128)(2,1)S(1)}, bf16[2,512,1,16]{1,3,2,0:T(8,128)(2,1)}, u32[]{:S(2)}) copy-start(bf16[2,512,1,16]{1,3,2,0:T(8,128)(2,1)} %param.23) | copy-start | bytes 98308
  64.9 26.2 %all-to-all-start.1 = ((bf16[32,16,512]{2,1,0:T(8,128)(2,1)}), bf16[32,16,512]{2,1,0:T(8,128)(2,1)S(1)}, u32[]{:S(2)}, u32[]{:S(2)}) async-start(bf16[32,16,512]{2,1,0:T(8,128)(2,1)} %add_convert_fusion), calls=%async_computation.1 | async-start | bytes 1048576 | tf_op jit(solution)/shard_map/all_to_all | solution.py:355
  74.5 1.0 copy-start.3
  92.3 16.3 %all-to-all-start.2 = ((f32[64,1,8]{2,1,0:T(1,128)}), f32[64,1,8]{2,1,0:T(1,128)S(1)}, u32[]{:S(2)}, u32[]{:S(2)}) async-start(f32[64,1,8]{2,1,0:T(1,128)} %broadcast_in_dim.2), calls=%async_computation.2 | async-start | bytes 65536 | tf_op jit(solution)/shard_map/all_to_all | solution.py:358

commit v7 on v5

--- a/solution.py
+++ b/solution.py
@@ -29,7 +29,6 @@
 STEPS = 4
 SHARED = 64
 ROWS_DEV = SPEC * SHARED
-PACKED = 136
 LAM_TILES = SPEC * (D // 128)
 SCALE_ONE = float(2**38)
 
@@ -44,7 +43,8 @@
     return (shifted >> 24).astype(F32).astype(BF16)
 
 
-def pack_kernel(half_ref, down_hbm, up_hbm, scale_hbm, out_ref, down_ref, up_ref, scale_ref, sems):
+def pack_kernel(half_ref, down_hbm, up_hbm, scale_hbm, *refs):
+    out_refs, (down_ref, up_ref, scale_ref, sems) = refs[:2], refs[2:]
     start = pl.multiple_of(half_ref[0] * PART, PART)
     copies = [
         pltpu.make_async_copy(down_hbm.at[:, pl.ds(start, PART)], down_ref, sems.at[0]),
@@ -53,25 +53,31 @@
     ]
     for copy in copies:
         copy.start()
-    out_ref[128:136, :] = jnp.zeros((8, D), I32)
+    for out_ref in out_refs:
+        out_ref[64:72, :] = jnp.zeros((8, D), I32)
     copies[0].wait()
     down = pack_codes([down_ref[m * 256 : (m + 1) * 256, :] for m in range(4)])
-    for k in range(4):
-        out_ref[0:64, k * PART : (k + 1) * PART] = down[k * 64 : (k + 1) * 64, :]
+    for h, out_ref in enumerate(out_refs):
+        for k in range(8):
+            cut = slice(k * 128, (k + 1) * 128)
+            out_ref[0:32, cut] = down[k * 32 : (k + 1) * 32, h * 128 : (h + 1) * 128]
     copies[1].wait()
-    out_ref[64:128, :] = pack_codes([up_ref[m * 64 : (m + 1) * 64, :] for m in range(4)])
     copies[2].wait()
     scale = (scale_ref[...] * SCALE_ONE).astype(I32)
-    out_ref[128:136, 0:PART] = jnp.broadcast_to(scale, (8, PART))
+    for h, out_ref in enumerate(out_refs):
+        rows = [h * 128 + m * 32 for m in range(4)]
+        out_ref[32:64, :] = pack_codes([up_ref[i : i + 32, :] for i in rows])
+        out_ref[64:72, 0:128] = jnp.broadcast_to(scale[:, h * 128 : (h + 1) * 128], (8, 128))
 
 
 def pack(half, q_down, q_up, up_scale):
+    smem, hbm = pl.BlockSpec(memory_space=pltpu.SMEM), pl.BlockSpec(memory_space=pltpu.HBM)
+    vmem = pl.BlockSpec(memory_space=pltpu.VMEM)
     return pl.pallas_call(
         pack_kernel,
-        out_shape=jax.ShapeDtypeStruct((PACKED, D), I32),
-        in_specs=[pl.BlockSpec(memory_space=pltpu.SMEM)]
-        + [pl.BlockSpec(memory_space=pltpu.HBM)] * 3,
-        out_specs=pl.BlockSpec(memory_space=pltpu.VMEM),
+        out_shape=(jax.ShapeDtypeStruct((72, D), I32),) * 2,
+        in_specs=[smem, hbm, hbm, hbm],
+        out_specs=(vmem, vmem),
         scratch_shapes=[
             pltpu.VMEM((D, PART), BF16),
             pltpu.VMEM((PART, D), BF16),
@@ -131,14 +137,17 @@
     for to in range(4):
         half, core = to // 2, to % 2
         for j in range(STEPS):
-            owner = row + (j + 1) % STEPS if core else row - (j + 1)
-            start = pl.multiple_of((owner & 7) * TH + half * PART, PART)
-            for kind in range(4):
-                ref = slopes_ref if kind < 2 else icpt_ref
-                values = ref[kind % 2, :, pl.ds(start, PART)]
-                for h in range(2):
-                    tile = LAM_TILES + (j * 4 + kind) * 2 + h
-                    out_ref[to, tile] = values[:, h * 128 : (h + 1) * 128]
+            if j < STEPS - 1:
+                owner = row + (j + 1) if core else row - (j + 1)
+                cuts = [(owner, 0), (owner, 1)]
+            else:
+                cuts = [(row + STEPS, core), (row, core)]
+            for h, (owner, chunk) in enumerate(cuts):
+                start = pl.multiple_of((owner & 7) * TH + half * PART + chunk * 128, 128)
+                for kind in range(4):
+                    ref = slopes_ref if kind < 2 else icpt_ref
+                    values = ref[kind % 2, :, pl.ds(start, 128)]
+                    out_ref[to, LAM_TILES + (j * 4 + kind) * 2 + h] = values
 
 
 def share(row, by_row, slopes, icpt):
@@ -155,7 +164,7 @@
 
 def channel_kernel(step, *refs):
     first, last = step == 0, step == STEPS - 1
-    core_ref, words_ref, *refs = refs
+    core_ref, *words, refs = refs[0], refs[1], refs[2], refs[3:]
     if first:
         down_scale_ref, got_ref, acc_ref, bias_ref, scaled_ref, bounds_ref, down, up = refs
         for q in range(4):
@@ -173,18 +182,25 @@
         acc_in, bias_in = acc_ref, None
     else:
         if last:
-            own_ref, *refs = refs
+            *own_words, refs = refs[0], refs[1], refs[2:]
         scaled_ref, bounds_ref, acc_in, bias_in, *outs, down, up = refs
-    words = words_ref[...]
+    words = [w[...] for w in words]
     if last:
-        words = jnp.where(core_ref[0] == 0, words, own_ref[...])
-    for m in range(4):
-        codes = unpack_codes(words[0:64], m)
-        for q in range(4):
-            rows = m * 256 + q * 64
-            down[rows : rows + 64, :] = codes[:, q * PART : (q + 1) * PART]
-        up[m * 64 : (m + 1) * 64, :] = unpack_codes(words[64:128], m)
-    scale = words[128:129, 0:PART].astype(F32) * (1.0 / SCALE_ONE)
+        own_core = core_ref[0] == 0
+        words = [
+            jnp.where(own_core, words[0], words[1]),
+            jnp.where(own_core, own_words[0][...], own_words[1][...]),
+        ]
+    for h, chunk in enumerate(words):
+        for m in range(4):
+            codes = unpack_codes(chunk[0:32], m)
+            for q in range(8):
+                rows = m * 256 + q * 32
+                down[rows : rows + 32, h * 128 : (h + 1) * 128] = codes[:, q * 128 : (q + 1) * 128]
+            rows = h * 128 + m * 32
+            up[rows : rows + 32, :] = unpack_codes(chunk[32:64], m)
+    scale = jnp.concatenate([chunk[64:65, 0:128] for chunk in words], axis=1)
+    scale = scale.astype(F32) * (1.0 / SCALE_ONE)
     pre = jnp.dot(scaled_ref[...], down[...], preferred_element_type=F32)
     pre = pre.reshape(SPEC, SHARED, PART)
     mid, terms = relaxed(pre, *(bounds_ref[step, kind] for kind in range(4)))
@@ -237,7 +253,7 @@
         compiler_params=pltpu.CompilerParams(vmem_limit_bytes=VMEM),
         cost_estimate=pl.CostEstimate(
             flops=4 * ROWS_DEV * PART * D,
-            bytes_accessed=PACKED * D * 4 + 3 * ROWS_DEV * D * 4,
+            bytes_accessed=144 * D * 4 + 3 * ROWS_DEV * D * 4,
             transcendentals=0,
         ),
         name="channel",
@@ -315,30 +331,26 @@
     behind = [(i * 2 + 1, (i - 1) % slices * 2 + 1) for i in range(slices)]
 
     def forward(words, pairs):
-        return lax.ppermute(words, ("rows", "core"), pairs)
+        return tuple(lax.ppermute(w, ("rows", "core"), pairs) for w in words)
 
     own = pack(half, q_down, q_up, up_scale)
     first = forward(own, ahead + behind)
-    blocks = share(
-        row,
-        jnp.swapaxes(lam_out, 0, 1),
-        chan_slopes.reshape(2, tok_dev, CH),
-        chan_icpt.reshape(2, tok_dev, CH),
-    )
+    _, lam, *bounds = lax.optimization_barrier((own, lam_out, chan_slopes, chan_icpt))
+    blocks = share(row, jnp.swapaxes(lam, 0, 1), *(b.reshape(2, tok_dev, CH) for b in bounds))
     _, blocks = lax.optimization_barrier((first, blocks))
     team = lax.all_to_all(blocks, TEAM, 0, 0, tiled=True)
     second = forward(first, ahead + behind)
     third = forward(second, ahead + behind)
-    far = forward(third, ahead)
+    far = forward(third[:1], ahead) + forward(third[1:], behind)
 
     dense_in, dense_out = dense_blocks(block_cells, tok_in_blocks, tok_out_blocks)
     slopes = jnp.transpose(tok_slopes, (0, 2, 3, 1)).reshape(2, 16, TH)
     icpt = jnp.transpose(tok_icpt, (0, 2, 3, 1)).reshape(2, 16, TH)
 
-    acc, chan_bias, *given = channel_part(0, core, first, down_scale.reshape(1, D), team)
-    acc, chan_bias = channel_part(1, core, second, *given, acc, chan_bias)
-    acc, chan_bias = channel_part(2, core, third, *given, acc, chan_bias)
-    keep, send, chan_bias = channel_part(3, core, far, own, *given, acc, chan_bias)
+    acc, chan_bias, *given = channel_part(0, core, *first, down_scale.reshape(1, D), team)
+    acc, chan_bias = channel_part(1, core, *second, *given, acc, chan_bias)
+    acc, chan_bias = channel_part(2, core, *third, *given, acc, chan_bias)
+    keep, send, chan_bias = channel_part(3, core, *far, *own, *given, acc, chan_bias)
     summed = (keep + lax.ppermute(send, "core", SWAP).astype(F32)).astype(BF16)
     got = lax.all_to_all(summed, ("z", "xh", "xl"), 0, 0, tiled=True)
     columns, mid, tok_bias = token_mlp(got, dense_out, slopes, icpt)

time: 110 us -> 107 us (0.973)
  waiting for transfers between devices: 44.9 us -> 33.4 us
  starting transfers between devices: 45.3 us -> 52.8 us
  Pallas kernels: 12.5 us -> 14.8 us
    ppermute x4 -> x8, starting transfers between devices: 16.4 us -> 24.5 us  [forward(): return tuple((lax.ppermute(w, ('rows', 'core'), pairs) for w in words))]
    all_to_all x1, waiting for transfers between devices: 7.21 us -> 0.01 us  [on_device(): team = lax.all_to_all(blocks, TEAM, 0, 0, tiled=True)]
    ppermute x4 -> x8, waiting for transfers between devices: 13.2 us -> 8.97 us  [forward(): return tuple((lax.ppermute(w, ('rows', 'core'), pairs) for w in words))]
    ppermute x1, starting transfers between devices: 6.59 us -> 3.33 us  [on_device(): summed = (keep + lax.ppermute(send, 'core', SWAP).astype(F32)).astype(BF16)]
    pallas_call x4, Pallas kernels: 5.44 us -> 7.77 us  [channel_part(): pl.pallas_call(functools.partial(channel_kernel, step), out_shape=out_sha...]
    all_to_all x1, starting transfers between devices: 7.68 us -> 9.7 us  [on_device(): team = lax.all_to_all(blocks, TEAM, 0, 0, tiled=True)]
    unnamed x21 -> x18, local copies, waits for them, and re-layouts: 2.98 us -> 1.07 us
  transfers between devices with their start and end apart: 8 -> 12, of which waited for: 6 -> 7; matrix products, arithmetic and copies ran while one was open for 1% -> 1% of each run, Pallas kernels for 8% -> 9%
where the time goes in v7:
time: 107 us; the launch traced here: 106 us
  starting transfers between devices  52.8 us (49%)
  waiting for transfers between devices  33.4 us (31%)
  Pallas kernels  14.8 us (14%)
  local copies, waits for them, and re-layouts  2.55 us (2%)
  other arithmetic  1.74 us (2%)
    ppermute x8, starting transfers between devices, forward(): return tuple((lax.ppermute(w, ('rows', 'core'), pairs) for w in words))  24.5 us
    all_to_all x1, waiting for transfers between devices, on_device(): got = lax.all_to_all(summed, ('z', 'xh', 'xl'), 0, 0, tiled=True)  14.6 us
    all_to_all x1, starting transfers between devices, on_device(): team = lax.all_to_all(blocks, TEAM, 0, 0, tiled=True)  9.7 us
    ppermute x8, waiting for transfers between devices, forward(): return tuple((lax.ppermute(w, ('rows', 'core'), pairs) for w in words))  8.97 us
    all_to_all x1, starting transfers between devices, on_device(): got = lax.all_to_all(summed, ('z', 'xh', 'xl'), 0, 0, tiled=True)  8.36 us
    all_to_all x1, waiting for transfers between devices, on_device(): lax.all_to_all(jnp.broadcast_to(own_bias[None, :], (64, SPEC)), MP, 0, 0,...  8.36 us
    pallas_call x4, Pallas kernels, channel_part(): pl.pallas_call(functools.partial(channel_kernel, step), out_shape=out_sha...  7.77 us
    all_to_all x1, starting transfers between devices, on_device(): lax.all_to_all(jnp.broadcast_to(own_bias[None, :], (64, SPEC)), MP, 0, 0,...  6.93 us
  transfers between devices with their start and end apart: 12, of which 7 were waited for; matrix products, arithmetic and copies ran while one was open for 1% of the time, Pallas kernels for 9%

profile of v7, /device:TPU:1, one launch (start us, length us, event | category | flops | bytes accessed | tf_op | source)
XLA Modules:
  0.0 106.3 jit_solution(3301145012702813066)
XLA Ops:
  0.6 0.0 copy-start.8
  0.6 2.2 %pack.1 = (s32[72,1024]{1,0:T(8,128)}, s32[72,1024]{1,0:T(8,128)}) custom-call(s32[1]{0:T(128)} %bitcast.1.half_ref, bf16[1024,512]{1,0:T(8,128)(2,1)} %down_hbm.1, bf16[512,1024]{1,0:T(8,128)(2,1)} %up_hbm.1, f32[1,512]{1,0:T(1,128)} %bitcast.30), custom_call_target="tpu_custom_call" | custom-call | tf_op jit(solution)/shard_map/pack/pallas_call | solution.py:76
  2.8 5.9 %collective-permute-start = (s32[72,1024]{1,0:T(8,128)}, s32[72,1024]{1,0:T(8,128)S(1)}, u32[]{:S(2)}, u32[]{:S(2)}) collective-permute-start(s32[72,1024]{1,0:T(8,128)} %get-tuple-element.24.refs_3_), channel_id=1, source_target_pairs={{0,64},{64,128},{128,192},{192,256},{256,320},{320,384},{384,448},... | collective-permute-start | bytes 884744 | tf_op jit(solution)/shard_map/ppermute | solution.py:334
  8.8 3.0 %collective-permute-start.4 = (s32[72,1024]{1,0:T(8,128)}, s32[72,1024]{1,0:T(8,128)S(1)}, u32[]{:S(2)}, u32[]{:S(2)}) collective-permute-start(s32[72,1024]{1,0:T(8,128)} %get-tuple-element.25.refs_4_), channel_id=1, source_target_pairs={{0,64},{64,128},{128,192},{192,256},{256,320},{320,384},{384,448},... | collective-permute-start | bytes 884744 | tf_op jit(solution)/shard_map/ppermute | solution.py:334
  11.8 0.0 copy-done.8
  11.8 0.9 copy.30
  12.6 2.5 %share.1 = bf16[4,96,16,128]{3,2,1,0:T(8,128)(2,1)} custom-call(s32[1]{0:T(128)} %bitcast.4.row_ref, bf16[8,16,1024]{2,1,0:T(8,128)(2,1)} %bitcast.26, bf16[2,16,4096]{2,1,0:T(8,128)(2,1)} %bitcast.27, bf16[2,16,4096]{2,1,0:T(8,128)(2,1)} %bitcast.28), custom_call_target="tpu_custom_call" | custom-call | tf_op jit(solution)/shard_map/share/pallas_call | solution.py:155
  15.1 0.0 collective-permute-done.refs_1_
  15.1 1.6 %collective-permute-done.4.refs_2_ = s32[72,1024]{1,0:T(8,128)S(1)} collective-permute-done((s32[72,1024]{1,0:T(8,128)}, s32[72,1024]{1,0:T(8,128)S(1)}, u32[]{:S(2)}, u32[]{:S(2)}) %collective-permute-start.4) | collective-permute-done | bytes 294944 | tf_op jit(solution)/shard_map/ppermute | solution.py:334
  16.8 9.7 %all-to-all-start = ((bf16[4,96,16,128]{3,2,1,0:T(8,128)(2,1)}), bf16[4,96,16,128]{3,2,1,0:T(8,128)(2,1)S(1)}, u32[]{:S(2)}, u32[]{:S(2)}) async-start(bf16[4,96,16,128]{3,2,1,0:T(8,128)(2,1)} %share.1), calls=%async_computation | async-start | bytes 3145728 | tf_op jit(solution)/shard_map/all_to_all | solution.py:341
  26.5 2.4 %collective-permute-start.1 = (s32[72,1024]{1,0:T(8,128)S(1)}, s32[72,1024]{1,0:T(8,128)S(1)}, u32[]{:S(2)}, u32[]{:S(2)}) collective-permute-start(s32[72,1024]{1,0:T(8,128)S(1)} %collective-permute-done.refs_1_), channel_id=1, source_target_pairs={{0,64},{64,128},{128,192},{192,256},{256,320},{320,384},{384,448},... | collective-permute-start | bytes 884744 | tf_op jit(solution)/shard_map/ppermute | solution.py:334
  28.9 1.9 %collective-permute-start.5 = (s32[72,1024]{1,0:T(8,128)S(1)}, s32[72,1024]{1,0:T(8,128)S(1)}, u32[]{:S(2)}, u32[]{:S(2)}) collective-permute-start(s32[72,1024]{1,0:T(8,128)S(1)} %collective-permute-done.4.refs_2_), channel_id=1, source_target_pairs={{0,64},{64,128},{128,192},{192,256},{256,320},{320,384},{384,448},... | collective-permute-start | bytes 884744 | tf_op jit(solution)/shard_map/ppermute | solution.py:334
  30.8 3.4 %collective-permute-done.1.refs_1_ = s32[72,1024]{1,0:T(8,128)S(1)} collective-permute-done((s32[72,1024]{1,0:T(8,128)S(1)}, s32[72,1024]{1,0:T(8,128)S(1)}, u32[]{:S(2)}, u32[]{:S(2)}) %collective-permute-start.1) | collective-permute-done | bytes 294944 | tf_op jit(solution)/shard_map/ppermute | solution.py:334
  34.2 3.3 %collective-permute-start.2 = (s32[72,1024]{1,0:T(8,128)S(1)}, s32[72,1024]{1,0:T(8,128)S(1)}, u32[]{:S(2)}, u32[]{:S(2)}) collective-permute-start(s32[72,1024]{1,0:T(8,128)S(1)} %collective-permute-done.1.refs_1_), channel_id=1, source_target_pairs={{0,64},{64,128},{128,192},{192,256},{256,320},{320,384},{384,448},... | collective-permute-start | bytes 884744 | tf_op jit(solution)/shard_map/ppermute | solution.py:334
  37.5 0.0 collective-permute-done.5.refs_2_
  37.5 3.1 %collective-permute-start.6 = (s32[72,1024]{1,0:T(8,128)S(1)}, s32[72,1024]{1,0:T(8,128)}, u32[]{:S(2)}, u32[]{:S(2)}) collective-permute-start(s32[72,1024]{1,0:T(8,128)S(1)} %collective-permute-done.5.refs_2_), channel_id=1, source_target_pairs={{0,64},{64,128},{128,192},{192,256},{256,320},{320,384},{384,448},... | collective-permute-start | bytes 884744 | tf_op jit(solution)/shard_map/ppermute | solution.py:334
  40.7 1.3 %collective-permute-done.2.refs_1_ = s32[72,1024]{1,0:T(8,128)S(1)} collective-permute-done((s32[72,1024]{1,0:T(8,128)S(1)}, s32[72,1024]{1,0:T(8,128)S(1)}, u32[]{:S(2)}, u32[]{:S(2)}) %collective-permute-start.2) | collective-permute-done | bytes 294944 | tf_op jit(solution)/shard_map/ppermute | solution.py:334
  42.0 0.7 collective-permute-start.3
  42.6 2.7 %collective-permute-done.6.refs_2_ = s32[72,1024]{1,0:T(8,128)} collective-permute-done((s32[72,1024]{1,0:T(8,128)S(1)}, s32[72,1024]{1,0:T(8,128)}, u32[]{:S(2)}, u32[]{:S(2)}) %collective-permute-start.6) | collective-permute-done | bytes 294944 | tf_op jit(solution)/shard_map/ppermute | solution.py:334
  45.3 4.2 %collective-permute-start.7 = (s32[72,1024]{1,0:T(8,128)}, s32[72,1024]{1,0:T(8,128)}, u32[]{:S(2)}, u32[]{:S(2)}) collective-permute-start(s32[72,1024]{1,0:T(8,128)} %collective-permute-done.6.refs_2_), channel_id=1, source_target_pairs={{1,449},{65,1},{129,65},{193,129},{257,193},{321,257},{385,321},{4... | collective-permute-start | bytes 884744 | tf_op jit(solution)/shard_map/ppermute | solution.py:334
  49.5 0.0 all-to-all-done.refs_4_
  49.5 0.0 copy-done.6
  49.5 1.4 %channel.4 = (f32[512,1024]{1,0:T(8,128)S(1)}, f32[8,8,128]{2,1,0:T(8,128)S(1)}, bf16[512,1024]{1,0:T(8,128)(2,1)S(1)}, bf16[4,4,64,256]{3,2,1,0:T(8,128)(2,1)S(1)}) custom-call(s32[1]{0:T(128)} %bitcast.refs_0_, s32[72,1024]{1,0:T(8,128)S(1)} %collective-permute-done.refs_1_, s32[72,1024]{1,0:T(8,128)S(1)} %collective-permute-done.4.refs_2_, ...), custom_call_target="tpu_custom_call" | custom-call | flops 536870912 | bytes 6881280 | tf_op jit(solution)/shard_map/channel/pallas_call | solution.py:246
  50.9 1.5 %channel.5 = (f32[512,1024]{1,0:T(8,128)S(1)}, f32[8,8,128]{2,1,0:T(8,128)S(1)}) custom-call(s32[1]{0:T(128)} %bitcast.refs_0_, s32[72,1024]{1,0:T(8,128)S(1)} %collective-permute-done.1.refs_1_, s32[72,1024]{1,0:T(8,128)S(1)} %collective-permute-done.5.refs_2_, ...), custom_call_target="tpu_custom_call", output_to_operand_aliasing={{0}: (5, {}), {1}: (6, {})} | custom-call | flops 536870912 | bytes 6881280 | tf_op jit(solution)/shard_map/channel/pallas_call | solution.py:246
  52.4 2.5 %channel.6 = (f32[512,1024]{1,0:T(8,128)S(1)}, f32[8,8,128]{2,1,0:T(8,128)S(1)}) custom-call(s32[1]{0:T(128)} %bitcast.refs_0_, s32[72,1024]{1,0:T(8,128)S(1)} %collective-permute-done.2.refs_1_, s32[72,1024]{1,0:T(8,128)} %collective-permute-done.6.refs_2_, ...), custom_call_target="tpu_custom_call", output_to_operand_aliasing={{0}: (5, {}), {1}: (6, {})} | custom-call | flops 536870912 | bytes 6881280 | tf_op jit(solution)/shard_map/channel/pallas_call | solution.py:246
  54.9 0.0 collective-permute-done.3.refs_1_
  54.9 0.0 collective-permute-done.7.refs_2_
  54.9 2.4 %channel.7 = (f32[32,16,512]{2,1,0:T(8,128)S(1)}, bf16[32,16,512]{2,1,0:T(8,128)(2,1)S(1)}, f32[8,8,128]{2,1,0:T(8,128)S(1)}) custom-call(s32[1]{0:T(128)} %bitcast.refs_0_, s32[72,1024]{1,0:T(8,128)S(1)} %collective-permute-done.3.refs_1_, s32[72,1024]{1,0:T(8,128)} %collective-permute-done.7.refs_2_, s32[72,1024]{1,0:T(8,128)S(1)} %copy-done.2, ...), custom_call_target="tpu_custom_call" | custom-call | flops 536870912 | bytes 6881280 | tf_op jit(solution)/shard_map/channel/pallas_call | solution.py:246
  57.3 0.0 copy-start
  57.4 0.0 copy-start.7
  57.4 3.3 %collective-permute-start.8 = (bf16[32,16,512]{2,1,0:T(8,128)(2,1)S(1)}, bf16[32,16,512]{2,1,0:T(8,128)(2,1)S(1)}, u32[]{:S(2)}, u32[]{:S(2)}) collective-permute-start(bf16[32,16,512]{2,1,0:T(8,128)(2,1)S(1)} %get-tuple-element.39), channel_id=1, source_target_pairs={{0,1},{1,0},{2,3},{3,2},{4,5},{5,4},{6,7},{7,6},{8,9},{9,8},{10,11... | collective-permute-start | bytes 1572872 | tf_op jit(solution)/shard_map/ppermute | solution.py:354
  60.7 1.5 %collective-permute-done.8 = bf16[32,16,512]{2,1,0:T(8,128)(2,1)S(1)} collective-permute-done((bf16[32,16,512]{2,1,0:T(8,128)(2,1)S(1)}, bf16[32,16,512]{2,1,0:T(8,128)(2,1)S(1)}, u32[]{:S(2)}, u32[]{:S(2)}) %collective-permute-start.8) | collective-permute-done | bytes 524320 | tf_op jit(solution)/shard_map/ppermute | solution.py:354
  62.2 1.0 add_convert_fusion
  63.2 8.4 %all-to-all-start.1 = ((bf16[32,16,512]{2,1,0:T(8,128)(2,1)}), bf16[32,16,512]{2,1,0:T(8,128)(2,1)S(1)}, u32[]{:S(2)}, u32[]{:S(2)}) async-start(bf16[32,16,512]{2,1,0:T(8,128)(2,1)} %add_convert_fusion), calls=%async_computation.1 | async-start | bytes 1048576 | tf_op jit(solution)/shard_map/all_to_all | solution.py:355
  71.6 0.0 copy-done
  71.6 0.0 copy-done.7
  71.6 0.0 copy-start.1
  71.6 1.0 copy-done.1
  72.7 0.9 dense.1
  73.6 14.6 %all-to-all-done.1.got_ref = bf16[32,16,512]{2,1,0:T(8,128)(2,1)S(1)} async-done(((bf16[32,16,512]{2,1,0:T(8,128)(2,1)}), bf16[32,16,512]{2,1,0:T(8,128)(2,1)S(1)}, u32[]{:S(2)}, u32[]{:S(2)}) %all-to-all-start.1) | async-done | bytes 524320 | tf_op jit(solution)/shard_map/all_to_all | solution.py:355
  88.2 0.0 copy-done.5
  88.2 0.4 token_.1
  88.6 0.1 add_reduce_fusion
  88.8 0.6 broadcast_in_dim.2
  89.4 6.9 %all-to-all-start.2 = ((f32[64,1,8]{2,1,0:T(1,128)}), f32[64,1,8]{2,1,0:T(1,128)S(1)}, u32[]{:S(2)}, u32[]{:S(2)}) async-start(f32[64,1,8]{2,1,0:T(1,128)} %broadcast_in_dim.2), calls=%async_computation.2 | async-start | bytes 65536 | tf_op jit(solution)/shard_map/all_to_all | solution.py:358
  96.3 1.0 back.1
  97.3 8.4 %all-to-all-done.2 = f32[64,1,8]{2,1,0:T(1,128)S(1)} async-done(((f32[64,1,8]{2,1,0:T(1,128)}), f32[64,1,8]{2,1,0:T(1,128)S(1)}, u32[]{:S(2)}, u32[]{:S(2)}) %all-to-all-start.2) | async-done | bytes 2080 | tf_op jit(solution)/shard_map/all_to_all | solution.py:358
  105.7 0.6 reduce_sum.19
  (8 shorter events, 0.0 us)
Async XLA Ops:
  0.6 11.1 %copy-start.8 = (bf16[16,8,1024]{2,1,0:T(8,128)(2,1)S(1)}, bf16[16,8,1024]{2,1,0:T(8,128)(2,1)}, u32[]{:S(2)}) copy-start(bf16[16,8,1024]{2,1,0:T(8,128)(2,1)} %param.12) | copy-start | bytes 786436
  2.8 12.3 %collective-permute-start = (s32[72,1024]{1,0:T(8,128)}, s32[72,1024]{1,0:T(8,128)S(1)}, u32[]{:S(2)}, u32[]{:S(2)}) collective-permute-start(s32[72,1024]{1,0:T(8,128)} %get-tuple-element.24.refs_3_), channel_id=1, source_target_pairs={{0,64},{64,128},{128,192},{192,256},{256,320},{320,384},{384,448},... | collective-permute-start | bytes 884744 | tf_op jit(solution)/shard_map/ppermute | solution.py:334
  8.8 8.0 %collective-permute-start.4 = (s32[72,1024]{1,0:T(8,128)}, s32[72,1024]{1,0:T(8,128)S(1)}, u32[]{:S(2)}, u32[]{:S(2)}) collective-permute-start(s32[72,1024]{1,0:T(8,128)} %get-tuple-element.25.refs_4_), channel_id=1, source_target_pairs={{0,64},{64,128},{128,192},{192,256},{256,320},{320,384},{384,448},... | collective-permute-start | bytes 884744 | tf_op jit(solution)/shard_map/ppermute | solution.py:334
  15.1 34.3 %copy-start.6 = (f32[1024]{0:T(1024)S(1)}, f32[1024]{0:T(1024)}, u32[]{:S(2)}) copy-start(f32[1024]{0:T(1024)} %param.14) | copy-start | bytes 12292
  16.8 32.7 %all-to-all-start = ((bf16[4,96,16,128]{3,2,1,0:T(8,128)(2,1)}), bf16[4,96,16,128]{3,2,1,0:T(8,128)(2,1)S(1)}, u32[]{:S(2)}, u32[]{:S(2)}) async-start(bf16[4,96,16,128]{3,2,1,0:T(8,128)(2,1)} %share.1), calls=%async_computation | async-start | bytes 3145728 | tf_op jit(solution)/shard_map/all_to_all | solution.py:341
  26.5 7.8 %collective-permute-start.1 = (s32[72,1024]{1,0:T(8,128)S(1)}, s32[72,1024]{1,0:T(8,128)S(1)}, u32[]{:S(2)}, u32[]{:S(2)}) collective-permute-start(s32[72,1024]{1,0:T(8,128)S(1)} %collective-permute-done.refs_1_), channel_id=1, source_target_pairs={{0,64},{64,128},{128,192},{192,256},{256,320},{320,384},{384,448},... | collective-permute-start | bytes 884744 | tf_op jit(solution)/shard_map/ppermute | solution.py:334
  28.9 8.7 %collective-permute-start.5 = (s32[72,1024]{1,0:T(8,128)S(1)}, s32[72,1024]{1,0:T(8,128)S(1)}, u32[]{:S(2)}, u32[]{:S(2)}) collective-permute-start(s32[72,1024]{1,0:T(8,128)S(1)} %collective-permute-done.4.refs_2_), channel_id=1, source_target_pairs={{0,64},{64,128},{128,192},{192,256},{256,320},{320,384},{384,448},... | collective-permute-start | bytes 884744 | tf_op jit(solution)/shard_map/ppermute | solution.py:334
  34.2 7.8 %collective-permute-start.2 = (s32[72,1024]{1,0:T(8,128)S(1)}, s32[72,1024]{1,0:T(8,128)S(1)}, u32[]{:S(2)}, u32[]{:S(2)}) collective-permute-start(s32[72,1024]{1,0:T(8,128)S(1)} %collective-permute-done.1.refs_1_), channel_id=1, source_target_pairs={{0,64},{64,128},{128,192},{192,256},{256,320},{320,384},{384,448},... | collective-permute-start | bytes 884744 | tf_op jit(solution)/shard_map/ppermute | solution.py:334
  37.5 7.8 %collective-permute-start.6 = (s32[72,1024]{1,0:T(8,128)S(1)}, s32[72,1024]{1,0:T(8,128)}, u32[]{:S(2)}, u32[]{:S(2)}) collective-permute-start(s32[72,1024]{1,0:T(8,128)S(1)} %collective-permute-done.5.refs_2_), channel_id=1, source_target_pairs={{0,64},{64,128},{128,192},{192,256},{256,320},{320,384},{384,448},... | collective-permute-start | bytes 884744 | tf_op jit(solution)/shard_map/ppermute | solution.py:334
  42.0 12.9 %collective-permute-start.3 = (s32[72,1024]{1,0:T(8,128)S(1)}, s32[72,1024]{1,0:T(8,128)S(1)}, u32[]{:S(2)}, u32[]{:S(2)}) collective-permute-start(s32[72,1024]{1,0:T(8,128)S(1)} %collective-permute-done.2.refs_1_), channel_id=1, source_target_pairs={{0,64},{64,128},{128,192},{192,256},{256,320},{320,384},{384,448},... | collective-permute-start | bytes 884744 | tf_op jit(solution)/shard_map/ppermute | solution.py:334
  45.3 9.6 %collective-permute-start.7 = (s32[72,1024]{1,0:T(8,128)}, s32[72,1024]{1,0:T(8,128)}, u32[]{:S(2)}, u32[]{:S(2)}) collective-permute-start(s32[72,1024]{1,0:T(8,128)} %collective-permute-done.6.refs_2_), channel_id=1, source_target_pairs={{1,449},{65,1},{129,65},{193,129},{257,193},{321,257},{385,321},{4... | collective-permute-start | bytes 884744 | tf_op jit(solution)/shard_map/ppermute | solution.py:334
  52.4 2.5 %copy-start.2 = (s32[72,1024]{1,0:T(8,128)S(1)}, s32[72,1024]{1,0:T(8,128)}, u32[]{:S(2)}) copy-start(s32[72,1024]{1,0:T(8,128)} %get-tuple-element.24.refs_3_) | copy-start | bytes 884740
  52.4 2.5 %copy-start.3 = (s32[72,1024]{1,0:T(8,128)S(1)}, s32[72,1024]{1,0:T(8,128)}, u32[]{:S(2)}) copy-start(s32[72,1024]{1,0:T(8,128)} %get-tuple-element.25.refs_4_) | copy-start | bytes 884740
  57.3 14.3 %copy-start = (bf16[16,128,128]{2,1,0:T(8,128)(2,1)S(1)}, bf16[16,128,128]{2,1,0:T(8,128)(2,1)}, u32[]{:S(2)}) copy-start(bf16[16,128,128]{2,1,0:T(8,128)(2,1)} %in_ref.1) | copy-start | bytes 1572868
  57.4 14.3 %copy-start.7 = (s32[16]{0:T(128)S(1)}, s32[16]{0:T(128)}, u32[]{:S(2)}) copy-start(s32[16]{0:T(128)} %cells_ref.1) | copy-start | bytes 196
  57.4 4.9 %collective-permute-start.8 = (bf16[32,16,512]{2,1,0:T(8,128)(2,1)S(1)}, bf16[32,16,512]{2,1,0:T(8,128)(2,1)S(1)}, u32[]{:S(2)}, u32[]{:S(2)}) collective-permute-start(bf16[32,16,512]{2,1,0:T(8,128)(2,1)S(1)} %get-tuple-element.39), channel_id=1, source_target_pairs={{0,1},{1,0},{2,3},{3,2},{4,5},{5,4},{6,7},{7,6},{8,9},{9,8},{10,11... | collective-permute-start | bytes 1572872 | tf_op jit(solution)/shard_map/ppermute | solution.py:354
  62.2 26.0 %copy-start.4 = (bf16[2,512,1,16]{1,3,2,0:T(8,128)(2,1)S(1)}, bf16[2,512,1,16]{1,3,2,0:T(8,128)(2,1)}, u32[]{:S(2)}) copy-start(bf16[2,512,1,16]{1,3,2,0:T(8,128)(2,1)} %param.22) | copy-start | bytes 98308
  62.2 26.0 %copy-start.5 = (bf16[2,512,1,16]{1,3,2,0:T(8,128)(2,1)S(1)}, bf16[2,512,1,16]{1,3,2,0:T(8,128)(2,1)}, u32[]{:S(2)}) copy-start(bf16[2,512,1,16]{1,3,2,0:T(8,128)(2,1)} %param.23) | copy-start | bytes 98308
  63.2 24.9 %all-to-all-start.1 = ((bf16[32,16,512]{2,1,0:T(8,128)(2,1)}), bf16[32,16,512]{2,1,0:T(8,128)(2,1)S(1)}, u32[]{:S(2)}, u32[]{:S(2)}) async-start(bf16[32,16,512]{2,1,0:T(8,128)(2,1)} %add_convert_fusion), calls=%async_computation.1 | async-start | bytes 1048576 | tf_op jit(solution)/shard_map/all_to_all | solution.py:355
  71.6 1.0 copy-start.1
  89.4 16.3 %all-to-all-start.2 = ((f32[64,1,8]{2,1,0:T(1,128)}), f32[64,1,8]{2,1,0:T(1,128)S(1)}, u32[]{:S(2)}, u32[]{:S(2)}) async-start(f32[64,1,8]{2,1,0:T(1,128)} %broadcast_in_dim.2), calls=%async_computation.2 | async-start | bytes 65536 | tf_op jit(solution)/shard_map/all_to_all | solution.py:358

commit v8 on v7

--- a/solution.py
+++ b/solution.py
@@ -20,15 +20,16 @@
 F32 = jnp.float32
 BF16 = jnp.bfloat16
 I32 = jnp.int32
-MP = ("z", "xh", "xl", "core")
-TEAM = ("xl", "core")
+MP = ("z", "x", "core")
 SWAP = [(0, 1), (1, 0)]
 VMEM = 32 * 1024 * 1024
 
-PART = 256
+PART = 512
+CHUNK = 256
 STEPS = 4
-SHARED = 64
+SHARED = 32
 ROWS_DEV = SPEC * SHARED
+PACKED = 136
 LAM_TILES = SPEC * (D // 128)
 SCALE_ONE = float(2**38)
 
@@ -43,50 +44,43 @@
     return (shifted >> 24).astype(F32).astype(BF16)
 
 
-def pack_kernel(half_ref, down_hbm, up_hbm, scale_hbm, *refs):
-    out_refs, (down_ref, up_ref, scale_ref, sems) = refs[:2], refs[2:]
-    start = pl.multiple_of(half_ref[0] * PART, PART)
+def pack_kernel(start, down_hbm, up_hbm, scale_hbm, out_ref, down_ref, up_ref, scale_ref, sems):
+    cut = pl.ds(start, CHUNK)
     copies = [
-        pltpu.make_async_copy(down_hbm.at[:, pl.ds(start, PART)], down_ref, sems.at[0]),
-        pltpu.make_async_copy(up_hbm.at[pl.ds(start, PART), :], up_ref, sems.at[1]),
-        pltpu.make_async_copy(scale_hbm.at[:, pl.ds(start, PART)], scale_ref, sems.at[2]),
+        pltpu.make_async_copy(down_hbm.at[:, cut], down_ref, sems.at[0]),
+        pltpu.make_async_copy(up_hbm.at[cut, :], up_ref, sems.at[1]),
+        pltpu.make_async_copy(scale_hbm.at[:, cut], scale_ref, sems.at[2]),
     ]
     for copy in copies:
         copy.start()
-    for out_ref in out_refs:
-        out_ref[64:72, :] = jnp.zeros((8, D), I32)
+    out_ref[128:136, :] = jnp.zeros((8, D), I32)
     copies[0].wait()
     down = pack_codes([down_ref[m * 256 : (m + 1) * 256, :] for m in range(4)])
-    for h, out_ref in enumerate(out_refs):
-        for k in range(8):
-            cut = slice(k * 128, (k + 1) * 128)
-            out_ref[0:32, cut] = down[k * 32 : (k + 1) * 32, h * 128 : (h + 1) * 128]
+    for k in range(4):
+        out_ref[0:64, k * CHUNK : (k + 1) * CHUNK] = down[k * 64 : (k + 1) * 64, :]
     copies[1].wait()
+    out_ref[64:128, :] = pack_codes([up_ref[m * 64 : (m + 1) * 64, :] for m in range(4)])
     copies[2].wait()
     scale = (scale_ref[...] * SCALE_ONE).astype(I32)
-    for h, out_ref in enumerate(out_refs):
-        rows = [h * 128 + m * 32 for m in range(4)]
-        out_ref[32:64, :] = pack_codes([up_ref[i : i + 32, :] for i in rows])
-        out_ref[64:72, 0:128] = jnp.broadcast_to(scale[:, h * 128 : (h + 1) * 128], (8, 128))
-
-
-def pack(half, q_down, q_up, up_scale):
-    smem, hbm = pl.BlockSpec(memory_space=pltpu.SMEM), pl.BlockSpec(memory_space=pltpu.HBM)
-    vmem = pl.BlockSpec(memory_space=pltpu.VMEM)
-    return pl.pallas_call(
-        pack_kernel,
-        out_shape=(jax.ShapeDtypeStruct((72, D), I32),) * 2,
-        in_specs=[smem, hbm, hbm, hbm],
-        out_specs=(vmem, vmem),
+    out_ref[128:136, 0:CHUNK] = jnp.broadcast_to(scale, (8, CHUNK))
+
+
+def pack(chunk, q_down, q_up, up_scale):
+    hbm, vmem = pl.BlockSpec(memory_space=pltpu.HBM), pl.BlockSpec(memory_space=pltpu.VMEM)
+    return pl.pallas_call(
+        functools.partial(pack_kernel, chunk * CHUNK),
+        out_shape=jax.ShapeDtypeStruct((PACKED, D), I32),
+        in_specs=[hbm, hbm, hbm],
+        out_specs=vmem,
         scratch_shapes=[
-            pltpu.VMEM((D, PART), BF16),
-            pltpu.VMEM((PART, D), BF16),
-            pltpu.VMEM((1, PART), F32),
+            pltpu.VMEM((D, CHUNK), BF16),
+            pltpu.VMEM((CHUNK, D), BF16),
+            pltpu.VMEM((1, CHUNK), F32),
             pltpu.SemaphoreType.DMA((3,)),
         ],
         compiler_params=pltpu.CompilerParams(vmem_limit_bytes=60 * 1024 * 1024),
         name="pack",
-    )(half, q_down, q_up, up_scale.reshape(1, -1))
+    )(q_down, q_up, up_scale.reshape(1, -1))
 
 
 def dense_kernel(cells_ref, in_ref, out_ref, dense_in_ref, dense_out_ref):
@@ -127,58 +121,62 @@
     return mid, pos * icpt_low.astype(F32) + neg * icpt_high.astype(F32)
 
 
-def share_kernel(row_ref, lam_ref, slopes_ref, icpt_ref, out_ref):
+def share_kernel(place_ref, lam_ref, slopes_ref, icpt_ref, *out_refs):
     for r in range(SPEC):
         for k in range(D // 128):
             tile = lam_ref[r, :, k * 128 : (k + 1) * 128]
-            for to in range(4):
-                out_ref[to, r * (D // 128) + k] = tile
-    row = row_ref[0]
-    for to in range(4):
-        half, core = to // 2, to % 2
+            for out_ref in out_refs:
+                out_ref[r * (D // 128) + k] = tile
+    row = place_ref[1]
+    for k, out_ref in enumerate(out_refs):
+        core = place_ref[0] ^ k
         for j in range(STEPS):
             if j < STEPS - 1:
-                owner = row + (j + 1) if core else row - (j + 1)
+                owner = row + (2 * core - 1) * (j + 1)
                 cuts = [(owner, 0), (owner, 1)]
             else:
                 cuts = [(row + STEPS, core), (row, core)]
             for h, (owner, chunk) in enumerate(cuts):
-                start = pl.multiple_of((owner & 7) * TH + half * PART + chunk * 128, 128)
+                start = pl.multiple_of((owner & 7) * PART + chunk * CHUNK, CHUNK)
                 for kind in range(4):
                     ref = slopes_ref if kind < 2 else icpt_ref
-                    values = ref[kind % 2, :, pl.ds(start, 128)]
-                    out_ref[to, LAM_TILES + (j * 4 + kind) * 2 + h] = values
-
-
-def share(row, by_row, slopes, icpt):
-    tiles = LAM_TILES + 4 * STEPS * 2
+                    values = ref[kind % 2, :, pl.ds(start, CHUNK)]
+                    tile = LAM_TILES + (j * 4 + kind) * 4 + h * 2
+                    out_ref[tile] = values[:, 0:128]
+                    out_ref[tile + 1] = values[:, 128:256]
+
+
+def share(place, by_row, slopes, icpt):
+    tiles = LAM_TILES + 4 * STEPS * 4
     return pl.pallas_call(
         share_kernel,
-        out_shape=jax.ShapeDtypeStruct((4, tiles, 16, 128), BF16),
+        out_shape=(jax.ShapeDtypeStruct((tiles, 16, 128), BF16),) * 2,
         in_specs=[pl.BlockSpec(memory_space=pltpu.SMEM)]
         + [pl.BlockSpec(memory_space=pltpu.VMEM)] * 3,
         compiler_params=pltpu.CompilerParams(vmem_limit_bytes=60 * 1024 * 1024),
         name="share",
-    )(row, by_row, slopes, icpt)
+    )(place, by_row, slopes, icpt)
 
 
 def channel_kernel(step, *refs):
     first, last = step == 0, step == STEPS - 1
     core_ref, *words, refs = refs[0], refs[1], refs[2], refs[3:]
     if first:
-        down_scale_ref, got_ref, acc_ref, bias_ref, scaled_ref, bounds_ref, down, up = refs
-        for q in range(4):
+        down_scale_ref, *team, acc_ref, bias_ref, scaled_ref, bounds_ref, down, up = refs
+        for k, got_ref in enumerate(team):
+            start = (core_ref[0] ^ k) * 16
             for r in range(SPEC):
-                rows = slice(r * SHARED + q * 16, r * SHARED + (q + 1) * 16)
+                rows = pl.ds(pl.multiple_of(r * SHARED + start, 16), 16)
                 for c in range(D // 128):
                     cut = slice(c * 128, (c + 1) * 128)
-                    lam = got_ref[q, r * (D // 128) + c].astype(F32)
+                    lam = got_ref[r * (D // 128) + c].astype(F32)
                     scaled_ref[rows, cut] = (lam * down_scale_ref[:, cut]).astype(BF16)
-                    acc_ref[rows, cut] = 0.25 * lam
+                    acc_ref[rows, cut] = 0.5 * lam
+            rows = pl.ds(pl.multiple_of(start, 16), 16)
             for i in range(STEPS * 4):
-                for h in range(2):
-                    tile = got_ref[q, LAM_TILES + i * 2 + h]
-                    bounds_ref[i // 4, i % 4, q * 16 : (q + 1) * 16, h * 128 : (h + 1) * 128] = tile
+                for h in range(4):
+                    tile = got_ref[LAM_TILES + i * 4 + h]
+                    bounds_ref[i // 4, i % 4, rows, h * 128 : (h + 1) * 128] = tile
         acc_in, bias_in = acc_ref, None
     else:
         if last:
@@ -193,19 +191,20 @@
         ]
     for h, chunk in enumerate(words):
         for m in range(4):
-            codes = unpack_codes(chunk[0:32], m)
-            for q in range(8):
-                rows = m * 256 + q * 32
-                down[rows : rows + 32, h * 128 : (h + 1) * 128] = codes[:, q * 128 : (q + 1) * 128]
-            rows = h * 128 + m * 32
-            up[rows : rows + 32, :] = unpack_codes(chunk[32:64], m)
-    scale = jnp.concatenate([chunk[64:65, 0:128] for chunk in words], axis=1)
+            codes = unpack_codes(chunk[0:64], m)
+            for q in range(4):
+                rows = m * 256 + q * 64
+                cut = slice(q * CHUNK, (q + 1) * CHUNK)
+                down[rows : rows + 64, h * CHUNK : (h + 1) * CHUNK] = codes[:, cut]
+            rows = h * CHUNK + m * 64
+            up[rows : rows + 64, :] = unpack_codes(chunk[64:128], m)
+    scale = jnp.concatenate([chunk[128:129, 0:CHUNK] for chunk in words], axis=1)
     scale = scale.astype(F32) * (1.0 / SCALE_ONE)
     pre = jnp.dot(scaled_ref[...], down[...], preferred_element_type=F32)
     pre = pre.reshape(SPEC, SHARED, PART)
     mid, terms = relaxed(pre, *(bounds_ref[step, kind] for kind in range(4)))
     terms = jnp.sum(terms.reshape(SPEC, SHARED // 8, 8, PART), axis=1)
-    bias = terms[:, :, 0:128] + terms[:, :, 128:256]
+    bias = sum(terms[:, :, k * 128 : (k + 1) * 128] for k in range(PART // 128))
     weighted = (mid.reshape(ROWS_DEV, PART) * scale).astype(BF16)
     part = jnp.dot(weighted, up[...], preferred_element_type=F32)
     total = acc_in[...] + part
@@ -253,7 +252,7 @@
         compiler_params=pltpu.CompilerParams(vmem_limit_bytes=VMEM),
         cost_estimate=pl.CostEstimate(
             flops=4 * ROWS_DEV * PART * D,
-            bytes_accessed=144 * D * 4 + 3 * ROWS_DEV * D * 4,
+            bytes_accessed=2 * PACKED * D * 4 + 3 * ROWS_DEV * D * 4,
             transcendentals=0,
         ),
         name="channel",
@@ -261,18 +260,22 @@
 
 
 def token_kernel(got_ref, dense_ref, slopes_ref, icpt_ref, columns_ref, mid_ref, bias_ref):
-    low = lax.broadcasted_iota(I32, (16, 128), 1) < SHARED
+    lane = lax.broadcasted_iota(I32, (16, 128), 1) // 32
     for u in range(NTB):
-        for a in range(SPEC // 2):
-            cut = slice(a * 128, (a + 1) * 128)
-            v = [
-                got_ref[s, :, cut].astype(F32) + got_ref[s + 1, :, cut].astype(F32)
-                for s in (4 * u, 4 * u + 2)
-            ]
-            even = jnp.where(low, v[0], pltpu.roll(v[1], SHARED, 1))
-            odd = jnp.where(low, pltpu.roll(v[0], SHARED, 1), v[1])
-            for r, value in ((2 * a, even), (2 * a + 1, odd)):
-                columns_ref[r * 16 : (r + 1) * 16, u * 128 : (u + 1) * 128] = value.astype(BF16)
+        for a in range(2):
+            v = [got_ref[4 * u + p, :, a * 128 : (a + 1) * 128].astype(F32) for p in range(4)]
+            for bit in (1, 2):
+                low = (lane & bit) == 0
+                new = list(v)
+                for p in range(4):
+                    if p & bit == 0:
+                        q = p + bit
+                        new[p] = jnp.where(low, v[p], pltpu.roll(v[q], 32 * bit, 1))
+                        new[q] = jnp.where(low, pltpu.roll(v[p], 128 - 32 * bit, 1), v[q])
+                v = new
+            for q in range(4):
+                r = 4 * a + q
+                columns_ref[r * 16 : (r + 1) * 16, u * 128 : (u + 1) * 128] = v[q].astype(BF16)
     pre = jnp.dot(columns_ref[...], dense_ref[...], preferred_element_type=F32)
     pre = pre.reshape(SPEC, 16, TH)
     mid, terms = relaxed(pre, slopes_ref[0], slopes_ref[1], icpt_ref[0], icpt_ref[1])
@@ -322,9 +325,8 @@
     tok_slopes,
     tok_icpt,
 ):
-    row = lax.axis_index("rows").astype(I32).reshape(1)
-    core = lax.axis_index("core").astype(I32).reshape(1)
-    half = lax.axis_index("xl").astype(I32).reshape(1)
+    core, row = lax.axis_index("core").astype(I32), lax.axis_index("rows").astype(I32)
+    place, core = jnp.stack([core, row]), core.reshape(1)
     tok_dev = lam_out.shape[0]
     slices = lax.axis_size("rows")
     ahead = [(i * 2, (i + 1) % slices * 2) for i in range(slices)]
@@ -333,12 +335,13 @@
     def forward(words, pairs):
         return tuple(lax.ppermute(w, ("rows", "core"), pairs) for w in words)
 
-    own = pack(half, q_down, q_up, up_scale)
+    own = tuple(pack(chunk, q_down, q_up, up_scale) for chunk in range(2))
     first = forward(own, ahead + behind)
     _, lam, *bounds = lax.optimization_barrier((own, lam_out, chan_slopes, chan_icpt))
-    blocks = share(row, jnp.swapaxes(lam, 0, 1), *(b.reshape(2, tok_dev, CH) for b in bounds))
-    _, blocks = lax.optimization_barrier((first, blocks))
-    team = lax.all_to_all(blocks, TEAM, 0, 0, tiled=True)
+    keep_part, send_part = share(
+        place, jnp.swapaxes(lam, 0, 1), *(b.reshape(2, tok_dev, CH) for b in bounds)
+    )
+    team = (keep_part, lax.ppermute(send_part, "core", SWAP))
     second = forward(first, ahead + behind)
     third = forward(second, ahead + behind)
     far = forward(third[:1], ahead) + forward(third[1:], behind)
@@ -347,12 +350,12 @@
     slopes = jnp.transpose(tok_slopes, (0, 2, 3, 1)).reshape(2, 16, TH)
     icpt = jnp.transpose(tok_icpt, (0, 2, 3, 1)).reshape(2, 16, TH)
 
-    acc, chan_bias, *given = channel_part(0, core, *first, down_scale.reshape(1, D), team)
+    acc, chan_bias, *given = channel_part(0, core, *first, down_scale.reshape(1, D), *team)
     acc, chan_bias = channel_part(1, core, *second, *given, acc, chan_bias)
     acc, chan_bias = channel_part(2, core, *third, *given, acc, chan_bias)
     keep, send, chan_bias = channel_part(3, core, *far, *own, *given, acc, chan_bias)
     summed = (keep + lax.ppermute(send, "core", SWAP).astype(F32)).astype(BF16)
-    got = lax.all_to_all(summed, ("z", "xh", "xl"), 0, 0, tiled=True)
+    got = lax.all_to_all(summed, ("z", "x"), 0, 0, tiled=True)
     columns, mid, tok_bias = token_mlp(got, dense_out, slopes, icpt)
     own_bias = jnp.sum(chan_bias + tok_bias, axis=(1, 2))
     all_bias = lax.all_to_all(
@@ -364,7 +367,7 @@
 
 
 def solution(mesh):
-    axes = Mesh(mesh.devices.reshape(8, 8, 2, 2, 2), ("rows",) + MP)
+    axes = Mesh(mesh.devices.reshape(8, 8, 4, 2), ("rows",) + MP)
     return jax.shard_map(
         on_device,
         mesh=axes,

time: 107 us -> 106 us (level)
  waiting for transfers between devices: 33.4 us -> 27.9 us
  starting transfers between devices: 52.8 us -> 57.8 us
  Pallas kernels: 14.8 us -> 13.6 us
    all_to_all x2 -> x1, starting transfers between devices: 18.1 us -> 8.81 us  [on_device(): got = lax.all_to_all(summed, ('z', 'x'), 0, 0, tiled=True)]
    ppermute x8, starting transfers between devices: 24.5 us -> 33.3 us  [forward(): return tuple((lax.ppermute(w, ('rows', 'core'), pairs) for w in words))]
    ppermute x0 -> x1, starting transfers between devices: none -> 6.74 us  [on_device(): team = (keep_part, lax.ppermute(send_part, 'core', SWAP))]
    all_to_all x2 -> x1, waiting for transfers between devices: 14.6 us -> 10.6 us  [on_device(): got = lax.all_to_all(summed, ('z', 'x'), 0, 0, tiled=True)]
    pallas_call x4, Pallas kernels: 7.77 us -> 4.39 us  [channel_part(): pl.pallas_call(functools.partial(channel_kernel, step), out_shape=out_sha...]
    pallas_call x2 -> x3, Pallas kernels: 4.71 us -> 6.72 us  [the longest x2 4.5 us: pack(): pl.pallas_call(functools.partial(pack_kernel, chunk * CHUNK), out_shape=j...]
    ppermute x8, waiting for transfers between devices: 8.97 us -> 7.68 us  [forward(): return tuple((lax.ppermute(w, ('rows', 'core'), pairs) for w in words))]
  transfers between devices with their start and end apart: 12 -> 12, of which waited for: 7 -> 8; matrix products, arithmetic and copies ran while one was open for 1% -> 1% of each run, Pallas kernels for 9% -> 9%
where the time goes in v8:
time: 106 us; the launch traced here: 105 us
  starting transfers between devices  57.8 us (55%)
  waiting for transfers between devices  27.9 us (26%)
  Pallas kernels  13.6 us (13%)
  local copies, waits for them, and re-layouts  2.55 us (2%)
  other arithmetic  2.11 us (2%)
    ppermute x8, starting transfers between devices, forward(): return tuple((lax.ppermute(w, ('rows', 'core'), pairs) for w in words))  33.3 us
    all_to_all x1, waiting for transfers between devices, on_device(): got = lax.all_to_all(summed, ('z', 'x'), 0, 0, tiled=True)  10.6 us
    all_to_all x1, starting transfers between devices, on_device(): got = lax.all_to_all(summed, ('z', 'x'), 0, 0, tiled=True)  8.81 us
    all_to_all x1, waiting for transfers between devices, on_device(): lax.all_to_all(jnp.broadcast_to(own_bias[None, :], (64, SPEC)), MP, 0, 0,...  8.46 us
    ppermute x8, waiting for transfers between devices, forward(): return tuple((lax.ppermute(w, ('rows', 'core'), pairs) for w in words))  7.68 us
    ppermute x1, starting transfers between devices, on_device(): team = (keep_part, lax.ppermute(send_part, 'core', SWAP))  6.74 us
    all_to_all x1, starting transfers between devices, on_device(): lax.all_to_all(jnp.broadcast_to(own_bias[None, :], (64, SPEC)), MP, 0, 0,...  6.36 us
    pallas_call x2, Pallas kernels, pack(): pl.pallas_call(functools.partial(pack_kernel, chunk * CHUNK), out_shape=j...  4.5 us
  transfers between devices with their start and end apart: 12, of which 8 were waited for; matrix products, arithmetic and copies ran while one was open for 1% of the time, Pallas kernels for 9%

profile of v8, /device:TPU:1, one launch (start us, length us, event | category | flops | bytes accessed | tf_op | source)
XLA Modules:
  0.0 104.9 jit_solution(4070346787139748251)
XLA Ops:
  0.6 2.2 %pack.2.refs_3_ = s32[136,1024]{1,0:T(8,128)} custom-call(bf16[1024,512]{1,0:T(8,128)(2,1)} %down_hbm.3, bf16[512,1024]{1,0:T(8,128)(2,1)} %up_hbm.3, f32[1,512]{1,0:T(1,128)} %bitcast.29), custom_call_target="tpu_custom_call" | custom-call | tf_op jit(solution)/shard_map/pack/pallas_call | solution.py:70
  2.9 0.0 copy-start.9
  2.9 6.1 %collective-permute-start = (s32[136,1024]{1,0:T(8,128)}, s32[136,1024]{1,0:T(8,128)S(1)}, u32[]{:S(2)}, u32[]{:S(2)}) collective-permute-start(s32[136,1024]{1,0:T(8,128)} %pack.2.refs_3_), channel_id=1, source_target_pairs={{0,64},{64,128},{128,192},{192,256},{256,320},{320,384},{384,448},... | collective-permute-start | bytes 1671176 | tf_op jit(solution)/shard_map/ppermute | solution.py:336
  9.0 2.3 %pack.3.refs_4_ = s32[136,1024]{1,0:T(8,128)} custom-call(bf16[1024,512]{1,0:T(8,128)(2,1)} %down_hbm.3, bf16[512,1024]{1,0:T(8,128)(2,1)} %up_hbm.3, f32[1,512]{1,0:T(1,128)} %bitcast.30), custom_call_target="tpu_custom_call" | custom-call | tf_op jit(solution)/shard_map/pack/pallas_call | solution.py:70
  11.2 3.0 %collective-permute-start.4 = (s32[136,1024]{1,0:T(8,128)}, s32[136,1024]{1,0:T(8,128)S(1)}, u32[]{:S(2)}, u32[]{:S(2)}) collective-permute-start(s32[136,1024]{1,0:T(8,128)} %pack.3.refs_4_), channel_id=1, source_target_pairs={{0,64},{64,128},{128,192},{192,256},{256,320},{320,384},{384,448},... | collective-permute-start | bytes 1671176 | tf_op jit(solution)/shard_map/ppermute | solution.py:336
  14.2 1.5 %collective-permute-done.refs_1_ = s32[136,1024]{1,0:T(8,128)S(1)} collective-permute-done((s32[136,1024]{1,0:T(8,128)}, s32[136,1024]{1,0:T(8,128)S(1)}, u32[]{:S(2)}, u32[]{:S(2)}) %collective-permute-start) | collective-permute-done | bytes 557088 | tf_op jit(solution)/shard_map/ppermute | solution.py:336
  15.7 4.9 %collective-permute-start.1 = (s32[136,1024]{1,0:T(8,128)S(1)}, s32[136,1024]{1,0:T(8,128)S(1)}, u32[]{:S(2)}, u32[]{:S(2)}) collective-permute-start(s32[136,1024]{1,0:T(8,128)S(1)} %collective-permute-done.refs_1_), channel_id=1, source_target_pairs={{0,64},{64,128},{128,192},{192,256},{256,320},{320,384},{384,448},... | collective-permute-start | bytes 1671176 | tf_op jit(solution)/shard_map/ppermute | solution.py:336
  20.6 1.4 %collective-permute-done.4.refs_2_ = s32[136,1024]{1,0:T(8,128)S(1)} collective-permute-done((s32[136,1024]{1,0:T(8,128)}, s32[136,1024]{1,0:T(8,128)S(1)}, u32[]{:S(2)}, u32[]{:S(2)}) %collective-permute-start.4) | collective-permute-done | bytes 557088 | tf_op jit(solution)/shard_map/ppermute | solution.py:336
  22.0 4.6 %collective-permute-start.5 = (s32[136,1024]{1,0:T(8,128)S(1)}, s32[136,1024]{1,0:T(8,128)S(1)}, u32[]{:S(2)}, u32[]{:S(2)}) collective-permute-start(s32[136,1024]{1,0:T(8,128)S(1)} %collective-permute-done.4.refs_2_), channel_id=1, source_target_pairs={{0,64},{64,128},{128,192},{192,256},{256,320},{320,384},{384,448},... | collective-permute-start | bytes 1671176 | tf_op jit(solution)/shard_map/ppermute | solution.py:336
  26.6 1.4 %collective-permute-done.1.refs_1_ = s32[136,1024]{1,0:T(8,128)S(1)} collective-permute-done((s32[136,1024]{1,0:T(8,128)S(1)}, s32[136,1024]{1,0:T(8,128)S(1)}, u32[]{:S(2)}, u32[]{:S(2)}) %collective-permute-start.1) | collective-permute-done | bytes 557088 | tf_op jit(solution)/shard_map/ppermute | solution.py:336
  28.0 4.6 %collective-permute-start.2 = (s32[136,1024]{1,0:T(8,128)S(1)}, s32[136,1024]{1,0:T(8,128)S(1)}, u32[]{:S(2)}, u32[]{:S(2)}) collective-permute-start(s32[136,1024]{1,0:T(8,128)S(1)} %collective-permute-done.1.refs_1_), channel_id=1, source_target_pairs={{0,64},{64,128},{128,192},{192,256},{256,320},{320,384},{384,448},... | collective-permute-start | bytes 1671176 | tf_op jit(solution)/shard_map/ppermute | solution.py:336
  32.6 1.4 %collective-permute-done.5.refs_2_ = s32[136,1024]{1,0:T(8,128)S(1)} collective-permute-done((s32[136,1024]{1,0:T(8,128)S(1)}, s32[136,1024]{1,0:T(8,128)S(1)}, u32[]{:S(2)}, u32[]{:S(2)}) %collective-permute-start.5) | collective-permute-done | bytes 557088 | tf_op jit(solution)/shard_map/ppermute | solution.py:336
  33.9 4.6 %collective-permute-start.6 = (s32[136,1024]{1,0:T(8,128)S(1)}, s32[136,1024]{1,0:T(8,128)S(1)}, u32[]{:S(2)}, u32[]{:S(2)}) collective-permute-start(s32[136,1024]{1,0:T(8,128)S(1)} %collective-permute-done.5.refs_2_), channel_id=1, source_target_pairs={{0,64},{64,128},{128,192},{192,256},{256,320},{320,384},{384,448},... | collective-permute-start | bytes 1671176 | tf_op jit(solution)/shard_map/ppermute | solution.py:336
  38.6 0.0 copy-done.9
  38.6 0.9 copy.30
  39.4 0.6 pad_add_fusion.place_ref
  40.0 2.2 %share.1 = (bf16[128,16,128]{2,1,0:T(8,128)(2,1)}, bf16[128,16,128]{2,1,0:T(8,128)(2,1)}) custom-call(s32[2]{0:T(128)} %pad_add_fusion.place_ref, bf16[8,16,1024]{2,1,0:T(8,128)(2,1)} %bitcast.25, bf16[2,16,4096]{2,1,0:T(8,128)(2,1)} %bitcast.26, bf16[2,16,4096]{2,1,0:T(8,128)(2,1)} %bitcast.27), custom_call_target="tpu_custom_call" | custom-call | tf_op jit(solution)/shard_map/share/pallas_call | solution.py:151
  42.2 6.7 %collective-permute-start.8 = (bf16[128,16,128]{2,1,0:T(8,128)(2,1)}, bf16[128,16,128]{2,1,0:T(8,128)(2,1)S(1)}, u32[]{:S(2)}, u32[]{:S(2)}) collective-permute-start(bf16[128,16,128]{2,1,0:T(8,128)(2,1)} %get-tuple-element.27), channel_id=1, source_target_pairs={{0,1},{1,0},{2,3},{3,2},{4,5},{5,4},{6,7},{7,6},{8,9},{9,8},{10,11... | collective-permute-start | bytes 1572872 | tf_op jit(solution)/shard_map/ppermute | solution.py:344
  49.0 0.0 collective-permute-done.2.refs_1_
  49.0 0.7 collective-permute-start.3
  49.7 0.0 collective-permute-done.6.refs_2_
  49.7 4.9 %collective-permute-start.7 = (s32[136,1024]{1,0:T(8,128)S(1)}, s32[136,1024]{1,0:T(8,128)S(1)}, u32[]{:S(2)}, u32[]{:S(2)}) collective-permute-start(s32[136,1024]{1,0:T(8,128)S(1)} %collective-permute-done.6.refs_2_), channel_id=1, source_target_pairs={{1,449},{65,1},{129,65},{193,129},{257,193},{321,257},{385,321},{4... | collective-permute-start | bytes 1671176 | tf_op jit(solution)/shard_map/ppermute | solution.py:336
  54.5 0.0 collective-permute-done.8.refs_5_
  54.6 1.0 copy-done.2
  55.6 1.2 %channel.4 = (f32[256,1024]{1,0:T(8,128)S(1)}, f32[8,8,128]{2,1,0:T(8,128)S(1)}, bf16[256,1024]{1,0:T(8,128)(2,1)S(1)}, bf16[4,4,32,512]{3,2,1,0:T(8,128)(2,1)S(1)}) custom-call(s32[1]{0:T(128)} %bitcast.refs_0_, s32[136,1024]{1,0:T(8,128)S(1)} %collective-permute-done.refs_1_, s32[136,1024]{1,0:T(8,128)S(1)} %collective-permute-done.4.refs_2_, ...), custom_call_target="tpu_custom_call" | custom-call | flops 536870912 | bytes 4259840 | tf_op jit(solution)/shard_map/channel/pallas_call | solution.py:245
  56.8 1.0 channel.5
  57.9 1.0 channel.6
  58.9 0.0 collective-permute-done.3.refs_1_
  58.9 2.1 %collective-permute-done.7.refs_2_ = s32[136,1024]{1,0:T(8,128)S(1)} collective-permute-done((s32[136,1024]{1,0:T(8,128)S(1)}, s32[136,1024]{1,0:T(8,128)S(1)}, u32[]{:S(2)}, u32[]{:S(2)}) %collective-permute-start.7) | collective-permute-done | bytes 557088 | tf_op jit(solution)/shard_map/ppermute | solution.py:336
  61.0 0.0 copy-done.1
  61.0 1.1 %channel.7 = (f32[32,16,256]{2,1,0:T(8,128)S(1)}, bf16[32,16,256]{2,1,0:T(8,128)(2,1)S(1)}, f32[8,8,128]{2,1,0:T(8,128)S(1)}) custom-call(s32[1]{0:T(128)} %bitcast.refs_0_, s32[136,1024]{1,0:T(8,128)S(1)} %collective-permute-done.3.refs_1_, s32[136,1024]{1,0:T(8,128)S(1)} %collective-permute-done.7.refs_2_, s32[136,1024]{1,0:T(8,128)S(1)} %copy-done, ...), custom_call_target="tpu_custom_call" | custom-call | flops 536870912 | bytes 4259840 | tf_op jit(solution)/shard_map/channel/pallas_call | solution.py:245
  62.1 2.5 %collective-permute-start.9 = (bf16[32,16,256]{2,1,0:T(8,128)(2,1)S(1)}, bf16[32,16,256]{2,1,0:T(8,128)(2,1)S(1)}, u32[]{:S(2)}, u32[]{:S(2)}) collective-permute-start(bf16[32,16,256]{2,1,0:T(8,128)(2,1)S(1)} %get-tuple-element.37), channel_id=1, source_target_pairs={{0,1},{1,0},{2,3},{3,2},{4,5},{5,4},{6,7},{7,6},{8,9},{9,8},{10,11... | collective-permute-start | bytes 786440 | tf_op jit(solution)/shard_map/ppermute | solution.py:357
  64.7 1.1 %collective-permute-done.9 = bf16[32,16,256]{2,1,0:T(8,128)(2,1)S(1)} collective-permute-done((bf16[32,16,256]{2,1,0:T(8,128)(2,1)S(1)}, bf16[32,16,256]{2,1,0:T(8,128)(2,1)S(1)}, u32[]{:S(2)}, u32[]{:S(2)}) %collective-permute-start.9) | collective-permute-done | bytes 262176 | tf_op jit(solution)/shard_map/ppermute | solution.py:357
  65.8 0.8 add_convert_fusion
  66.6 8.8 %all-to-all-start = ((bf16[32,16,256]{2,1,0:T(8,128)(2,1)}), bf16[32,16,256]{2,1,0:T(8,128)(2,1)S(1)}, u32[]{:S(2)}, u32[]{:S(2)}) async-start(bf16[32,16,256]{2,1,0:T(8,128)(2,1)} %add_convert_fusion), calls=%async_computation | async-start | bytes 524288 | tf_op jit(solution)/shard_map/all_to_all | solution.py:358
  75.5 0.0 copy-done.4
  75.5 0.0 copy-done.8
  75.5 0.0 copy-start.5
  75.5 0.0 copy-start.6
  75.5 0.9 dense.1
  76.4 10.6 %all-to-all-done.got_ref = bf16[32,16,256]{2,1,0:T(8,128)(2,1)S(1)} async-done(((bf16[32,16,256]{2,1,0:T(8,128)(2,1)}), bf16[32,16,256]{2,1,0:T(8,128)(2,1)S(1)}, u32[]{:S(2)}, u32[]{:S(2)}) %all-to-all-start) | async-done | bytes 262176 | tf_op jit(solution)/shard_map/all_to_all | solution.py:358
  87.0 0.6 token_.1
  87.7 0.1 add_reduce_fusion
  87.8 0.6 broadcast_in_dim.2
  88.4 6.4 %all-to-all-start.1 = ((f32[64,1,8]{2,1,0:T(1,128)}), f32[64,1,8]{2,1,0:T(1,128)S(1)}, u32[]{:S(2)}, u32[]{:S(2)}) async-start(f32[64,1,8]{2,1,0:T(1,128)} %broadcast_in_dim.2), calls=%async_computation.1 | async-start | bytes 65536 | tf_op jit(solution)/shard_map/all_to_all | solution.py:361
  94.8 1.0 back.1
  95.8 8.5 %all-to-all-done.1 = f32[64,1,8]{2,1,0:T(1,128)S(1)} async-done(((f32[64,1,8]{2,1,0:T(1,128)}), f32[64,1,8]{2,1,0:T(1,128)S(1)}, u32[]{:S(2)}, u32[]{:S(2)}) %all-to-all-start.1) | async-done | bytes 2080 | tf_op jit(solution)/shard_map/all_to_all | solution.py:361
  104.3 0.6 reduce_sum.19
  (12 shorter events, 0.0 us)
Async XLA Ops:
  2.9 35.7 %copy-start.9 = (bf16[16,8,1024]{2,1,0:T(8,128)(2,1)S(1)}, bf16[16,8,1024]{2,1,0:T(8,128)(2,1)}, u32[]{:S(2)}) copy-start(bf16[16,8,1024]{2,1,0:T(8,128)(2,1)} %param.12) | copy-start | bytes 786436
  2.9 12.8 %collective-permute-start = (s32[136,1024]{1,0:T(8,128)}, s32[136,1024]{1,0:T(8,128)S(1)}, u32[]{:S(2)}, u32[]{:S(2)}) collective-permute-start(s32[136,1024]{1,0:T(8,128)} %pack.2.refs_3_), channel_id=1, source_target_pairs={{0,64},{64,128},{128,192},{192,256},{256,320},{320,384},{384,448},... | collective-permute-start | bytes 1671176 | tf_op jit(solution)/shard_map/ppermute | solution.py:336
  11.2 10.8 %collective-permute-start.4 = (s32[136,1024]{1,0:T(8,128)}, s32[136,1024]{1,0:T(8,128)S(1)}, u32[]{:S(2)}, u32[]{:S(2)}) collective-permute-start(s32[136,1024]{1,0:T(8,128)} %pack.3.refs_4_), channel_id=1, source_target_pairs={{0,64},{64,128},{128,192},{192,256},{256,320},{320,384},{384,448},... | collective-permute-start | bytes 1671176 | tf_op jit(solution)/shard_map/ppermute | solution.py:336
  15.7 12.2 %collective-permute-start.1 = (s32[136,1024]{1,0:T(8,128)S(1)}, s32[136,1024]{1,0:T(8,128)S(1)}, u32[]{:S(2)}, u32[]{:S(2)}) collective-permute-start(s32[136,1024]{1,0:T(8,128)S(1)} %collective-permute-done.refs_1_), channel_id=1, source_target_pairs={{0,64},{64,128},{128,192},{192,256},{256,320},{320,384},{384,448},... | collective-permute-start | bytes 1671176 | tf_op jit(solution)/shard_map/ppermute | solution.py:336
  22.0 11.9 %collective-permute-start.5 = (s32[136,1024]{1,0:T(8,128)S(1)}, s32[136,1024]{1,0:T(8,128)S(1)}, u32[]{:S(2)}, u32[]{:S(2)}) collective-permute-start(s32[136,1024]{1,0:T(8,128)S(1)} %collective-permute-done.4.refs_2_), channel_id=1, source_target_pairs={{0,64},{64,128},{128,192},{192,256},{256,320},{320,384},{384,448},... | collective-permute-start | bytes 1671176 | tf_op jit(solution)/shard_map/ppermute | solution.py:336
  28.0 21.0 %collective-permute-start.2 = (s32[136,1024]{1,0:T(8,128)S(1)}, s32[136,1024]{1,0:T(8,128)S(1)}, u32[]{:S(2)}, u32[]{:S(2)}) collective-permute-start(s32[136,1024]{1,0:T(8,128)S(1)} %collective-permute-done.1.refs_1_), channel_id=1, source_target_pairs={{0,64},{64,128},{128,192},{192,256},{256,320},{320,384},{384,448},... | collective-permute-start | bytes 1671176 | tf_op jit(solution)/shard_map/ppermute | solution.py:336
  33.9 15.7 %collective-permute-start.6 = (s32[136,1024]{1,0:T(8,128)S(1)}, s32[136,1024]{1,0:T(8,128)S(1)}, u32[]{:S(2)}, u32[]{:S(2)}) collective-permute-start(s32[136,1024]{1,0:T(8,128)S(1)} %collective-permute-done.5.refs_2_), channel_id=1, source_target_pairs={{0,64},{64,128},{128,192},{192,256},{256,320},{320,384},{384,448},... | collective-permute-start | bytes 1671176 | tf_op jit(solution)/shard_map/ppermute | solution.py:336
  42.2 12.3 %copy-start.7 = (f32[1024]{0:T(1024)S(1)}, f32[1024]{0:T(1024)}, u32[]{:S(2)}) copy-start(f32[1024]{0:T(1024)} %param.14) | copy-start | bytes 12292
  42.2 12.3 %collective-permute-start.8 = (bf16[128,16,128]{2,1,0:T(8,128)(2,1)}, bf16[128,16,128]{2,1,0:T(8,128)(2,1)S(1)}, u32[]{:S(2)}, u32[]{:S(2)}) collective-permute-start(bf16[128,16,128]{2,1,0:T(8,128)(2,1)} %get-tuple-element.27), channel_id=1, source_target_pairs={{0,1},{1,0},{2,3},{3,2},{4,5},{5,4},{6,7},{7,6},{8,9},{9,8},{10,11... | collective-permute-start | bytes 1572872 | tf_op jit(solution)/shard_map/ppermute | solution.py:344
  49.0 9.9 %collective-permute-start.3 = (s32[136,1024]{1,0:T(8,128)S(1)}, s32[136,1024]{1,0:T(8,128)S(1)}, u32[]{:S(2)}, u32[]{:S(2)}) collective-permute-start(s32[136,1024]{1,0:T(8,128)S(1)} %collective-permute-done.2.refs_1_), channel_id=1, source_target_pairs={{0,64},{64,128},{128,192},{192,256},{256,320},{320,384},{384,448},... | collective-permute-start | bytes 1671176 | tf_op jit(solution)/shard_map/ppermute | solution.py:336
  49.7 11.3 %collective-permute-start.7 = (s32[136,1024]{1,0:T(8,128)S(1)}, s32[136,1024]{1,0:T(8,128)S(1)}, u32[]{:S(2)}, u32[]{:S(2)}) collective-permute-start(s32[136,1024]{1,0:T(8,128)S(1)} %collective-permute-done.6.refs_2_), channel_id=1, source_target_pairs={{1,449},{65,1},{129,65},{193,129},{257,193},{321,257},{385,321},{4... | collective-permute-start | bytes 1671176 | tf_op jit(solution)/shard_map/ppermute | solution.py:336
  54.6 1.0 copy-start.2
  57.8 3.2 %copy-start = (s32[136,1024]{1,0:T(8,128)S(1)}, s32[136,1024]{1,0:T(8,128)}, u32[]{:S(2)}) copy-start(s32[136,1024]{1,0:T(8,128)} %pack.2.refs_3_) | copy-start | bytes 1671172
  57.8 3.2 %copy-start.1 = (s32[136,1024]{1,0:T(8,128)S(1)}, s32[136,1024]{1,0:T(8,128)}, u32[]{:S(2)}) copy-start(s32[136,1024]{1,0:T(8,128)} %pack.3.refs_4_) | copy-start | bytes 1671172
  62.1 3.7 %collective-permute-start.9 = (bf16[32,16,256]{2,1,0:T(8,128)(2,1)S(1)}, bf16[32,16,256]{2,1,0:T(8,128)(2,1)S(1)}, u32[]{:S(2)}, u32[]{:S(2)}) collective-permute-start(bf16[32,16,256]{2,1,0:T(8,128)(2,1)S(1)} %get-tuple-element.37), channel_id=1, source_target_pairs={{0,1},{1,0},{2,3},{3,2},{4,5},{5,4},{6,7},{7,6},{8,9},{9,8},{10,11... | collective-permute-start | bytes 786440 | tf_op jit(solution)/shard_map/ppermute | solution.py:357
  65.8 9.6 %copy-start.4 = (bf16[16,128,128]{2,1,0:T(8,128)(2,1)S(1)}, bf16[16,128,128]{2,1,0:T(8,128)(2,1)}, u32[]{:S(2)}) copy-start(bf16[16,128,128]{2,1,0:T(8,128)(2,1)} %out_ref.1) | copy-start | bytes 1572868
  65.8 9.6 %copy-start.8 = (s32[16]{0:T(128)S(1)}, s32[16]{0:T(128)}, u32[]{:S(2)}) copy-start(s32[16]{0:T(128)} %cells_ref.1) | copy-start | bytes 196
  66.6 8.8 %copy-start.3 = (bf16[16,128,128]{2,1,0:T(8,128)(2,1)S(1)}, bf16[16,128,128]{2,1,0:T(8,128)(2,1)}, u32[]{:S(2)}) copy-start(bf16[16,128,128]{2,1,0:T(8,128)(2,1)} %in_ref.1) | copy-start | bytes 1572868
  66.6 20.4 %all-to-all-start = ((bf16[32,16,256]{2,1,0:T(8,128)(2,1)}), bf16[32,16,256]{2,1,0:T(8,128)(2,1)S(1)}, u32[]{:S(2)}, u32[]{:S(2)}) async-start(bf16[32,16,256]{2,1,0:T(8,128)(2,1)} %add_convert_fusion), calls=%async_computation | async-start | bytes 524288 | tf_op jit(solution)/shard_map/all_to_all | solution.py:358
  75.5 11.6 %copy-start.5 = (bf16[2,512,1,16]{1,3,2,0:T(8,128)(2,1)S(1)}, bf16[2,512,1,16]{1,3,2,0:T(8,128)(2,1)}, u32[]{:S(2)}) copy-start(bf16[2,512,1,16]{1,3,2,0:T(8,128)(2,1)} %param.22) | copy-start | bytes 98308
  75.5 11.5 %copy-start.6 = (bf16[2,512,1,16]{1,3,2,0:T(8,128)(2,1)S(1)}, bf16[2,512,1,16]{1,3,2,0:T(8,128)(2,1)}, u32[]{:S(2)}) copy-start(bf16[2,512,1,16]{1,3,2,0:T(8,128)(2,1)} %param.23) | copy-start | bytes 98308
  88.4 15.8 %all-to-all-start.1 = ((f32[64,1,8]{2,1,0:T(1,128)}), f32[64,1,8]{2,1,0:T(1,128)S(1)}, u32[]{:S(2)}, u32[]{:S(2)}) async-start(f32[64,1,8]{2,1,0:T(1,128)} %broadcast_in_dim.2), calls=%async_computation.1 | async-start | bytes 65536 | tf_op jit(solution)/shard_map/all_to_all | solution.py:361

commit v9 on v8

--- a/solution.py
+++ b/solution.py
@@ -29,7 +29,7 @@
 STEPS = 4
 SHARED = 32
 ROWS_DEV = SPEC * SHARED
-PACKED = 136
+PACKED = 1032
 LAM_TILES = SPEC * (D // 128)
 SCALE_ONE = float(2**38)
 
@@ -53,23 +53,27 @@
     ]
     for copy in copies:
         copy.start()
-    out_ref[128:136, :] = jnp.zeros((8, D), I32)
+    out_ref[1024:1032, :] = jnp.zeros((8, 128), I32)
     copies[0].wait()
     down = pack_codes([down_ref[m * 256 : (m + 1) * 256, :] for m in range(4)])
-    for k in range(4):
-        out_ref[0:64, k * CHUNK : (k + 1) * CHUNK] = down[k * 64 : (k + 1) * 64, :]
+    for k in range(8):
+        rows, cut = slice(k // 2 * 64, (k // 2 + 1) * 64), slice(k % 2 * 128, (k % 2 + 1) * 128)
+        out_ref[k * 64 : (k + 1) * 64, :] = down[rows, cut]
     copies[1].wait()
-    out_ref[64:128, :] = pack_codes([up_ref[m * 64 : (m + 1) * 64, :] for m in range(4)])
+    up = pack_codes([up_ref[m * 64 : (m + 1) * 64, :] for m in range(4)])
+    for k in range(8):
+        out_ref[512 + k * 64 : 512 + (k + 1) * 64, :] = up[:, k * 128 : (k + 1) * 128]
     copies[2].wait()
     scale = (scale_ref[...] * SCALE_ONE).astype(I32)
-    out_ref[128:136, 0:CHUNK] = jnp.broadcast_to(scale, (8, CHUNK))
+    for h in range(2):
+        out_ref[1024 + h : 1025 + h, :] = scale[:, h * 128 : (h + 1) * 128]
 
 
 def pack(chunk, q_down, q_up, up_scale):
     hbm, vmem = pl.BlockSpec(memory_space=pltpu.HBM), pl.BlockSpec(memory_space=pltpu.VMEM)
     return pl.pallas_call(
         functools.partial(pack_kernel, chunk * CHUNK),
-        out_shape=jax.ShapeDtypeStruct((PACKED, D), I32),
+        out_shape=jax.ShapeDtypeStruct((PACKED, 128), I32),
         in_specs=[hbm, hbm, hbm],
         out_specs=vmem,
         scratch_shapes=[
@@ -121,15 +125,15 @@
     return mid, pos * icpt_low.astype(F32) + neg * icpt_high.astype(F32)
 
 
-def share_kernel(place_ref, lam_ref, slopes_ref, icpt_ref, *out_refs):
+def share_kernel(core_ref, row_ref, lam_ref, slopes_ref, icpt_ref, *out_refs):
     for r in range(SPEC):
         for k in range(D // 128):
             tile = lam_ref[r, :, k * 128 : (k + 1) * 128]
             for out_ref in out_refs:
                 out_ref[r * (D // 128) + k] = tile
-    row = place_ref[1]
+    row = row_ref[0]
     for k, out_ref in enumerate(out_refs):
-        core = place_ref[0] ^ k
+        core = core_ref[0] ^ k
         for j in range(STEPS):
             if j < STEPS - 1:
                 owner = row + (2 * core - 1) * (j + 1)
@@ -146,16 +150,16 @@
                     out_ref[tile + 1] = values[:, 128:256]
 
 
-def share(place, by_row, slopes, icpt):
+def share(core, row, by_row, slopes, icpt):
     tiles = LAM_TILES + 4 * STEPS * 4
     return pl.pallas_call(
         share_kernel,
         out_shape=(jax.ShapeDtypeStruct((tiles, 16, 128), BF16),) * 2,
-        in_specs=[pl.BlockSpec(memory_space=pltpu.SMEM)]
+        in_specs=[pl.BlockSpec(memory_space=pltpu.SMEM)] * 2
         + [pl.BlockSpec(memory_space=pltpu.VMEM)] * 3,
         compiler_params=pltpu.CompilerParams(vmem_limit_bytes=60 * 1024 * 1024),
         name="share",
-    )(place, by_row, slopes, icpt)
+    )(core, row, by_row, slopes, icpt)
 
 
 def channel_kernel(step, *refs):
@@ -191,15 +195,16 @@
         ]
     for h, chunk in enumerate(words):
         for m in range(4):
-            codes = unpack_codes(chunk[0:64], m)
-            for q in range(4):
-                rows = m * 256 + q * 64
-                cut = slice(q * CHUNK, (q + 1) * CHUNK)
-                down[rows : rows + 64, h * CHUNK : (h + 1) * CHUNK] = codes[:, cut]
-            rows = h * CHUNK + m * 64
-            up[rows : rows + 64, :] = unpack_codes(chunk[64:128], m)
-    scale = jnp.concatenate([chunk[128:129, 0:CHUNK] for chunk in words], axis=1)
-    scale = scale.astype(F32) * (1.0 / SCALE_ONE)
+            for k in range(8):
+                rows = m * 256 + k // 2 * 64
+                cut = h * CHUNK + k % 2 * 128
+                codes = unpack_codes(chunk[k * 64 : (k + 1) * 64], m)
+                down[rows : rows + 64, cut : cut + 128] = codes
+                rows = h * CHUNK + m * 64
+                codes = unpack_codes(chunk[512 + k * 64 : 512 + (k + 1) * 64], m)
+                up[rows : rows + 64, k * 128 : (k + 1) * 128] = codes
+    scale = [chunk[1024 + h : 1025 + h] for chunk in words for h in range(2)]
+    scale = jnp.concatenate(scale, axis=1).astype(F32) * (1.0 / SCALE_ONE)
     pre = jnp.dot(scaled_ref[...], down[...], preferred_element_type=F32)
     pre = pre.reshape(SPEC, SHARED, PART)
     mid, terms = relaxed(pre, *(bounds_ref[step, kind] for kind in range(4)))
@@ -252,14 +257,16 @@
         compiler_params=pltpu.CompilerParams(vmem_limit_bytes=VMEM),
         cost_estimate=pl.CostEstimate(
             flops=4 * ROWS_DEV * PART * D,
-            bytes_accessed=2 * PACKED * D * 4 + 3 * ROWS_DEV * D * 4,
+            bytes_accessed=2 * PACKED * 128 * 4 + 3 * ROWS_DEV * D * 4,
             transcendentals=0,
         ),
         name="channel",
     )(*operands)
 
 
-def token_kernel(got_ref, dense_ref, slopes_ref, icpt_ref, columns_ref, mid_ref, bias_ref):
+def token_kernel(
+    got_ref, dense_ref, slopes_ref, icpt_ref, chan_bias_ref, columns_ref, mid_ref, bias_ref
+):
     lane = lax.broadcasted_iota(I32, (16, 128), 1) // 32
     for u in range(NTB):
         for a in range(2):
@@ -281,20 +288,25 @@
     mid, terms = relaxed(pre, slopes_ref[0], slopes_ref[1], icpt_ref[0], icpt_ref[1])
     mid_ref[...] = mid.reshape(SPEC * 16, TH).astype(BF16)
     terms = terms[:, 0:8, :] + terms[:, 8:16, :]
-    bias_ref[...] = sum(terms[:, :, k * 128 : (k + 1) * 128] for k in range(NHB))
-
-
-def token_mlp(got, dense_out, slopes, icpt):
+    terms = sum(terms[:, :, k * 128 : (k + 1) * 128] for k in range(NHB)) + chan_bias_ref[...]
+    by_row = jnp.sum(jnp.sum(terms, axis=1), axis=1, keepdims=True)
+    row = lax.broadcasted_iota(I32, (SPEC, 128), 0)
+    lane = lax.broadcasted_iota(I32, (SPEC, 128), 1)
+    line = jnp.sum(jnp.where(row == lane, by_row, 0.0), axis=0, keepdims=True)
+    bias_ref[...] = jnp.broadcast_to(line[None], bias_ref.shape)
+
+
+def token_mlp(got, dense_out, slopes, icpt, chan_bias):
     return pl.pallas_call(
         token_kernel,
         out_shape=(
             jax.ShapeDtypeStruct((SPEC * 16, TOK), BF16),
             jax.ShapeDtypeStruct((SPEC * 16, TH), BF16),
-            jax.ShapeDtypeStruct((SPEC, 8, 128), F32),
+            jax.ShapeDtypeStruct((64, 1, 128), F32),
         ),
         compiler_params=pltpu.CompilerParams(vmem_limit_bytes=VMEM),
         name="token",
-    )(got, dense_out, slopes, icpt)
+    )(got, dense_out, slopes, icpt, chan_bias)
 
 
 def back_kernel(columns_ref, mid_ref, dense_ref, out_ref):
@@ -325,8 +337,8 @@
     tok_slopes,
     tok_icpt,
 ):
-    core, row = lax.axis_index("core").astype(I32), lax.axis_index("rows").astype(I32)
-    place, core = jnp.stack([core, row]), core.reshape(1)
+    core = lax.axis_index("core").astype(I32).reshape(1)
+    row = lax.axis_index("rows").astype(I32).reshape(1)
     tok_dev = lam_out.shape[0]
     slices = lax.axis_size("rows")
     ahead = [(i * 2, (i + 1) % slices * 2) for i in range(slices)]
@@ -339,31 +351,32 @@
     first = forward(own, ahead + behind)
     _, lam, *bounds = lax.optimization_barrier((own, lam_out, chan_slopes, chan_icpt))
     keep_part, send_part = share(
-        place, jnp.swapaxes(lam, 0, 1), *(b.reshape(2, tok_dev, CH) for b in bounds)
+        core, row, jnp.swapaxes(lam, 0, 1), *(b.reshape(2, tok_dev, CH) for b in bounds)
     )
-    team = (keep_part, lax.ppermute(send_part, "core", SWAP))
-    second = forward(first, ahead + behind)
-    third = forward(second, ahead + behind)
-    far = forward(third[:1], ahead) + forward(third[1:], behind)
+    words, send_part = lax.optimization_barrier((first[0], send_part))
+    second = forward((words, first[1]), ahead + behind)
+    other_part = lax.ppermute(send_part, "core", SWAP)
+    words, other_part = lax.optimization_barrier((second[0], other_part))
+    third = forward((words, second[1]), ahead + behind)
+    carried = channel_part(0, core, *first, down_scale.reshape(1, D), keep_part, other_part)
+    acc, chan_bias, *given = carried
+    acc, chan_bias = channel_part(1, core, *second, *given, acc, chan_bias)
+    words, acc = lax.optimization_barrier((third[0], acc))
+    far = forward((words,), ahead) + forward(third[1:], behind)
 
     dense_in, dense_out = dense_blocks(block_cells, tok_in_blocks, tok_out_blocks)
     slopes = jnp.transpose(tok_slopes, (0, 2, 3, 1)).reshape(2, 16, TH)
     icpt = jnp.transpose(tok_icpt, (0, 2, 3, 1)).reshape(2, 16, TH)
 
-    acc, chan_bias, *given = channel_part(0, core, *first, down_scale.reshape(1, D), *team)
-    acc, chan_bias = channel_part(1, core, *second, *given, acc, chan_bias)
     acc, chan_bias = channel_part(2, core, *third, *given, acc, chan_bias)
     keep, send, chan_bias = channel_part(3, core, *far, *own, *given, acc, chan_bias)
     summed = (keep + lax.ppermute(send, "core", SWAP).astype(F32)).astype(BF16)
     got = lax.all_to_all(summed, ("z", "x"), 0, 0, tiled=True)
-    columns, mid, tok_bias = token_mlp(got, dense_out, slopes, icpt)
-    own_bias = jnp.sum(chan_bias + tok_bias, axis=(1, 2))
-    all_bias = lax.all_to_all(
-        jnp.broadcast_to(own_bias[None, :], (64, SPEC)), MP, 0, 0, tiled=True
-    )
+    columns, mid, own_bias = token_mlp(got, dense_out, slopes, icpt, chan_bias)
+    all_bias = lax.all_to_all(own_bias, MP, 0, 0, tiled=True)
     lam_in = token_back(columns, mid, dense_in)
     lam_in = jnp.transpose(lam_in.reshape(SPEC, 16, TOK), (2, 0, 1))
-    return (lam_in, jnp.sum(all_bias, axis=0))
+    return (lam_in, jnp.sum(all_bias, axis=(0, 1))[:SPEC])
 
 
 def solution(mesh):

time: 106 us -> 107 us (level)
  the two profiles are of different devices: /device:TPU:1 before, /device:TPU:25 now
where the time goes in v9:
time: 107 us; the launch traced here: 106 us
  waiting for transfers between devices  44.3 us (41%)
  starting transfers between devices  42.3 us (40%)
  Pallas kernels  15.6 us (15%)
  local copies, waits for them, and re-layouts  1.93 us (2%)
  other arithmetic  1.38 us (1%)
    ppermute x8, waiting for transfers between devices, forward(): return tuple((lax.ppermute(w, ('rows', 'core'), pairs) for w in words))  21.8 us
    ppermute x8, starting transfers between devices, forward(): return tuple((lax.ppermute(w, ('rows', 'core'), pairs) for w in words))  14.7 us
    all_to_all x1, starting transfers between devices, on_device(): got = lax.all_to_all(summed, ('z', 'x'), 0, 0, tiled=True)  13 us
    all_to_all x1, waiting for transfers between devices, on_device(): got = lax.all_to_all(summed, ('z', 'x'), 0, 0, tiled=True)  10.9 us
    all_to_all x1, waiting for transfers between devices, on_device(): all_bias = lax.all_to_all(own_bias, MP, 0, 0, tiled=True)  8.46 us
    ppermute x1, starting transfers between devices, on_device(): other_part = lax.ppermute(send_part, 'core', SWAP)  6.51 us
    all_to_all x1, starting transfers between devices, on_device(): all_bias = lax.all_to_all(own_bias, MP, 0, 0, tiled=True)  6.2 us
    pallas_call x4, Pallas kernels, channel_part(): pl.pallas_call(functools.partial(channel_kernel, step), out_shape=out_sha...  5.65 us
  transfers between devices with their start and end apart: 12, of which 9 were waited for; matrix products, arithmetic and copies ran while one was open for 1% of the time, Pallas kernels for 10%

profile of v9, /device:TPU:25, one launch (start us, length us, event | category | flops | bytes accessed | tf_op | source)
XLA Modules:
  0.0 106.4 jit_solution(11226007816203766784)
XLA Ops:
  0.6 2.2 %pack.2.refs_3_ = s32[1032,128]{1,0:T(8,128)} custom-call(bf16[1024,512]{1,0:T(8,128)(2,1)} %down_hbm.3, bf16[512,1024]{1,0:T(8,128)(2,1)} %up_hbm.3, f32[1,512]{1,0:T(1,128)} %bitcast.30), custom_call_target="tpu_custom_call" | custom-call | tf_op jit(solution)/shard_map/pack/pallas_call | solution.py:74
  2.9 0.0 copy-start.9
  2.9 2.2 %collective-permute-start = (s32[1032,128]{1,0:T(8,128)}, s32[1032,128]{1,0:T(8,128)S(1)}, u32[]{:S(2)}, u32[]{:S(2)}) collective-permute-start(s32[1032,128]{1,0:T(8,128)} %pack.2.refs_3_), channel_id=1, source_target_pairs={{0,64},{64,128},{128,192},{192,256},{256,320},{320,384},{384,448},... | collective-permute-start | bytes 1585160 | tf_op jit(solution)/shard_map/ppermute | solution.py:348
  5.1 2.2 %pack.3.refs_4_ = s32[1032,128]{1,0:T(8,128)} custom-call(bf16[1024,512]{1,0:T(8,128)(2,1)} %down_hbm.3, bf16[512,1024]{1,0:T(8,128)(2,1)} %up_hbm.3, f32[1,512]{1,0:T(1,128)} %bitcast.31), custom_call_target="tpu_custom_call" | custom-call | tf_op jit(solution)/shard_map/pack/pallas_call | solution.py:74
  7.3 2.1 %collective-permute-start.4 = (s32[1032,128]{1,0:T(8,128)}, s32[1032,128]{1,0:T(8,128)S(1)}, u32[]{:S(2)}, u32[]{:S(2)}) collective-permute-start(s32[1032,128]{1,0:T(8,128)} %pack.3.refs_4_), channel_id=1, source_target_pairs={{0,64},{64,128},{128,192},{192,256},{256,320},{320,384},{384,448},... | collective-permute-start | bytes 1585160 | tf_op jit(solution)/shard_map/ppermute | solution.py:348
  9.4 0.0 copy-done.9
  9.4 0.9 copy.22
  10.3 2.2 %share.1 = (bf16[128,16,128]{2,1,0:T(8,128)(2,1)}, bf16[128,16,128]{2,1,0:T(8,128)(2,1)}) custom-call(s32[1]{0:T(128)} %bitcast.core_ref.refs_0_, s32[1]{0:T(128)} %bitcast.2.row_ref, bf16[8,16,1024]{2,1,0:T(8,128)(2,1)} %bitcast.26, bf16[2,16,4096]{2,1,0:T(8,128)(2,1)} %bitcast.27, bf16[2,16,4096]{2,1,0:T(8,128)(2,1)} %bitcast.28), custom_call_target="tpu_custom_call" | custom-call | tf_op jit(solution)/shard_map/share/pallas_call | solution.py:155
  12.5 1.9 %collective-permute-done.refs_1_ = s32[1032,128]{1,0:T(8,128)S(1)} collective-permute-done((s32[1032,128]{1,0:T(8,128)}, s32[1032,128]{1,0:T(8,128)S(1)}, u32[]{:S(2)}, u32[]{:S(2)}) %collective-permute-start) | collective-permute-done | bytes 528416 | tf_op jit(solution)/shard_map/ppermute | solution.py:348
  14.4 1.9 %collective-permute-start.1 = (s32[1032,128]{1,0:T(8,128)S(1)}, s32[1032,128]{1,0:T(8,128)S(1)}, u32[]{:S(2)}, u32[]{:S(2)}) collective-permute-start(s32[1032,128]{1,0:T(8,128)S(1)} %collective-permute-done.refs_1_), channel_id=1, source_target_pairs={{0,64},{64,128},{128,192},{192,256},{256,320},{320,384},{384,448},... | collective-permute-start | bytes 1585160 | tf_op jit(solution)/shard_map/ppermute | solution.py:348
  16.3 3.7 %collective-permute-done.4.refs_2_ = s32[1032,128]{1,0:T(8,128)S(1)} collective-permute-done((s32[1032,128]{1,0:T(8,128)}, s32[1032,128]{1,0:T(8,128)S(1)}, u32[]{:S(2)}, u32[]{:S(2)}) %collective-permute-start.4) | collective-permute-done | bytes 528416 | tf_op jit(solution)/shard_map/ppermute | solution.py:348
  20.1 1.9 %collective-permute-start.5 = (s32[1032,128]{1,0:T(8,128)S(1)}, s32[1032,128]{1,0:T(8,128)S(1)}, u32[]{:S(2)}, u32[]{:S(2)}) collective-permute-start(s32[1032,128]{1,0:T(8,128)S(1)} %collective-permute-done.4.refs_2_), channel_id=1, source_target_pairs={{0,64},{64,128},{128,192},{192,256},{256,320},{320,384},{384,448},... | collective-permute-start | bytes 1585160 | tf_op jit(solution)/shard_map/ppermute | solution.py:348
  22.0 6.5 %collective-permute-start.2 = (bf16[128,16,128]{2,1,0:T(8,128)(2,1)}, bf16[128,16,128]{2,1,0:T(8,128)(2,1)S(1)}, u32[]{:S(2)}, u32[]{:S(2)}) collective-permute-start(bf16[128,16,128]{2,1,0:T(8,128)(2,1)} %get-tuple-element.34), channel_id=1, source_target_pairs={{0,1},{1,0},{2,3},{3,2},{4,5},{5,4},{6,7},{7,6},{8,9},{9,8},{10,11... | collective-permute-start | bytes 1572872 | tf_op jit(solution)/shard_map/ppermute | solution.py:358
  28.5 1.7 %collective-permute-done.2.refs_5_ = bf16[128,16,128]{2,1,0:T(8,128)(2,1)S(1)} collective-permute-done((bf16[128,16,128]{2,1,0:T(8,128)(2,1)}, bf16[128,16,128]{2,1,0:T(8,128)(2,1)S(1)}, u32[]{:S(2)}, u32[]{:S(2)}) %collective-permute-start.2) | collective-permute-done | bytes 524320 | tf_op jit(solution)/shard_map/ppermute | solution.py:358
  30.2 0.0 collective-permute-done.1.refs_1_
  30.2 1.9 %collective-permute-start.3 = (s32[1032,128]{1,0:T(8,128)S(1)}, s32[1032,128]{1,0:T(8,128)S(1)}, u32[]{:S(2)}, u32[]{:S(2)}) collective-permute-start(s32[1032,128]{1,0:T(8,128)S(1)} %collective-permute-done.1.refs_1_), channel_id=1, source_target_pairs={{0,64},{64,128},{128,192},{192,256},{256,320},{320,384},{384,448},... | collective-permute-start | bytes 1585160 | tf_op jit(solution)/shard_map/ppermute | solution.py:348
  32.1 0.0 collective-permute-done.5.refs_2_
  32.2 2.1 %collective-permute-start.7 = (s32[1032,128]{1,0:T(8,128)S(1)}, s32[1032,128]{1,0:T(8,128)S(1)}, u32[]{:S(2)}, u32[]{:S(2)}) collective-permute-start(s32[1032,128]{1,0:T(8,128)S(1)} %collective-permute-done.5.refs_2_), channel_id=1, source_target_pairs={{0,64},{64,128},{128,192},{192,256},{256,320},{320,384},{384,448},... | collective-permute-start | bytes 1585160 | tf_op jit(solution)/shard_map/ppermute | solution.py:348
  34.2 0.0 copy-done.7
  34.2 0.0 copy-start.2
  34.2 1.0 copy-done.2
  35.3 1.5 %channel.4 = (f32[256,1024]{1,0:T(8,128)S(1)}, f32[8,8,128]{2,1,0:T(8,128)S(1)}, bf16[256,1024]{1,0:T(8,128)(2,1)S(1)}, bf16[4,4,32,512]{3,2,1,0:T(8,128)(2,1)S(1)}) custom-call(s32[1]{0:T(128)} %bitcast.core_ref.refs_0_, s32[1032,128]{1,0:T(8,128)S(1)} %collective-permute-done.refs_1_, s32[1032,128]{1,0:T(8,128)S(1)} %collective-permute-done.4.refs_2_, ...), custom_call_target="tpu_custom_call" | custom-call | flops 536870912 | bytes 4202496 | tf_op jit(solution)/shard_map/channel/pallas_call | solution.py:250
  36.8 1.3 %channel.5 = (f32[256,1024]{1,0:T(8,128)S(1)}, f32[8,8,128]{2,1,0:T(8,128)S(1)}) custom-call(s32[1]{0:T(128)} %bitcast.core_ref.refs_0_, s32[1032,128]{1,0:T(8,128)S(1)} %collective-permute-done.1.refs_1_, s32[1032,128]{1,0:T(8,128)S(1)} %collective-permute-done.5.refs_2_, ...), custom_call_target="tpu_custom_call", output_to_operand_aliasing={{0}: (5, {}), {1}: (6, {})} | custom-call | flops 536870912 | bytes 4202496 | tf_op jit(solution)/shard_map/channel/pallas_call | solution.py:250
  38.1 3.3 %collective-permute-done.3.refs_1_ = s32[1032,128]{1,0:T(8,128)S(1)} collective-permute-done((s32[1032,128]{1,0:T(8,128)S(1)}, s32[1032,128]{1,0:T(8,128)S(1)}, u32[]{:S(2)}, u32[]{:S(2)}) %collective-permute-start.3) | collective-permute-done | bytes 528416 | tf_op jit(solution)/shard_map/ppermute | solution.py:348
  41.4 0.7 collective-permute-start.6
  42.1 5.0 %collective-permute-done.7.refs_2_ = s32[1032,128]{1,0:T(8,128)S(1)} collective-permute-done((s32[1032,128]{1,0:T(8,128)S(1)}, s32[1032,128]{1,0:T(8,128)S(1)}, u32[]{:S(2)}, u32[]{:S(2)}) %collective-permute-start.7) | collective-permute-done | bytes 528416 | tf_op jit(solution)/shard_map/ppermute | solution.py:348
  47.1 1.9 %collective-permute-start.8 = (s32[1032,128]{1,0:T(8,128)S(1)}, s32[1032,128]{1,0:T(8,128)S(1)}, u32[]{:S(2)}, u32[]{:S(2)}) collective-permute-start(s32[1032,128]{1,0:T(8,128)S(1)} %collective-permute-done.7.refs_2_), channel_id=1, source_target_pairs={{1,449},{65,1},{129,65},{193,129},{257,193},{321,257},{385,321},{4... | collective-permute-start | bytes 1585160 | tf_op jit(solution)/shard_map/ppermute | solution.py:348
  49.0 0.0 copy-start
  49.0 0.0 copy-start.1
  49.0 1.3 %channel.6 = (f32[256,1024]{1,0:T(8,128)S(1)}, f32[8,8,128]{2,1,0:T(8,128)S(1)}) custom-call(s32[1]{0:T(128)} %bitcast.core_ref.refs_0_, s32[1032,128]{1,0:T(8,128)S(1)} %collective-permute-done.3.refs_1_, s32[1032,128]{1,0:T(8,128)S(1)} %collective-permute-done.7.refs_2_, ...), custom_call_target="tpu_custom_call", output_to_operand_aliasing={{0}: (5, {}), {1}: (6, {})} | custom-call | flops 536870912 | bytes 4202496 | tf_op jit(solution)/shard_map/channel/pallas_call | solution.py:250
  50.3 0.0 collective-permute-done.6.refs_1_
  50.3 7.9 %collective-permute-done.8.refs_2_ = s32[1032,128]{1,0:T(8,128)S(1)} collective-permute-done((s32[1032,128]{1,0:T(8,128)S(1)}, s32[1032,128]{1,0:T(8,128)S(1)}, u32[]{:S(2)}, u32[]{:S(2)}) %collective-permute-start.8) | collective-permute-done | bytes 528416 | tf_op jit(solution)/shard_map/ppermute | solution.py:348
  58.2 0.0 copy-done.1
  58.2 1.5 %channel.7 = (f32[32,16,256]{2,1,0:T(8,128)S(1)}, bf16[32,16,256]{2,1,0:T(8,128)(2,1)S(1)}, f32[8,8,128]{2,1,0:T(8,128)S(1)}) custom-call(s32[1]{0:T(128)} %bitcast.core_ref.refs_0_, s32[1032,128]{1,0:T(8,128)S(1)} %collective-permute-done.6.refs_1_, s32[1032,128]{1,0:T(8,128)S(1)} %collective-permute-done.8.refs_2_, s32[1032,128]{1,0:T(8,128)S(1)} %copy-done, ...), custom_call_target="tpu_custom_call" | custom-call | flops 536870912 | bytes 4202496 | tf_op jit(solution)/shard_map/channel/pallas_call | solution.py:250
  59.7 1.9 %collective-permute-start.9 = (bf16[32,16,256]{2,1,0:T(8,128)(2,1)S(1)}, bf16[32,16,256]{2,1,0:T(8,128)(2,1)S(1)}, u32[]{:S(2)}, u32[]{:S(2)}) collective-permute-start(bf16[32,16,256]{2,1,0:T(8,128)(2,1)S(1)} %get-tuple-element.49), channel_id=1, source_target_pairs={{0,1},{1,0},{2,3},{3,2},{4,5},{5,4},{6,7},{7,6},{8,9},{9,8},{10,11... | collective-permute-start | bytes 786440 | tf_op jit(solution)/shard_map/ppermute | solution.py:373
  61.7 1.5 %collective-permute-done.9 = bf16[32,16,256]{2,1,0:T(8,128)(2,1)S(1)} collective-permute-done((bf16[32,16,256]{2,1,0:T(8,128)(2,1)S(1)}, bf16[32,16,256]{2,1,0:T(8,128)(2,1)S(1)}, u32[]{:S(2)}, u32[]{:S(2)}) %collective-permute-start.9) | collective-permute-done | bytes 262176 | tf_op jit(solution)/shard_map/ppermute | solution.py:373
  63.2 0.8 add_convert_fusion
  64.0 13.0 %all-to-all-start = ((bf16[32,16,256]{2,1,0:T(8,128)(2,1)}), bf16[32,16,256]{2,1,0:T(8,128)(2,1)S(1)}, u32[]{:S(2)}, u32[]{:S(2)}) async-start(bf16[32,16,256]{2,1,0:T(8,128)(2,1)} %add_convert_fusion), calls=%async_computation | async-start | bytes 524288 | tf_op jit(solution)/shard_map/all_to_all | solution.py:374
  77.0 0.0 copy-start.5
  77.0 0.0 copy-start.6
  77.0 0.9 dense.1
  78.0 10.9 %all-to-all-done.got_ref = bf16[32,16,256]{2,1,0:T(8,128)(2,1)S(1)} async-done(((bf16[32,16,256]{2,1,0:T(8,128)(2,1)}), bf16[32,16,256]{2,1,0:T(8,128)(2,1)S(1)}, u32[]{:S(2)}, u32[]{:S(2)}) %all-to-all-start) | async-done | bytes 262176 | tf_op jit(solution)/shard_map/all_to_all | solution.py:374
  88.8 0.0 copy-done.6
  88.8 1.3 %token_.1 = (bf16[128,1024]{1,0:T(8,128)(2,1)S(1)}, bf16[128,512]{1,0:T(8,128)(2,1)S(1)}, f32[64,1,128]{2,1,0:T(1,128)}) custom-call(bf16[32,16,256]{2,1,0:T(8,128)(2,1)S(1)} %all-to-all-done.got_ref, bf16[1024,512]{1,0:T(8,128)(2,1)S(1)} %get-tuple-element.50.dense_ref, bf16[2,16,512]{2,1,0:T(8,128)(2,1)S(1)} %bitcast.23, bf16[2,16,512]{2,1,0:T(8,128)(2,1)S(1)} %bitcast.24, ...), custom_call_target="tpu_custom_call" | custom-call | tf_op jit(solution)/shard_map/token/pallas_call | solution.py:300
  90.1 6.2 %all-to-all-start.1 = ((f32[64,1,128]{2,1,0:T(1,128)}), f32[64,1,128]{2,1,0:T(1,128)S(1)}, u32[]{:S(2)}, u32[]{:S(2)}) async-start(f32[64,1,128]{2,1,0:T(1,128)} %get-tuple-element.55), calls=%async_computation.1 | async-start | bytes 65536 | tf_op jit(solution)/shard_map/all_to_all | solution.py:376
  96.4 1.0 back.1
  97.4 8.5 %all-to-all-done.1 = f32[64,1,128]{2,1,0:T(1,128)S(1)} async-done(((f32[64,1,128]{2,1,0:T(1,128)}), f32[64,1,128]{2,1,0:T(1,128)S(1)}, u32[]{:S(2)}, u32[]{:S(2)}) %all-to-all-start.1) | async-done | bytes 32800 | tf_op jit(solution)/shard_map/all_to_all | solution.py:376
  105.8 0.6 reduce_sum.9
  (9 shorter events, 0.0 us)
Async XLA Ops:
  2.9 6.6 %copy-start.9 = (bf16[16,8,1024]{2,1,0:T(8,128)(2,1)S(1)}, bf16[16,8,1024]{2,1,0:T(8,128)(2,1)}, u32[]{:S(2)}) copy-start(bf16[16,8,1024]{2,1,0:T(8,128)(2,1)} %param.12) | copy-start | bytes 786436
  2.9 11.5 %collective-permute-start = (s32[1032,128]{1,0:T(8,128)}, s32[1032,128]{1,0:T(8,128)S(1)}, u32[]{:S(2)}, u32[]{:S(2)}) collective-permute-start(s32[1032,128]{1,0:T(8,128)} %pack.2.refs_3_), channel_id=1, source_target_pairs={{0,64},{64,128},{128,192},{192,256},{256,320},{320,384},{384,448},... | collective-permute-start | bytes 1585160 | tf_op jit(solution)/shard_map/ppermute | solution.py:348
  7.3 12.7 %collective-permute-start.4 = (s32[1032,128]{1,0:T(8,128)}, s32[1032,128]{1,0:T(8,128)S(1)}, u32[]{:S(2)}, u32[]{:S(2)}) collective-permute-start(s32[1032,128]{1,0:T(8,128)} %pack.3.refs_4_), channel_id=1, source_target_pairs={{0,64},{64,128},{128,192},{192,256},{256,320},{320,384},{384,448},... | collective-permute-start | bytes 1585160 | tf_op jit(solution)/shard_map/ppermute | solution.py:348
  12.5 21.7 %copy-start.7 = (f32[1024]{0:T(1024)S(1)}, f32[1024]{0:T(1024)}, u32[]{:S(2)}) copy-start(f32[1024]{0:T(1024)} %param.14) | copy-start | bytes 12292
  14.4 15.8 %collective-permute-start.1 = (s32[1032,128]{1,0:T(8,128)S(1)}, s32[1032,128]{1,0:T(8,128)S(1)}, u32[]{:S(2)}, u32[]{:S(2)}) collective-permute-start(s32[1032,128]{1,0:T(8,128)S(1)} %collective-permute-done.refs_1_), channel_id=1, source_target_pairs={{0,64},{64,128},{128,192},{192,256},{256,320},{320,384},{384,448},... | collective-permute-start | bytes 1585160 | tf_op jit(solution)/shard_map/ppermute | solution.py:348
  20.1 12.1 %collective-permute-start.5 = (s32[1032,128]{1,0:T(8,128)S(1)}, s32[1032,128]{1,0:T(8,128)S(1)}, u32[]{:S(2)}, u32[]{:S(2)}) collective-permute-start(s32[1032,128]{1,0:T(8,128)S(1)} %collective-permute-done.4.refs_2_), channel_id=1, source_target_pairs={{0,64},{64,128},{128,192},{192,256},{256,320},{320,384},{384,448},... | collective-permute-start | bytes 1585160 | tf_op jit(solution)/shard_map/ppermute | solution.py:348
  22.0 8.2 %collective-permute-start.2 = (bf16[128,16,128]{2,1,0:T(8,128)(2,1)}, bf16[128,16,128]{2,1,0:T(8,128)(2,1)S(1)}, u32[]{:S(2)}, u32[]{:S(2)}) collective-permute-start(bf16[128,16,128]{2,1,0:T(8,128)(2,1)} %get-tuple-element.34), channel_id=1, source_target_pairs={{0,1},{1,0},{2,3},{3,2},{4,5},{5,4},{6,7},{7,6},{8,9},{9,8},{10,11... | collective-permute-start | bytes 1572872 | tf_op jit(solution)/shard_map/ppermute | solution.py:358
  30.2 11.2 %collective-permute-start.3 = (s32[1032,128]{1,0:T(8,128)S(1)}, s32[1032,128]{1,0:T(8,128)S(1)}, u32[]{:S(2)}, u32[]{:S(2)}) collective-permute-start(s32[1032,128]{1,0:T(8,128)S(1)} %collective-permute-done.1.refs_1_), channel_id=1, source_target_pairs={{0,64},{64,128},{128,192},{192,256},{256,320},{320,384},{384,448},... | collective-permute-start | bytes 1585160 | tf_op jit(solution)/shard_map/ppermute | solution.py:348
  32.2 14.9 %collective-permute-start.7 = (s32[1032,128]{1,0:T(8,128)S(1)}, s32[1032,128]{1,0:T(8,128)S(1)}, u32[]{:S(2)}, u32[]{:S(2)}) collective-permute-start(s32[1032,128]{1,0:T(8,128)S(1)} %collective-permute-done.5.refs_2_), channel_id=1, source_target_pairs={{0,64},{64,128},{128,192},{192,256},{256,320},{320,384},{384,448},... | collective-permute-start | bytes 1585160 | tf_op jit(solution)/shard_map/ppermute | solution.py:348
  34.2 1.0 copy-start.2
  41.4 8.9 %collective-permute-start.6 = (s32[1032,128]{1,0:T(8,128)S(1)}, s32[1032,128]{1,0:T(8,128)S(1)}, u32[]{:S(2)}, u32[]{:S(2)}) collective-permute-start(s32[1032,128]{1,0:T(8,128)S(1)} %collective-permute-done.3.refs_1_), channel_id=1, source_target_pairs={{0,64},{64,128},{128,192},{192,256},{256,320},{320,384},{384,448},... | collective-permute-start | bytes 1585160 | tf_op jit(solution)/shard_map/ppermute | solution.py:348
  47.1 11.2 %collective-permute-start.8 = (s32[1032,128]{1,0:T(8,128)S(1)}, s32[1032,128]{1,0:T(8,128)S(1)}, u32[]{:S(2)}, u32[]{:S(2)}) collective-permute-start(s32[1032,128]{1,0:T(8,128)S(1)} %collective-permute-done.7.refs_2_), channel_id=1, source_target_pairs={{1,449},{65,1},{129,65},{193,129},{257,193},{321,257},{385,321},{4... | collective-permute-start | bytes 1585160 | tf_op jit(solution)/shard_map/ppermute | solution.py:348
  49.0 9.3 %copy-start = (s32[1032,128]{1,0:T(8,128)S(1)}, s32[1032,128]{1,0:T(8,128)}, u32[]{:S(2)}) copy-start(s32[1032,128]{1,0:T(8,128)} %pack.2.refs_3_) | copy-start | bytes 1585156
  49.0 9.2 %copy-start.1 = (s32[1032,128]{1,0:T(8,128)S(1)}, s32[1032,128]{1,0:T(8,128)}, u32[]{:S(2)}) copy-start(s32[1032,128]{1,0:T(8,128)} %pack.3.refs_4_) | copy-start | bytes 1585156
  59.7 3.4 %collective-permute-start.9 = (bf16[32,16,256]{2,1,0:T(8,128)(2,1)S(1)}, bf16[32,16,256]{2,1,0:T(8,128)(2,1)S(1)}, u32[]{:S(2)}, u32[]{:S(2)}) collective-permute-start(bf16[32,16,256]{2,1,0:T(8,128)(2,1)S(1)} %get-tuple-element.49), channel_id=1, source_target_pairs={{0,1},{1,0},{2,3},{3,2},{4,5},{5,4},{6,7},{7,6},{8,9},{9,8},{10,11... | collective-permute-start | bytes 786440 | tf_op jit(solution)/shard_map/ppermute | solution.py:373
  63.2 13.8 %copy-start.4 = (bf16[16,128,128]{2,1,0:T(8,128)(2,1)S(1)}, bf16[16,128,128]{2,1,0:T(8,128)(2,1)}, u32[]{:S(2)}) copy-start(bf16[16,128,128]{2,1,0:T(8,128)(2,1)} %out_ref.1) | copy-start | bytes 1572868
  63.2 13.8 %copy-start.8 = (s32[16]{0:T(128)S(1)}, s32[16]{0:T(128)}, u32[]{:S(2)}) copy-start(s32[16]{0:T(128)} %cells_ref.1) | copy-start | bytes 196
  63.9 13.1 %copy-start.3 = (bf16[16,128,128]{2,1,0:T(8,128)(2,1)S(1)}, bf16[16,128,128]{2,1,0:T(8,128)(2,1)}, u32[]{:S(2)}) copy-start(bf16[16,128,128]{2,1,0:T(8,128)(2,1)} %in_ref.1) | copy-start | bytes 1572868
  64.0 24.9 %all-to-all-start = ((bf16[32,16,256]{2,1,0:T(8,128)(2,1)}), bf16[32,16,256]{2,1,0:T(8,128)(2,1)S(1)}, u32[]{:S(2)}, u32[]{:S(2)}) async-start(bf16[32,16,256]{2,1,0:T(8,128)(2,1)} %add_convert_fusion), calls=%async_computation | async-start | bytes 524288 | tf_op jit(solution)/shard_map/all_to_all | solution.py:374
  77.0 11.8 %copy-start.5 = (bf16[2,512,1,16]{1,3,2,0:T(8,128)(2,1)S(1)}, bf16[2,512,1,16]{1,3,2,0:T(8,128)(2,1)}, u32[]{:S(2)}) copy-start(bf16[2,512,1,16]{1,3,2,0:T(8,128)(2,1)} %param.22) | copy-start | bytes 98308
  77.0 11.8 %copy-start.6 = (bf16[2,512,1,16]{1,3,2,0:T(8,128)(2,1)S(1)}, bf16[2,512,1,16]{1,3,2,0:T(8,128)(2,1)}, u32[]{:S(2)}) copy-start(bf16[2,512,1,16]{1,3,2,0:T(8,128)(2,1)} %param.23) | copy-start | bytes 98308
  90.1 15.7 %all-to-all-start.1 = ((f32[64,1,128]{2,1,0:T(1,128)}), f32[64,1,128]{2,1,0:T(1,128)S(1)}, u32[]{:S(2)}, u32[]{:S(2)}) async-start(f32[64,1,128]{2,1,0:T(1,128)} %get-tuple-element.55), calls=%async_computation.1 | async-start | bytes 65536 | tf_op jit(solution)/shard_map/all_to_all | solution.py:376

commit v10 on v9

--- a/solution.py
+++ b/solution.py
@@ -44,8 +44,8 @@
     return (shifted >> 24).astype(F32).astype(BF16)
 
 
-def pack_kernel(start, down_hbm, up_hbm, scale_hbm, out_ref, down_ref, up_ref, scale_ref, sems):
-    cut = pl.ds(start, CHUNK)
+def pack_kernel(chain, core_ref, down_hbm, up_hbm, scale_hbm, out_ref, down_ref, up_ref, scale_ref, sems):
+    cut = pl.ds(pl.multiple_of((core_ref[0] ^ chain) * CHUNK, CHUNK), CHUNK)
     copies = [
         pltpu.make_async_copy(down_hbm.at[:, cut], down_ref, sems.at[0]),
         pltpu.make_async_copy(up_hbm.at[cut, :], up_ref, sems.at[1]),
@@ -69,12 +69,14 @@
         out_ref[1024 + h : 1025 + h, :] = scale[:, h * 128 : (h + 1) * 128]
 
 
-def pack(chunk, q_down, q_up, up_scale):
-    hbm, vmem = pl.BlockSpec(memory_space=pltpu.HBM), pl.BlockSpec(memory_space=pltpu.VMEM)
-    return pl.pallas_call(
-        functools.partial(pack_kernel, chunk * CHUNK),
+def pack(chain, core, q_down, q_up, up_scale):
+    smem, hbm, vmem = (
+        pl.BlockSpec(memory_space=space) for space in (pltpu.SMEM, pltpu.HBM, pltpu.VMEM)
+    )
+    return pl.pallas_call(
+        functools.partial(pack_kernel, chain),
         out_shape=jax.ShapeDtypeStruct((PACKED, 128), I32),
-        in_specs=[hbm, hbm, hbm],
+        in_specs=[smem, hbm, hbm, hbm],
         out_specs=vmem,
         scratch_shapes=[
             pltpu.VMEM((D, CHUNK), BF16),
@@ -84,7 +86,7 @@
         ],
         compiler_params=pltpu.CompilerParams(vmem_limit_bytes=60 * 1024 * 1024),
         name="pack",
-    )(q_down, q_up, up_scale.reshape(1, -1))
+    )(core, q_down, q_up, up_scale.reshape(1, -1))
 
 
 def dense_kernel(cells_ref, in_ref, out_ref, dense_in_ref, dense_out_ref):
@@ -137,7 +139,7 @@
         for j in range(STEPS):
             if j < STEPS - 1:
                 owner = row + (2 * core - 1) * (j + 1)
-                cuts = [(owner, 0), (owner, 1)]
+                cuts = [(owner, core), (owner, 1 - core)]
             else:
                 cuts = [(row + STEPS, core), (row, core)]
             for h, (owner, chunk) in enumerate(cuts):
@@ -183,16 +185,8 @@
                     bounds_ref[i // 4, i % 4, rows, h * 128 : (h + 1) * 128] = tile
         acc_in, bias_in = acc_ref, None
     else:
-        if last:
-            *own_words, refs = refs[0], refs[1], refs[2:]
         scaled_ref, bounds_ref, acc_in, bias_in, *outs, down, up = refs
     words = [w[...] for w in words]
-    if last:
-        own_core = core_ref[0] == 0
-        words = [
-            jnp.where(own_core, words[0], words[1]),
-            jnp.where(own_core, own_words[0][...], own_words[1][...]),
-        ]
     for h, chunk in enumerate(words):
         for m in range(4):
             for k in range(8):
@@ -347,7 +341,7 @@
     def forward(words, pairs):
         return tuple(lax.ppermute(w, ("rows", "core"), pairs) for w in words)
 
-    own = tuple(pack(chunk, q_down, q_up, up_scale) for chunk in range(2))
+    own = tuple(pack(chain, core, q_down, q_up, up_scale) for chain in range(2))
     first = forward(own, ahead + behind)
     _, lam, *bounds = lax.optimization_barrier((own, lam_out, chan_slopes, chan_icpt))
     keep_part, send_part = share(
@@ -362,14 +356,14 @@
     acc, chan_bias, *given = carried
     acc, chan_bias = channel_part(1, core, *second, *given, acc, chan_bias)
     words, acc = lax.optimization_barrier((third[0], acc))
-    far = forward((words,), ahead) + forward(third[1:], behind)
+    far = forward((words,), ahead + behind)
 
     dense_in, dense_out = dense_blocks(block_cells, tok_in_blocks, tok_out_blocks)
     slopes = jnp.transpose(tok_slopes, (0, 2, 3, 1)).reshape(2, 16, TH)
     icpt = jnp.transpose(tok_icpt, (0, 2, 3, 1)).reshape(2, 16, TH)
 
     acc, chan_bias = channel_part(2, core, *third, *given, acc, chan_bias)
-    keep, send, chan_bias = channel_part(3, core, *far, *own, *given, acc, chan_bias)
+    keep, send, chan_bias = channel_part(3, core, *far, own[0], *given, acc, chan_bias)
     summed = (keep + lax.ppermute(send, "core", SWAP).astype(F32)).astype(BF16)
     got = lax.all_to_all(summed, ("z", "x"), 0, 0, tiled=True)
     columns, mid, own_bias = token_mlp(got, dense_out, slopes, icpt, chan_bias)

time: 107 us -> 103 us (0.963)
  the two profiles are of different devices: /device:TPU:25 before, /device:TPU:1 now
where the time goes in v10:
time: 103 us; the launch traced here: 102 us
  starting transfers between devices  50.9 us (49%)
  waiting for transfers between devices  31.4 us (30%)
  Pallas kernels  15.6 us (15%)
  local copies, waits for them, and re-layouts  1.92 us (2%)
  other arithmetic  1.39 us (1%)
    ppermute x7, starting transfers between devices, forward(): return tuple((lax.ppermute(w, ('rows', 'core'), pairs) for w in words))  25.8 us
    ppermute x7, waiting for transfers between devices, forward(): return tuple((lax.ppermute(w, ('rows', 'core'), pairs) for w in words))  11.2 us
    all_to_all x1, waiting for transfers between devices, on_device(): got = lax.all_to_all(summed, ('z', 'x'), 0, 0, tiled=True)  10.6 us
    all_to_all x1, waiting for transfers between devices, on_device(): all_bias = lax.all_to_all(own_bias, MP, 0, 0, tiled=True)  8.43 us
    all_to_all x1, starting transfers between devices, on_device(): got = lax.all_to_all(summed, ('z', 'x'), 0, 0, tiled=True)  8.06 us
    all_to_all x1, starting transfers between devices, on_device(): all_bias = lax.all_to_all(own_bias, MP, 0, 0, tiled=True)  6.32 us
    ppermute x1, starting transfers between devices, on_device(): other_part = lax.ppermute(send_part, 'core', SWAP)  5.93 us
    pallas_call x4, Pallas kernels, channel_part(): pl.pallas_call(functools.partial(channel_kernel, step), out_shape=out_sha...  5.59 us
  transfers between devices with their start and end apart: 11, of which 6 were waited for; matrix products, arithmetic and copies ran while one was open for 1% of the time, Pallas kernels for 10%

profile of v10, /device:TPU:1, one launch (start us, length us, event | category | flops | bytes accessed | tf_op | source)
XLA Modules:
  0.0 102.1 jit_solution(16758207935852858952)
XLA Ops:
  0.6 2.2 %pack.2.refs_2_ = s32[1032,128]{1,0:T(8,128)} custom-call(s32[1]{0:T(128)} %bitcast.core_ref.refs_0_, bf16[1024,512]{1,0:T(8,128)(2,1)} %down_hbm.3, bf16[512,1024]{1,0:T(8,128)(2,1)} %up_hbm.3, f32[1,512]{1,0:T(1,128)} %bitcast.30), custom_call_target="tpu_custom_call" | custom-call | tf_op jit(solution)/shard_map/pack/pallas_call | solution.py:76
  2.9 0.0 copy-start.8
  2.9 6.1 %collective-permute-start = (s32[1032,128]{1,0:T(8,128)}, s32[1032,128]{1,0:T(8,128)S(1)}, u32[]{:S(2)}, u32[]{:S(2)}) collective-permute-start(s32[1032,128]{1,0:T(8,128)} %pack.2.refs_2_), channel_id=1, source_target_pairs={{0,64},{64,128},{128,192},{192,256},{256,320},{320,384},{384,448},... | collective-permute-start | bytes 1585160 | tf_op jit(solution)/shard_map/ppermute | solution.py:342
  9.0 2.2 %pack.3 = s32[1032,128]{1,0:T(8,128)} custom-call(s32[1]{0:T(128)} %bitcast.core_ref.refs_0_, bf16[1024,512]{1,0:T(8,128)(2,1)} %down_hbm.3, bf16[512,1024]{1,0:T(8,128)(2,1)} %up_hbm.3, f32[1,512]{1,0:T(1,128)} %bitcast.31), custom_call_target="tpu_custom_call" | custom-call | tf_op jit(solution)/shard_map/pack/pallas_call | solution.py:76
  11.2 3.0 %collective-permute-start.4 = (s32[1032,128]{1,0:T(8,128)}, s32[1032,128]{1,0:T(8,128)S(1)}, u32[]{:S(2)}, u32[]{:S(2)}) collective-permute-start(s32[1032,128]{1,0:T(8,128)} %pack.3), channel_id=1, source_target_pairs={{0,64},{64,128},{128,192},{192,256},{256,320},{320,384},{384,448},... | collective-permute-start | bytes 1585160 | tf_op jit(solution)/shard_map/ppermute | solution.py:342
  14.2 0.0 copy-done.8
  14.2 0.9 copy.22
  15.1 2.2 %share.1 = (bf16[128,16,128]{2,1,0:T(8,128)(2,1)}, bf16[128,16,128]{2,1,0:T(8,128)(2,1)}) custom-call(s32[1]{0:T(128)} %bitcast.core_ref.refs_0_, s32[1]{0:T(128)} %bitcast.2.row_ref, bf16[8,16,1024]{2,1,0:T(8,128)(2,1)} %bitcast.26, bf16[2,16,4096]{2,1,0:T(8,128)(2,1)} %bitcast.27, bf16[2,16,4096]{2,1,0:T(8,128)(2,1)} %bitcast.28), custom_call_target="tpu_custom_call" | custom-call | tf_op jit(solution)/shard_map/share/pallas_call | solution.py:157
  17.3 0.0 collective-permute-done.refs_1_
  17.3 3.1 %collective-permute-start.1 = (s32[1032,128]{1,0:T(8,128)S(1)}, s32[1032,128]{1,0:T(8,128)S(1)}, u32[]{:S(2)}, u32[]{:S(2)}) collective-permute-start(s32[1032,128]{1,0:T(8,128)S(1)} %collective-permute-done.refs_1_), channel_id=1, source_target_pairs={{0,64},{64,128},{128,192},{192,256},{256,320},{320,384},{384,448},... | collective-permute-start | bytes 1585160 | tf_op jit(solution)/shard_map/ppermute | solution.py:342
  20.3 5.9 %collective-permute-start.2 = (bf16[128,16,128]{2,1,0:T(8,128)(2,1)}, bf16[128,16,128]{2,1,0:T(8,128)(2,1)S(1)}, u32[]{:S(2)}, u32[]{:S(2)}) collective-permute-start(bf16[128,16,128]{2,1,0:T(8,128)(2,1)} %get-tuple-element.34), channel_id=1, source_target_pairs={{0,1},{1,0},{2,3},{3,2},{4,5},{5,4},{6,7},{7,6},{8,9},{9,8},{10,11... | collective-permute-start | bytes 1572872 | tf_op jit(solution)/shard_map/ppermute | solution.py:352
  26.3 0.0 collective-permute-done.4.refs_2_
  26.3 4.9 %collective-permute-start.5 = (s32[1032,128]{1,0:T(8,128)S(1)}, s32[1032,128]{1,0:T(8,128)S(1)}, u32[]{:S(2)}, u32[]{:S(2)}) collective-permute-start(s32[1032,128]{1,0:T(8,128)S(1)} %collective-permute-done.4.refs_2_), channel_id=1, source_target_pairs={{0,64},{64,128},{128,192},{192,256},{256,320},{320,384},{384,448},... | collective-permute-start | bytes 1585160 | tf_op jit(solution)/shard_map/ppermute | solution.py:342
  31.1 0.0 collective-permute-done.2.refs_5_
  31.2 0.0 collective-permute-done.1.refs_1_
  31.2 1.9 %collective-permute-start.3 = (s32[1032,128]{1,0:T(8,128)S(1)}, s32[1032,128]{1,0:T(8,128)S(1)}, u32[]{:S(2)}, u32[]{:S(2)}) collective-permute-start(s32[1032,128]{1,0:T(8,128)S(1)} %collective-permute-done.1.refs_1_), channel_id=1, source_target_pairs={{0,64},{64,128},{128,192},{192,256},{256,320},{320,384},{384,448},... | collective-permute-start | bytes 1585160 | tf_op jit(solution)/shard_map/ppermute | solution.py:342
  33.1 4.2 %collective-permute-done.5.refs_2_ = s32[1032,128]{1,0:T(8,128)S(1)} collective-permute-done((s32[1032,128]{1,0:T(8,128)S(1)}, s32[1032,128]{1,0:T(8,128)S(1)}, u32[]{:S(2)}, u32[]{:S(2)}) %collective-permute-start.5) | collective-permute-done | bytes 528416 | tf_op jit(solution)/shard_map/ppermute | solution.py:342
  37.3 5.0 %collective-permute-start.7 = (s32[1032,128]{1,0:T(8,128)S(1)}, s32[1032,128]{1,0:T(8,128)S(1)}, u32[]{:S(2)}, u32[]{:S(2)}) collective-permute-start(s32[1032,128]{1,0:T(8,128)S(1)} %collective-permute-done.5.refs_2_), channel_id=1, source_target_pairs={{0,64},{64,128},{128,192},{192,256},{256,320},{320,384},{384,448},... | collective-permute-start | bytes 1585160 | tf_op jit(solution)/shard_map/ppermute | solution.py:342
  42.3 0.0 copy-done.6
  42.3 0.0 copy-start.1
  42.3 1.0 %copy-done.1 = bf16[128,16,128]{2,1,0:T(8,128)(2,1)S(1)} copy-done((bf16[128,16,128]{2,1,0:T(8,128)(2,1)S(1)}, bf16[128,16,128]{2,1,0:T(8,128)(2,1)}, u32[]{:S(2)}) %copy-start.1) | copy-done | bytes 524312
  43.4 1.5 %channel.4 = (f32[256,1024]{1,0:T(8,128)S(1)}, f32[8,8,128]{2,1,0:T(8,128)S(1)}, bf16[256,1024]{1,0:T(8,128)(2,1)S(1)}, bf16[4,4,32,512]{3,2,1,0:T(8,128)(2,1)S(1)}) custom-call(s32[1]{0:T(128)} %bitcast.core_ref.refs_0_, s32[1032,128]{1,0:T(8,128)S(1)} %collective-permute-done.refs_1_, s32[1032,128]{1,0:T(8,128)S(1)} %collective-permute-done.4.refs_2_, ...), custom_call_target="tpu_custom_call" | custom-call | flops 536870912 | bytes 4202496 | tf_op jit(solution)/shard_map/channel/pallas_call | solution.py:244
  44.9 1.3 %channel.5 = (f32[256,1024]{1,0:T(8,128)S(1)}, f32[8,8,128]{2,1,0:T(8,128)S(1)}) custom-call(s32[1]{0:T(128)} %bitcast.core_ref.refs_0_, s32[1032,128]{1,0:T(8,128)S(1)} %collective-permute-done.1.refs_1_, s32[1032,128]{1,0:T(8,128)S(1)} %collective-permute-done.5.refs_2_, ...), custom_call_target="tpu_custom_call", output_to_operand_aliasing={{0}: (5, {}), {1}: (6, {})} | custom-call | flops 536870912 | bytes 4202496 | tf_op jit(solution)/shard_map/channel/pallas_call | solution.py:244
  46.2 0.0 collective-permute-done.3.refs_1_
  46.2 1.9 %collective-permute-start.6 = (s32[1032,128]{1,0:T(8,128)S(1)}, s32[1032,128]{1,0:T(8,128)S(1)}, u32[]{:S(2)}, u32[]{:S(2)}) collective-permute-start(s32[1032,128]{1,0:T(8,128)S(1)} %collective-permute-done.3.refs_1_), channel_id=1, source_target_pairs={{0,64},{64,128},{128,192},{192,256},{256,320},{320,384},{384,448},... | collective-permute-start | bytes 1585160 | tf_op jit(solution)/shard_map/ppermute | solution.py:342
  48.2 0.5 collective-permute-done.7.refs_2_
  48.6 1.3 %channel.6 = (f32[256,1024]{1,0:T(8,128)S(1)}, f32[8,8,128]{2,1,0:T(8,128)S(1)}) custom-call(s32[1]{0:T(128)} %bitcast.core_ref.refs_0_, s32[1032,128]{1,0:T(8,128)S(1)} %collective-permute-done.3.refs_1_, s32[1032,128]{1,0:T(8,128)S(1)} %collective-permute-done.7.refs_2_, ...), custom_call_target="tpu_custom_call", output_to_operand_aliasing={{0}: (5, {}), {1}: (6, {})} | custom-call | flops 536870912 | bytes 4202496 | tf_op jit(solution)/shard_map/channel/pallas_call | solution.py:244
  50.0 6.5 %collective-permute-done.6.refs_1_ = s32[1032,128]{1,0:T(8,128)S(1)} collective-permute-done((s32[1032,128]{1,0:T(8,128)S(1)}, s32[1032,128]{1,0:T(8,128)S(1)}, u32[]{:S(2)}, u32[]{:S(2)}) %collective-permute-start.6) | collective-permute-done | bytes 528416 | tf_op jit(solution)/shard_map/ppermute | solution.py:342
  56.5 0.0 copy-done
  56.5 1.4 %channel.7 = (f32[32,16,256]{2,1,0:T(8,128)S(1)}, bf16[32,16,256]{2,1,0:T(8,128)(2,1)S(1)}, f32[8,8,128]{2,1,0:T(8,128)S(1)}) custom-call(s32[1]{0:T(128)} %bitcast.core_ref.refs_0_, s32[1032,128]{1,0:T(8,128)S(1)} %collective-permute-done.6.refs_1_, s32[1032,128]{1,0:T(8,128)S(1)} %copy-done, bf16[256,1024]{1,0:T(8,128)(2,1)S(1)} %get-tuple-element.38.refs_3_, ...), custom_call_target="tpu_custom_call" | custom-call | flops 536870912 | bytes 4202496 | tf_op jit(solution)/shard_map/channel/pallas_call | solution.py:244
  57.9 4.8 %collective-permute-start.8 = (bf16[32,16,256]{2,1,0:T(8,128)(2,1)S(1)}, bf16[32,16,256]{2,1,0:T(8,128)(2,1)S(1)}, u32[]{:S(2)}, u32[]{:S(2)}) collective-permute-start(bf16[32,16,256]{2,1,0:T(8,128)(2,1)S(1)} %get-tuple-element.49), channel_id=1, source_target_pairs={{0,1},{1,0},{2,3},{3,2},{4,5},{5,4},{6,7},{7,6},{8,9},{9,8},{10,11... | collective-permute-start | bytes 786440 | tf_op jit(solution)/shard_map/ppermute | solution.py:367
  62.8 1.1 %collective-permute-done.8 = bf16[32,16,256]{2,1,0:T(8,128)(2,1)S(1)} collective-permute-done((bf16[32,16,256]{2,1,0:T(8,128)(2,1)S(1)}, bf16[32,16,256]{2,1,0:T(8,128)(2,1)S(1)}, u32[]{:S(2)}, u32[]{:S(2)}) %collective-permute-start.8) | collective-permute-done | bytes 262176 | tf_op jit(solution)/shard_map/ppermute | solution.py:367
  63.9 0.8 add_convert_fusion
  64.7 8.1 %all-to-all-start = ((bf16[32,16,256]{2,1,0:T(8,128)(2,1)}), bf16[32,16,256]{2,1,0:T(8,128)(2,1)S(1)}, u32[]{:S(2)}, u32[]{:S(2)}) async-start(bf16[32,16,256]{2,1,0:T(8,128)(2,1)} %add_convert_fusion), calls=%async_computation | async-start | bytes 524288 | tf_op jit(solution)/shard_map/all_to_all | solution.py:368
  72.8 0.0 copy-done.3
  72.8 0.0 copy-done.7
  72.8 0.0 copy-done.2
  72.8 0.0 copy-start.4
  72.8 0.0 copy-start.5
  72.8 0.9 dense.1
  73.8 10.6 %all-to-all-done.got_ref = bf16[32,16,256]{2,1,0:T(8,128)(2,1)S(1)} async-done(((bf16[32,16,256]{2,1,0:T(8,128)(2,1)}), bf16[32,16,256]{2,1,0:T(8,128)(2,1)S(1)}, u32[]{:S(2)}, u32[]{:S(2)}) %all-to-all-start) | async-done | bytes 262176 | tf_op jit(solution)/shard_map/all_to_all | solution.py:368
  84.4 0.0 copy-done.4
  84.4 0.0 copy-done.5
  84.4 1.3 %token_.1 = (bf16[128,1024]{1,0:T(8,128)(2,1)S(1)}, bf16[128,512]{1,0:T(8,128)(2,1)S(1)}, f32[64,1,128]{2,1,0:T(1,128)}) custom-call(bf16[32,16,256]{2,1,0:T(8,128)(2,1)S(1)} %all-to-all-done.got_ref, bf16[1024,512]{1,0:T(8,128)(2,1)S(1)} %get-tuple-element.50.dense_ref, bf16[2,16,512]{2,1,0:T(8,128)(2,1)S(1)} %bitcast.23, bf16[2,16,512]{2,1,0:T(8,128)(2,1)S(1)} %bitcast.24, ...), custom_call_target="tpu_custom_call" | custom-call | tf_op jit(solution)/shard_map/token/pallas_call | solution.py:294
  85.7 6.3 %all-to-all-start.1 = ((f32[64,1,128]{2,1,0:T(1,128)}), f32[64,1,128]{2,1,0:T(1,128)S(1)}, u32[]{:S(2)}, u32[]{:S(2)}) async-start(f32[64,1,128]{2,1,0:T(1,128)} %get-tuple-element.55), calls=%async_computation.1 | async-start | bytes 65536 | tf_op jit(solution)/shard_map/all_to_all | solution.py:370
  92.0 1.0 back.1
  93.0 8.4 %all-to-all-done.1 = f32[64,1,128]{2,1,0:T(1,128)S(1)} async-done(((f32[64,1,128]{2,1,0:T(1,128)}), f32[64,1,128]{2,1,0:T(1,128)S(1)}, u32[]{:S(2)}, u32[]{:S(2)}) %all-to-all-start.1) | async-done | bytes 32800 | tf_op jit(solution)/shard_map/all_to_all | solution.py:370
  101.5 0.6 reduce_sum.9
  (5 shorter events, 0.0 us)
Async XLA Ops:
  2.9 11.3 %copy-start.8 = (bf16[16,8,1024]{2,1,0:T(8,128)(2,1)S(1)}, bf16[16,8,1024]{2,1,0:T(8,128)(2,1)}, u32[]{:S(2)}) copy-start(bf16[16,8,1024]{2,1,0:T(8,128)(2,1)} %param.12) | copy-start | bytes 786436
  2.9 14.4 %collective-permute-start = (s32[1032,128]{1,0:T(8,128)}, s32[1032,128]{1,0:T(8,128)S(1)}, u32[]{:S(2)}, u32[]{:S(2)}) collective-permute-start(s32[1032,128]{1,0:T(8,128)} %pack.2.refs_2_), channel_id=1, source_target_pairs={{0,64},{64,128},{128,192},{192,256},{256,320},{320,384},{384,448},... | collective-permute-start | bytes 1585160 | tf_op jit(solution)/shard_map/ppermute | solution.py:342
  11.2 15.1 %collective-permute-start.4 = (s32[1032,128]{1,0:T(8,128)}, s32[1032,128]{1,0:T(8,128)S(1)}, u32[]{:S(2)}, u32[]{:S(2)}) collective-permute-start(s32[1032,128]{1,0:T(8,128)} %pack.3), channel_id=1, source_target_pairs={{0,64},{64,128},{128,192},{192,256},{256,320},{320,384},{384,448},... | collective-permute-start | bytes 1585160 | tf_op jit(solution)/shard_map/ppermute | solution.py:342
  17.3 25.1 %copy-start.6 = (f32[1024]{0:T(1024)S(1)}, f32[1024]{0:T(1024)}, u32[]{:S(2)}) copy-start(f32[1024]{0:T(1024)} %param.14) | copy-start | bytes 12292
  17.3 13.9 %collective-permute-start.1 = (s32[1032,128]{1,0:T(8,128)S(1)}, s32[1032,128]{1,0:T(8,128)S(1)}, u32[]{:S(2)}, u32[]{:S(2)}) collective-permute-start(s32[1032,128]{1,0:T(8,128)S(1)} %collective-permute-done.refs_1_), channel_id=1, source_target_pairs={{0,64},{64,128},{128,192},{192,256},{256,320},{320,384},{384,448},... | collective-permute-start | bytes 1585160 | tf_op jit(solution)/shard_map/ppermute | solution.py:342
  20.3 10.8 %collective-permute-start.2 = (bf16[128,16,128]{2,1,0:T(8,128)(2,1)}, bf16[128,16,128]{2,1,0:T(8,128)(2,1)S(1)}, u32[]{:S(2)}, u32[]{:S(2)}) collective-permute-start(bf16[128,16,128]{2,1,0:T(8,128)(2,1)} %get-tuple-element.34), channel_id=1, source_target_pairs={{0,1},{1,0},{2,3},{3,2},{4,5},{5,4},{6,7},{7,6},{8,9},{9,8},{10,11... | collective-permute-start | bytes 1572872 | tf_op jit(solution)/shard_map/ppermute | solution.py:352
  26.3 11.0 %collective-permute-start.5 = (s32[1032,128]{1,0:T(8,128)S(1)}, s32[1032,128]{1,0:T(8,128)S(1)}, u32[]{:S(2)}, u32[]{:S(2)}) collective-permute-start(s32[1032,128]{1,0:T(8,128)S(1)} %collective-permute-done.4.refs_2_), channel_id=1, source_target_pairs={{0,64},{64,128},{128,192},{192,256},{256,320},{320,384},{384,448},... | collective-permute-start | bytes 1585160 | tf_op jit(solution)/shard_map/ppermute | solution.py:342
  31.2 15.0 %collective-permute-start.3 = (s32[1032,128]{1,0:T(8,128)S(1)}, s32[1032,128]{1,0:T(8,128)S(1)}, u32[]{:S(2)}, u32[]{:S(2)}) collective-permute-start(s32[1032,128]{1,0:T(8,128)S(1)} %collective-permute-done.1.refs_1_), channel_id=1, source_target_pairs={{0,64},{64,128},{128,192},{192,256},{256,320},{320,384},{384,448},... | collective-permute-start | bytes 1585160 | tf_op jit(solution)/shard_map/ppermute | solution.py:342
  37.3 11.3 %collective-permute-start.7 = (s32[1032,128]{1,0:T(8,128)S(1)}, s32[1032,128]{1,0:T(8,128)S(1)}, u32[]{:S(2)}, u32[]{:S(2)}) collective-permute-start(s32[1032,128]{1,0:T(8,128)S(1)} %collective-permute-done.5.refs_2_), channel_id=1, source_target_pairs={{0,64},{64,128},{128,192},{192,256},{256,320},{320,384},{384,448},... | collective-permute-start | bytes 1585160 | tf_op jit(solution)/shard_map/ppermute | solution.py:342
  42.3 1.0 %copy-start.1 = (bf16[128,16,128]{2,1,0:T(8,128)(2,1)S(1)}, bf16[128,16,128]{2,1,0:T(8,128)(2,1)}, u32[]{:S(2)}) copy-start(bf16[128,16,128]{2,1,0:T(8,128)(2,1)} %get-tuple-element.36.refs_4_) | copy-start | bytes 1572868
  46.2 10.3 %collective-permute-start.6 = (s32[1032,128]{1,0:T(8,128)S(1)}, s32[1032,128]{1,0:T(8,128)S(1)}, u32[]{:S(2)}, u32[]{:S(2)}) collective-permute-start(s32[1032,128]{1,0:T(8,128)S(1)} %collective-permute-done.3.refs_1_), channel_id=1, source_target_pairs={{0,64},{64,128},{128,192},{192,256},{256,320},{320,384},{384,448},... | collective-permute-start | bytes 1585160 | tf_op jit(solution)/shard_map/ppermute | solution.py:342
  48.6 7.9 %copy-start = (s32[1032,128]{1,0:T(8,128)S(1)}, s32[1032,128]{1,0:T(8,128)}, u32[]{:S(2)}) copy-start(s32[1032,128]{1,0:T(8,128)} %pack.2.refs_2_) | copy-start | bytes 1585156
  57.9 6.0 %collective-permute-start.8 = (bf16[32,16,256]{2,1,0:T(8,128)(2,1)S(1)}, bf16[32,16,256]{2,1,0:T(8,128)(2,1)S(1)}, u32[]{:S(2)}, u32[]{:S(2)}) collective-permute-start(bf16[32,16,256]{2,1,0:T(8,128)(2,1)S(1)} %get-tuple-element.49), channel_id=1, source_target_pairs={{0,1},{1,0},{2,3},{3,2},{4,5},{5,4},{6,7},{7,6},{8,9},{9,8},{10,11... | collective-permute-start | bytes 786440 | tf_op jit(solution)/shard_map/ppermute | solution.py:367
  63.9 8.9 %copy-start.3 = (bf16[16,128,128]{2,1,0:T(8,128)(2,1)S(1)}, bf16[16,128,128]{2,1,0:T(8,128)(2,1)}, u32[]{:S(2)}) copy-start(bf16[16,128,128]{2,1,0:T(8,128)(2,1)} %out_ref.1) | copy-start | bytes 1572868
  63.9 8.9 %copy-start.7 = (s32[16]{0:T(128)S(1)}, s32[16]{0:T(128)}, u32[]{:S(2)}) copy-start(s32[16]{0:T(128)} %cells_ref.1) | copy-start | bytes 196
  64.7 8.1 %copy-start.2 = (bf16[16,128,128]{2,1,0:T(8,128)(2,1)S(1)}, bf16[16,128,128]{2,1,0:T(8,128)(2,1)}, u32[]{:S(2)}) copy-start(bf16[16,128,128]{2,1,0:T(8,128)(2,1)} %in_ref.1) | copy-start | bytes 1572868
  64.7 19.6 %all-to-all-start = ((bf16[32,16,256]{2,1,0:T(8,128)(2,1)}), bf16[32,16,256]{2,1,0:T(8,128)(2,1)S(1)}, u32[]{:S(2)}, u32[]{:S(2)}) async-start(bf16[32,16,256]{2,1,0:T(8,128)(2,1)} %add_convert_fusion), calls=%async_computation | async-start | bytes 524288 | tf_op jit(solution)/shard_map/all_to_all | solution.py:368
  72.8 11.6 %copy-start.4 = (bf16[2,512,1,16]{1,3,2,0:T(8,128)(2,1)S(1)}, bf16[2,512,1,16]{1,3,2,0:T(8,128)(2,1)}, u32[]{:S(2)}) copy-start(bf16[2,512,1,16]{1,3,2,0:T(8,128)(2,1)} %param.22) | copy-start | bytes 98308
  72.8 11.5 %copy-start.5 = (bf16[2,512,1,16]{1,3,2,0:T(8,128)(2,1)S(1)}, bf16[2,512,1,16]{1,3,2,0:T(8,128)(2,1)}, u32[]{:S(2)}) copy-start(bf16[2,512,1,16]{1,3,2,0:T(8,128)(2,1)} %param.23) | copy-start | bytes 98308
  85.7 15.8 %all-to-all-start.1 = ((f32[64,1,128]{2,1,0:T(1,128)}), f32[64,1,128]{2,1,0:T(1,128)S(1)}, u32[]{:S(2)}, u32[]{:S(2)}) async-start(f32[64,1,128]{2,1,0:T(1,128)} %get-tuple-element.55), calls=%async_computation.1 | async-start | bytes 65536 | tf_op jit(solution)/shard_map/all_to_all | solution.py:370

commit v11 on v10

--- a/solution.py
+++ b/solution.py
@@ -166,7 +166,8 @@
 
 def channel_kernel(step, *refs):
     first, last = step == 0, step == STEPS - 1
-    core_ref, *words, refs = refs[0], refs[1], refs[2], refs[3:]
+    count = (3, 2, 2, 1)[step]
+    core_ref, words, refs = refs[0], refs[1 : 1 + count], refs[1 + count :]
     if first:
         down_scale_ref, *team, acc_ref, bias_ref, scaled_ref, bounds_ref, down, up = refs
         for k, got_ref in enumerate(team):
@@ -200,11 +201,19 @@
     scale = [chunk[1024 + h : 1025 + h] for chunk in words for h in range(2)]
     scale = jnp.concatenate(scale, axis=1).astype(F32) * (1.0 / SCALE_ONE)
     pre = jnp.dot(scaled_ref[...], down[...], preferred_element_type=F32)
-    pre = pre.reshape(SPEC, SHARED, PART)
-    mid, terms = relaxed(pre, *(bounds_ref[step, kind] for kind in range(4)))
-    terms = jnp.sum(terms.reshape(SPEC, SHARED // 8, 8, PART), axis=1)
-    bias = sum(terms[:, :, k * 128 : (k + 1) * 128] for k in range(PART // 128))
-    weighted = (mid.reshape(ROWS_DEV, PART) * scale).astype(BF16)
+    width = count * CHUNK
+    pre = pre.reshape(SPEC, SHARED, width)
+    if first:
+        bounds = [
+            jnp.concatenate([bounds_ref[0, kind], bounds_ref[STEPS - 1, kind, :, CHUNK:PART]], axis=1)
+            for kind in range(4)
+        ]
+    else:
+        bounds = [bounds_ref[step, kind, :, 0:width] for kind in range(4)]
+    mid, terms = relaxed(pre, *bounds)
+    terms = jnp.sum(terms.reshape(SPEC, SHARED // 8, 8, width), axis=1)
+    bias = sum(terms[:, :, k * 128 : (k + 1) * 128] for k in range(width // 128))
+    weighted = (mid.reshape(ROWS_DEV, width) * scale).astype(BF16)
     part = jnp.dot(weighted, up[...], preferred_element_type=F32)
     total = acc_in[...] + part
     if not first:
@@ -226,6 +235,7 @@
     acc_shape = jax.ShapeDtypeStruct((ROWS_DEV, D), F32)
     bias_shape = jax.ShapeDtypeStruct((SPEC, 8, 128), F32)
     operands = [core, *rest]
+    width = (3, 2, 2, 1)[step] * CHUNK
     aliases = {}
     if step == 0:
         scaled_shape = jax.ShapeDtypeStruct((ROWS_DEV, D), BF16)
@@ -246,11 +256,11 @@
         out_shape=out_shape,
         in_specs=[smem] + [vmem] * (len(operands) - 1),
         out_specs=(vmem,) * len(out_shape),
-        scratch_shapes=[pltpu.VMEM((D, PART), BF16), pltpu.VMEM((PART, D), BF16)],
+        scratch_shapes=[pltpu.VMEM((D, width), BF16), pltpu.VMEM((width, D), BF16)],
         input_output_aliases=aliases,
         compiler_params=pltpu.CompilerParams(vmem_limit_bytes=VMEM),
         cost_estimate=pl.CostEstimate(
-            flops=4 * ROWS_DEV * PART * D,
+            flops=4 * ROWS_DEV * width * D,
             bytes_accessed=2 * PACKED * 128 * 4 + 3 * ROWS_DEV * D * 4,
             transcendentals=0,
         ),
@@ -352,18 +362,17 @@
     other_part = lax.ppermute(send_part, "core", SWAP)
     words, other_part = lax.optimization_barrier((second[0], other_part))
     third = forward((words, second[1]), ahead + behind)
-    carried = channel_part(0, core, *first, down_scale.reshape(1, D), keep_part, other_part)
+    carried = channel_part(0, core, *first, own[0], down_scale.reshape(1, D), keep_part, other_part)
     acc, chan_bias, *given = carried
     acc, chan_bias = channel_part(1, core, *second, *given, acc, chan_bias)
-    words, acc = lax.optimization_barrier((third[0], acc))
-    far = forward((words,), ahead + behind)
+    far = forward(third[:1], ahead + behind)
 
     dense_in, dense_out = dense_blocks(block_cells, tok_in_blocks, tok_out_blocks)
     slopes = jnp.transpose(tok_slopes, (0, 2, 3, 1)).reshape(2, 16, TH)
     icpt = jnp.transpose(tok_icpt, (0, 2, 3, 1)).reshape(2, 16, TH)
 
     acc, chan_bias = channel_part(2, core, *third, *given, acc, chan_bias)
-    keep, send, chan_bias = channel_part(3, core, *far, own[0], *given, acc, chan_bias)
+    keep, send, chan_bias = channel_part(3, core, *far, *given, acc, chan_bias)
     summed = (keep + lax.ppermute(send, "core", SWAP).astype(F32)).astype(BF16)
     got = lax.all_to_all(summed, ("z", "x"), 0, 0, tiled=True)
     columns, mid, own_bias = token_mlp(got, dense_out, slopes, icpt, chan_bias)

time: 103 us -> 102 us (level)
  waiting for transfers between devices: 31.4 us -> 25.5 us
  starting transfers between devices: 50.9 us -> 56 us
    ppermute x7, waiting for transfers between devices: 11.2 us -> 5.29 us  [forward(): return tuple((lax.ppermute(w, ('rows', 'core'), pairs) for w in words))]
    ppermute x7, starting transfers between devices: 25.8 us -> 28.8 us  [forward(): return tuple((lax.ppermute(w, ('rows', 'core'), pairs) for w in words))]
    ppermute x1, starting transfers between devices: 4.83 us -> 7.03 us  [on_device(): summed = (keep + lax.ppermute(send, 'core', SWAP).astype(F32)).astype(BF16)]
  transfers between devices with their start and end apart: 11 -> 11, of which waited for: 6 -> 6; matrix products, arithmetic and copies ran while one was open for 1% -> 1% of each run, Pallas kernels for 10% -> 11%
where the time goes in v11:
time: 102 us; the launch traced here: 101 us
  starting transfers between devices  56 us (55%)
  waiting for transfers between devices  25.5 us (25%)
  Pallas kernels  15.7 us (15%)
  local copies, waits for them, and re-layouts  1.92 us (2%)
  other arithmetic  1.39 us (1%)
    ppermute x7, starting transfers between devices, forward(): return tuple((lax.ppermute(w, ('rows', 'core'), pairs) for w in words))  28.8 us
    all_to_all x1, waiting for transfers between devices, on_device(): got = lax.all_to_all(summed, ('z', 'x'), 0, 0, tiled=True)  10.6 us
    all_to_all x1, waiting for transfers between devices, on_device(): all_bias = lax.all_to_all(own_bias, MP, 0, 0, tiled=True)  8.43 us
    all_to_all x1, starting transfers between devices, on_device(): got = lax.all_to_all(summed, ('z', 'x'), 0, 0, tiled=True)  7.89 us
    ppermute x1, starting transfers between devices, on_device(): summed = (keep + lax.ppermute(send, 'core', SWAP).astype(F32)).astype(BF16)  7.03 us
    all_to_all x1, starting transfers between devices, on_device(): all_bias = lax.all_to_all(own_bias, MP, 0, 0, tiled=True)  6.32 us
    ppermute x1, starting transfers between devices, on_device(): other_part = lax.ppermute(send_part, 'core', SWAP)  5.93 us
    pallas_call x4, Pallas kernels, channel_part(): pl.pallas_call(functools.partial(channel_kernel, step), out_shape=out_sha...  5.7 us
  transfers between devices with their start and end apart: 11, of which 6 were waited for; matrix products, arithmetic and copies ran while one was open for 1% of the time, Pallas kernels for 11%

profile of v11, /device:TPU:1, one launch (start us, length us, event | category | flops | bytes accessed | tf_op | source)
XLA Modules:
  0.0 101.4 jit_solution(12131092897281886910)
XLA Ops:
  0.6 2.2 %pack.2.refs_3_ = s32[1032,128]{1,0:T(8,128)} custom-call(s32[1]{0:T(128)} %bitcast.core_ref.refs_0_, bf16[1024,512]{1,0:T(8,128)(2,1)} %down_hbm.3, bf16[512,1024]{1,0:T(8,128)(2,1)} %up_hbm.3, f32[1,512]{1,0:T(1,128)} %bitcast.30), custom_call_target="tpu_custom_call" | custom-call | tf_op jit(solution)/shard_map/pack/pallas_call | solution.py:76
  2.9 0.0 copy-start.8
  2.9 6.1 %collective-permute-start = (s32[1032,128]{1,0:T(8,128)}, s32[1032,128]{1,0:T(8,128)S(1)}, u32[]{:S(2)}, u32[]{:S(2)}) collective-permute-start(s32[1032,128]{1,0:T(8,128)} %pack.2.refs_3_), channel_id=1, source_target_pairs={{0,64},{64,128},{128,192},{192,256},{256,320},{320,384},{384,448},... | collective-permute-start | bytes 1585160 | tf_op jit(solution)/shard_map/ppermute | solution.py:352
  9.0 2.2 %pack.3 = s32[1032,128]{1,0:T(8,128)} custom-call(s32[1]{0:T(128)} %bitcast.core_ref.refs_0_, bf16[1024,512]{1,0:T(8,128)(2,1)} %down_hbm.3, bf16[512,1024]{1,0:T(8,128)(2,1)} %up_hbm.3, f32[1,512]{1,0:T(1,128)} %bitcast.31), custom_call_target="tpu_custom_call" | custom-call | tf_op jit(solution)/shard_map/pack/pallas_call | solution.py:76
  11.2 3.0 %collective-permute-start.5 = (s32[1032,128]{1,0:T(8,128)}, s32[1032,128]{1,0:T(8,128)S(1)}, u32[]{:S(2)}, u32[]{:S(2)}) collective-permute-start(s32[1032,128]{1,0:T(8,128)} %pack.3), channel_id=1, source_target_pairs={{0,64},{64,128},{128,192},{192,256},{256,320},{320,384},{384,448},... | collective-permute-start | bytes 1585160 | tf_op jit(solution)/shard_map/ppermute | solution.py:352
  14.2 0.0 copy-done.8
  14.2 0.9 copy.22
  15.1 2.3 %share.1 = (bf16[128,16,128]{2,1,0:T(8,128)(2,1)}, bf16[128,16,128]{2,1,0:T(8,128)(2,1)}) custom-call(s32[1]{0:T(128)} %bitcast.core_ref.refs_0_, s32[1]{0:T(128)} %bitcast.2.row_ref, bf16[8,16,1024]{2,1,0:T(8,128)(2,1)} %bitcast.26, bf16[2,16,4096]{2,1,0:T(8,128)(2,1)} %bitcast.27, bf16[2,16,4096]{2,1,0:T(8,128)(2,1)} %bitcast.28), custom_call_target="tpu_custom_call" | custom-call | tf_op jit(solution)/shard_map/share/pallas_call | solution.py:157
  17.3 0.0 collective-permute-done.refs_1_
  17.3 3.0 %collective-permute-start.1 = (s32[1032,128]{1,0:T(8,128)S(1)}, s32[1032,128]{1,0:T(8,128)S(1)}, u32[]{:S(2)}, u32[]{:S(2)}) collective-permute-start(s32[1032,128]{1,0:T(8,128)S(1)} %collective-permute-done.refs_1_), channel_id=1, source_target_pairs={{0,64},{64,128},{128,192},{192,256},{256,320},{320,384},{384,448},... | collective-permute-start | bytes 1585160 | tf_op jit(solution)/shard_map/ppermute | solution.py:352
  20.3 5.9 %collective-permute-start.2 = (bf16[128,16,128]{2,1,0:T(8,128)(2,1)}, bf16[128,16,128]{2,1,0:T(8,128)(2,1)S(1)}, u32[]{:S(2)}, u32[]{:S(2)}) collective-permute-start(bf16[128,16,128]{2,1,0:T(8,128)(2,1)} %get-tuple-element.32), channel_id=1, source_target_pairs={{0,1},{1,0},{2,3},{3,2},{4,5},{5,4},{6,7},{7,6},{8,9},{9,8},{10,11... | collective-permute-start | bytes 1572872 | tf_op jit(solution)/shard_map/ppermute | solution.py:362
  26.3 0.0 collective-permute-done.5.refs_2_
  26.3 4.9 %collective-permute-start.6 = (s32[1032,128]{1,0:T(8,128)S(1)}, s32[1032,128]{1,0:T(8,128)S(1)}, u32[]{:S(2)}, u32[]{:S(2)}) collective-permute-start(s32[1032,128]{1,0:T(8,128)S(1)} %collective-permute-done.5.refs_2_), channel_id=1, source_target_pairs={{0,64},{64,128},{128,192},{192,256},{256,320},{320,384},{384,448},... | collective-permute-start | bytes 1585160 | tf_op jit(solution)/shard_map/ppermute | solution.py:352
  31.1 0.0 collective-permute-done.2.refs_6_
  31.2 0.0 collective-permute-done.1.refs_1_
  31.2 1.9 %collective-permute-start.3 = (s32[1032,128]{1,0:T(8,128)S(1)}, s32[1032,128]{1,0:T(8,128)S(1)}, u32[]{:S(2)}, u32[]{:S(2)}) collective-permute-start(s32[1032,128]{1,0:T(8,128)S(1)} %collective-permute-done.1.refs_1_), channel_id=1, source_target_pairs={{0,64},{64,128},{128,192},{192,256},{256,320},{320,384},{384,448},... | collective-permute-start | bytes 1585160 | tf_op jit(solution)/shard_map/ppermute | solution.py:352
  33.1 4.2 %collective-permute-done.6.refs_2_ = s32[1032,128]{1,0:T(8,128)S(1)} collective-permute-done((s32[1032,128]{1,0:T(8,128)S(1)}, s32[1032,128]{1,0:T(8,128)S(1)}, u32[]{:S(2)}, u32[]{:S(2)}) %collective-permute-start.6) | collective-permute-done | bytes 528416 | tf_op jit(solution)/shard_map/ppermute | solution.py:352
  37.3 5.0 %collective-permute-start.7 = (s32[1032,128]{1,0:T(8,128)S(1)}, s32[1032,128]{1,0:T(8,128)S(1)}, u32[]{:S(2)}, u32[]{:S(2)}) collective-permute-start(s32[1032,128]{1,0:T(8,128)S(1)} %collective-permute-done.6.refs_2_), channel_id=1, source_target_pairs={{0,64},{64,128},{128,192},{192,256},{256,320},{320,384},{384,448},... | collective-permute-start | bytes 1585160 | tf_op jit(solution)/shard_map/ppermute | solution.py:352
  42.3 0.6 collective-permute-done.3.refs_1_
  43.0 5.0 %collective-permute-start.4 = (s32[1032,128]{1,0:T(8,128)S(1)}, s32[1032,128]{1,0:T(8,128)S(1)}, u32[]{:S(2)}, u32[]{:S(2)}) collective-permute-start(s32[1032,128]{1,0:T(8,128)S(1)} %collective-permute-done.3.refs_1_), channel_id=1, source_target_pairs={{0,64},{64,128},{128,192},{192,256},{256,320},{320,384},{384,448},... | collective-permute-start | bytes 1585160 | tf_op jit(solution)/shard_map/ppermute | solution.py:352
  48.0 0.0 copy-done
  48.0 0.0 copy-done.7
  48.0 0.0 copy-start.6
  48.0 1.0 %copy-done.6 = bf16[128,16,128]{2,1,0:T(8,128)(2,1)S(1)} copy-done((bf16[128,16,128]{2,1,0:T(8,128)(2,1)S(1)}, bf16[128,16,128]{2,1,0:T(8,128)(2,1)}, u32[]{:S(2)}) %copy-start.6) | copy-done | bytes 524312
  49.0 2.1 %channel.4 = (f32[256,1024]{1,0:T(8,128)S(1)}, f32[8,8,128]{2,1,0:T(8,128)S(1)}, bf16[256,1024]{1,0:T(8,128)(2,1)S(1)}, bf16[4,4,32,512]{3,2,1,0:T(8,128)(2,1)S(1)}) custom-call(s32[1]{0:T(128)} %bitcast.core_ref.refs_0_, s32[1032,128]{1,0:T(8,128)S(1)} %collective-permute-done.refs_1_, s32[1032,128]{1,0:T(8,128)S(1)} %collective-permute-done.5.refs_2_, ...), custom_call_target="tpu_custom_call" | custom-call | flops 805306368 | bytes 4202496 | tf_op jit(solution)/shard_map/channel/pallas_call | solution.py:254
  51.1 1.3 %channel.5 = (f32[256,1024]{1,0:T(8,128)S(1)}, f32[8,8,128]{2,1,0:T(8,128)S(1)}) custom-call(s32[1]{0:T(128)} %bitcast.core_ref.refs_0_, s32[1032,128]{1,0:T(8,128)S(1)} %collective-permute-done.1.refs_1_, s32[1032,128]{1,0:T(8,128)S(1)} %collective-permute-done.6.refs_2_, ...), custom_call_target="tpu_custom_call", output_to_operand_aliasing={{0}: (5, {}), {1}: (6, {})} | custom-call | flops 536870912 | bytes 4202496 | tf_op jit(solution)/shard_map/channel/pallas_call | solution.py:254
  52.5 0.0 collective-permute-done.7.refs_2_
  52.5 1.4 %channel.6 = (f32[256,1024]{1,0:T(8,128)S(1)}, f32[8,8,128]{2,1,0:T(8,128)S(1)}) custom-call(s32[1]{0:T(128)} %bitcast.core_ref.refs_0_, s32[1032,128]{1,0:T(8,128)S(1)} %collective-permute-done.3.refs_1_, s32[1032,128]{1,0:T(8,128)S(1)} %collective-permute-done.7.refs_2_, ...), custom_call_target="tpu_custom_call", output_to_operand_aliasing={{0}: (5, {}), {1}: (6, {})} | custom-call | flops 536870912 | bytes 4202496 | tf_op jit(solution)/shard_map/channel/pallas_call | solution.py:254
  53.8 0.4 collective-permute-done.4.refs_1_
  54.3 0.9 channel.7
  55.2 7.0 %collective-permute-start.8 = (bf16[32,16,256]{2,1,0:T(8,128)(2,1)S(1)}, bf16[32,16,256]{2,1,0:T(8,128)(2,1)S(1)}, u32[]{:S(2)}, u32[]{:S(2)}) collective-permute-start(bf16[32,16,256]{2,1,0:T(8,128)(2,1)S(1)} %get-tuple-element.45), channel_id=1, source_target_pairs={{0,1},{1,0},{2,3},{3,2},{4,5},{5,4},{6,7},{7,6},{8,9},{9,8},{10,11... | collective-permute-start | bytes 786440 | tf_op jit(solution)/shard_map/ppermute | solution.py:376
  62.3 1.1 %collective-permute-done.8 = bf16[32,16,256]{2,1,0:T(8,128)(2,1)S(1)} collective-permute-done((bf16[32,16,256]{2,1,0:T(8,128)(2,1)S(1)}, bf16[32,16,256]{2,1,0:T(8,128)(2,1)S(1)}, u32[]{:S(2)}, u32[]{:S(2)}) %collective-permute-start.8) | collective-permute-done | bytes 262176 | tf_op jit(solution)/shard_map/ppermute | solution.py:376
  63.4 0.8 add_convert_fusion
  64.2 7.9 %all-to-all-start = ((bf16[32,16,256]{2,1,0:T(8,128)(2,1)}), bf16[32,16,256]{2,1,0:T(8,128)(2,1)S(1)}, u32[]{:S(2)}, u32[]{:S(2)}) async-start(bf16[32,16,256]{2,1,0:T(8,128)(2,1)} %add_convert_fusion), calls=%async_computation | async-start | bytes 524288 | tf_op jit(solution)/shard_map/all_to_all | solution.py:377
  72.1 0.0 copy-done.2
  72.1 0.0 copy-done.5
  72.1 0.0 copy-done.1
  72.1 0.0 copy-start.3
  72.1 0.0 copy-start.4
  72.1 0.9 dense.1
  73.1 10.6 %all-to-all-done.got_ref = bf16[32,16,256]{2,1,0:T(8,128)(2,1)S(1)} async-done(((bf16[32,16,256]{2,1,0:T(8,128)(2,1)}), bf16[32,16,256]{2,1,0:T(8,128)(2,1)S(1)}, u32[]{:S(2)}, u32[]{:S(2)}) %all-to-all-start) | async-done | bytes 262176 | tf_op jit(solution)/shard_map/all_to_all | solution.py:377
  83.7 0.0 copy-done.3
  83.7 0.0 copy-done.4
  83.7 1.3 %token_.1 = (bf16[128,1024]{1,0:T(8,128)(2,1)S(1)}, bf16[128,512]{1,0:T(8,128)(2,1)S(1)}, f32[64,1,128]{2,1,0:T(1,128)}) custom-call(bf16[32,16,256]{2,1,0:T(8,128)(2,1)S(1)} %all-to-all-done.got_ref, bf16[1024,512]{1,0:T(8,128)(2,1)S(1)} %get-tuple-element.46.dense_ref, bf16[2,16,512]{2,1,0:T(8,128)(2,1)S(1)} %bitcast.23, bf16[2,16,512]{2,1,0:T(8,128)(2,1)S(1)} %bitcast.24, ...), custom_call_target="tpu_custom_call" | custom-call | tf_op jit(solution)/shard_map/token/pallas_call | solution.py:304
  85.0 6.3 %all-to-all-start.1 = ((f32[64,1,128]{2,1,0:T(1,128)}), f32[64,1,128]{2,1,0:T(1,128)S(1)}, u32[]{:S(2)}, u32[]{:S(2)}) async-start(f32[64,1,128]{2,1,0:T(1,128)} %get-tuple-element.51), calls=%async_computation.1 | async-start | bytes 65536 | tf_op jit(solution)/shard_map/all_to_all | solution.py:379
  91.3 1.0 %back.1 = bf16[128,1024]{1,0:T(8,128)(2,1)} custom-call(bf16[128,1024]{1,0:T(8,128)(2,1)S(1)} %get-tuple-element.48.columns_ref, bf16[128,512]{1,0:T(8,128)(2,1)S(1)} %get-tuple-element.49.mid_ref, bf16[512,1024]{1,0:T(8,128)(2,1)S(1)} %get-tuple-element.50.dense_ref), custom_call_target="tpu_custom_call" | custom-call | tf_op jit(solution)/shard_map/back/pallas_call | solution.py:322
  92.4 8.4 %all-to-all-done.1 = f32[64,1,128]{2,1,0:T(1,128)S(1)} async-done(((f32[64,1,128]{2,1,0:T(1,128)}), f32[64,1,128]{2,1,0:T(1,128)S(1)}, u32[]{:S(2)}, u32[]{:S(2)}) %all-to-all-start.1) | async-done | bytes 32800 | tf_op jit(solution)/shard_map/all_to_all | solution.py:379
  100.8 0.6 reduce_sum.9
  (5 shorter events, 0.0 us)
Async XLA Ops:
  2.9 11.3 %copy-start.8 = (bf16[16,8,1024]{2,1,0:T(8,128)(2,1)S(1)}, bf16[16,8,1024]{2,1,0:T(8,128)(2,1)}, u32[]{:S(2)}) copy-start(bf16[16,8,1024]{2,1,0:T(8,128)(2,1)} %param.12) | copy-start | bytes 786436
  2.9 14.4 %collective-permute-start = (s32[1032,128]{1,0:T(8,128)}, s32[1032,128]{1,0:T(8,128)S(1)}, u32[]{:S(2)}, u32[]{:S(2)}) collective-permute-start(s32[1032,128]{1,0:T(8,128)} %pack.2.refs_3_), channel_id=1, source_target_pairs={{0,64},{64,128},{128,192},{192,256},{256,320},{320,384},{384,448},... | collective-permute-start | bytes 1585160 | tf_op jit(solution)/shard_map/ppermute | solution.py:352
  11.2 15.1 %collective-permute-start.5 = (s32[1032,128]{1,0:T(8,128)}, s32[1032,128]{1,0:T(8,128)S(1)}, u32[]{:S(2)}, u32[]{:S(2)}) collective-permute-start(s32[1032,128]{1,0:T(8,128)} %pack.3), channel_id=1, source_target_pairs={{0,64},{64,128},{128,192},{192,256},{256,320},{320,384},{384,448},... | collective-permute-start | bytes 1585160 | tf_op jit(solution)/shard_map/ppermute | solution.py:352
  15.1 32.9 %copy-start = (s32[1032,128]{1,0:T(8,128)S(1)}, s32[1032,128]{1,0:T(8,128)}, u32[]{:S(2)}) copy-start(s32[1032,128]{1,0:T(8,128)} %pack.2.refs_3_) | copy-start | bytes 1585156
  17.3 30.7 %copy-start.7 = (f32[1024]{0:T(1024)S(1)}, f32[1024]{0:T(1024)}, u32[]{:S(2)}) copy-start(f32[1024]{0:T(1024)} %param.14) | copy-start | bytes 12292
  17.3 13.8 %collective-permute-start.1 = (s32[1032,128]{1,0:T(8,128)S(1)}, s32[1032,128]{1,0:T(8,128)S(1)}, u32[]{:S(2)}, u32[]{:S(2)}) collective-permute-start(s32[1032,128]{1,0:T(8,128)S(1)} %collective-permute-done.refs_1_), channel_id=1, source_target_pairs={{0,64},{64,128},{128,192},{192,256},{256,320},{320,384},{384,448},... | collective-permute-start | bytes 1585160 | tf_op jit(solution)/shard_map/ppermute | solution.py:352
  20.3 10.8 %collective-permute-start.2 = (bf16[128,16,128]{2,1,0:T(8,128)(2,1)}, bf16[128,16,128]{2,1,0:T(8,128)(2,1)S(1)}, u32[]{:S(2)}, u32[]{:S(2)}) collective-permute-start(bf16[128,16,128]{2,1,0:T(8,128)(2,1)} %get-tuple-element.32), channel_id=1, source_target_pairs={{0,1},{1,0},{2,3},{3,2},{4,5},{5,4},{6,7},{7,6},{8,9},{9,8},{10,11... | collective-permute-start | bytes 1572872 | tf_op jit(solution)/shard_map/ppermute | solution.py:362
  26.3 11.0 %collective-permute-start.6 = (s32[1032,128]{1,0:T(8,128)S(1)}, s32[1032,128]{1,0:T(8,128)S(1)}, u32[]{:S(2)}, u32[]{:S(2)}) collective-permute-start(s32[1032,128]{1,0:T(8,128)S(1)} %collective-permute-done.5.refs_2_), channel_id=1, source_target_pairs={{0,64},{64,128},{128,192},{192,256},{256,320},{320,384},{384,448},... | collective-permute-start | bytes 1585160 | tf_op jit(solution)/shard_map/ppermute | solution.py:352
  31.2 11.8 %collective-permute-start.3 = (s32[1032,128]{1,0:T(8,128)S(1)}, s32[1032,128]{1,0:T(8,128)S(1)}, u32[]{:S(2)}, u32[]{:S(2)}) collective-permute-start(s32[1032,128]{1,0:T(8,128)S(1)} %collective-permute-done.1.refs_1_), channel_id=1, source_target_pairs={{0,64},{64,128},{128,192},{192,256},{256,320},{320,384},{384,448},... | collective-permute-start | bytes 1585160 | tf_op jit(solution)/shard_map/ppermute | solution.py:352
  37.3 15.2 %collective-permute-start.7 = (s32[1032,128]{1,0:T(8,128)S(1)}, s32[1032,128]{1,0:T(8,128)S(1)}, u32[]{:S(2)}, u32[]{:S(2)}) collective-permute-start(s32[1032,128]{1,0:T(8,128)S(1)} %collective-permute-done.6.refs_2_), channel_id=1, source_target_pairs={{0,64},{64,128},{128,192},{192,256},{256,320},{320,384},{384,448},... | collective-permute-start | bytes 1585160 | tf_op jit(solution)/shard_map/ppermute | solution.py:352
  43.0 11.3 %collective-permute-start.4 = (s32[1032,128]{1,0:T(8,128)S(1)}, s32[1032,128]{1,0:T(8,128)S(1)}, u32[]{:S(2)}, u32[]{:S(2)}) collective-permute-start(s32[1032,128]{1,0:T(8,128)S(1)} %collective-permute-done.3.refs_1_), channel_id=1, source_target_pairs={{0,64},{64,128},{128,192},{192,256},{256,320},{320,384},{384,448},... | collective-permute-start | bytes 1585160 | tf_op jit(solution)/shard_map/ppermute | solution.py:352
  48.0 1.0 %copy-start.6 = (bf16[128,16,128]{2,1,0:T(8,128)(2,1)S(1)}, bf16[128,16,128]{2,1,0:T(8,128)(2,1)}, u32[]{:S(2)}) copy-start(bf16[128,16,128]{2,1,0:T(8,128)(2,1)} %get-tuple-element.34.refs_5_) | copy-start | bytes 1572868
  55.2 8.2 %collective-permute-start.8 = (bf16[32,16,256]{2,1,0:T(8,128)(2,1)S(1)}, bf16[32,16,256]{2,1,0:T(8,128)(2,1)S(1)}, u32[]{:S(2)}, u32[]{:S(2)}) collective-permute-start(bf16[32,16,256]{2,1,0:T(8,128)(2,1)S(1)} %get-tuple-element.45), channel_id=1, source_target_pairs={{0,1},{1,0},{2,3},{3,2},{4,5},{5,4},{6,7},{7,6},{8,9},{9,8},{10,11... | collective-permute-start | bytes 786440 | tf_op jit(solution)/shard_map/ppermute | solution.py:376
  63.4 8.7 %copy-start.2 = (bf16[16,128,128]{2,1,0:T(8,128)(2,1)S(1)}, bf16[16,128,128]{2,1,0:T(8,128)(2,1)}, u32[]{:S(2)}) copy-start(bf16[16,128,128]{2,1,0:T(8,128)(2,1)} %out_ref.1) | copy-start | bytes 1572868
  63.4 8.7 %copy-start.5 = (s32[16]{0:T(128)S(1)}, s32[16]{0:T(128)}, u32[]{:S(2)}) copy-start(s32[16]{0:T(128)} %cells_ref.1) | copy-start | bytes 196
  64.2 7.9 %copy-start.1 = (bf16[16,128,128]{2,1,0:T(8,128)(2,1)S(1)}, bf16[16,128,128]{2,1,0:T(8,128)(2,1)}, u32[]{:S(2)}) copy-start(bf16[16,128,128]{2,1,0:T(8,128)(2,1)} %in_ref.1) | copy-start | bytes 1572868
  64.2 19.5 %all-to-all-start = ((bf16[32,16,256]{2,1,0:T(8,128)(2,1)}), bf16[32,16,256]{2,1,0:T(8,128)(2,1)S(1)}, u32[]{:S(2)}, u32[]{:S(2)}) async-start(bf16[32,16,256]{2,1,0:T(8,128)(2,1)} %add_convert_fusion), calls=%async_computation | async-start | bytes 524288 | tf_op jit(solution)/shard_map/all_to_all | solution.py:377
  72.1 11.6 %copy-start.3 = (bf16[2,512,1,16]{1,3,2,0:T(8,128)(2,1)S(1)}, bf16[2,512,1,16]{1,3,2,0:T(8,128)(2,1)}, u32[]{:S(2)}) copy-start(bf16[2,512,1,16]{1,3,2,0:T(8,128)(2,1)} %param.22) | copy-start | bytes 98308
  72.1 11.5 %copy-start.4 = (bf16[2,512,1,16]{1,3,2,0:T(8,128)(2,1)S(1)}, bf16[2,512,1,16]{1,3,2,0:T(8,128)(2,1)}, u32[]{:S(2)}) copy-start(bf16[2,512,1,16]{1,3,2,0:T(8,128)(2,1)} %param.23) | copy-start | bytes 98308
  85.0 15.8 %all-to-all-start.1 = ((f32[64,1,128]{2,1,0:T(1,128)}), f32[64,1,128]{2,1,0:T(1,128)S(1)}, u32[]{:S(2)}, u32[]{:S(2)}) async-start(f32[64,1,128]{2,1,0:T(1,128)} %get-tuple-element.51), calls=%async_computation.1 | async-start | bytes 65536 | tf_op jit(solution)/shard_map/all_to_all | solution.py:379

commit v12 on v11

--- a/solution.py
+++ b/solution.py
@@ -219,11 +219,8 @@
     if not first:
         bias = bias + bias_in[...]
     if last:
-        keep_ref, send_ref, bias_ref = outs
-        own = core_ref[0] == 0
-        turned = total.T.reshape(32, 2, 16, ROWS_DEV)
-        keep_ref[...] = jnp.where(own, turned[:, 0], turned[:, 1])
-        send_ref[...] = jnp.where(own, turned[:, 1], turned[:, 0]).astype(BF16)
+        part_ref, bias_ref = outs
+        part_ref[...] = total.T.reshape(64, 16, ROWS_DEV).astype(BF16)
     else:
         if not first:
             acc_ref, bias_ref = outs
@@ -242,11 +239,7 @@
         bounds_shape = jax.ShapeDtypeStruct((STEPS, 4, SHARED, PART), BF16)
         out_shape = (acc_shape, bias_shape, scaled_shape, bounds_shape)
     elif step == STEPS - 1:
-        out_shape = (
-            jax.ShapeDtypeStruct((32, 16, ROWS_DEV), F32),
-            jax.ShapeDtypeStruct((32, 16, ROWS_DEV), BF16),
-            bias_shape,
-        )
+        out_shape = (jax.ShapeDtypeStruct((64, 16, ROWS_DEV), BF16), bias_shape)
     else:
         out_shape = (acc_shape, bias_shape)
         aliases = {len(operands) - 2: 0, len(operands) - 1: 1}
@@ -274,7 +267,11 @@
     lane = lax.broadcasted_iota(I32, (16, 128), 1) // 32
     for u in range(NTB):
         for a in range(2):
-            v = [got_ref[4 * u + p, :, a * 128 : (a + 1) * 128].astype(F32) for p in range(4)]
+            cut = slice(a * 128, (a + 1) * 128)
+            v = [
+                got_ref[s, :, cut].astype(F32) + got_ref[s + 1, :, cut].astype(F32)
+                for s in range(8 * u, 8 * u + 8, 2)
+            ]
             for bit in (1, 2):
                 low = (lane & bit) == 0
                 new = list(v)
@@ -372,9 +369,8 @@
     icpt = jnp.transpose(tok_icpt, (0, 2, 3, 1)).reshape(2, 16, TH)
 
     acc, chan_bias = channel_part(2, core, *third, *given, acc, chan_bias)
-    keep, send, chan_bias = channel_part(3, core, *far, *given, acc, chan_bias)
-    summed = (keep + lax.ppermute(send, "core", SWAP).astype(F32)).astype(BF16)
-    got = lax.all_to_all(summed, ("z", "x"), 0, 0, tiled=True)
+    parts, chan_bias = channel_part(3, core, *far, *given, acc, chan_bias)
+    got = lax.all_to_all(parts, MP, 0, 0, tiled=True)
     columns, mid, own_bias = token_mlp(got, dense_out, slopes, icpt, chan_bias)
     all_bias = lax.all_to_all(own_bias, MP, 0, 0, tiled=True)
     lam_in = token_back(columns, mid, dense_in)

time: 102 us -> 105 us (1.029)
  waiting for transfers between devices: 25.5 us -> 29.4 us
  starting transfers between devices: 56 us -> 54 us
    ppermute x1 -> x0, starting transfers between devices: 7.03 us -> none  [on_device(): summed = (keep + lax.ppermute(send, 'core', SWAP).astype(F32)).astype(BF16)]
    all_to_all x1, starting transfers between devices: 7.89 us -> 13.5 us  [on_device(): got = lax.all_to_all(parts, MP, 0, 0, tiled=True)]
    all_to_all x1, waiting for transfers between devices: 10.6 us -> 15.7 us  [on_device(): got = lax.all_to_all(parts, MP, 0, 0, tiled=True)]
    ppermute x1 -> x0, waiting for transfers between devices: 1.14 us -> none  [on_device(): summed = (keep + lax.ppermute(send, 'core', SWAP).astype(F32)).astype(BF16)]
  transfers between devices with their start and end apart: 11 -> 10, of which waited for: 6 -> 5; matrix products, arithmetic and copies ran while one was open for 1% -> 1% of each run, Pallas kernels for 11% -> 11%
where the time goes in v12:
time: 105 us; the launch traced here: 104 us
  starting transfers between devices  54 us (51%)
  waiting for transfers between devices  29.4 us (28%)
  Pallas kernels  16.5 us (16%)
  local copies, waits for them, and re-layouts  2.95 us (3%)
    ppermute x7, starting transfers between devices, forward(): return tuple((lax.ppermute(w, ('rows', 'core'), pairs) for w in words))  28.9 us
    all_to_all x1, waiting for transfers between devices, on_device(): got = lax.all_to_all(parts, MP, 0, 0, tiled=True)  15.7 us
    all_to_all x1, starting transfers between devices, on_device(): got = lax.all_to_all(parts, MP, 0, 0, tiled=True)  13.5 us
    all_to_all x1, waiting for transfers between devices, on_device(): all_bias = lax.all_to_all(own_bias, MP, 0, 0, tiled=True)  8.36 us
    pallas_call x4, Pallas kernels, channel_part(): pl.pallas_call(functools.partial(channel_kernel, step), out_shape=out_sha...  6.51 us
    ppermute x1, starting transfers between devices, on_device(): other_part = lax.ppermute(send_part, 'core', SWAP)  5.93 us
    all_to_all x1, starting transfers between devices, on_device(): all_bias = lax.all_to_all(own_bias, MP, 0, 0, tiled=True)  5.72 us
    ppermute x7, waiting for transfers between devices, forward(): return tuple((lax.ppermute(w, ('rows', 'core'), pairs) for w in words))  5.29 us
  transfers between devices with their start and end apart: 10, of which 5 were waited for; matrix products, arithmetic and copies ran while one was open for 1% of the time, Pallas kernels for 11%

profile of v12, /device:TPU:1, one launch (start us, length us, event | category | flops | bytes accessed | tf_op | source)
XLA Modules:
  0.0 104.2 jit_solution(4070685000500556936)
XLA Ops:
  0.6 2.2 %pack.2.refs_3_ = s32[1032,128]{1,0:T(8,128)} custom-call(s32[1]{0:T(128)} %bitcast.core_ref.refs_0_, bf16[1024,512]{1,0:T(8,128)(2,1)} %down_hbm.3, bf16[512,1024]{1,0:T(8,128)(2,1)} %up_hbm.3, f32[1,512]{1,0:T(1,128)} %bitcast.30), custom_call_target="tpu_custom_call" | custom-call | tf_op jit(solution)/shard_map/pack/pallas_call | solution.py:76
  2.9 0.0 copy-start.8
  2.9 6.1 %collective-permute-start = (s32[1032,128]{1,0:T(8,128)}, s32[1032,128]{1,0:T(8,128)S(1)}, u32[]{:S(2)}, u32[]{:S(2)}) collective-permute-start(s32[1032,128]{1,0:T(8,128)} %pack.2.refs_3_), channel_id=1, source_target_pairs={{0,64},{64,128},{128,192},{192,256},{256,320},{320,384},{384,448},... | collective-permute-start | bytes 1585160 | tf_op jit(solution)/shard_map/ppermute | solution.py:349
  8.9 2.2 %pack.3 = s32[1032,128]{1,0:T(8,128)} custom-call(s32[1]{0:T(128)} %bitcast.core_ref.refs_0_, bf16[1024,512]{1,0:T(8,128)(2,1)} %down_hbm.3, bf16[512,1024]{1,0:T(8,128)(2,1)} %up_hbm.3, f32[1,512]{1,0:T(1,128)} %bitcast.31), custom_call_target="tpu_custom_call" | custom-call | tf_op jit(solution)/shard_map/pack/pallas_call | solution.py:76
  11.2 3.0 %collective-permute-start.5 = (s32[1032,128]{1,0:T(8,128)}, s32[1032,128]{1,0:T(8,128)S(1)}, u32[]{:S(2)}, u32[]{:S(2)}) collective-permute-start(s32[1032,128]{1,0:T(8,128)} %pack.3), channel_id=1, source_target_pairs={{0,64},{64,128},{128,192},{192,256},{256,320},{320,384},{384,448},... | collective-permute-start | bytes 1585160 | tf_op jit(solution)/shard_map/ppermute | solution.py:349
  14.2 0.0 copy-done.8
  14.2 0.9 copy.22
  15.0 0.0 copy-start
  15.0 2.3 %share.1 = (bf16[128,16,128]{2,1,0:T(8,128)(2,1)}, bf16[128,16,128]{2,1,0:T(8,128)(2,1)}) custom-call(s32[1]{0:T(128)} %bitcast.core_ref.refs_0_, s32[1]{0:T(128)} %bitcast.2.row_ref, bf16[8,16,1024]{2,1,0:T(8,128)(2,1)} %bitcast.26, bf16[2,16,4096]{2,1,0:T(8,128)(2,1)} %bitcast.27, bf16[2,16,4096]{2,1,0:T(8,128)(2,1)} %bitcast.28), custom_call_target="tpu_custom_call" | custom-call | tf_op jit(solution)/shard_map/share/pallas_call | solution.py:157
  17.3 0.0 copy-start.7
  17.3 0.0 collective-permute-done.refs_1_
  17.3 3.0 %collective-permute-start.1 = (s32[1032,128]{1,0:T(8,128)S(1)}, s32[1032,128]{1,0:T(8,128)S(1)}, u32[]{:S(2)}, u32[]{:S(2)}) collective-permute-start(s32[1032,128]{1,0:T(8,128)S(1)} %collective-permute-done.refs_1_), channel_id=1, source_target_pairs={{0,64},{64,128},{128,192},{192,256},{256,320},{320,384},{384,448},... | collective-permute-start | bytes 1585160 | tf_op jit(solution)/shard_map/ppermute | solution.py:349
  20.3 5.9 %collective-permute-start.2 = (bf16[128,16,128]{2,1,0:T(8,128)(2,1)}, bf16[128,16,128]{2,1,0:T(8,128)(2,1)S(1)}, u32[]{:S(2)}, u32[]{:S(2)}) collective-permute-start(bf16[128,16,128]{2,1,0:T(8,128)(2,1)} %get-tuple-element.31), channel_id=1, source_target_pairs={{0,1},{1,0},{2,3},{3,2},{4,5},{5,4},{6,7},{7,6},{8,9},{9,8},{10,11... | collective-permute-start | bytes 1572872 | tf_op jit(solution)/shard_map/ppermute | solution.py:359
  26.3 0.0 collective-permute-done.5.refs_2_
  26.3 4.9 %collective-permute-start.6 = (s32[1032,128]{1,0:T(8,128)S(1)}, s32[1032,128]{1,0:T(8,128)S(1)}, u32[]{:S(2)}, u32[]{:S(2)}) collective-permute-start(s32[1032,128]{1,0:T(8,128)S(1)} %collective-permute-done.5.refs_2_), channel_id=1, source_target_pairs={{0,64},{64,128},{128,192},{192,256},{256,320},{320,384},{384,448},... | collective-permute-start | bytes 1585160 | tf_op jit(solution)/shard_map/ppermute | solution.py:349
  31.1 0.0 collective-permute-done.2.refs_6_
  31.1 0.0 collective-permute-done.1.refs_1_
  31.2 1.9 %collective-permute-start.3 = (s32[1032,128]{1,0:T(8,128)S(1)}, s32[1032,128]{1,0:T(8,128)S(1)}, u32[]{:S(2)}, u32[]{:S(2)}) collective-permute-start(s32[1032,128]{1,0:T(8,128)S(1)} %collective-permute-done.1.refs_1_), channel_id=1, source_target_pairs={{0,64},{64,128},{128,192},{192,256},{256,320},{320,384},{384,448},... | collective-permute-start | bytes 1585160 | tf_op jit(solution)/shard_map/ppermute | solution.py:349
  33.1 4.2 %collective-permute-done.6.refs_2_ = s32[1032,128]{1,0:T(8,128)S(1)} collective-permute-done((s32[1032,128]{1,0:T(8,128)S(1)}, s32[1032,128]{1,0:T(8,128)S(1)}, u32[]{:S(2)}, u32[]{:S(2)}) %collective-permute-start.6) | collective-permute-done | bytes 528416 | tf_op jit(solution)/shard_map/ppermute | solution.py:349
  37.3 5.0 %collective-permute-start.7 = (s32[1032,128]{1,0:T(8,128)S(1)}, s32[1032,128]{1,0:T(8,128)S(1)}, u32[]{:S(2)}, u32[]{:S(2)}) collective-permute-start(s32[1032,128]{1,0:T(8,128)S(1)} %collective-permute-done.6.refs_2_), channel_id=1, source_target_pairs={{0,64},{64,128},{128,192},{192,256},{256,320},{320,384},{384,448},... | collective-permute-start | bytes 1585160 | tf_op jit(solution)/shard_map/ppermute | solution.py:349
  42.3 0.6 collective-permute-done.3.refs_1_
  42.9 5.0 %collective-permute-start.4 = (s32[1032,128]{1,0:T(8,128)S(1)}, s32[1032,128]{1,0:T(8,128)S(1)}, u32[]{:S(2)}, u32[]{:S(2)}) collective-permute-start(s32[1032,128]{1,0:T(8,128)S(1)} %collective-permute-done.3.refs_1_), channel_id=1, source_target_pairs={{0,64},{64,128},{128,192},{192,256},{256,320},{320,384},{384,448},... | collective-permute-start | bytes 1585160 | tf_op jit(solution)/shard_map/ppermute | solution.py:349
  48.0 0.0 copy-done
  48.0 0.0 copy-done.7
  48.0 0.0 copy-start.6
  48.0 1.0 copy-done.6
  49.0 2.1 %channel.4 = (f32[256,1024]{1,0:T(8,128)S(1)}, f32[8,8,128]{2,1,0:T(8,128)S(1)}, bf16[256,1024]{1,0:T(8,128)(2,1)S(1)}, bf16[4,4,32,512]{3,2,1,0:T(8,128)(2,1)S(1)}) custom-call(s32[1]{0:T(128)} %bitcast.core_ref.refs_0_, s32[1032,128]{1,0:T(8,128)S(1)} %collective-permute-done.refs_1_, s32[1032,128]{1,0:T(8,128)S(1)} %collective-permute-done.5.refs_2_, ...), custom_call_target="tpu_custom_call" | custom-call | flops 805306368 | bytes 4202496 | tf_op jit(solution)/shard_map/channel/pallas_call | solution.py:247
  51.1 1.3 %channel.5 = (f32[256,1024]{1,0:T(8,128)S(1)}, f32[8,8,128]{2,1,0:T(8,128)S(1)}) custom-call(s32[1]{0:T(128)} %bitcast.core_ref.refs_0_, s32[1032,128]{1,0:T(8,128)S(1)} %collective-permute-done.1.refs_1_, s32[1032,128]{1,0:T(8,128)S(1)} %collective-permute-done.6.refs_2_, ...), custom_call_target="tpu_custom_call", output_to_operand_aliasing={{0}: (5, {}), {1}: (6, {})} | custom-call | flops 536870912 | bytes 4202496 | tf_op jit(solution)/shard_map/channel/pallas_call | solution.py:247
  52.5 0.0 collective-permute-done.7.refs_2_
  52.5 1.4 %channel.6 = (f32[256,1024]{1,0:T(8,128)S(1)}, f32[8,8,128]{2,1,0:T(8,128)S(1)}) custom-call(s32[1]{0:T(128)} %bitcast.core_ref.refs_0_, s32[1032,128]{1,0:T(8,128)S(1)} %collective-permute-done.3.refs_1_, s32[1032,128]{1,0:T(8,128)S(1)} %collective-permute-done.7.refs_2_, ...), custom_call_target="tpu_custom_call", output_to_operand_aliasing={{0}: (5, {}), {1}: (6, {})} | custom-call | flops 536870912 | bytes 4202496 | tf_op jit(solution)/shard_map/channel/pallas_call | solution.py:247
  53.8 0.4 collective-permute-done.4.refs_1_
  54.3 1.7 %channel.7 = (bf16[64,16,256]{2,1,0:T(8,128)(2,1)}, f32[8,8,128]{2,1,0:T(8,128)S(1)}) custom-call(s32[1]{0:T(128)} %bitcast.core_ref.refs_0_, s32[1032,128]{1,0:T(8,128)S(1)} %collective-permute-done.4.refs_1_, bf16[256,1024]{1,0:T(8,128)(2,1)S(1)} %get-tuple-element.35.refs_3_.refs_2_, bf16[4,4,32,512]{3,2,1,0:T(8,128)(2,1)S(1)} %get-tuple-element.36.refs_4_.refs_3_, ...), custom_call_target="tpu_custom_call" | custom-call | flops 268435456 | bytes 4202496 | tf_op jit(solution)/shard_map/channel/pallas_call | solution.py:247
  56.0 0.0 copy-start.1
  56.0 0.0 copy-start.5
  56.0 13.5 %all-to-all-start = ((bf16[64,16,256]{2,1,0:T(8,128)(2,1)}), bf16[64,16,256]{2,1,0:T(8,128)(2,1)S(1)}, u32[]{:S(2)}, u32[]{:S(2)}) async-start(bf16[64,16,256]{2,1,0:T(8,128)(2,1)} %get-tuple-element.43), calls=%async_computation | async-start | bytes 1048576 | tf_op jit(solution)/shard_map/all_to_all | solution.py:373
  69.5 0.0 copy-done.1
  69.5 0.0 copy-done.5
  69.5 0.0 copy-start.2
  69.5 1.0 copy-done.2
  70.5 0.9 dense.1
  71.5 15.7 %all-to-all-done.got_ref = bf16[64,16,256]{2,1,0:T(8,128)(2,1)S(1)} async-done(((bf16[64,16,256]{2,1,0:T(8,128)(2,1)}), bf16[64,16,256]{2,1,0:T(8,128)(2,1)S(1)}, u32[]{:S(2)}, u32[]{:S(2)}) %all-to-all-start) | async-done | bytes 524320 | tf_op jit(solution)/shard_map/all_to_all | solution.py:373
  87.2 0.0 copy-done.3
  87.2 0.0 copy-done.4
  87.2 1.3 %token_.1 = (bf16[128,1024]{1,0:T(8,128)(2,1)S(1)}, bf16[128,512]{1,0:T(8,128)(2,1)S(1)}, f32[64,1,128]{2,1,0:T(1,128)}) custom-call(bf16[64,16,256]{2,1,0:T(8,128)(2,1)S(1)} %all-to-all-done.got_ref, bf16[1024,512]{1,0:T(8,128)(2,1)S(1)} %get-tuple-element.44.dense_ref, bf16[2,16,512]{2,1,0:T(8,128)(2,1)S(1)} %bitcast.23, bf16[2,16,512]{2,1,0:T(8,128)(2,1)S(1)} %bitcast.24, ...), custom_call_target="tpu_custom_call" | custom-call | tf_op jit(solution)/shard_map/token/pallas_call | solution.py:301
  88.5 5.7 %all-to-all-start.1 = ((f32[64,1,128]{2,1,0:T(1,128)}), f32[64,1,128]{2,1,0:T(1,128)S(1)}, u32[]{:S(2)}, u32[]{:S(2)}) async-start(f32[64,1,128]{2,1,0:T(1,128)} %get-tuple-element.49), calls=%async_computation.1 | async-start | bytes 65536 | tf_op jit(solution)/shard_map/all_to_all | solution.py:375
  94.3 1.0 back.1
  95.3 8.4 %all-to-all-done.1 = f32[64,1,128]{2,1,0:T(1,128)S(1)} async-done(((f32[64,1,128]{2,1,0:T(1,128)}), f32[64,1,128]{2,1,0:T(1,128)S(1)}, u32[]{:S(2)}, u32[]{:S(2)}) %all-to-all-start.1) | async-done | bytes 32800 | tf_op jit(solution)/shard_map/all_to_all | solution.py:375
  103.6 0.6 reduce_sum.9
  (2 shorter events, 0.0 us)
Async XLA Ops:
  2.9 11.3 %copy-start.8 = (bf16[16,8,1024]{2,1,0:T(8,128)(2,1)S(1)}, bf16[16,8,1024]{2,1,0:T(8,128)(2,1)}, u32[]{:S(2)}) copy-start(bf16[16,8,1024]{2,1,0:T(8,128)(2,1)} %param.12) | copy-start | bytes 786436
  2.9 14.4 %collective-permute-start = (s32[1032,128]{1,0:T(8,128)}, s32[1032,128]{1,0:T(8,128)S(1)}, u32[]{:S(2)}, u32[]{:S(2)}) collective-permute-start(s32[1032,128]{1,0:T(8,128)} %pack.2.refs_3_), channel_id=1, source_target_pairs={{0,64},{64,128},{128,192},{192,256},{256,320},{320,384},{384,448},... | collective-permute-start | bytes 1585160 | tf_op jit(solution)/shard_map/ppermute | solution.py:349
  11.2 15.1 %collective-permute-start.5 = (s32[1032,128]{1,0:T(8,128)}, s32[1032,128]{1,0:T(8,128)S(1)}, u32[]{:S(2)}, u32[]{:S(2)}) collective-permute-start(s32[1032,128]{1,0:T(8,128)} %pack.3), channel_id=1, source_target_pairs={{0,64},{64,128},{128,192},{192,256},{256,320},{320,384},{384,448},... | collective-permute-start | bytes 1585160 | tf_op jit(solution)/shard_map/ppermute | solution.py:349
  15.0 32.9 %copy-start = (s32[1032,128]{1,0:T(8,128)S(1)}, s32[1032,128]{1,0:T(8,128)}, u32[]{:S(2)}) copy-start(s32[1032,128]{1,0:T(8,128)} %pack.2.refs_3_) | copy-start | bytes 1585156
  17.3 30.7 %copy-start.7 = (f32[1024]{0:T(1024)S(1)}, f32[1024]{0:T(1024)}, u32[]{:S(2)}) copy-start(f32[1024]{0:T(1024)} %param.14) | copy-start | bytes 12292
  17.3 13.8 %collective-permute-start.1 = (s32[1032,128]{1,0:T(8,128)S(1)}, s32[1032,128]{1,0:T(8,128)S(1)}, u32[]{:S(2)}, u32[]{:S(2)}) collective-permute-start(s32[1032,128]{1,0:T(8,128)S(1)} %collective-permute-done.refs_1_), channel_id=1, source_target_pairs={{0,64},{64,128},{128,192},{192,256},{256,320},{320,384},{384,448},... | collective-permute-start | bytes 1585160 | tf_op jit(solution)/shard_map/ppermute | solution.py:349
  20.3 10.8 %collective-permute-start.2 = (bf16[128,16,128]{2,1,0:T(8,128)(2,1)}, bf16[128,16,128]{2,1,0:T(8,128)(2,1)S(1)}, u32[]{:S(2)}, u32[]{:S(2)}) collective-permute-start(bf16[128,16,128]{2,1,0:T(8,128)(2,1)} %get-tuple-element.31), channel_id=1, source_target_pairs={{0,1},{1,0},{2,3},{3,2},{4,5},{5,4},{6,7},{7,6},{8,9},{9,8},{10,11... | collective-permute-start | bytes 1572872 | tf_op jit(solution)/shard_map/ppermute | solution.py:359
  26.3 11.0 %collective-permute-start.6 = (s32[1032,128]{1,0:T(8,128)S(1)}, s32[1032,128]{1,0:T(8,128)S(1)}, u32[]{:S(2)}, u32[]{:S(2)}) collective-permute-start(s32[1032,128]{1,0:T(8,128)S(1)} %collective-permute-done.5.refs_2_), channel_id=1, source_target_pairs={{0,64},{64,128},{128,192},{192,256},{256,320},{320,384},{384,448},... | collective-permute-start | bytes 1585160 | tf_op jit(solution)/shard_map/ppermute | solution.py:349
  31.2 11.8 %collective-permute-start.3 = (s32[1032,128]{1,0:T(8,128)S(1)}, s32[1032,128]{1,0:T(8,128)S(1)}, u32[]{:S(2)}, u32[]{:S(2)}) collective-permute-start(s32[1032,128]{1,0:T(8,128)S(1)} %collective-permute-done.1.refs_1_), channel_id=1, source_target_pairs={{0,64},{64,128},{128,192},{192,256},{256,320},{320,384},{384,448},... | collective-permute-start | bytes 1585160 | tf_op jit(solution)/shard_map/ppermute | solution.py:349
  37.3 15.2 %collective-permute-start.7 = (s32[1032,128]{1,0:T(8,128)S(1)}, s32[1032,128]{1,0:T(8,128)S(1)}, u32[]{:S(2)}, u32[]{:S(2)}) collective-permute-start(s32[1032,128]{1,0:T(8,128)S(1)} %collective-permute-done.6.refs_2_), channel_id=1, source_target_pairs={{0,64},{64,128},{128,192},{192,256},{256,320},{320,384},{384,448},... | collective-permute-start | bytes 1585160 | tf_op jit(solution)/shard_map/ppermute | solution.py:349
  42.9 11.3 %collective-permute-start.4 = (s32[1032,128]{1,0:T(8,128)S(1)}, s32[1032,128]{1,0:T(8,128)S(1)}, u32[]{:S(2)}, u32[]{:S(2)}) collective-permute-start(s32[1032,128]{1,0:T(8,128)S(1)} %collective-permute-done.3.refs_1_), channel_id=1, source_target_pairs={{0,64},{64,128},{128,192},{192,256},{256,320},{320,384},{384,448},... | collective-permute-start | bytes 1585160 | tf_op jit(solution)/shard_map/ppermute | solution.py:349
  48.0 1.0 %copy-start.6 = (bf16[128,16,128]{2,1,0:T(8,128)(2,1)S(1)}, bf16[128,16,128]{2,1,0:T(8,128)(2,1)}, u32[]{:S(2)}) copy-start(bf16[128,16,128]{2,1,0:T(8,128)(2,1)} %get-tuple-element.33.refs_5_) | copy-start | bytes 1572868
  56.0 13.5 %copy-start.1 = (bf16[16,128,128]{2,1,0:T(8,128)(2,1)S(1)}, bf16[16,128,128]{2,1,0:T(8,128)(2,1)}, u32[]{:S(2)}) copy-start(bf16[16,128,128]{2,1,0:T(8,128)(2,1)} %in_ref.1) | copy-start | bytes 1572868
  56.0 13.5 %copy-start.5 = (s32[16]{0:T(128)S(1)}, s32[16]{0:T(128)}, u32[]{:S(2)}) copy-start(s32[16]{0:T(128)} %cells_ref.1) | copy-start | bytes 196
  56.0 31.2 %all-to-all-start = ((bf16[64,16,256]{2,1,0:T(8,128)(2,1)}), bf16[64,16,256]{2,1,0:T(8,128)(2,1)S(1)}, u32[]{:S(2)}, u32[]{:S(2)}) async-start(bf16[64,16,256]{2,1,0:T(8,128)(2,1)} %get-tuple-element.43), calls=%async_computation | async-start | bytes 1048576 | tf_op jit(solution)/shard_map/all_to_all | solution.py:373
  69.5 1.0 %copy-start.2 = (bf16[16,128,128]{2,1,0:T(8,128)(2,1)S(1)}, bf16[16,128,128]{2,1,0:T(8,128)(2,1)}, u32[]{:S(2)}) copy-start(bf16[16,128,128]{2,1,0:T(8,128)(2,1)} %out_ref.1) | copy-start | bytes 1572868
  70.5 16.7 %copy-start.3 = (bf16[2,512,1,16]{1,3,2,0:T(8,128)(2,1)S(1)}, bf16[2,512,1,16]{1,3,2,0:T(8,128)(2,1)}, u32[]{:S(2)}) copy-start(bf16[2,512,1,16]{1,3,2,0:T(8,128)(2,1)} %param.22) | copy-start | bytes 98308
  70.5 16.7 %copy-start.4 = (bf16[2,512,1,16]{1,3,2,0:T(8,128)(2,1)S(1)}, bf16[2,512,1,16]{1,3,2,0:T(8,128)(2,1)}, u32[]{:S(2)}) copy-start(bf16[2,512,1,16]{1,3,2,0:T(8,128)(2,1)} %param.23) | copy-start | bytes 98308
  88.5 15.1 %all-to-all-start.1 = ((f32[64,1,128]{2,1,0:T(1,128)}), f32[64,1,128]{2,1,0:T(1,128)S(1)}, u32[]{:S(2)}, u32[]{:S(2)}) async-start(f32[64,1,128]{2,1,0:T(1,128)} %get-tuple-element.49), calls=%async_computation.1 | async-start | bytes 65536 | tf_op jit(solution)/shard_map/all_to_all | solution.py:375

commit v13 on v11

--- a/solution.py
+++ b/solution.py
@@ -221,9 +221,11 @@
     if last:
         keep_ref, send_ref, bias_ref = outs
         own = core_ref[0] == 0
-        turned = total.T.reshape(32, 2, 16, ROWS_DEV)
-        keep_ref[...] = jnp.where(own, turned[:, 0], turned[:, 1])
-        send_ref[...] = jnp.where(own, turned[:, 1], turned[:, 0]).astype(BF16)
+        turned = total.T.reshape(8, 4, 2, 16, ROWS_DEV)
+        for x in range(4):
+            chips = slice(x * 8, (x + 1) * 8)
+            keep_ref[chips] = jnp.where(own, turned[:, x, 0], turned[:, x, 1])
+            send_ref[chips] = jnp.where(own, turned[:, x, 1], turned[:, x, 0]).astype(BF16)
     else:
         if not first:
             acc_ref, bias_ref = outs
@@ -274,7 +276,7 @@
     lane = lax.broadcasted_iota(I32, (16, 128), 1) // 32
     for u in range(NTB):
         for a in range(2):
-            v = [got_ref[4 * u + p, :, a * 128 : (a + 1) * 128].astype(F32) for p in range(4)]
+            v = [got_ref[8 * p + u, :, a * 128 : (a + 1) * 128].astype(F32) for p in range(4)]
             for bit in (1, 2):
                 low = (lane & bit) == 0
                 new = list(v)
@@ -374,7 +376,7 @@
     acc, chan_bias = channel_part(2, core, *third, *given, acc, chan_bias)
     keep, send, chan_bias = channel_part(3, core, *far, *given, acc, chan_bias)
     summed = (keep + lax.ppermute(send, "core", SWAP).astype(F32)).astype(BF16)
-    got = lax.all_to_all(summed, ("z", "x"), 0, 0, tiled=True)
+    got = lax.all_to_all(summed, ("x", "z"), 0, 0, tiled=True)
     columns, mid, own_bias = token_mlp(got, dense_out, slopes, icpt, chan_bias)
     all_bias = lax.all_to_all(own_bias, MP, 0, 0, tiled=True)
     lam_in = token_back(columns, mid, dense_in)

time: 102 us -> 102 us (level)
  starting transfers between devices: 56 us -> 58 us
  waiting for transfers between devices: 25.5 us -> 23.5 us
    all_to_all x1, starting transfers between devices: 6.32 us -> 8.29 us  [on_device(): all_bias = lax.all_to_all(own_bias, MP, 0, 0, tiled=True)]
    all_to_all x1, waiting for transfers between devices: 10.6 us -> 8.7 us  [on_device(): got = lax.all_to_all(summed, ('x', 'z'), 0, 0, tiled=True)]
where the time goes in v13:
time: 102 us; the launch traced here: 101 us
  starting transfers between devices  58 us (57%)
  waiting for transfers between devices  23.5 us (23%)
  Pallas kernels  15.7 us (15%)
  local copies, waits for them, and re-layouts  1.92 us (2%)
  other arithmetic  1.39 us (1%)
    ppermute x7, starting transfers between devices, forward(): return tuple((lax.ppermute(w, ('rows', 'core'), pairs) for w in words))  28.8 us
    all_to_all x1, waiting for transfers between devices, on_device(): got = lax.all_to_all(summed, ('x', 'z'), 0, 0, tiled=True)  8.7 us
    all_to_all x1, waiting for transfers between devices, on_device(): all_bias = lax.all_to_all(own_bias, MP, 0, 0, tiled=True)  8.36 us
    all_to_all x1, starting transfers between devices, on_device(): all_bias = lax.all_to_all(own_bias, MP, 0, 0, tiled=True)  8.29 us
    all_to_all x1, starting transfers between devices, on_device(): got = lax.all_to_all(summed, ('x', 'z'), 0, 0, tiled=True)  7.89 us
    ppermute x1, starting transfers between devices, on_device(): summed = (keep + lax.ppermute(send, 'core', SWAP).astype(F32)).astype(BF16)  7.03 us
    ppermute x1, starting transfers between devices, on_device(): other_part = lax.ppermute(send_part, 'core', SWAP)  5.93 us
    pallas_call x4, Pallas kernels, channel_part(): pl.pallas_call(functools.partial(channel_kernel, step), out_shape=out_sha...  5.7 us
  transfers between devices with their start and end apart: 11, of which 6 were waited for; matrix products, arithmetic and copies ran while one was open for 1% of the time, Pallas kernels for 11%

profile of v13, /device:TPU:1, one launch (start us, length us, event | category | flops | bytes accessed | tf_op | source)
XLA Modules:
  0.0 101.4 jit_solution(16575753640209743284)
XLA Ops:
  0.6 2.2 %pack.2.refs_3_ = s32[1032,128]{1,0:T(8,128)} custom-call(s32[1]{0:T(128)} %bitcast.core_ref.refs_0_, bf16[1024,512]{1,0:T(8,128)(2,1)} %down_hbm.3, bf16[512,1024]{1,0:T(8,128)(2,1)} %up_hbm.3, f32[1,512]{1,0:T(1,128)} %bitcast.30), custom_call_target="tpu_custom_call" | custom-call | tf_op jit(solution)/shard_map/pack/pallas_call | solution.py:76
  2.9 0.0 copy-start.8
  2.9 6.1 %collective-permute-start = (s32[1032,128]{1,0:T(8,128)}, s32[1032,128]{1,0:T(8,128)S(1)}, u32[]{:S(2)}, u32[]{:S(2)}) collective-permute-start(s32[1032,128]{1,0:T(8,128)} %pack.2.refs_3_), channel_id=1, source_target_pairs={{0,64},{64,128},{128,192},{192,256},{256,320},{320,384},{384,448},... | collective-permute-start | bytes 1585160 | tf_op jit(solution)/shard_map/ppermute | solution.py:354
  9.0 2.2 %pack.3 = s32[1032,128]{1,0:T(8,128)} custom-call(s32[1]{0:T(128)} %bitcast.core_ref.refs_0_, bf16[1024,512]{1,0:T(8,128)(2,1)} %down_hbm.3, bf16[512,1024]{1,0:T(8,128)(2,1)} %up_hbm.3, f32[1,512]{1,0:T(1,128)} %bitcast.31), custom_call_target="tpu_custom_call" | custom-call | tf_op jit(solution)/shard_map/pack/pallas_call | solution.py:76
  11.2 3.0 %collective-permute-start.5 = (s32[1032,128]{1,0:T(8,128)}, s32[1032,128]{1,0:T(8,128)S(1)}, u32[]{:S(2)}, u32[]{:S(2)}) collective-permute-start(s32[1032,128]{1,0:T(8,128)} %pack.3), channel_id=1, source_target_pairs={{0,64},{64,128},{128,192},{192,256},{256,320},{320,384},{384,448},... | collective-permute-start | bytes 1585160 | tf_op jit(solution)/shard_map/ppermute | solution.py:354
  14.2 0.0 copy-done.8
  14.2 0.9 copy.22
  15.1 2.3 %share.1 = (bf16[128,16,128]{2,1,0:T(8,128)(2,1)}, bf16[128,16,128]{2,1,0:T(8,128)(2,1)}) custom-call(s32[1]{0:T(128)} %bitcast.core_ref.refs_0_, s32[1]{0:T(128)} %bitcast.2.row_ref, bf16[8,16,1024]{2,1,0:T(8,128)(2,1)} %bitcast.26, bf16[2,16,4096]{2,1,0:T(8,128)(2,1)} %bitcast.27, bf16[2,16,4096]{2,1,0:T(8,128)(2,1)} %bitcast.28), custom_call_target="tpu_custom_call" | custom-call | tf_op jit(solution)/shard_map/share/pallas_call | solution.py:157
  17.3 0.0 collective-permute-done.refs_1_
  17.3 3.0 %collective-permute-start.1 = (s32[1032,128]{1,0:T(8,128)S(1)}, s32[1032,128]{1,0:T(8,128)S(1)}, u32[]{:S(2)}, u32[]{:S(2)}) collective-permute-start(s32[1032,128]{1,0:T(8,128)S(1)} %collective-permute-done.refs_1_), channel_id=1, source_target_pairs={{0,64},{64,128},{128,192},{192,256},{256,320},{320,384},{384,448},... | collective-permute-start | bytes 1585160 | tf_op jit(solution)/shard_map/ppermute | solution.py:354
  20.3 5.9 %collective-permute-start.2 = (bf16[128,16,128]{2,1,0:T(8,128)(2,1)}, bf16[128,16,128]{2,1,0:T(8,128)(2,1)S(1)}, u32[]{:S(2)}, u32[]{:S(2)}) collective-permute-start(bf16[128,16,128]{2,1,0:T(8,128)(2,1)} %get-tuple-element.32), channel_id=1, source_target_pairs={{0,1},{1,0},{2,3},{3,2},{4,5},{5,4},{6,7},{7,6},{8,9},{9,8},{10,11... | collective-permute-start | bytes 1572872 | tf_op jit(solution)/shard_map/ppermute | solution.py:364
  26.3 0.0 collective-permute-done.5.refs_2_
  26.3 4.9 %collective-permute-start.6 = (s32[1032,128]{1,0:T(8,128)S(1)}, s32[1032,128]{1,0:T(8,128)S(1)}, u32[]{:S(2)}, u32[]{:S(2)}) collective-permute-start(s32[1032,128]{1,0:T(8,128)S(1)} %collective-permute-done.5.refs_2_), channel_id=1, source_target_pairs={{0,64},{64,128},{128,192},{192,256},{256,320},{320,384},{384,448},... | collective-permute-start | bytes 1585160 | tf_op jit(solution)/shard_map/ppermute | solution.py:354
  31.1 0.0 collective-permute-done.2.refs_6_
  31.2 0.0 collective-permute-done.1.refs_1_
  31.2 1.9 %collective-permute-start.3 = (s32[1032,128]{1,0:T(8,128)S(1)}, s32[1032,128]{1,0:T(8,128)S(1)}, u32[]{:S(2)}, u32[]{:S(2)}) collective-permute-start(s32[1032,128]{1,0:T(8,128)S(1)} %collective-permute-done.1.refs_1_), channel_id=1, source_target_pairs={{0,64},{64,128},{128,192},{192,256},{256,320},{320,384},{384,448},... | collective-permute-start | bytes 1585160 | tf_op jit(solution)/shard_map/ppermute | solution.py:354
  33.1 4.2 %collective-permute-done.6.refs_2_ = s32[1032,128]{1,0:T(8,128)S(1)} collective-permute-done((s32[1032,128]{1,0:T(8,128)S(1)}, s32[1032,128]{1,0:T(8,128)S(1)}, u32[]{:S(2)}, u32[]{:S(2)}) %collective-permute-start.6) | collective-permute-done | bytes 528416 | tf_op jit(solution)/shard_map/ppermute | solution.py:354
  37.3 5.0 %collective-permute-start.7 = (s32[1032,128]{1,0:T(8,128)S(1)}, s32[1032,128]{1,0:T(8,128)S(1)}, u32[]{:S(2)}, u32[]{:S(2)}) collective-permute-start(s32[1032,128]{1,0:T(8,128)S(1)} %collective-permute-done.6.refs_2_), channel_id=1, source_target_pairs={{0,64},{64,128},{128,192},{192,256},{256,320},{320,384},{384,448},... | collective-permute-start | bytes 1585160 | tf_op jit(solution)/shard_map/ppermute | solution.py:354
  42.3 0.6 collective-permute-done.3.refs_1_
  43.0 5.0 %collective-permute-start.4 = (s32[1032,128]{1,0:T(8,128)S(1)}, s32[1032,128]{1,0:T(8,128)S(1)}, u32[]{:S(2)}, u32[]{:S(2)}) collective-permute-start(s32[1032,128]{1,0:T(8,128)S(1)} %collective-permute-done.3.refs_1_), channel_id=1, source_target_pairs={{0,64},{64,128},{128,192},{192,256},{256,320},{320,384},{384,448},... | collective-permute-start | bytes 1585160 | tf_op jit(solution)/shard_map/ppermute | solution.py:354
  48.0 0.0 copy-done
  48.0 0.0 copy-done.7
  48.0 0.0 copy-start.6
  48.0 1.0 %copy-done.6 = bf16[128,16,128]{2,1,0:T(8,128)(2,1)S(1)} copy-done((bf16[128,16,128]{2,1,0:T(8,128)(2,1)S(1)}, bf16[128,16,128]{2,1,0:T(8,128)(2,1)}, u32[]{:S(2)}) %copy-start.6) | copy-done | bytes 524312
  49.0 2.1 %channel.4 = (f32[256,1024]{1,0:T(8,128)S(1)}, f32[8,8,128]{2,1,0:T(8,128)S(1)}, bf16[256,1024]{1,0:T(8,128)(2,1)S(1)}, bf16[4,4,32,512]{3,2,1,0:T(8,128)(2,1)S(1)}) custom-call(s32[1]{0:T(128)} %bitcast.core_ref.refs_0_, s32[1032,128]{1,0:T(8,128)S(1)} %collective-permute-done.refs_1_, s32[1032,128]{1,0:T(8,128)S(1)} %collective-permute-done.5.refs_2_, ...), custom_call_target="tpu_custom_call" | custom-call | flops 805306368 | bytes 4202496 | tf_op jit(solution)/shard_map/channel/pallas_call | solution.py:256
  51.1 1.3 %channel.5 = (f32[256,1024]{1,0:T(8,128)S(1)}, f32[8,8,128]{2,1,0:T(8,128)S(1)}) custom-call(s32[1]{0:T(128)} %bitcast.core_ref.refs_0_, s32[1032,128]{1,0:T(8,128)S(1)} %collective-permute-done.1.refs_1_, s32[1032,128]{1,0:T(8,128)S(1)} %collective-permute-done.6.refs_2_, ...), custom_call_target="tpu_custom_call", output_to_operand_aliasing={{0}: (5, {}), {1}: (6, {})} | custom-call | flops 536870912 | bytes 4202496 | tf_op jit(solution)/shard_map/channel/pallas_call | solution.py:256
  52.5 0.0 collective-permute-done.7.refs_2_
  52.5 1.4 %channel.6 = (f32[256,1024]{1,0:T(8,128)S(1)}, f32[8,8,128]{2,1,0:T(8,128)S(1)}) custom-call(s32[1]{0:T(128)} %bitcast.core_ref.refs_0_, s32[1032,128]{1,0:T(8,128)S(1)} %collective-permute-done.3.refs_1_, s32[1032,128]{1,0:T(8,128)S(1)} %collective-permute-done.7.refs_2_, ...), custom_call_target="tpu_custom_call", output_to_operand_aliasing={{0}: (5, {}), {1}: (6, {})} | custom-call | flops 536870912 | bytes 4202496 | tf_op jit(solution)/shard_map/channel/pallas_call | solution.py:256
  53.8 0.4 collective-permute-done.4.refs_1_
  54.3 0.9 channel.7
  55.2 7.0 %collective-permute-start.8 = (bf16[32,16,256]{2,1,0:T(8,128)(2,1)S(1)}, bf16[32,16,256]{2,1,0:T(8,128)(2,1)S(1)}, u32[]{:S(2)}, u32[]{:S(2)}) collective-permute-start(bf16[32,16,256]{2,1,0:T(8,128)(2,1)S(1)} %get-tuple-element.45), channel_id=1, source_target_pairs={{0,1},{1,0},{2,3},{3,2},{4,5},{5,4},{6,7},{7,6},{8,9},{9,8},{10,11... | collective-permute-start | bytes 786440 | tf_op jit(solution)/shard_map/ppermute | solution.py:378
  62.3 1.1 %collective-permute-done.8 = bf16[32,16,256]{2,1,0:T(8,128)(2,1)S(1)} collective-permute-done((bf16[32,16,256]{2,1,0:T(8,128)(2,1)S(1)}, bf16[32,16,256]{2,1,0:T(8,128)(2,1)S(1)}, u32[]{:S(2)}, u32[]{:S(2)}) %collective-permute-start.8) | collective-permute-done | bytes 262176 | tf_op jit(solution)/shard_map/ppermute | solution.py:378
  63.4 0.8 add_convert_fusion
  64.2 7.9 %all-to-all-start = ((bf16[32,16,256]{2,1,0:T(8,128)(2,1)}), bf16[32,16,256]{2,1,0:T(8,128)(2,1)S(1)}, u32[]{:S(2)}, u32[]{:S(2)}) async-start(bf16[32,16,256]{2,1,0:T(8,128)(2,1)} %add_convert_fusion), calls=%async_computation | async-start | bytes 524288 | tf_op jit(solution)/shard_map/all_to_all | solution.py:379
  72.1 0.0 copy-done.2
  72.1 0.0 copy-done.5
  72.1 0.0 copy-done.1
  72.1 0.0 copy-start.3
  72.1 0.0 copy-start.4
  72.1 0.9 dense.1
  73.1 8.7 %all-to-all-done.got_ref = bf16[32,16,256]{2,1,0:T(8,128)(2,1)S(1)} async-done(((bf16[32,16,256]{2,1,0:T(8,128)(2,1)}), bf16[32,16,256]{2,1,0:T(8,128)(2,1)S(1)}, u32[]{:S(2)}, u32[]{:S(2)}) %all-to-all-start) | async-done | bytes 262176 | tf_op jit(solution)/shard_map/all_to_all | solution.py:379
  81.8 0.0 copy-done.3
  81.8 0.0 copy-done.4
  81.8 1.4 %token_.1 = (bf16[128,1024]{1,0:T(8,128)(2,1)S(1)}, bf16[128,512]{1,0:T(8,128)(2,1)S(1)}, f32[64,1,128]{2,1,0:T(1,128)}) custom-call(bf16[32,16,256]{2,1,0:T(8,128)(2,1)S(1)} %all-to-all-done.got_ref, bf16[1024,512]{1,0:T(8,128)(2,1)S(1)} %get-tuple-element.46.dense_ref, bf16[2,16,512]{2,1,0:T(8,128)(2,1)S(1)} %bitcast.23, bf16[2,16,512]{2,1,0:T(8,128)(2,1)S(1)} %bitcast.24, ...), custom_call_target="tpu_custom_call" | custom-call | tf_op jit(solution)/shard_map/token/pallas_call | solution.py:306
  83.1 8.3 %all-to-all-start.1 = ((f32[64,1,128]{2,1,0:T(1,128)}), f32[64,1,128]{2,1,0:T(1,128)S(1)}, u32[]{:S(2)}, u32[]{:S(2)}) async-start(f32[64,1,128]{2,1,0:T(1,128)} %get-tuple-element.51), calls=%async_computation.1 | async-start | bytes 65536 | tf_op jit(solution)/shard_map/all_to_all | solution.py:381
  91.4 1.0 %back.1 = bf16[128,1024]{1,0:T(8,128)(2,1)} custom-call(bf16[128,1024]{1,0:T(8,128)(2,1)S(1)} %get-tuple-element.48.columns_ref, bf16[128,512]{1,0:T(8,128)(2,1)S(1)} %get-tuple-element.49.mid_ref, bf16[512,1024]{1,0:T(8,128)(2,1)S(1)} %get-tuple-element.50.dense_ref), custom_call_target="tpu_custom_call" | custom-call | tf_op jit(solution)/shard_map/back/pallas_call | solution.py:324
  92.4 8.4 %all-to-all-done.1 = f32[64,1,128]{2,1,0:T(1,128)S(1)} async-done(((f32[64,1,128]{2,1,0:T(1,128)}), f32[64,1,128]{2,1,0:T(1,128)S(1)}, u32[]{:S(2)}, u32[]{:S(2)}) %all-to-all-start.1) | async-done | bytes 32800 | tf_op jit(solution)/shard_map/all_to_all | solution.py:381
  100.8 0.6 reduce_sum.9
  (5 shorter events, 0.0 us)
Async XLA Ops:
  2.9 11.3 %copy-start.8 = (bf16[16,8,1024]{2,1,0:T(8,128)(2,1)S(1)}, bf16[16,8,1024]{2,1,0:T(8,128)(2,1)}, u32[]{:S(2)}) copy-start(bf16[16,8,1024]{2,1,0:T(8,128)(2,1)} %param.12) | copy-start | bytes 786436
  2.9 14.4 %collective-permute-start = (s32[1032,128]{1,0:T(8,128)}, s32[1032,128]{1,0:T(8,128)S(1)}, u32[]{:S(2)}, u32[]{:S(2)}) collective-permute-start(s32[1032,128]{1,0:T(8,128)} %pack.2.refs_3_), channel_id=1, source_target_pairs={{0,64},{64,128},{128,192},{192,256},{256,320},{320,384},{384,448},... | collective-permute-start | bytes 1585160 | tf_op jit(solution)/shard_map/ppermute | solution.py:354
  11.2 15.1 %collective-permute-start.5 = (s32[1032,128]{1,0:T(8,128)}, s32[1032,128]{1,0:T(8,128)S(1)}, u32[]{:S(2)}, u32[]{:S(2)}) collective-permute-start(s32[1032,128]{1,0:T(8,128)} %pack.3), channel_id=1, source_target_pairs={{0,64},{64,128},{128,192},{192,256},{256,320},{320,384},{384,448},... | collective-permute-start | bytes 1585160 | tf_op jit(solution)/shard_map/ppermute | solution.py:354
  15.1 32.9 %copy-start = (s32[1032,128]{1,0:T(8,128)S(1)}, s32[1032,128]{1,0:T(8,128)}, u32[]{:S(2)}) copy-start(s32[1032,128]{1,0:T(8,128)} %pack.2.refs_3_) | copy-start | bytes 1585156
  17.3 30.7 %copy-start.7 = (f32[1024]{0:T(1024)S(1)}, f32[1024]{0:T(1024)}, u32[]{:S(2)}) copy-start(f32[1024]{0:T(1024)} %param.14) | copy-start | bytes 12292
  17.3 13.8 %collective-permute-start.1 = (s32[1032,128]{1,0:T(8,128)S(1)}, s32[1032,128]{1,0:T(8,128)S(1)}, u32[]{:S(2)}, u32[]{:S(2)}) collective-permute-start(s32[1032,128]{1,0:T(8,128)S(1)} %collective-permute-done.refs_1_), channel_id=1, source_target_pairs={{0,64},{64,128},{128,192},{192,256},{256,320},{320,384},{384,448},... | collective-permute-start | bytes 1585160 | tf_op jit(solution)/shard_map/ppermute | solution.py:354
  20.3 10.8 %collective-permute-start.2 = (bf16[128,16,128]{2,1,0:T(8,128)(2,1)}, bf16[128,16,128]{2,1,0:T(8,128)(2,1)S(1)}, u32[]{:S(2)}, u32[]{:S(2)}) collective-permute-start(bf16[128,16,128]{2,1,0:T(8,128)(2,1)} %get-tuple-element.32), channel_id=1, source_target_pairs={{0,1},{1,0},{2,3},{3,2},{4,5},{5,4},{6,7},{7,6},{8,9},{9,8},{10,11... | collective-permute-start | bytes 1572872 | tf_op jit(solution)/shard_map/ppermute | solution.py:364
  26.3 11.0 %collective-permute-start.6 = (s32[1032,128]{1,0:T(8,128)S(1)}, s32[1032,128]{1,0:T(8,128)S(1)}, u32[]{:S(2)}, u32[]{:S(2)}) collective-permute-start(s32[1032,128]{1,0:T(8,128)S(1)} %collective-permute-done.5.refs_2_), channel_id=1, source_target_pairs={{0,64},{64,128},{128,192},{192,256},{256,320},{320,384},{384,448},... | collective-permute-start | bytes 1585160 | tf_op jit(solution)/shard_map/ppermute | solution.py:354
  31.2 11.8 %collective-permute-start.3 = (s32[1032,128]{1,0:T(8,128)S(1)}, s32[1032,128]{1,0:T(8,128)S(1)}, u32[]{:S(2)}, u32[]{:S(2)}) collective-permute-start(s32[1032,128]{1,0:T(8,128)S(1)} %collective-permute-done.1.refs_1_), channel_id=1, source_target_pairs={{0,64},{64,128},{128,192},{192,256},{256,320},{320,384},{384,448},... | collective-permute-start | bytes 1585160 | tf_op jit(solution)/shard_map/ppermute | solution.py:354
  37.3 15.2 %collective-permute-start.7 = (s32[1032,128]{1,0:T(8,128)S(1)}, s32[1032,128]{1,0:T(8,128)S(1)}, u32[]{:S(2)}, u32[]{:S(2)}) collective-permute-start(s32[1032,128]{1,0:T(8,128)S(1)} %collective-permute-done.6.refs_2_), channel_id=1, source_target_pairs={{0,64},{64,128},{128,192},{192,256},{256,320},{320,384},{384,448},... | collective-permute-start | bytes 1585160 | tf_op jit(solution)/shard_map/ppermute | solution.py:354
  43.0 11.3 %collective-permute-start.4 = (s32[1032,128]{1,0:T(8,128)S(1)}, s32[1032,128]{1,0:T(8,128)S(1)}, u32[]{:S(2)}, u32[]{:S(2)}) collective-permute-start(s32[1032,128]{1,0:T(8,128)S(1)} %collective-permute-done.3.refs_1_), channel_id=1, source_target_pairs={{0,64},{64,128},{128,192},{192,256},{256,320},{320,384},{384,448},... | collective-permute-start | bytes 1585160 | tf_op jit(solution)/shard_map/ppermute | solution.py:354
  48.0 1.0 %copy-start.6 = (bf16[128,16,128]{2,1,0:T(8,128)(2,1)S(1)}, bf16[128,16,128]{2,1,0:T(8,128)(2,1)}, u32[]{:S(2)}) copy-start(bf16[128,16,128]{2,1,0:T(8,128)(2,1)} %get-tuple-element.34.refs_5_) | copy-start | bytes 1572868
  55.2 8.2 %collective-permute-start.8 = (bf16[32,16,256]{2,1,0:T(8,128)(2,1)S(1)}, bf16[32,16,256]{2,1,0:T(8,128)(2,1)S(1)}, u32[]{:S(2)}, u32[]{:S(2)}) collective-permute-start(bf16[32,16,256]{2,1,0:T(8,128)(2,1)S(1)} %get-tuple-element.45), channel_id=1, source_target_pairs={{0,1},{1,0},{2,3},{3,2},{4,5},{5,4},{6,7},{7,6},{8,9},{9,8},{10,11... | collective-permute-start | bytes 786440 | tf_op jit(solution)/shard_map/ppermute | solution.py:378
  63.4 8.7 %copy-start.2 = (bf16[16,128,128]{2,1,0:T(8,128)(2,1)S(1)}, bf16[16,128,128]{2,1,0:T(8,128)(2,1)}, u32[]{:S(2)}) copy-start(bf16[16,128,128]{2,1,0:T(8,128)(2,1)} %out_ref.1) | copy-start | bytes 1572868
  63.4 8.7 %copy-start.5 = (s32[16]{0:T(128)S(1)}, s32[16]{0:T(128)}, u32[]{:S(2)}) copy-start(s32[16]{0:T(128)} %cells_ref.1) | copy-start | bytes 196
  64.2 7.9 %copy-start.1 = (bf16[16,128,128]{2,1,0:T(8,128)(2,1)S(1)}, bf16[16,128,128]{2,1,0:T(8,128)(2,1)}, u32[]{:S(2)}) copy-start(bf16[16,128,128]{2,1,0:T(8,128)(2,1)} %in_ref.1) | copy-start | bytes 1572868
  64.2 17.6 %all-to-all-start = ((bf16[32,16,256]{2,1,0:T(8,128)(2,1)}), bf16[32,16,256]{2,1,0:T(8,128)(2,1)S(1)}, u32[]{:S(2)}, u32[]{:S(2)}) async-start(bf16[32,16,256]{2,1,0:T(8,128)(2,1)} %add_convert_fusion), calls=%async_computation | async-start | bytes 524288 | tf_op jit(solution)/shard_map/all_to_all | solution.py:379
  72.1 9.7 %copy-start.3 = (bf16[2,512,1,16]{1,3,2,0:T(8,128)(2,1)S(1)}, bf16[2,512,1,16]{1,3,2,0:T(8,128)(2,1)}, u32[]{:S(2)}) copy-start(bf16[2,512,1,16]{1,3,2,0:T(8,128)(2,1)} %param.22) | copy-start | bytes 98308
  72.1 9.6 %copy-start.4 = (bf16[2,512,1,16]{1,3,2,0:T(8,128)(2,1)S(1)}, bf16[2,512,1,16]{1,3,2,0:T(8,128)(2,1)}, u32[]{:S(2)}) copy-start(bf16[2,512,1,16]{1,3,2,0:T(8,128)(2,1)} %param.23) | copy-start | bytes 98308
  83.1 17.7 %all-to-all-start.1 = ((f32[64,1,128]{2,1,0:T(1,128)}), f32[64,1,128]{2,1,0:T(1,128)S(1)}, u32[]{:S(2)}, u32[]{:S(2)}) async-start(f32[64,1,128]{2,1,0:T(1,128)} %get-tuple-element.51), calls=%async_computation.1 | async-start | bytes 65536 | tf_op jit(solution)/shard_map/all_to_all | solution.py:381

commit v14 on v13

--- a/solution.py
+++ b/solution.py
@@ -35,13 +35,17 @@
 
 
 def pack_codes(parts):
-    a, b, c, d = (p.astype(F32).astype(I32) for p in parts)
-    return (a & 255) | ((b & 255) << 8) | ((c & 255) << 16) | (d << 24)
+    a, b, c, d = (p.astype(F32) for p in parts)
+    low, high = ((y * 256.0 + (x + 128.0)).astype(I32) for x, y in ((a, b), (c, d)))
+    return (low & 65535) | (high << 16)
 
 
 def unpack_codes(words, m):
-    shifted = words << (24 - 8 * m) if m < 3 else words
-    return (shifted >> 24).astype(F32).astype(BF16)
+    if m % 2 == 0:
+        codes = ((words if m == 0 else words >> 16) & 255) - 128
+    else:
+        codes = (words << 16 if m == 1 else words) >> 24
+    return codes.astype(F32).astype(BF16)
 
 
 def pack_kernel(chain, core_ref, down_hbm, up_hbm, scale_hbm, out_ref, down_ref, up_ref, scale_ref, sems):
@@ -378,7 +382,7 @@
     summed = (keep + lax.ppermute(send, "core", SWAP).astype(F32)).astype(BF16)
     got = lax.all_to_all(summed, ("x", "z"), 0, 0, tiled=True)
     columns, mid, own_bias = token_mlp(got, dense_out, slopes, icpt, chan_bias)
-    all_bias = lax.all_to_all(own_bias, MP, 0, 0, tiled=True)
+    all_bias = lax.all_to_all(own_bias, ("x", "z", "core"), 0, 0, tiled=True)
     lam_in = token_back(columns, mid, dense_in)
     lam_in = jnp.transpose(lam_in.reshape(SPEC, 16, TOK), (2, 0, 1))
     return (lam_in, jnp.sum(all_bias, axis=(0, 1))[:SPEC])

time: 102 us -> 102 us (level)
  no operation moved by 1% of the time
where the time goes in v14:
time: 102 us; the launch traced here: 101 us
  starting transfers between devices  58 us (57%)
  waiting for transfers between devices  23.3 us (23%)
  Pallas kernels  15.7 us (15%)
  local copies, waits for them, and re-layouts  1.92 us (2%)
  other arithmetic  1.39 us (1%)
    ppermute x7, starting transfers between devices, forward(): return tuple((lax.ppermute(w, ('rows', 'core'), pairs) for w in words))  28.9 us
    all_to_all x1, waiting for transfers between devices, on_device(): got = lax.all_to_all(summed, ('x', 'z'), 0, 0, tiled=True)  8.7 us
    all_to_all x1, starting transfers between devices, on_device(): all_bias = lax.all_to_all(own_bias, ('x', 'z', 'core'), 0, 0, tiled=True)  8.29 us
    all_to_all x1, waiting for transfers between devices, on_device(): all_bias = lax.all_to_all(own_bias, ('x', 'z', 'core'), 0, 0, tiled=True)  8.27 us
    all_to_all x1, starting transfers between devices, on_device(): got = lax.all_to_all(summed, ('x', 'z'), 0, 0, tiled=True)  7.89 us
    ppermute x1, starting transfers between devices, on_device(): summed = (keep + lax.ppermute(send, 'core', SWAP).astype(F32)).astype(BF16)  7.03 us
    ppermute x1, starting transfers between devices, on_device(): other_part = lax.ppermute(send_part, 'core', SWAP)  5.93 us
    pallas_call x4, Pallas kernels, channel_part(): pl.pallas_call(functools.partial(channel_kernel, step), out_shape=out_sha...  5.78 us
  transfers between devices with their start and end apart: 11, of which 6 were waited for; matrix products, arithmetic and copies ran while one was open for 1% of the time, Pallas kernels for 11%

profile of v14, /device:TPU:1, one launch (start us, length us, event | category | flops | bytes accessed | tf_op | source)
XLA Modules:
  0.0 101.3 jit_solution(5227116163730105510)
XLA Ops:
  0.6 2.2 %pack.2.refs_3_ = s32[1032,128]{1,0:T(8,128)} custom-call(s32[1]{0:T(128)} %bitcast.core_ref.refs_0_, bf16[1024,512]{1,0:T(8,128)(2,1)} %down_hbm.3, bf16[512,1024]{1,0:T(8,128)(2,1)} %up_hbm.3, f32[1,512]{1,0:T(1,128)} %bitcast.30), custom_call_target="tpu_custom_call" | custom-call | tf_op jit(solution)/shard_map/pack/pallas_call | solution.py:80
  2.8 0.0 copy-start.8
  2.8 6.1 %collective-permute-start = (s32[1032,128]{1,0:T(8,128)}, s32[1032,128]{1,0:T(8,128)S(1)}, u32[]{:S(2)}, u32[]{:S(2)}) collective-permute-start(s32[1032,128]{1,0:T(8,128)} %pack.2.refs_3_), channel_id=1, source_target_pairs={{0,64},{64,128},{128,192},{192,256},{256,320},{320,384},{384,448},... | collective-permute-start | bytes 1585160 | tf_op jit(solution)/shard_map/ppermute | solution.py:358
  8.9 2.2 %pack.3 = s32[1032,128]{1,0:T(8,128)} custom-call(s32[1]{0:T(128)} %bitcast.core_ref.refs_0_, bf16[1024,512]{1,0:T(8,128)(2,1)} %down_hbm.3, bf16[512,1024]{1,0:T(8,128)(2,1)} %up_hbm.3, f32[1,512]{1,0:T(1,128)} %bitcast.31), custom_call_target="tpu_custom_call" | custom-call | tf_op jit(solution)/shard_map/pack/pallas_call | solution.py:80
  11.1 3.0 %collective-permute-start.5 = (s32[1032,128]{1,0:T(8,128)}, s32[1032,128]{1,0:T(8,128)S(1)}, u32[]{:S(2)}, u32[]{:S(2)}) collective-permute-start(s32[1032,128]{1,0:T(8,128)} %pack.3), channel_id=1, source_target_pairs={{0,64},{64,128},{128,192},{192,256},{256,320},{320,384},{384,448},... | collective-permute-start | bytes 1585160 | tf_op jit(solution)/shard_map/ppermute | solution.py:358
  14.1 0.0 copy-done.8
  14.1 0.9 copy.22
  15.0 2.3 %share.1 = (bf16[128,16,128]{2,1,0:T(8,128)(2,1)}, bf16[128,16,128]{2,1,0:T(8,128)(2,1)}) custom-call(s32[1]{0:T(128)} %bitcast.core_ref.refs_0_, s32[1]{0:T(128)} %bitcast.2.row_ref, bf16[8,16,1024]{2,1,0:T(8,128)(2,1)} %bitcast.26, bf16[2,16,4096]{2,1,0:T(8,128)(2,1)} %bitcast.27, bf16[2,16,4096]{2,1,0:T(8,128)(2,1)} %bitcast.28), custom_call_target="tpu_custom_call" | custom-call | tf_op jit(solution)/shard_map/share/pallas_call | solution.py:161
  17.2 0.0 collective-permute-done.refs_1_
  17.2 3.1 %collective-permute-start.1 = (s32[1032,128]{1,0:T(8,128)S(1)}, s32[1032,128]{1,0:T(8,128)S(1)}, u32[]{:S(2)}, u32[]{:S(2)}) collective-permute-start(s32[1032,128]{1,0:T(8,128)S(1)} %collective-permute-done.refs_1_), channel_id=1, source_target_pairs={{0,64},{64,128},{128,192},{192,256},{256,320},{320,384},{384,448},... | collective-permute-start | bytes 1585160 | tf_op jit(solution)/shard_map/ppermute | solution.py:358
  20.3 5.9 %collective-permute-start.2 = (bf16[128,16,128]{2,1,0:T(8,128)(2,1)}, bf16[128,16,128]{2,1,0:T(8,128)(2,1)S(1)}, u32[]{:S(2)}, u32[]{:S(2)}) collective-permute-start(bf16[128,16,128]{2,1,0:T(8,128)(2,1)} %get-tuple-element.32), channel_id=1, source_target_pairs={{0,1},{1,0},{2,3},{3,2},{4,5},{5,4},{6,7},{7,6},{8,9},{9,8},{10,11... | collective-permute-start | bytes 1572872 | tf_op jit(solution)/shard_map/ppermute | solution.py:368
  26.2 0.0 collective-permute-done.5.refs_2_
  26.2 4.9 %collective-permute-start.6 = (s32[1032,128]{1,0:T(8,128)S(1)}, s32[1032,128]{1,0:T(8,128)S(1)}, u32[]{:S(2)}, u32[]{:S(2)}) collective-permute-start(s32[1032,128]{1,0:T(8,128)S(1)} %collective-permute-done.5.refs_2_), channel_id=1, source_target_pairs={{0,64},{64,128},{128,192},{192,256},{256,320},{320,384},{384,448},... | collective-permute-start | bytes 1585160 | tf_op jit(solution)/shard_map/ppermute | solution.py:358
  31.1 0.0 collective-permute-done.2.refs_6_
  31.1 0.0 collective-permute-done.1.refs_1_
  31.1 1.9 %collective-permute-start.3 = (s32[1032,128]{1,0:T(8,128)S(1)}, s32[1032,128]{1,0:T(8,128)S(1)}, u32[]{:S(2)}, u32[]{:S(2)}) collective-permute-start(s32[1032,128]{1,0:T(8,128)S(1)} %collective-permute-done.1.refs_1_), channel_id=1, source_target_pairs={{0,64},{64,128},{128,192},{192,256},{256,320},{320,384},{384,448},... | collective-permute-start | bytes 1585160 | tf_op jit(solution)/shard_map/ppermute | solution.py:358
  33.0 4.2 %collective-permute-done.6.refs_2_ = s32[1032,128]{1,0:T(8,128)S(1)} collective-permute-done((s32[1032,128]{1,0:T(8,128)S(1)}, s32[1032,128]{1,0:T(8,128)S(1)}, u32[]{:S(2)}, u32[]{:S(2)}) %collective-permute-start.6) | collective-permute-done | bytes 528416 | tf_op jit(solution)/shard_map/ppermute | solution.py:358
  37.2 5.0 %collective-permute-start.7 = (s32[1032,128]{1,0:T(8,128)S(1)}, s32[1032,128]{1,0:T(8,128)S(1)}, u32[]{:S(2)}, u32[]{:S(2)}) collective-permute-start(s32[1032,128]{1,0:T(8,128)S(1)} %collective-permute-done.6.refs_2_), channel_id=1, source_target_pairs={{0,64},{64,128},{128,192},{192,256},{256,320},{320,384},{384,448},... | collective-permute-start | bytes 1585160 | tf_op jit(solution)/shard_map/ppermute | solution.py:358
  42.3 0.6 collective-permute-done.3.refs_1_
  42.9 5.0 %collective-permute-start.4 = (s32[1032,128]{1,0:T(8,128)S(1)}, s32[1032,128]{1,0:T(8,128)S(1)}, u32[]{:S(2)}, u32[]{:S(2)}) collective-permute-start(s32[1032,128]{1,0:T(8,128)S(1)} %collective-permute-done.3.refs_1_), channel_id=1, source_target_pairs={{0,64},{64,128},{128,192},{192,256},{256,320},{320,384},{384,448},... | collective-permute-start | bytes 1585160 | tf_op jit(solution)/shard_map/ppermute | solution.py:358
  47.9 0.0 copy-done
  47.9 0.0 copy-done.7
  48.0 0.0 copy-start.6
  48.0 1.0 %copy-done.6 = bf16[128,16,128]{2,1,0:T(8,128)(2,1)S(1)} copy-done((bf16[128,16,128]{2,1,0:T(8,128)(2,1)S(1)}, bf16[128,16,128]{2,1,0:T(8,128)(2,1)}, u32[]{:S(2)}) %copy-start.6) | copy-done | bytes 524312
  49.0 2.1 %channel.4 = (f32[256,1024]{1,0:T(8,128)S(1)}, f32[8,8,128]{2,1,0:T(8,128)S(1)}, bf16[256,1024]{1,0:T(8,128)(2,1)S(1)}, bf16[4,4,32,512]{3,2,1,0:T(8,128)(2,1)S(1)}) custom-call(s32[1]{0:T(128)} %bitcast.core_ref.refs_0_, s32[1032,128]{1,0:T(8,128)S(1)} %collective-permute-done.refs_1_, s32[1032,128]{1,0:T(8,128)S(1)} %collective-permute-done.5.refs_2_, ...), custom_call_target="tpu_custom_call" | custom-call | flops 805306368 | bytes 4202496 | tf_op jit(solution)/shard_map/channel/pallas_call | solution.py:260
  51.1 1.4 %channel.5 = (f32[256,1024]{1,0:T(8,128)S(1)}, f32[8,8,128]{2,1,0:T(8,128)S(1)}) custom-call(s32[1]{0:T(128)} %bitcast.core_ref.refs_0_, s32[1032,128]{1,0:T(8,128)S(1)} %collective-permute-done.1.refs_1_, s32[1032,128]{1,0:T(8,128)S(1)} %collective-permute-done.6.refs_2_, ...), custom_call_target="tpu_custom_call", output_to_operand_aliasing={{0}: (5, {}), {1}: (6, {})} | custom-call | flops 536870912 | bytes 4202496 | tf_op jit(solution)/shard_map/channel/pallas_call | solution.py:260
  52.5 0.0 collective-permute-done.7.refs_2_
  52.5 1.4 %channel.6 = (f32[256,1024]{1,0:T(8,128)S(1)}, f32[8,8,128]{2,1,0:T(8,128)S(1)}) custom-call(s32[1]{0:T(128)} %bitcast.core_ref.refs_0_, s32[1032,128]{1,0:T(8,128)S(1)} %collective-permute-done.3.refs_1_, s32[1032,128]{1,0:T(8,128)S(1)} %collective-permute-done.7.refs_2_, ...), custom_call_target="tpu_custom_call", output_to_operand_aliasing={{0}: (5, {}), {1}: (6, {})} | custom-call | flops 536870912 | bytes 4202496 | tf_op jit(solution)/shard_map/channel/pallas_call | solution.py:260
  53.9 0.4 collective-permute-done.4.refs_1_
  54.2 0.9 channel.7
  55.2 7.0 %collective-permute-start.8 = (bf16[32,16,256]{2,1,0:T(8,128)(2,1)S(1)}, bf16[32,16,256]{2,1,0:T(8,128)(2,1)S(1)}, u32[]{:S(2)}, u32[]{:S(2)}) collective-permute-start(bf16[32,16,256]{2,1,0:T(8,128)(2,1)S(1)} %get-tuple-element.45), channel_id=1, source_target_pairs={{0,1},{1,0},{2,3},{3,2},{4,5},{5,4},{6,7},{7,6},{8,9},{9,8},{10,11... | collective-permute-start | bytes 786440 | tf_op jit(solution)/shard_map/ppermute | solution.py:382
  62.2 1.1 %collective-permute-done.8 = bf16[32,16,256]{2,1,0:T(8,128)(2,1)S(1)} collective-permute-done((bf16[32,16,256]{2,1,0:T(8,128)(2,1)S(1)}, bf16[32,16,256]{2,1,0:T(8,128)(2,1)S(1)}, u32[]{:S(2)}, u32[]{:S(2)}) %collective-permute-start.8) | collective-permute-done | bytes 262176 | tf_op jit(solution)/shard_map/ppermute | solution.py:382
  63.4 0.8 add_convert_fusion
  64.2 7.9 %all-to-all-start = ((bf16[32,16,256]{2,1,0:T(8,128)(2,1)}), bf16[32,16,256]{2,1,0:T(8,128)(2,1)S(1)}, u32[]{:S(2)}, u32[]{:S(2)}) async-start(bf16[32,16,256]{2,1,0:T(8,128)(2,1)} %add_convert_fusion), calls=%async_computation | async-start | bytes 524288 | tf_op jit(solution)/shard_map/all_to_all | solution.py:383
  72.0 0.0 copy-done.2
  72.1 0.0 copy-done.5
  72.1 0.0 copy-done.1
  72.1 0.0 copy-start.3
  72.1 0.0 copy-start.4
  72.1 0.9 dense.1
  73.0 8.7 %all-to-all-done.got_ref = bf16[32,16,256]{2,1,0:T(8,128)(2,1)S(1)} async-done(((bf16[32,16,256]{2,1,0:T(8,128)(2,1)}), bf16[32,16,256]{2,1,0:T(8,128)(2,1)S(1)}, u32[]{:S(2)}, u32[]{:S(2)}) %all-to-all-start) | async-done | bytes 262176 | tf_op jit(solution)/shard_map/all_to_all | solution.py:383
  81.7 0.0 copy-done.3
  81.7 0.0 copy-done.4
  81.7 1.4 %token_.1 = (bf16[128,1024]{1,0:T(8,128)(2,1)S(1)}, bf16[128,512]{1,0:T(8,128)(2,1)S(1)}, f32[64,1,128]{2,1,0:T(1,128)}) custom-call(bf16[32,16,256]{2,1,0:T(8,128)(2,1)S(1)} %all-to-all-done.got_ref, bf16[1024,512]{1,0:T(8,128)(2,1)S(1)} %get-tuple-element.46.dense_ref, bf16[2,16,512]{2,1,0:T(8,128)(2,1)S(1)} %bitcast.23, bf16[2,16,512]{2,1,0:T(8,128)(2,1)S(1)} %bitcast.24, ...), custom_call_target="tpu_custom_call" | custom-call | tf_op jit(solution)/shard_map/token/pallas_call | solution.py:310
  83.1 8.3 %all-to-all-start.1 = ((f32[64,1,128]{2,1,0:T(1,128)}), f32[64,1,128]{2,1,0:T(1,128)S(1)}, u32[]{:S(2)}, u32[]{:S(2)}) async-start(f32[64,1,128]{2,1,0:T(1,128)} %get-tuple-element.51), calls=%async_computation.1 | async-start | bytes 65536 | tf_op jit(solution)/shard_map/all_to_all | solution.py:385
  91.4 1.0 %back.1 = bf16[128,1024]{1,0:T(8,128)(2,1)} custom-call(bf16[128,1024]{1,0:T(8,128)(2,1)S(1)} %get-tuple-element.48.columns_ref, bf16[128,512]{1,0:T(8,128)(2,1)S(1)} %get-tuple-element.49.mid_ref, bf16[512,1024]{1,0:T(8,128)(2,1)S(1)} %get-tuple-element.50.dense_ref), custom_call_target="tpu_custom_call" | custom-call | tf_op jit(solution)/shard_map/back/pallas_call | solution.py:328
  92.4 8.3 %all-to-all-done.1 = f32[64,1,128]{2,1,0:T(1,128)S(1)} async-done(((f32[64,1,128]{2,1,0:T(1,128)}), f32[64,1,128]{2,1,0:T(1,128)S(1)}, u32[]{:S(2)}, u32[]{:S(2)}) %all-to-all-start.1) | async-done | bytes 32800 | tf_op jit(solution)/shard_map/all_to_all | solution.py:385
  100.7 0.6 reduce_sum.9
  (5 shorter events, 0.0 us)
Async XLA Ops:
  2.8 11.3 %copy-start.8 = (bf16[16,8,1024]{2,1,0:T(8,128)(2,1)S(1)}, bf16[16,8,1024]{2,1,0:T(8,128)(2,1)}, u32[]{:S(2)}) copy-start(bf16[16,8,1024]{2,1,0:T(8,128)(2,1)} %param.12) | copy-start | bytes 786436
  2.8 14.4 %collective-permute-start = (s32[1032,128]{1,0:T(8,128)}, s32[1032,128]{1,0:T(8,128)S(1)}, u32[]{:S(2)}, u32[]{:S(2)}) collective-permute-start(s32[1032,128]{1,0:T(8,128)} %pack.2.refs_3_), channel_id=1, source_target_pairs={{0,64},{64,128},{128,192},{192,256},{256,320},{320,384},{384,448},... | collective-permute-start | bytes 1585160 | tf_op jit(solution)/shard_map/ppermute | solution.py:358
  11.1 15.1 %collective-permute-start.5 = (s32[1032,128]{1,0:T(8,128)}, s32[1032,128]{1,0:T(8,128)S(1)}, u32[]{:S(2)}, u32[]{:S(2)}) collective-permute-start(s32[1032,128]{1,0:T(8,128)} %pack.3), channel_id=1, source_target_pairs={{0,64},{64,128},{128,192},{192,256},{256,320},{320,384},{384,448},... | collective-permute-start | bytes 1585160 | tf_op jit(solution)/shard_map/ppermute | solution.py:358
  15.0 33.0 %copy-start = (s32[1032,128]{1,0:T(8,128)S(1)}, s32[1032,128]{1,0:T(8,128)}, u32[]{:S(2)}) copy-start(s32[1032,128]{1,0:T(8,128)} %pack.2.refs_3_) | copy-start | bytes 1585156
  17.2 30.7 %copy-start.7 = (f32[1024]{0:T(1024)S(1)}, f32[1024]{0:T(1024)}, u32[]{:S(2)}) copy-start(f32[1024]{0:T(1024)} %param.14) | copy-start | bytes 12292
  17.2 13.9 %collective-permute-start.1 = (s32[1032,128]{1,0:T(8,128)S(1)}, s32[1032,128]{1,0:T(8,128)S(1)}, u32[]{:S(2)}, u32[]{:S(2)}) collective-permute-start(s32[1032,128]{1,0:T(8,128)S(1)} %collective-permute-done.refs_1_), channel_id=1, source_target_pairs={{0,64},{64,128},{128,192},{192,256},{256,320},{320,384},{384,448},... | collective-permute-start | bytes 1585160 | tf_op jit(solution)/shard_map/ppermute | solution.py:358
  20.3 10.8 %collective-permute-start.2 = (bf16[128,16,128]{2,1,0:T(8,128)(2,1)}, bf16[128,16,128]{2,1,0:T(8,128)(2,1)S(1)}, u32[]{:S(2)}, u32[]{:S(2)}) collective-permute-start(bf16[128,16,128]{2,1,0:T(8,128)(2,1)} %get-tuple-element.32), channel_id=1, source_target_pairs={{0,1},{1,0},{2,3},{3,2},{4,5},{5,4},{6,7},{7,6},{8,9},{9,8},{10,11... | collective-permute-start | bytes 1572872 | tf_op jit(solution)/shard_map/ppermute | solution.py:368
  26.2 11.0 %collective-permute-start.6 = (s32[1032,128]{1,0:T(8,128)S(1)}, s32[1032,128]{1,0:T(8,128)S(1)}, u32[]{:S(2)}, u32[]{:S(2)}) collective-permute-start(s32[1032,128]{1,0:T(8,128)S(1)} %collective-permute-done.5.refs_2_), channel_id=1, source_target_pairs={{0,64},{64,128},{128,192},{192,256},{256,320},{320,384},{384,448},... | collective-permute-start | bytes 1585160 | tf_op jit(solution)/shard_map/ppermute | solution.py:358
  31.1 11.8 %collective-permute-start.3 = (s32[1032,128]{1,0:T(8,128)S(1)}, s32[1032,128]{1,0:T(8,128)S(1)}, u32[]{:S(2)}, u32[]{:S(2)}) collective-permute-start(s32[1032,128]{1,0:T(8,128)S(1)} %collective-permute-done.1.refs_1_), channel_id=1, source_target_pairs={{0,64},{64,128},{128,192},{192,256},{256,320},{320,384},{384,448},... | collective-permute-start | bytes 1585160 | tf_op jit(solution)/shard_map/ppermute | solution.py:358
  37.2 15.2 %collective-permute-start.7 = (s32[1032,128]{1,0:T(8,128)S(1)}, s32[1032,128]{1,0:T(8,128)S(1)}, u32[]{:S(2)}, u32[]{:S(2)}) collective-permute-start(s32[1032,128]{1,0:T(8,128)S(1)} %collective-permute-done.6.refs_2_), channel_id=1, source_target_pairs={{0,64},{64,128},{128,192},{192,256},{256,320},{320,384},{384,448},... | collective-permute-start | bytes 1585160 | tf_op jit(solution)/shard_map/ppermute | solution.py:358
  42.9 11.3 %collective-permute-start.4 = (s32[1032,128]{1,0:T(8,128)S(1)}, s32[1032,128]{1,0:T(8,128)S(1)}, u32[]{:S(2)}, u32[]{:S(2)}) collective-permute-start(s32[1032,128]{1,0:T(8,128)S(1)} %collective-permute-done.3.refs_1_), channel_id=1, source_target_pairs={{0,64},{64,128},{128,192},{192,256},{256,320},{320,384},{384,448},... | collective-permute-start | bytes 1585160 | tf_op jit(solution)/shard_map/ppermute | solution.py:358
  48.0 1.0 %copy-start.6 = (bf16[128,16,128]{2,1,0:T(8,128)(2,1)S(1)}, bf16[128,16,128]{2,1,0:T(8,128)(2,1)}, u32[]{:S(2)}) copy-start(bf16[128,16,128]{2,1,0:T(8,128)(2,1)} %get-tuple-element.34.refs_5_) | copy-start | bytes 1572868
  55.2 8.2 %collective-permute-start.8 = (bf16[32,16,256]{2,1,0:T(8,128)(2,1)S(1)}, bf16[32,16,256]{2,1,0:T(8,128)(2,1)S(1)}, u32[]{:S(2)}, u32[]{:S(2)}) collective-permute-start(bf16[32,16,256]{2,1,0:T(8,128)(2,1)S(1)} %get-tuple-element.45), channel_id=1, source_target_pairs={{0,1},{1,0},{2,3},{3,2},{4,5},{5,4},{6,7},{7,6},{8,9},{9,8},{10,11... | collective-permute-start | bytes 786440 | tf_op jit(solution)/shard_map/ppermute | solution.py:382
  63.4 8.7 %copy-start.2 = (bf16[16,128,128]{2,1,0:T(8,128)(2,1)S(1)}, bf16[16,128,128]{2,1,0:T(8,128)(2,1)}, u32[]{:S(2)}) copy-start(bf16[16,128,128]{2,1,0:T(8,128)(2,1)} %out_ref.1) | copy-start | bytes 1572868
  63.4 8.7 %copy-start.5 = (s32[16]{0:T(128)S(1)}, s32[16]{0:T(128)}, u32[]{:S(2)}) copy-start(s32[16]{0:T(128)} %cells_ref.1) | copy-start | bytes 196
  64.1 7.9 %copy-start.1 = (bf16[16,128,128]{2,1,0:T(8,128)(2,1)S(1)}, bf16[16,128,128]{2,1,0:T(8,128)(2,1)}, u32[]{:S(2)}) copy-start(bf16[16,128,128]{2,1,0:T(8,128)(2,1)} %in_ref.1) | copy-start | bytes 1572868
  64.2 17.6 %all-to-all-start = ((bf16[32,16,256]{2,1,0:T(8,128)(2,1)}), bf16[32,16,256]{2,1,0:T(8,128)(2,1)S(1)}, u32[]{:S(2)}, u32[]{:S(2)}) async-start(bf16[32,16,256]{2,1,0:T(8,128)(2,1)} %add_convert_fusion), calls=%async_computation | async-start | bytes 524288 | tf_op jit(solution)/shard_map/all_to_all | solution.py:383
  72.1 9.7 %copy-start.3 = (bf16[2,512,1,16]{1,3,2,0:T(8,128)(2,1)S(1)}, bf16[2,512,1,16]{1,3,2,0:T(8,128)(2,1)}, u32[]{:S(2)}) copy-start(bf16[2,512,1,16]{1,3,2,0:T(8,128)(2,1)} %param.22) | copy-start | bytes 98308
  72.1 9.6 %copy-start.4 = (bf16[2,512,1,16]{1,3,2,0:T(8,128)(2,1)S(1)}, bf16[2,512,1,16]{1,3,2,0:T(8,128)(2,1)}, u32[]{:S(2)}) copy-start(bf16[2,512,1,16]{1,3,2,0:T(8,128)(2,1)} %param.23) | copy-start | bytes 98308
  83.1 17.6 %all-to-all-start.1 = ((f32[64,1,128]{2,1,0:T(1,128)}), f32[64,1,128]{2,1,0:T(1,128)S(1)}, u32[]{:S(2)}, u32[]{:S(2)}) async-start(f32[64,1,128]{2,1,0:T(1,128)} %get-tuple-element.51), calls=%async_computation.1 | async-start | bytes 65536 | tf_op jit(solution)/shard_map/all_to_all | solution.py:385

commit v15 on v14

--- a/solution.py
+++ b/solution.py
@@ -50,24 +50,34 @@
 
 def pack_kernel(chain, core_ref, down_hbm, up_hbm, scale_hbm, out_ref, down_ref, up_ref, scale_ref, sems):
     cut = pl.ds(pl.multiple_of((core_ref[0] ^ chain) * CHUNK, CHUNK), CHUNK)
-    copies = [
-        pltpu.make_async_copy(down_hbm.at[:, cut], down_ref, sems.at[0]),
-        pltpu.make_async_copy(up_hbm.at[cut, :], up_ref, sems.at[1]),
-        pltpu.make_async_copy(scale_hbm.at[:, cut], scale_ref, sems.at[2]),
-    ]
-    for copy in copies:
+    base = (core_ref[0] ^ chain) * CHUNK
+    downs, ups = [], []
+    for m in range(4):
+        rows = pl.ds(m * 256, 256)
+        downs.append(
+            pltpu.make_async_copy(down_hbm.at[rows, cut], down_ref.at[rows, :], sems.at[m])
+        )
+    for m in range(4):
+        rows, source = pl.ds(m * 64, 64), pl.ds(pl.multiple_of(base + m * 64, 64), 64)
+        ups.append(
+            pltpu.make_async_copy(up_hbm.at[source, :], up_ref.at[rows, :], sems.at[4 + m])
+        )
+    scale_copy = pltpu.make_async_copy(scale_hbm.at[:, cut], scale_ref, sems.at[8])
+    for copy in (*downs, *ups, scale_copy):
         copy.start()
     out_ref[1024:1032, :] = jnp.zeros((8, 128), I32)
-    copies[0].wait()
+    for copy in downs:
+        copy.wait()
     down = pack_codes([down_ref[m * 256 : (m + 1) * 256, :] for m in range(4)])
     for k in range(8):
         rows, cut = slice(k // 2 * 64, (k // 2 + 1) * 64), slice(k % 2 * 128, (k % 2 + 1) * 128)
         out_ref[k * 64 : (k + 1) * 64, :] = down[rows, cut]
-    copies[1].wait()
+    for copy in ups:
+        copy.wait()
     up = pack_codes([up_ref[m * 64 : (m + 1) * 64, :] for m in range(4)])
     for k in range(8):
         out_ref[512 + k * 64 : 512 + (k + 1) * 64, :] = up[:, k * 128 : (k + 1) * 128]
-    copies[2].wait()
+    scale_copy.wait()
     scale = (scale_ref[...] * SCALE_ONE).astype(I32)
     for h in range(2):
         out_ref[1024 + h : 1025 + h, :] = scale[:, h * 128 : (h + 1) * 128]
@@ -86,7 +96,7 @@
             pltpu.VMEM((D, CHUNK), BF16),
             pltpu.VMEM((CHUNK, D), BF16),
             pltpu.VMEM((1, CHUNK), F32),
-            pltpu.SemaphoreType.DMA((3,)),
+            pltpu.SemaphoreType.DMA((9,)),
         ],
         compiler_params=pltpu.CompilerParams(vmem_limit_bytes=60 * 1024 * 1024),
         name="pack",

time: 102 us -> 102 us (level)
  no operation moved by 1% of the time
where the time goes in v15:
time: 102 us; the launch traced here: 101 us
  starting transfers between devices  57.9 us (57%)
  waiting for transfers between devices  23.3 us (23%)
  Pallas kernels  16 us (16%)
  local copies, waits for them, and re-layouts  1.92 us (2%)
  other arithmetic  1.39 us (1%)
    ppermute x7, starting transfers between devices, forward(): return tuple((lax.ppermute(w, ('rows', 'core'), pairs) for w in words))  28.9 us
    all_to_all x1, waiting for transfers between devices, on_device(): got = lax.all_to_all(summed, ('x', 'z'), 0, 0, tiled=True)  8.7 us
    all_to_all x1, starting transfers between devices, on_device(): all_bias = lax.all_to_all(own_bias, ('x', 'z', 'core'), 0, 0, tiled=True)  8.29 us
    all_to_all x1, waiting for transfers between devices, on_device(): all_bias = lax.all_to_all(own_bias, ('x', 'z', 'core'), 0, 0, tiled=True)  8.27 us
    all_to_all x1, starting transfers between devices, on_device(): got = lax.all_to_all(summed, ('x', 'z'), 0, 0, tiled=True)  7.89 us
    ppermute x1, starting transfers between devices, on_device(): summed = (keep + lax.ppermute(send, 'core', SWAP).astype(F32)).astype(BF16)  7.03 us
    pallas_call x4, Pallas kernels, channel_part(): pl.pallas_call(functools.partial(channel_kernel, step), out_shape=out_sha...  5.78 us
    ppermute x1, starting transfers between devices, on_device(): other_part = lax.ppermute(send_part, 'core', SWAP)  5.75 us
  transfers between devices with their start and end apart: 11, of which 6 were waited for; matrix products, arithmetic and copies ran while one was open for 1% of the time, Pallas kernels for 11%

profile of v15, /device:TPU:1, one launch (start us, length us, event | category | flops | bytes accessed | tf_op | source)
XLA Modules:
  0.0 101.4 jit_solution(2791677209638755932)
XLA Ops:
  0.6 2.3 %pack.2.refs_3_ = s32[1032,128]{1,0:T(8,128)} custom-call(s32[1]{0:T(128)} %bitcast.core_ref.refs_0_, bf16[1024,512]{1,0:T(8,128)(2,1)} %down_hbm.3, bf16[512,1024]{1,0:T(8,128)(2,1)} %up_hbm.3, f32[1,512]{1,0:T(1,128)} %bitcast.30), custom_call_target="tpu_custom_call" | custom-call | tf_op jit(solution)/shard_map/pack/pallas_call | solution.py:90
  3.0 0.0 copy-start.8
  3.0 6.1 %collective-permute-start = (s32[1032,128]{1,0:T(8,128)}, s32[1032,128]{1,0:T(8,128)S(1)}, u32[]{:S(2)}, u32[]{:S(2)}) collective-permute-start(s32[1032,128]{1,0:T(8,128)} %pack.2.refs_3_), channel_id=1, source_target_pairs={{0,64},{64,128},{128,192},{192,256},{256,320},{320,384},{384,448},... | collective-permute-start | bytes 1585160 | tf_op jit(solution)/shard_map/ppermute | solution.py:368
  9.0 2.3 %pack.3 = s32[1032,128]{1,0:T(8,128)} custom-call(s32[1]{0:T(128)} %bitcast.core_ref.refs_0_, bf16[1024,512]{1,0:T(8,128)(2,1)} %down_hbm.3, bf16[512,1024]{1,0:T(8,128)(2,1)} %up_hbm.3, f32[1,512]{1,0:T(1,128)} %bitcast.31), custom_call_target="tpu_custom_call" | custom-call | tf_op jit(solution)/shard_map/pack/pallas_call | solution.py:90
  11.4 3.0 %collective-permute-start.5 = (s32[1032,128]{1,0:T(8,128)}, s32[1032,128]{1,0:T(8,128)S(1)}, u32[]{:S(2)}, u32[]{:S(2)}) collective-permute-start(s32[1032,128]{1,0:T(8,128)} %pack.3), channel_id=1, source_target_pairs={{0,64},{64,128},{128,192},{192,256},{256,320},{320,384},{384,448},... | collective-permute-start | bytes 1585160 | tf_op jit(solution)/shard_map/ppermute | solution.py:368
  14.4 0.0 copy-done.8
  14.4 0.9 copy.22
  15.2 2.3 %share.1 = (bf16[128,16,128]{2,1,0:T(8,128)(2,1)}, bf16[128,16,128]{2,1,0:T(8,128)(2,1)}) custom-call(s32[1]{0:T(128)} %bitcast.core_ref.refs_0_, s32[1]{0:T(128)} %bitcast.2.row_ref, bf16[8,16,1024]{2,1,0:T(8,128)(2,1)} %bitcast.26, bf16[2,16,4096]{2,1,0:T(8,128)(2,1)} %bitcast.27, bf16[2,16,4096]{2,1,0:T(8,128)(2,1)} %bitcast.28), custom_call_target="tpu_custom_call" | custom-call | tf_op jit(solution)/shard_map/share/pallas_call | solution.py:171
  17.5 0.0 collective-permute-done.refs_1_
  17.5 3.1 %collective-permute-start.1 = (s32[1032,128]{1,0:T(8,128)S(1)}, s32[1032,128]{1,0:T(8,128)S(1)}, u32[]{:S(2)}, u32[]{:S(2)}) collective-permute-start(s32[1032,128]{1,0:T(8,128)S(1)} %collective-permute-done.refs_1_), channel_id=1, source_target_pairs={{0,64},{64,128},{128,192},{192,256},{256,320},{320,384},{384,448},... | collective-permute-start | bytes 1585160 | tf_op jit(solution)/shard_map/ppermute | solution.py:368
  20.6 5.7 %collective-permute-start.2 = (bf16[128,16,128]{2,1,0:T(8,128)(2,1)}, bf16[128,16,128]{2,1,0:T(8,128)(2,1)S(1)}, u32[]{:S(2)}, u32[]{:S(2)}) collective-permute-start(bf16[128,16,128]{2,1,0:T(8,128)(2,1)} %get-tuple-element.32), channel_id=1, source_target_pairs={{0,1},{1,0},{2,3},{3,2},{4,5},{5,4},{6,7},{7,6},{8,9},{9,8},{10,11... | collective-permute-start | bytes 1572872 | tf_op jit(solution)/shard_map/ppermute | solution.py:378
  26.4 0.0 collective-permute-done.5.refs_2_
  26.4 4.9 %collective-permute-start.6 = (s32[1032,128]{1,0:T(8,128)S(1)}, s32[1032,128]{1,0:T(8,128)S(1)}, u32[]{:S(2)}, u32[]{:S(2)}) collective-permute-start(s32[1032,128]{1,0:T(8,128)S(1)} %collective-permute-done.5.refs_2_), channel_id=1, source_target_pairs={{0,64},{64,128},{128,192},{192,256},{256,320},{320,384},{384,448},... | collective-permute-start | bytes 1585160 | tf_op jit(solution)/shard_map/ppermute | solution.py:368
  31.2 0.0 collective-permute-done.2.refs_6_
  31.2 0.0 collective-permute-done.1.refs_1_
  31.3 1.9 %collective-permute-start.3 = (s32[1032,128]{1,0:T(8,128)S(1)}, s32[1032,128]{1,0:T(8,128)S(1)}, u32[]{:S(2)}, u32[]{:S(2)}) collective-permute-start(s32[1032,128]{1,0:T(8,128)S(1)} %collective-permute-done.1.refs_1_), channel_id=1, source_target_pairs={{0,64},{64,128},{128,192},{192,256},{256,320},{320,384},{384,448},... | collective-permute-start | bytes 1585160 | tf_op jit(solution)/shard_map/ppermute | solution.py:368
  33.2 4.2 %collective-permute-done.6.refs_2_ = s32[1032,128]{1,0:T(8,128)S(1)} collective-permute-done((s32[1032,128]{1,0:T(8,128)S(1)}, s32[1032,128]{1,0:T(8,128)S(1)}, u32[]{:S(2)}, u32[]{:S(2)}) %collective-permute-start.6) | collective-permute-done | bytes 528416 | tf_op jit(solution)/shard_map/ppermute | solution.py:368
  37.4 5.0 %collective-permute-start.7 = (s32[1032,128]{1,0:T(8,128)S(1)}, s32[1032,128]{1,0:T(8,128)S(1)}, u32[]{:S(2)}, u32[]{:S(2)}) collective-permute-start(s32[1032,128]{1,0:T(8,128)S(1)} %collective-permute-done.6.refs_2_), channel_id=1, source_target_pairs={{0,64},{64,128},{128,192},{192,256},{256,320},{320,384},{384,448},... | collective-permute-start | bytes 1585160 | tf_op jit(solution)/shard_map/ppermute | solution.py:368
  42.4 0.6 collective-permute-done.3.refs_1_
  43.0 5.0 %collective-permute-start.4 = (s32[1032,128]{1,0:T(8,128)S(1)}, s32[1032,128]{1,0:T(8,128)S(1)}, u32[]{:S(2)}, u32[]{:S(2)}) collective-permute-start(s32[1032,128]{1,0:T(8,128)S(1)} %collective-permute-done.3.refs_1_), channel_id=1, source_target_pairs={{0,64},{64,128},{128,192},{192,256},{256,320},{320,384},{384,448},... | collective-permute-start | bytes 1585160 | tf_op jit(solution)/shard_map/ppermute | solution.py:368
  48.1 0.0 copy-done
  48.1 0.0 copy-done.7
  48.1 0.0 copy-start.6
  48.1 1.0 %copy-done.6 = bf16[128,16,128]{2,1,0:T(8,128)(2,1)S(1)} copy-done((bf16[128,16,128]{2,1,0:T(8,128)(2,1)S(1)}, bf16[128,16,128]{2,1,0:T(8,128)(2,1)}, u32[]{:S(2)}) %copy-start.6) | copy-done | bytes 524312
  49.1 2.1 %channel.4 = (f32[256,1024]{1,0:T(8,128)S(1)}, f32[8,8,128]{2,1,0:T(8,128)S(1)}, bf16[256,1024]{1,0:T(8,128)(2,1)S(1)}, bf16[4,4,32,512]{3,2,1,0:T(8,128)(2,1)S(1)}) custom-call(s32[1]{0:T(128)} %bitcast.core_ref.refs_0_, s32[1032,128]{1,0:T(8,128)S(1)} %collective-permute-done.refs_1_, s32[1032,128]{1,0:T(8,128)S(1)} %collective-permute-done.5.refs_2_, ...), custom_call_target="tpu_custom_call" | custom-call | flops 805306368 | bytes 4202496 | tf_op jit(solution)/shard_map/channel/pallas_call | solution.py:270
  51.2 1.4 %channel.5 = (f32[256,1024]{1,0:T(8,128)S(1)}, f32[8,8,128]{2,1,0:T(8,128)S(1)}) custom-call(s32[1]{0:T(128)} %bitcast.core_ref.refs_0_, s32[1032,128]{1,0:T(8,128)S(1)} %collective-permute-done.1.refs_1_, s32[1032,128]{1,0:T(8,128)S(1)} %collective-permute-done.6.refs_2_, ...), custom_call_target="tpu_custom_call", output_to_operand_aliasing={{0}: (5, {}), {1}: (6, {})} | custom-call | flops 536870912 | bytes 4202496 | tf_op jit(solution)/shard_map/channel/pallas_call | solution.py:270
  52.6 0.0 collective-permute-done.7.refs_2_
  52.6 1.4 %channel.6 = (f32[256,1024]{1,0:T(8,128)S(1)}, f32[8,8,128]{2,1,0:T(8,128)S(1)}) custom-call(s32[1]{0:T(128)} %bitcast.core_ref.refs_0_, s32[1032,128]{1,0:T(8,128)S(1)} %collective-permute-done.3.refs_1_, s32[1032,128]{1,0:T(8,128)S(1)} %collective-permute-done.7.refs_2_, ...), custom_call_target="tpu_custom_call", output_to_operand_aliasing={{0}: (5, {}), {1}: (6, {})} | custom-call | flops 536870912 | bytes 4202496 | tf_op jit(solution)/shard_map/channel/pallas_call | solution.py:270
  54.0 0.4 collective-permute-done.4.refs_1_
  54.4 0.9 channel.7
  55.3 7.0 %collective-permute-start.8 = (bf16[32,16,256]{2,1,0:T(8,128)(2,1)S(1)}, bf16[32,16,256]{2,1,0:T(8,128)(2,1)S(1)}, u32[]{:S(2)}, u32[]{:S(2)}) collective-permute-start(bf16[32,16,256]{2,1,0:T(8,128)(2,1)S(1)} %get-tuple-element.45), channel_id=1, source_target_pairs={{0,1},{1,0},{2,3},{3,2},{4,5},{5,4},{6,7},{7,6},{8,9},{9,8},{10,11... | collective-permute-start | bytes 786440 | tf_op jit(solution)/shard_map/ppermute | solution.py:392
  62.3 1.1 %collective-permute-done.8 = bf16[32,16,256]{2,1,0:T(8,128)(2,1)S(1)} collective-permute-done((bf16[32,16,256]{2,1,0:T(8,128)(2,1)S(1)}, bf16[32,16,256]{2,1,0:T(8,128)(2,1)S(1)}, u32[]{:S(2)}, u32[]{:S(2)}) %collective-permute-start.8) | collective-permute-done | bytes 262176 | tf_op jit(solution)/shard_map/ppermute | solution.py:392
  63.5 0.8 add_convert_fusion
  64.3 7.9 %all-to-all-start = ((bf16[32,16,256]{2,1,0:T(8,128)(2,1)}), bf16[32,16,256]{2,1,0:T(8,128)(2,1)S(1)}, u32[]{:S(2)}, u32[]{:S(2)}) async-start(bf16[32,16,256]{2,1,0:T(8,128)(2,1)} %add_convert_fusion), calls=%async_computation | async-start | bytes 524288 | tf_op jit(solution)/shard_map/all_to_all | solution.py:393
  72.2 0.0 copy-done.2
  72.2 0.0 copy-done.5
  72.2 0.0 copy-done.1
  72.2 0.0 copy-start.3
  72.2 0.0 copy-start.4
  72.2 0.9 dense.1
  73.2 8.7 %all-to-all-done.got_ref = bf16[32,16,256]{2,1,0:T(8,128)(2,1)S(1)} async-done(((bf16[32,16,256]{2,1,0:T(8,128)(2,1)}), bf16[32,16,256]{2,1,0:T(8,128)(2,1)S(1)}, u32[]{:S(2)}, u32[]{:S(2)}) %all-to-all-start) | async-done | bytes 262176 | tf_op jit(solution)/shard_map/all_to_all | solution.py:393
  81.9 0.0 copy-done.3
  81.9 0.0 copy-done.4
  81.9 1.4 %token_.1 = (bf16[128,1024]{1,0:T(8,128)(2,1)S(1)}, bf16[128,512]{1,0:T(8,128)(2,1)S(1)}, f32[64,1,128]{2,1,0:T(1,128)}) custom-call(bf16[32,16,256]{2,1,0:T(8,128)(2,1)S(1)} %all-to-all-done.got_ref, bf16[1024,512]{1,0:T(8,128)(2,1)S(1)} %get-tuple-element.46.dense_ref, bf16[2,16,512]{2,1,0:T(8,128)(2,1)S(1)} %bitcast.23, bf16[2,16,512]{2,1,0:T(8,128)(2,1)S(1)} %bitcast.24, ...), custom_call_target="tpu_custom_call" | custom-call | tf_op jit(solution)/shard_map/token/pallas_call | solution.py:320
  83.2 8.3 %all-to-all-start.1 = ((f32[64,1,128]{2,1,0:T(1,128)}), f32[64,1,128]{2,1,0:T(1,128)S(1)}, u32[]{:S(2)}, u32[]{:S(2)}) async-start(f32[64,1,128]{2,1,0:T(1,128)} %get-tuple-element.51), calls=%async_computation.1 | async-start | bytes 65536 | tf_op jit(solution)/shard_map/all_to_all | solution.py:395
  91.5 1.0 %back.1 = bf16[128,1024]{1,0:T(8,128)(2,1)} custom-call(bf16[128,1024]{1,0:T(8,128)(2,1)S(1)} %get-tuple-element.48.columns_ref, bf16[128,512]{1,0:T(8,128)(2,1)S(1)} %get-tuple-element.49.mid_ref, bf16[512,1024]{1,0:T(8,128)(2,1)S(1)} %get-tuple-element.50.dense_ref), custom_call_target="tpu_custom_call" | custom-call | tf_op jit(solution)/shard_map/back/pallas_call | solution.py:338
  92.5 8.3 %all-to-all-done.1 = f32[64,1,128]{2,1,0:T(1,128)S(1)} async-done(((f32[64,1,128]{2,1,0:T(1,128)}), f32[64,1,128]{2,1,0:T(1,128)S(1)}, u32[]{:S(2)}, u32[]{:S(2)}) %all-to-all-start.1) | async-done | bytes 32800 | tf_op jit(solution)/shard_map/all_to_all | solution.py:395
  100.8 0.6 reduce_sum.9
  (5 shorter events, 0.0 us)
Async XLA Ops:
  3.0 11.4 %copy-start.8 = (bf16[16,8,1024]{2,1,0:T(8,128)(2,1)S(1)}, bf16[16,8,1024]{2,1,0:T(8,128)(2,1)}, u32[]{:S(2)}) copy-start(bf16[16,8,1024]{2,1,0:T(8,128)(2,1)} %param.12) | copy-start | bytes 786436
  3.0 14.5 %collective-permute-start = (s32[1032,128]{1,0:T(8,128)}, s32[1032,128]{1,0:T(8,128)S(1)}, u32[]{:S(2)}, u32[]{:S(2)}) collective-permute-start(s32[1032,128]{1,0:T(8,128)} %pack.2.refs_3_), channel_id=1, source_target_pairs={{0,64},{64,128},{128,192},{192,256},{256,320},{320,384},{384,448},... | collective-permute-start | bytes 1585160 | tf_op jit(solution)/shard_map/ppermute | solution.py:368
  11.4 15.0 %collective-permute-start.5 = (s32[1032,128]{1,0:T(8,128)}, s32[1032,128]{1,0:T(8,128)S(1)}, u32[]{:S(2)}, u32[]{:S(2)}) collective-permute-start(s32[1032,128]{1,0:T(8,128)} %pack.3), channel_id=1, source_target_pairs={{0,64},{64,128},{128,192},{192,256},{256,320},{320,384},{384,448},... | collective-permute-start | bytes 1585160 | tf_op jit(solution)/shard_map/ppermute | solution.py:368
  15.2 32.8 %copy-start = (s32[1032,128]{1,0:T(8,128)S(1)}, s32[1032,128]{1,0:T(8,128)}, u32[]{:S(2)}) copy-start(s32[1032,128]{1,0:T(8,128)} %pack.2.refs_3_) | copy-start | bytes 1585156
  17.5 30.6 %copy-start.7 = (f32[1024]{0:T(1024)S(1)}, f32[1024]{0:T(1024)}, u32[]{:S(2)}) copy-start(f32[1024]{0:T(1024)} %param.14) | copy-start | bytes 12292
  17.5 13.7 %collective-permute-start.1 = (s32[1032,128]{1,0:T(8,128)S(1)}, s32[1032,128]{1,0:T(8,128)S(1)}, u32[]{:S(2)}, u32[]{:S(2)}) collective-permute-start(s32[1032,128]{1,0:T(8,128)S(1)} %collective-permute-done.refs_1_), channel_id=1, source_target_pairs={{0,64},{64,128},{128,192},{192,256},{256,320},{320,384},{384,448},... | collective-permute-start | bytes 1585160 | tf_op jit(solution)/shard_map/ppermute | solution.py:368
  20.6 10.6 %collective-permute-start.2 = (bf16[128,16,128]{2,1,0:T(8,128)(2,1)}, bf16[128,16,128]{2,1,0:T(8,128)(2,1)S(1)}, u32[]{:S(2)}, u32[]{:S(2)}) collective-permute-start(bf16[128,16,128]{2,1,0:T(8,128)(2,1)} %get-tuple-element.32), channel_id=1, source_target_pairs={{0,1},{1,0},{2,3},{3,2},{4,5},{5,4},{6,7},{7,6},{8,9},{9,8},{10,11... | collective-permute-start | bytes 1572872 | tf_op jit(solution)/shard_map/ppermute | solution.py:378
  26.4 11.0 %collective-permute-start.6 = (s32[1032,128]{1,0:T(8,128)S(1)}, s32[1032,128]{1,0:T(8,128)S(1)}, u32[]{:S(2)}, u32[]{:S(2)}) collective-permute-start(s32[1032,128]{1,0:T(8,128)S(1)} %collective-permute-done.5.refs_2_), channel_id=1, source_target_pairs={{0,64},{64,128},{128,192},{192,256},{256,320},{320,384},{384,448},... | collective-permute-start | bytes 1585160 | tf_op jit(solution)/shard_map/ppermute | solution.py:368
  31.3 11.8 %collective-permute-start.3 = (s32[1032,128]{1,0:T(8,128)S(1)}, s32[1032,128]{1,0:T(8,128)S(1)}, u32[]{:S(2)}, u32[]{:S(2)}) collective-permute-start(s32[1032,128]{1,0:T(8,128)S(1)} %collective-permute-done.1.refs_1_), channel_id=1, source_target_pairs={{0,64},{64,128},{128,192},{192,256},{256,320},{320,384},{384,448},... | collective-permute-start | bytes 1585160 | tf_op jit(solution)/shard_map/ppermute | solution.py:368
  37.4 15.2 %collective-permute-start.7 = (s32[1032,128]{1,0:T(8,128)S(1)}, s32[1032,128]{1,0:T(8,128)S(1)}, u32[]{:S(2)}, u32[]{:S(2)}) collective-permute-start(s32[1032,128]{1,0:T(8,128)S(1)} %collective-permute-done.6.refs_2_), channel_id=1, source_target_pairs={{0,64},{64,128},{128,192},{192,256},{256,320},{320,384},{384,448},... | collective-permute-start | bytes 1585160 | tf_op jit(solution)/shard_map/ppermute | solution.py:368
  43.0 11.3 %collective-permute-start.4 = (s32[1032,128]{1,0:T(8,128)S(1)}, s32[1032,128]{1,0:T(8,128)S(1)}, u32[]{:S(2)}, u32[]{:S(2)}) collective-permute-start(s32[1032,128]{1,0:T(8,128)S(1)} %collective-permute-done.3.refs_1_), channel_id=1, source_target_pairs={{0,64},{64,128},{128,192},{192,256},{256,320},{320,384},{384,448},... | collective-permute-start | bytes 1585160 | tf_op jit(solution)/shard_map/ppermute | solution.py:368
  48.1 1.0 %copy-start.6 = (bf16[128,16,128]{2,1,0:T(8,128)(2,1)S(1)}, bf16[128,16,128]{2,1,0:T(8,128)(2,1)}, u32[]{:S(2)}) copy-start(bf16[128,16,128]{2,1,0:T(8,128)(2,1)} %get-tuple-element.34.refs_5_) | copy-start | bytes 1572868
  55.3 8.2 %collective-permute-start.8 = (bf16[32,16,256]{2,1,0:T(8,128)(2,1)S(1)}, bf16[32,16,256]{2,1,0:T(8,128)(2,1)S(1)}, u32[]{:S(2)}, u32[]{:S(2)}) collective-permute-start(bf16[32,16,256]{2,1,0:T(8,128)(2,1)S(1)} %get-tuple-element.45), channel_id=1, source_target_pairs={{0,1},{1,0},{2,3},{3,2},{4,5},{5,4},{6,7},{7,6},{8,9},{9,8},{10,11... | collective-permute-start | bytes 786440 | tf_op jit(solution)/shard_map/ppermute | solution.py:392
  63.5 8.7 %copy-start.2 = (bf16[16,128,128]{2,1,0:T(8,128)(2,1)S(1)}, bf16[16,128,128]{2,1,0:T(8,128)(2,1)}, u32[]{:S(2)}) copy-start(bf16[16,128,128]{2,1,0:T(8,128)(2,1)} %out_ref.1) | copy-start | bytes 1572868
  63.5 8.7 %copy-start.5 = (s32[16]{0:T(128)S(1)}, s32[16]{0:T(128)}, u32[]{:S(2)}) copy-start(s32[16]{0:T(128)} %cells_ref.1) | copy-start | bytes 196
  64.3 7.9 %copy-start.1 = (bf16[16,128,128]{2,1,0:T(8,128)(2,1)S(1)}, bf16[16,128,128]{2,1,0:T(8,128)(2,1)}, u32[]{:S(2)}) copy-start(bf16[16,128,128]{2,1,0:T(8,128)(2,1)} %in_ref.1) | copy-start | bytes 1572868
  64.3 17.6 %all-to-all-start = ((bf16[32,16,256]{2,1,0:T(8,128)(2,1)}), bf16[32,16,256]{2,1,0:T(8,128)(2,1)S(1)}, u32[]{:S(2)}, u32[]{:S(2)}) async-start(bf16[32,16,256]{2,1,0:T(8,128)(2,1)} %add_convert_fusion), calls=%async_computation | async-start | bytes 524288 | tf_op jit(solution)/shard_map/all_to_all | solution.py:393
  72.2 9.7 %copy-start.3 = (bf16[2,512,1,16]{1,3,2,0:T(8,128)(2,1)S(1)}, bf16[2,512,1,16]{1,3,2,0:T(8,128)(2,1)}, u32[]{:S(2)}) copy-start(bf16[2,512,1,16]{1,3,2,0:T(8,128)(2,1)} %param.22) | copy-start | bytes 98308
  72.2 9.6 %copy-start.4 = (bf16[2,512,1,16]{1,3,2,0:T(8,128)(2,1)S(1)}, bf16[2,512,1,16]{1,3,2,0:T(8,128)(2,1)}, u32[]{:S(2)}) copy-start(bf16[2,512,1,16]{1,3,2,0:T(8,128)(2,1)} %param.23) | copy-start | bytes 98308
  83.2 17.6 %all-to-all-start.1 = ((f32[64,1,128]{2,1,0:T(1,128)}), f32[64,1,128]{2,1,0:T(1,128)S(1)}, u32[]{:S(2)}, u32[]{:S(2)}) async-start(f32[64,1,128]{2,1,0:T(1,128)} %get-tuple-element.51), calls=%async_computation.1 | async-start | bytes 65536 | tf_op jit(solution)/shard_map/all_to_all | solution.py:395

commit v16 on v13

--- a/solution.py
+++ b/solution.py
@@ -359,8 +359,8 @@
     keep_part, send_part = share(
         core, row, jnp.swapaxes(lam, 0, 1), *(b.reshape(2, tok_dev, CH) for b in bounds)
     )
-    words, send_part = lax.optimization_barrier((first[0], send_part))
-    second = forward((words, first[1]), ahead + behind)
+    words, send_part = lax.optimization_barrier((first[1], send_part))
+    second = forward((first[0], words), ahead + behind)
     other_part = lax.ppermute(send_part, "core", SWAP)
     words, other_part = lax.optimization_barrier((second[0], other_part))
     third = forward((words, second[1]), ahead + behind)

time: 102 us -> 104 us (1.020)
  waiting for transfers between devices: 23.5 us -> 24.8 us
    ppermute x1, starting transfers between devices: 7.03 us -> 4.71 us  [on_device(): summed = (keep + lax.ppermute(send, 'core', SWAP).astype(F32)).astype(BF16)]
    ppermute x7, starting transfers between devices: 28.8 us -> 30.3 us  [forward(): return tuple((lax.ppermute(w, ('rows', 'core'), pairs) for w in words))]
    ppermute x7, waiting for transfers between devices: 5.29 us -> 6.57 us  [forward(): return tuple((lax.ppermute(w, ('rows', 'core'), pairs) for w in words))]
    all_to_all x1, starting transfers between devices: 7.89 us -> 9.02 us  [on_device(): got = lax.all_to_all(summed, ('x', 'z'), 0, 0, tiled=True)]
  transfers between devices with their start and end apart: 11 -> 11, of which waited for: 6 -> 7; matrix products, arithmetic and copies ran while one was open for 1% -> 1% of each run, Pallas kernels for 11% -> 11%
where the time goes in v16:
time: 104 us; the launch traced here: 103 us
  starting transfers between devices  58.8 us (57%)
  waiting for transfers between devices  24.8 us (24%)
  Pallas kernels  15.7 us (15%)
  local copies, waits for them, and re-layouts  1.92 us (2%)
  other arithmetic  1.39 us (1%)
    ppermute x7, starting transfers between devices, forward(): return tuple((lax.ppermute(w, ('rows', 'core'), pairs) for w in words))  30.3 us
    all_to_all x1, starting transfers between devices, on_device(): got = lax.all_to_all(summed, ('x', 'z'), 0, 0, tiled=True)  9.02 us
    all_to_all x1, waiting for transfers between devices, on_device(): got = lax.all_to_all(summed, ('x', 'z'), 0, 0, tiled=True)  8.7 us
    all_to_all x1, waiting for transfers between devices, on_device(): all_bias = lax.all_to_all(own_bias, MP, 0, 0, tiled=True)  8.36 us
    all_to_all x1, starting transfers between devices, on_device(): all_bias = lax.all_to_all(own_bias, MP, 0, 0, tiled=True)  8.29 us
    ppermute x7, waiting for transfers between devices, forward(): return tuple((lax.ppermute(w, ('rows', 'core'), pairs) for w in words))  6.57 us
    ppermute x1, starting transfers between devices, on_device(): other_part = lax.ppermute(send_part, 'core', SWAP)  6.52 us
    pallas_call x4, Pallas kernels, channel_part(): pl.pallas_call(functools.partial(channel_kernel, step), out_shape=out_sha...  5.66 us
  transfers between devices with their start and end apart: 11, of which 7 were waited for; matrix products, arithmetic and copies ran while one was open for 1% of the time, Pallas kernels for 11%

profile of v16, /device:TPU:1, one launch (start us, length us, event | category | flops | bytes accessed | tf_op | source)
XLA Modules:
  0.0 103.5 jit_solution(10378225262984499161)
XLA Ops:
  0.6 2.2 %pack.2.refs_3_ = s32[1032,128]{1,0:T(8,128)} custom-call(s32[1]{0:T(128)} %bitcast.core_ref.refs_0_, bf16[1024,512]{1,0:T(8,128)(2,1)} %down_hbm.3, bf16[512,1024]{1,0:T(8,128)(2,1)} %up_hbm.3, f32[1,512]{1,0:T(1,128)} %bitcast.30), custom_call_target="tpu_custom_call" | custom-call | tf_op jit(solution)/shard_map/pack/pallas_call | solution.py:76
  2.9 0.0 copy-start.8
  2.9 6.1 %collective-permute-start = (s32[1032,128]{1,0:T(8,128)}, s32[1032,128]{1,0:T(8,128)S(1)}, u32[]{:S(2)}, u32[]{:S(2)}) collective-permute-start(s32[1032,128]{1,0:T(8,128)} %pack.2.refs_3_), channel_id=1, source_target_pairs={{0,64},{64,128},{128,192},{192,256},{256,320},{320,384},{384,448},... | collective-permute-start | bytes 1585160 | tf_op jit(solution)/shard_map/ppermute | solution.py:354
  9.0 2.2 %pack.3 = s32[1032,128]{1,0:T(8,128)} custom-call(s32[1]{0:T(128)} %bitcast.core_ref.refs_0_, bf16[1024,512]{1,0:T(8,128)(2,1)} %down_hbm.3, bf16[512,1024]{1,0:T(8,128)(2,1)} %up_hbm.3, f32[1,512]{1,0:T(1,128)} %bitcast.31), custom_call_target="tpu_custom_call" | custom-call | tf_op jit(solution)/shard_map/pack/pallas_call | solution.py:76
  11.2 3.0 %collective-permute-start.2 = (s32[1032,128]{1,0:T(8,128)}, s32[1032,128]{1,0:T(8,128)S(1)}, u32[]{:S(2)}, u32[]{:S(2)}) collective-permute-start(s32[1032,128]{1,0:T(8,128)} %pack.3), channel_id=1, source_target_pairs={{0,64},{64,128},{128,192},{192,256},{256,320},{320,384},{384,448},... | collective-permute-start | bytes 1585160 | tf_op jit(solution)/shard_map/ppermute | solution.py:354
  14.2 1.2 %collective-permute-done.refs_1_ = s32[1032,128]{1,0:T(8,128)S(1)} collective-permute-done((s32[1032,128]{1,0:T(8,128)}, s32[1032,128]{1,0:T(8,128)S(1)}, u32[]{:S(2)}, u32[]{:S(2)}) %collective-permute-start) | collective-permute-done | bytes 528416 | tf_op jit(solution)/shard_map/ppermute | solution.py:354
  15.4 4.9 %collective-permute-start.1 = (s32[1032,128]{1,0:T(8,128)S(1)}, s32[1032,128]{1,0:T(8,128)S(1)}, u32[]{:S(2)}, u32[]{:S(2)}) collective-permute-start(s32[1032,128]{1,0:T(8,128)S(1)} %collective-permute-done.refs_1_), channel_id=1, source_target_pairs={{0,64},{64,128},{128,192},{192,256},{256,320},{320,384},{384,448},... | collective-permute-start | bytes 1585160 | tf_op jit(solution)/shard_map/ppermute | solution.py:354
  20.3 0.0 copy-done.8
  20.4 0.9 copy.22
  21.2 2.3 %share.1 = (bf16[128,16,128]{2,1,0:T(8,128)(2,1)}, bf16[128,16,128]{2,1,0:T(8,128)(2,1)}) custom-call(s32[1]{0:T(128)} %bitcast.core_ref.refs_0_, s32[1]{0:T(128)} %bitcast.2.row_ref, bf16[8,16,1024]{2,1,0:T(8,128)(2,1)} %bitcast.26, bf16[2,16,4096]{2,1,0:T(8,128)(2,1)} %bitcast.27, bf16[2,16,4096]{2,1,0:T(8,128)(2,1)} %bitcast.28), custom_call_target="tpu_custom_call" | custom-call | tf_op jit(solution)/shard_map/share/pallas_call | solution.py:157
  23.5 0.0 collective-permute-done.2.refs_2_
  23.5 6.5 %collective-permute-start.3 = (bf16[128,16,128]{2,1,0:T(8,128)(2,1)}, bf16[128,16,128]{2,1,0:T(8,128)(2,1)S(1)}, u32[]{:S(2)}, u32[]{:S(2)}) collective-permute-start(bf16[128,16,128]{2,1,0:T(8,128)(2,1)} %get-tuple-element.31), channel_id=1, source_target_pairs={{0,1},{1,0},{2,3},{3,2},{4,5},{5,4},{6,7},{7,6},{8,9},{9,8},{10,11... | collective-permute-start | bytes 1572872 | tf_op jit(solution)/shard_map/ppermute | solution.py:364
  30.0 4.4 %collective-permute-start.6 = (s32[1032,128]{1,0:T(8,128)S(1)}, s32[1032,128]{1,0:T(8,128)S(1)}, u32[]{:S(2)}, u32[]{:S(2)}) collective-permute-start(s32[1032,128]{1,0:T(8,128)S(1)} %collective-permute-done.2.refs_2_), channel_id=1, source_target_pairs={{0,64},{64,128},{128,192},{192,256},{256,320},{320,384},{384,448},... | collective-permute-start | bytes 1585160 | tf_op jit(solution)/shard_map/ppermute | solution.py:354
  34.4 0.0 collective-permute-done.3.refs_6_
  34.4 0.0 collective-permute-done.1.refs_1_
  34.4 1.9 %collective-permute-start.4 = (s32[1032,128]{1,0:T(8,128)S(1)}, s32[1032,128]{1,0:T(8,128)S(1)}, u32[]{:S(2)}, u32[]{:S(2)}) collective-permute-start(s32[1032,128]{1,0:T(8,128)S(1)} %collective-permute-done.1.refs_1_), channel_id=1, source_target_pairs={{0,64},{64,128},{128,192},{192,256},{256,320},{320,384},{384,448},... | collective-permute-start | bytes 1585160 | tf_op jit(solution)/shard_map/ppermute | solution.py:354
  36.3 4.2 %collective-permute-done.6.refs_2_ = s32[1032,128]{1,0:T(8,128)S(1)} collective-permute-done((s32[1032,128]{1,0:T(8,128)S(1)}, s32[1032,128]{1,0:T(8,128)S(1)}, u32[]{:S(2)}, u32[]{:S(2)}) %collective-permute-start.6) | collective-permute-done | bytes 528416 | tf_op jit(solution)/shard_map/ppermute | solution.py:354
  40.5 5.0 %collective-permute-start.7 = (s32[1032,128]{1,0:T(8,128)S(1)}, s32[1032,128]{1,0:T(8,128)S(1)}, u32[]{:S(2)}, u32[]{:S(2)}) collective-permute-start(s32[1032,128]{1,0:T(8,128)S(1)} %collective-permute-done.6.refs_2_), channel_id=1, source_target_pairs={{0,64},{64,128},{128,192},{192,256},{256,320},{320,384},{384,448},... | collective-permute-start | bytes 1585160 | tf_op jit(solution)/shard_map/ppermute | solution.py:354
  45.6 0.6 collective-permute-done.4.refs_1_
  46.2 5.0 %collective-permute-start.5 = (s32[1032,128]{1,0:T(8,128)S(1)}, s32[1032,128]{1,0:T(8,128)S(1)}, u32[]{:S(2)}, u32[]{:S(2)}) collective-permute-start(s32[1032,128]{1,0:T(8,128)S(1)} %collective-permute-done.4.refs_1_), channel_id=1, source_target_pairs={{0,64},{64,128},{128,192},{192,256},{256,320},{320,384},{384,448},... | collective-permute-start | bytes 1585160 | tf_op jit(solution)/shard_map/ppermute | solution.py:354
  51.2 0.0 copy-done
  51.2 0.0 copy-done.7
  51.3 0.0 copy-start.6
  51.3 1.0 copy-done.6
  52.3 2.1 %channel.4 = (f32[256,1024]{1,0:T(8,128)S(1)}, f32[8,8,128]{2,1,0:T(8,128)S(1)}, bf16[256,1024]{1,0:T(8,128)(2,1)S(1)}, bf16[4,4,32,512]{3,2,1,0:T(8,128)(2,1)S(1)}) custom-call(s32[1]{0:T(128)} %bitcast.core_ref.refs_0_, s32[1032,128]{1,0:T(8,128)S(1)} %collective-permute-done.refs_1_, s32[1032,128]{1,0:T(8,128)S(1)} %collective-permute-done.2.refs_2_, ...), custom_call_target="tpu_custom_call" | custom-call | flops 805306368 | bytes 4202496 | tf_op jit(solution)/shard_map/channel/pallas_call | solution.py:256
  54.4 1.3 %channel.5 = (f32[256,1024]{1,0:T(8,128)S(1)}, f32[8,8,128]{2,1,0:T(8,128)S(1)}) custom-call(s32[1]{0:T(128)} %bitcast.core_ref.refs_0_, s32[1032,128]{1,0:T(8,128)S(1)} %collective-permute-done.1.refs_1_, s32[1032,128]{1,0:T(8,128)S(1)} %collective-permute-done.6.refs_2_, ...), custom_call_target="tpu_custom_call", output_to_operand_aliasing={{0}: (5, {}), {1}: (6, {})} | custom-call | flops 536870912 | bytes 4202496 | tf_op jit(solution)/shard_map/channel/pallas_call | solution.py:256
  55.7 0.0 collective-permute-done.7.refs_2_
  55.7 1.3 %channel.6 = (f32[256,1024]{1,0:T(8,128)S(1)}, f32[8,8,128]{2,1,0:T(8,128)S(1)}) custom-call(s32[1]{0:T(128)} %bitcast.core_ref.refs_0_, s32[1032,128]{1,0:T(8,128)S(1)} %collective-permute-done.4.refs_1_, s32[1032,128]{1,0:T(8,128)S(1)} %collective-permute-done.7.refs_2_, ...), custom_call_target="tpu_custom_call", output_to_operand_aliasing={{0}: (5, {}), {1}: (6, {})} | custom-call | flops 536870912 | bytes 4202496 | tf_op jit(solution)/shard_map/channel/pallas_call | solution.py:256
  57.0 0.5 collective-permute-done.5.refs_1_
  57.5 0.9 channel.7
  58.5 4.7 %collective-permute-start.8 = (bf16[32,16,256]{2,1,0:T(8,128)(2,1)S(1)}, bf16[32,16,256]{2,1,0:T(8,128)(2,1)S(1)}, u32[]{:S(2)}, u32[]{:S(2)}) collective-permute-start(bf16[32,16,256]{2,1,0:T(8,128)(2,1)S(1)} %get-tuple-element.45), channel_id=1, source_target_pairs={{0,1},{1,0},{2,3},{3,2},{4,5},{5,4},{6,7},{7,6},{8,9},{9,8},{10,11... | collective-permute-start | bytes 786440 | tf_op jit(solution)/shard_map/ppermute | solution.py:378
  63.2 1.1 %collective-permute-done.8 = bf16[32,16,256]{2,1,0:T(8,128)(2,1)S(1)} collective-permute-done((bf16[32,16,256]{2,1,0:T(8,128)(2,1)S(1)}, bf16[32,16,256]{2,1,0:T(8,128)(2,1)S(1)}, u32[]{:S(2)}, u32[]{:S(2)}) %collective-permute-start.8) | collective-permute-done | bytes 262176 | tf_op jit(solution)/shard_map/ppermute | solution.py:378
  64.3 0.8 add_convert_fusion
  65.1 9.0 %all-to-all-start = ((bf16[32,16,256]{2,1,0:T(8,128)(2,1)}), bf16[32,16,256]{2,1,0:T(8,128)(2,1)S(1)}, u32[]{:S(2)}, u32[]{:S(2)}) async-start(bf16[32,16,256]{2,1,0:T(8,128)(2,1)} %add_convert_fusion), calls=%async_computation | async-start | bytes 524288 | tf_op jit(solution)/shard_map/all_to_all | solution.py:379
  74.2 0.0 copy-done.2
  74.2 0.0 copy-done.5
  74.2 0.0 copy-done.1
  74.2 0.0 copy-start.3
  74.2 0.0 copy-start.4
  74.2 0.9 dense.1
  75.1 8.7 %all-to-all-done.got_ref = bf16[32,16,256]{2,1,0:T(8,128)(2,1)S(1)} async-done(((bf16[32,16,256]{2,1,0:T(8,128)(2,1)}), bf16[32,16,256]{2,1,0:T(8,128)(2,1)S(1)}, u32[]{:S(2)}, u32[]{:S(2)}) %all-to-all-start) | async-done | bytes 262176 | tf_op jit(solution)/shard_map/all_to_all | solution.py:379
  83.8 0.0 copy-done.3
  83.8 0.0 copy-done.4
  83.8 1.4 %token_.1 = (bf16[128,1024]{1,0:T(8,128)(2,1)S(1)}, bf16[128,512]{1,0:T(8,128)(2,1)S(1)}, f32[64,1,128]{2,1,0:T(1,128)}) custom-call(bf16[32,16,256]{2,1,0:T(8,128)(2,1)S(1)} %all-to-all-done.got_ref, bf16[1024,512]{1,0:T(8,128)(2,1)S(1)} %get-tuple-element.46.dense_ref, bf16[2,16,512]{2,1,0:T(8,128)(2,1)S(1)} %bitcast.23, bf16[2,16,512]{2,1,0:T(8,128)(2,1)S(1)} %bitcast.24, ...), custom_call_target="tpu_custom_call" | custom-call | tf_op jit(solution)/shard_map/token/pallas_call | solution.py:306
  85.2 8.3 %all-to-all-start.1 = ((f32[64,1,128]{2,1,0:T(1,128)}), f32[64,1,128]{2,1,0:T(1,128)S(1)}, u32[]{:S(2)}, u32[]{:S(2)}) async-start(f32[64,1,128]{2,1,0:T(1,128)} %get-tuple-element.51), calls=%async_computation.1 | async-start | bytes 65536 | tf_op jit(solution)/shard_map/all_to_all | solution.py:381
  93.5 1.0 back.1
  94.5 8.4 %all-to-all-done.1 = f32[64,1,128]{2,1,0:T(1,128)S(1)} async-done(((f32[64,1,128]{2,1,0:T(1,128)}), f32[64,1,128]{2,1,0:T(1,128)S(1)}, u32[]{:S(2)}, u32[]{:S(2)}) %all-to-all-start.1) | async-done | bytes 32800 | tf_op jit(solution)/shard_map/all_to_all | solution.py:381
  102.9 0.6 reduce_sum.9
  (5 shorter events, 0.0 us)
Async XLA Ops:
  2.9 17.5 %copy-start.8 = (bf16[16,8,1024]{2,1,0:T(8,128)(2,1)S(1)}, bf16[16,8,1024]{2,1,0:T(8,128)(2,1)}, u32[]{:S(2)}) copy-start(bf16[16,8,1024]{2,1,0:T(8,128)(2,1)} %param.12) | copy-start | bytes 786436
  2.9 12.5 %collective-permute-start = (s32[1032,128]{1,0:T(8,128)}, s32[1032,128]{1,0:T(8,128)S(1)}, u32[]{:S(2)}, u32[]{:S(2)}) collective-permute-start(s32[1032,128]{1,0:T(8,128)} %pack.2.refs_3_), channel_id=1, source_target_pairs={{0,64},{64,128},{128,192},{192,256},{256,320},{320,384},{384,448},... | collective-permute-start | bytes 1585160 | tf_op jit(solution)/shard_map/ppermute | solution.py:354
  11.2 12.3 %collective-permute-start.2 = (s32[1032,128]{1,0:T(8,128)}, s32[1032,128]{1,0:T(8,128)S(1)}, u32[]{:S(2)}, u32[]{:S(2)}) collective-permute-start(s32[1032,128]{1,0:T(8,128)} %pack.3), channel_id=1, source_target_pairs={{0,64},{64,128},{128,192},{192,256},{256,320},{320,384},{384,448},... | collective-permute-start | bytes 1585160 | tf_op jit(solution)/shard_map/ppermute | solution.py:354
  15.4 19.0 %collective-permute-start.1 = (s32[1032,128]{1,0:T(8,128)S(1)}, s32[1032,128]{1,0:T(8,128)S(1)}, u32[]{:S(2)}, u32[]{:S(2)}) collective-permute-start(s32[1032,128]{1,0:T(8,128)S(1)} %collective-permute-done.refs_1_), channel_id=1, source_target_pairs={{0,64},{64,128},{128,192},{192,256},{256,320},{320,384},{384,448},... | collective-permute-start | bytes 1585160 | tf_op jit(solution)/shard_map/ppermute | solution.py:354
  21.2 30.0 %copy-start = (s32[1032,128]{1,0:T(8,128)S(1)}, s32[1032,128]{1,0:T(8,128)}, u32[]{:S(2)}) copy-start(s32[1032,128]{1,0:T(8,128)} %pack.2.refs_3_) | copy-start | bytes 1585156
  23.5 27.8 %copy-start.7 = (f32[1024]{0:T(1024)S(1)}, f32[1024]{0:T(1024)}, u32[]{:S(2)}) copy-start(f32[1024]{0:T(1024)} %param.14) | copy-start | bytes 12292
  23.5 10.9 %collective-permute-start.3 = (bf16[128,16,128]{2,1,0:T(8,128)(2,1)}, bf16[128,16,128]{2,1,0:T(8,128)(2,1)S(1)}, u32[]{:S(2)}, u32[]{:S(2)}) collective-permute-start(bf16[128,16,128]{2,1,0:T(8,128)(2,1)} %get-tuple-element.31), channel_id=1, source_target_pairs={{0,1},{1,0},{2,3},{3,2},{4,5},{5,4},{6,7},{7,6},{8,9},{9,8},{10,11... | collective-permute-start | bytes 1572872 | tf_op jit(solution)/shard_map/ppermute | solution.py:364
  30.0 10.5 %collective-permute-start.6 = (s32[1032,128]{1,0:T(8,128)S(1)}, s32[1032,128]{1,0:T(8,128)S(1)}, u32[]{:S(2)}, u32[]{:S(2)}) collective-permute-start(s32[1032,128]{1,0:T(8,128)S(1)} %collective-permute-done.2.refs_2_), channel_id=1, source_target_pairs={{0,64},{64,128},{128,192},{192,256},{256,320},{320,384},{384,448},... | collective-permute-start | bytes 1585160 | tf_op jit(solution)/shard_map/ppermute | solution.py:354
  34.4 11.8 %collective-permute-start.4 = (s32[1032,128]{1,0:T(8,128)S(1)}, s32[1032,128]{1,0:T(8,128)S(1)}, u32[]{:S(2)}, u32[]{:S(2)}) collective-permute-start(s32[1032,128]{1,0:T(8,128)S(1)} %collective-permute-done.1.refs_1_), channel_id=1, source_target_pairs={{0,64},{64,128},{128,192},{192,256},{256,320},{320,384},{384,448},... | collective-permute-start | bytes 1585160 | tf_op jit(solution)/shard_map/ppermute | solution.py:354
  40.5 15.2 %collective-permute-start.7 = (s32[1032,128]{1,0:T(8,128)S(1)}, s32[1032,128]{1,0:T(8,128)S(1)}, u32[]{:S(2)}, u32[]{:S(2)}) collective-permute-start(s32[1032,128]{1,0:T(8,128)S(1)} %collective-permute-done.6.refs_2_), channel_id=1, source_target_pairs={{0,64},{64,128},{128,192},{192,256},{256,320},{320,384},{384,448},... | collective-permute-start | bytes 1585160 | tf_op jit(solution)/shard_map/ppermute | solution.py:354
  46.2 11.3 %collective-permute-start.5 = (s32[1032,128]{1,0:T(8,128)S(1)}, s32[1032,128]{1,0:T(8,128)S(1)}, u32[]{:S(2)}, u32[]{:S(2)}) collective-permute-start(s32[1032,128]{1,0:T(8,128)S(1)} %collective-permute-done.4.refs_1_), channel_id=1, source_target_pairs={{0,64},{64,128},{128,192},{192,256},{256,320},{320,384},{384,448},... | collective-permute-start | bytes 1585160 | tf_op jit(solution)/shard_map/ppermute | solution.py:354
  51.3 1.0 %copy-start.6 = (bf16[128,16,128]{2,1,0:T(8,128)(2,1)S(1)}, bf16[128,16,128]{2,1,0:T(8,128)(2,1)}, u32[]{:S(2)}) copy-start(bf16[128,16,128]{2,1,0:T(8,128)(2,1)} %get-tuple-element.33.refs_5_) | copy-start | bytes 1572868
  58.5 5.9 %collective-permute-start.8 = (bf16[32,16,256]{2,1,0:T(8,128)(2,1)S(1)}, bf16[32,16,256]{2,1,0:T(8,128)(2,1)S(1)}, u32[]{:S(2)}, u32[]{:S(2)}) collective-permute-start(bf16[32,16,256]{2,1,0:T(8,128)(2,1)S(1)} %get-tuple-element.45), channel_id=1, source_target_pairs={{0,1},{1,0},{2,3},{3,2},{4,5},{5,4},{6,7},{7,6},{8,9},{9,8},{10,11... | collective-permute-start | bytes 786440 | tf_op jit(solution)/shard_map/ppermute | solution.py:378
  64.3 9.8 %copy-start.2 = (bf16[16,128,128]{2,1,0:T(8,128)(2,1)S(1)}, bf16[16,128,128]{2,1,0:T(8,128)(2,1)}, u32[]{:S(2)}) copy-start(bf16[16,128,128]{2,1,0:T(8,128)(2,1)} %out_ref.1) | copy-start | bytes 1572868
  64.3 9.8 %copy-start.5 = (s32[16]{0:T(128)S(1)}, s32[16]{0:T(128)}, u32[]{:S(2)}) copy-start(s32[16]{0:T(128)} %cells_ref.1) | copy-start | bytes 196
  65.1 9.1 %copy-start.1 = (bf16[16,128,128]{2,1,0:T(8,128)(2,1)S(1)}, bf16[16,128,128]{2,1,0:T(8,128)(2,1)}, u32[]{:S(2)}) copy-start(bf16[16,128,128]{2,1,0:T(8,128)(2,1)} %in_ref.1) | copy-start | bytes 1572868
  65.1 18.7 %all-to-all-start = ((bf16[32,16,256]{2,1,0:T(8,128)(2,1)}), bf16[32,16,256]{2,1,0:T(8,128)(2,1)S(1)}, u32[]{:S(2)}, u32[]{:S(2)}) async-start(bf16[32,16,256]{2,1,0:T(8,128)(2,1)} %add_convert_fusion), calls=%async_computation | async-start | bytes 524288 | tf_op jit(solution)/shard_map/all_to_all | solution.py:379
  74.2 9.7 %copy-start.3 = (bf16[2,512,1,16]{1,3,2,0:T(8,128)(2,1)S(1)}, bf16[2,512,1,16]{1,3,2,0:T(8,128)(2,1)}, u32[]{:S(2)}) copy-start(bf16[2,512,1,16]{1,3,2,0:T(8,128)(2,1)} %param.22) | copy-start | bytes 98308
  74.2 9.6 %copy-start.4 = (bf16[2,512,1,16]{1,3,2,0:T(8,128)(2,1)S(1)}, bf16[2,512,1,16]{1,3,2,0:T(8,128)(2,1)}, u32[]{:S(2)}) copy-start(bf16[2,512,1,16]{1,3,2,0:T(8,128)(2,1)} %param.23) | copy-start | bytes 98308
  85.2 17.7 %all-to-all-start.1 = ((f32[64,1,128]{2,1,0:T(1,128)}), f32[64,1,128]{2,1,0:T(1,128)S(1)}, u32[]{:S(2)}, u32[]{:S(2)}) async-start(f32[64,1,128]{2,1,0:T(1,128)} %get-tuple-element.51), calls=%async_computation.1 | async-start | bytes 65536 | tf_op jit(solution)/shard_map/all_to_all | solution.py:381
